TPU v7x, 512 devices: a whole 4x4x16 slice. The times are simulated.
512 devices in a mesh: rows: 128 (over y_hi, z, x), cols: 4 (over y_lo, core).
Axes of the slice: x: 4, y: 4 (y_hi: 2, y_lo: 2; y = y_hi * 2 + y_lo), z: 16, core: 2. Of those that a mesh axis runs over, the one named last changes fastest.
Arguments:
- features: bfloat16 [524288, 256], P('rows', 'cols'), may hold values from -6 to 6
- weight: bfloat16 [256, 256], P(None, 'cols'), may hold values from -0.375 to 0.375
- tile_values: bfloat16 [11264, 128, 128], P('rows'), as said below
- tile_rows: int32 [11264], P('rows'), may hold values from 0 to 31
- tile_cols: int32 [11264], P('rows'), may hold values from 0 to 159, as said below
- tile_count: int32 [128], P('rows'), may hold values from 44 to 88, as said below
- cotangent: bfloat16 [524288, 256], P('rows', 'cols'), may hold values from -6 to 6
Outputs:
- output: bfloat16 [524288, 256], P('rows', 'cols')
- feature_grad: bfloat16 [524288, 256], P('rows', 'cols')
- weight_grad: float32 [256, 256], P(None, 'cols')
Inputs may be any that keep to these rules, and one draw needn't show every extreme that they name: `tile_count`: live tile slots of a partition, at least 44; some partition has all 88 slots live in every draw. `tile_cols`: slot s of a partition (counted from the partition's first slot) draws its source from the partition (s mod 5) - 2 steps away around the loop, so c div (32) = s mod 5. `tile_values`: edge weights are zero or positive.
All inputs are finite; a program needn't handle non-finite values.
Results may differ from a plain program's by a relative error of at most 0.02.
Values may be sent and summed in bfloat16 or wider, within the bound.
No kernel may reach another device: no remote copies, remote signals or barrier semaphores. Data moves between devices by JAX's collectives and lax.ppermute only.
A program may use at most 64 MiB of HBM per device.

v0:
```python
import jax
import jax.numpy as jnp
from jax import lax
from jax.sharding import PartitionSpec as P


def passed_along(value, axis, steps):
    count = lax.axis_size(axis)
    pairs = [(source, (source + steps) % count) for source in range(count)]
    return lax.ppermute(value, axis, pairs)


def silu_grad(value):
    sigmoid_val = jax.nn.sigmoid(value)
    return sigmoid_val * (1.0 + value * (1.0 - sigmoid_val))


def local(features, weight, tile_values, tile_rows, tile_cols, tile_count, cotangent):
    node_count, feat_cols = features.shape
    slot_count, tile_size = (tile_values.shape[0], tile_values.shape[1])
    block_count = node_count // tile_size
    block_ids = jnp.arange(block_count, dtype=jnp.int32)
    live_slots = (jnp.arange(slot_count, dtype=jnp.int32) < tile_count[0]).astype(jnp.float32)
    going_down = features
    going_up = features
    lower_blocks = []
    upper_blocks = []
    for section in range(2):
        going_down = passed_along(going_down, "rows", 1)
        lower_blocks.append(going_down)
        going_up = passed_along(going_up, "rows", -1)
        upper_blocks.append(going_up)
    band_rows = jnp.concatenate(
        [lower_blocks[1], lower_blocks[0], features, upper_blocks[0], upper_blocks[1]], 0
    )
    band_rows = band_rows.reshape(5 * block_count, tile_size, feat_cols)
    source = band_rows[tile_cols]
    products = (
        jnp.einsum("tij,tjf->tif", tile_values, source, preferred_element_type=jnp.float32)
        * live_slots[:, None, None]
    )
    row_select = (tile_rows[None, :] == block_ids[:, None]).astype(jnp.float32)
    hidden_part = (
        jnp.einsum("bt,tif->bif", row_select, products)
        .reshape(node_count, feat_cols)
        .astype(jnp.bfloat16)
    )
    hidden = lax.all_gather(hidden_part, "cols", axis=1, tiled=True)
    preact = jnp.dot(hidden, weight, preferred_element_type=jnp.float32)
    output = jax.nn.silu(preact).astype(jnp.bfloat16)
    grad_pre = (cotangent.astype(jnp.float32) * silu_grad(preact)).astype(jnp.bfloat16)
    total_nodes = node_count * lax.axis_size("rows")
    weight_term = lax.dot_general(
        hidden, grad_pre, (((0,), (0,)), ((), ())), preferred_element_type=jnp.float32
    )
    weight_grad = lax.psum(weight_term, "rows") * (1.0 / total_nodes**0.5)
    partial_terms = lax.dot_general(
        grad_pre, weight, (((1,), (1,)), ((), ())), preferred_element_type=jnp.float32
    )
    hidden_grad = lax.psum_scatter(
        partial_terms.astype(jnp.bfloat16), "cols", scatter_dimension=1, tiled=True
    )
    grad_blocks = hidden_grad.reshape(block_count, tile_size, feat_cols)
    grad_source = grad_blocks[tile_rows]
    contrib = (
        jnp.einsum("tji,tjf->tif", tile_values, grad_source, preferred_element_type=jnp.float32)
        * live_slots[:, None, None]
    )
    band_select = (
        tile_cols[None, :] == jnp.arange(5 * block_count, dtype=jnp.int32)[:, None]
    ).astype(jnp.float32)
    outgoing = jnp.einsum("ct,tif->cif", band_select, contrib).reshape(5, node_count, feat_cols)
    moving_up = outgoing[4]
    moving_down = outgoing[0]
    for section in range(2):
        moving_up = passed_along(moving_up.astype(jnp.bfloat16), "rows", 1).astype(moving_up.dtype)
        moving_down = passed_along(moving_down.astype(jnp.bfloat16), "rows", -1).astype(
            moving_down.dtype
        )
        if section == 0:
            moving_up = moving_up + outgoing[3]
            moving_down = moving_down + outgoing[1]
    gathered = outgoing[2] + moving_up + moving_down
    feature_grad = gathered.astype(jnp.bfloat16)
    return (output, feature_grad, weight_grad)


def solution(mesh):
    in_specs = (
        P("rows", "cols"),
        P(None, "cols"),
        P("rows", None, None),
        P("rows"),
        P("rows"),
        P("rows"),
        P("rows", "cols"),
    )
    out_specs = (P("rows", "cols"), P("rows", "cols"), P(None, "cols"))
    return jax.shard_map(local, mesh=mesh, in_specs=in_specs, out_specs=out_specs, check_vma=False)
```

profile of v0, /device:TPU:1, one launch (start us, length us, event | category | flops | bytes accessed | tf_op | source)
XLA Modules:
  0.0 1349.5 jit_solution(18113469015568557949)
XLA Ops:
  7.2 4.2 collective-permute-start
  11.4 14.8 %collective-permute-start.2 = (bf16[4096,64]{0,1:T(8,128)(2,1)}, bf16[4096,64]{0,1:T(8,128)(2,1)S(1)}, u32[]{:S(2)}, u32[]{:S(2)}) collective-permute-start(bf16[4096,64]{0,1:T(8,128)(2,1)} %param.7), channel_id=1, source_target_pairs={{0,508},{4,0},{8,4},{12,8},{16,12},{20,16},{24,20},{28,24},{32,28}... | collective-permute-start | bytes 1572872 | tf_op jit(solution)/shard_map/ppermute | solution.py:10
  26.2 9.9 collective-permute-done
  36.1 1.9 collective-permute-start.1
  39.4 9.1 collective-permute-start.3
  48.5 7.5 collective-permute-done.1
  56.0 1.1 constant_dynamic-update-slice_fusion.2
  57.1 1.0 collective-permute-done.3
  58.2 2.3 copy_bitcast_fusion
  60.4 3.7 gather_fusion
  64.1 3.4 multiply_bitcast_fusion.1
  67.6 1.0 fusion.4
  69.7 32.8 %all-gather.2.cloned.1.call-done = bf16[4096,256]{0,1:T(8,128)(2,1)} async-done(((bf16[4096,64]{0,1:T(8,128)(2,1)}), bf16[4096,256]{0,1:T(8,128)(2,1)}) %all-gather.2.cloned.1.call-update) | async-done | bytes 2097168 | tf_op jit(solution)/shard_map/all_gather | solution.py:48
  102.6 3.2 multiply_convert_fusion
  106.6 2.0 convolution_convert_fusion
  108.7 36.8 %reduce-scatter.2.cloned.1.call-done = bf16[4096,64]{0,1:T(8,128)(2,1)} async-done(((bf16[4096,256]{0,1:T(8,128)(2,1)}), bf16[4096,64]{0,1:T(8,128)(2,1)}) %reduce-scatter.2.cloned.1.call-update) | async-done | bytes 524304 | tf_op jit(solution)/shard_map/reduce_scatter | solution.py:60
  145.5 1.2 copy_bitcast_fusion.4
  146.7 1.9 gather_fusion.1
  148.6 2.3 multiply_bitcast_fusion
  150.9 1.6 fusion.19
  152.7 10.0 collective-permute-start.6
  162.9 1.9 collective-permute-start.4
  164.8 1.3 fusion.17
  166.1 7.4 collective-permute-done.6
  173.6 1.4 fusion.7
  175.0 9.8 collective-permute-start.7
  184.8 1.4 fusion.8
  186.2 1.9 collective-permute-start.5
  188.1 1.4 fusion.20
  189.6 1149.2 %all-reduce.2.cloned.1.call-done = f32[256,64]{0,1:T(8,128)} async-done(((f32[256,64]{0,1:T(8,128)}), f32[256,64]{0,1:T(8,128)}) %all-reduce.2.cloned.1.call-update) | async-done | bytes 65552 | tf_op jit(solution)/shard_map/psum | solution.py:56
  1338.7 1.5 broadcast_multiply_fusion
  1340.2 2.8 fusion.10
  (37 shorter events, 3.3 us)
Async XLA Ops:
  7.2 56.9 %copy-start = (bf16[88,128,128]{2,1,0:T(8,128)(2,1)S(1)}, bf16[88,128,128]{2,1,0:T(8,128)(2,1)}, u32[]{:S(2)}) copy-start(bf16[88,128,128]{2,1,0:T(8,128)(2,1)} %param.9) | copy-start | bytes 8650756
  7.2 95.4 %all-gather.2.cloned.1.call-start = ((), (), s32[]{:S(2)}) async-start(), calls=%async_computation.1 | async-start | bytes 2621440 | tf_op jit(solution)/shard_map/all_gather | solution.py:48
  7.2 28.9 %collective-permute-start = (bf16[4096,64]{0,1:T(8,128)(2,1)}, bf16[4096,64]{0,1:T(8,128)(2,1)S(1)}, u32[]{:S(2)}, u32[]{:S(2)}) collective-permute-start(bf16[4096,64]{0,1:T(8,128)(2,1)} %param.7), channel_id=1, source_target_pairs={{0,4},{4,8},{8,12},{12,16},{16,20},{20,24},{24,28},{28,32},{32,36}... | collective-permute-start | bytes 1572872 | tf_op jit(solution)/shard_map/ppermute | solution.py:10
  11.4 27.9 %collective-permute-start.2 = (bf16[4096,64]{0,1:T(8,128)(2,1)}, bf16[4096,64]{0,1:T(8,128)(2,1)S(1)}, u32[]{:S(2)}, u32[]{:S(2)}) collective-permute-start(bf16[4096,64]{0,1:T(8,128)(2,1)} %param.7), channel_id=1, source_target_pairs={{0,508},{4,0},{8,4},{12,8},{16,12},{20,16},{24,20},{28,24},{32,28}... | collective-permute-start | bytes 1572872 | tf_op jit(solution)/shard_map/ppermute | solution.py:10
  36.1 19.8 %collective-permute-start.1 = (bf16[4096,64]{0,1:T(8,128)(2,1)S(1)}, bf16[4096,64]{0,1:T(8,128)(2,1)S(1)}, u32[]{:S(2)}, u32[]{:S(2)}) collective-permute-start(bf16[4096,64]{0,1:T(8,128)(2,1)S(1)} %collective-permute-done), channel_id=1, source_target_pairs={{0,4},{4,8},{8,12},{12,16},{16,20},{20,24},{24,28},{28,32},{32,36}... | collective-permute-start | bytes 1572872 | tf_op jit(solution)/shard_map/ppermute | solution.py:10
  39.4 18.8 %collective-permute-start.3 = (bf16[4096,64]{0,1:T(8,128)(2,1)S(1)}, bf16[4096,64]{0,1:T(8,128)(2,1)S(1)}, u32[]{:S(2)}, u32[]{:S(2)}) collective-permute-start(bf16[4096,64]{0,1:T(8,128)(2,1)S(1)} %collective-permute-done.2), channel_id=1, source_target_pairs={{0,508},{4,0},{8,4},{12,8},{16,12},{20,16},{24,20},{28,24},{32,28}... | collective-permute-start | bytes 1572872 | tf_op jit(solution)/shard_map/ppermute | solution.py:10
  64.1 3.5 copy-start.5
  67.6 35.0 %copy-start.4 = (bf16[256,64]{0,1:T(8,128)(2,1)S(1)}, bf16[256,64]{0,1:T(8,128)(2,1)}, u32[]{:S(2)}) copy-start(bf16[256,64]{0,1:T(8,128)(2,1)} %param.8) | copy-start | bytes 98308
  69.7 75.8 %reduce-scatter.2.cloned.1.call-start = ((), (), s32[]{:S(2)}) async-start(), calls=%async_computation.2 | async-start | bytes 2621440 | tf_op jit(solution)/shard_map/reduce_scatter | solution.py:60
  105.8 0.8 copy-start.2
  108.6 1230.1 %all-reduce.2.cloned.1.call-start = ((), (), s32[]{:S(2)}) async-start(), calls=%async_computation.3 | async-start | bytes 131072 | tf_op jit(solution)/shard_map/psum | solution.py:56
  148.6 2.3 copy-start.6
  152.7 20.8 %collective-permute-start.6 = (bf16[4096,64]{0,1:T(8,128)(2,1)S(1)}, bf16[4096,64]{0,1:T(8,128)(2,1)S(1)}, u32[]{:S(2)}, u32[]{:S(2)}) collective-permute-start(bf16[4096,64]{0,1:T(8,128)(2,1)S(1)} %bitcast.83), channel_id=1, source_target_pairs={{0,508},{4,0},{8,4},{12,8},{16,12},{20,16},{24,20},{28,24},{32,28}... | collective-permute-start | bytes 1572872 | tf_op jit(solution)/shard_map/ppermute | solution.py:10
  162.9 21.9 %collective-permute-start.4 = (bf16[4096,64]{0,1:T(8,128)(2,1)S(1)}, bf16[4096,64]{0,1:T(8,128)(2,1)S(1)}, u32[]{:S(2)}, u32[]{:S(2)}) collective-permute-start(bf16[4096,64]{0,1:T(8,128)(2,1)S(1)} %bitcast.82), channel_id=1, source_target_pairs={{0,4},{4,8},{8,12},{12,16},{16,20},{20,24},{24,28},{28,32},{32,36}... | collective-permute-start | bytes 1572872 | tf_op jit(solution)/shard_map/ppermute | solution.py:10
  166.1 22.0 %copy-start.1 = (bf16[4096,256]{0,1:T(8,128)(2,1)S(1)}, bf16[4096,256]{0,1:T(8,128)(2,1)}, u32[]{:S(2)}) copy-start(bf16[4096,256]{0,1:T(8,128)(2,1)} %all-gather.2.cloned.1.call-done) | copy-start | bytes 6291460
  166.1 22.0 %copy-start.3 = (bf16[4096,64]{0,1:T(8,128)(2,1)S(1)}, bf16[4096,64]{0,1:T(8,128)(2,1)}, u32[]{:S(2)}) copy-start(bf16[4096,64]{0,1:T(8,128)(2,1)} %copy-done.2) | copy-start | bytes 1572868
  175.0 1165.2 %collective-permute-start.7 = (bf16[4096,64]{0,1:T(8,128)(2,1)}, bf16[4096,64]{0,1:T(8,128)(2,1)S(1)}, u32[]{:S(2)}, u32[]{:S(2)}) collective-permute-start(bf16[4096,64]{0,1:T(8,128)(2,1)} %fusion.7), channel_id=1, source_target_pairs={{0,508},{4,0},{8,4},{12,8},{16,12},{20,16},{24,20},{28,24},{32,28}... | collective-permute-start | bytes 1572872 | tf_op jit(solution)/shard_map/ppermute | solution.py:10
  186.2 1154.0 %collective-permute-start.5 = (bf16[4096,64]{0,1:T(8,128)(2,1)}, bf16[4096,64]{0,1:T(8,128)(2,1)}, u32[]{:S(2)}, u32[]{:S(2)}) collective-permute-start(bf16[4096,64]{0,1:T(8,128)(2,1)} %fusion.8), channel_id=1, source_target_pairs={{0,4},{4,8},{8,12},{12,16},{16,20},{20,24},{24,28},{28,32},{32,36}... | collective-permute-start | bytes 1572872 | tf_op jit(solution)/shard_map/ppermute | solution.py:10
Sparse Core Ops, SparseCore 0:
  69.8 32.7 all-gather.1
  108.8 36.6 reduce-scatter.1
  189.7 1148.9 all-reduce.1
where the time goes:
time: 1380 us; the launch traced here: 1350 us
  waiting for transfers between devices  1240 us (90%)
  starting transfers between devices  53.7 us (4%)
  matrix products  15 us (1%)
  between operations  14.6 us (1%)
  local copies, waits for them, and re-layouts  13.9 us (1%)
    psum x1, waiting for transfers between devices, local(): weight_grad = lax.psum(weight_term, 'rows') * (1.0 / total_nodes ** 0.5)  1150 us
    ppermute x8, starting transfers between devices, passed_along(): return lax.ppermute(value, axis, pairs)  53.6 us
    reduce_scatter x1, waiting for transfers between devices, local(): lax.psum_scatter(partial_terms.astype(jnp.bfloat16), 'cols', scatter_dime...  36.8 us
    all_gather x1, waiting for transfers between devices, local(): hidden = lax.all_gather(hidden_part, 'cols', axis=1, tiled=True)  32.8 us
  transfers between devices with their start and end apart: 11, of which 7 were waited for; matrix products, arithmetic and copies ran while one was open for 1% of the time, Pallas kernels for 0%

commit v1 on v0

v1 whole, which is shorter than its diff:
```python
import jax
import jax.numpy as jnp
from jax import lax
from jax.experimental import pallas as pl
from jax.experimental.pallas import tpu as pltpu
from jax.sharding import Mesh, PartitionSpec as P

ROWS = ("yh", "z", "x")
COLS = ("yl", "core")
BLOCK = 128
NEAR = 5
VMEM = pl.BlockSpec(memory_space=pltpu.VMEM)
SMEM = pl.BlockSpec(memory_space=pltpu.SMEM)
BATCH = 6


def swap_pairs(count, odd):
    pairs = []
    for first in range(odd, count, 2):
        second = (first + 1) % count
        pairs += [(first, second), (second, first)]
    return pairs


def lanes(index):
    return pl.ds(pl.multiple_of(index * BLOCK, BLOCK), BLOCK)


def each_tile(offset, count, values_ref, term, add):
    slots = values_ref.shape[0]
    per_offset = -(-slots // NEAR)
    for first in range(0, per_offset, BATCH):
        held = []
        for k in range(first, min(first + BATCH, per_offset)):
            slot = k * NEAR + offset
            live = (slot < count).astype(jnp.float32)
            slot = jnp.minimum(slot, slots - 1)
            held.append((slot, term(slot) * live))
        for slot, product in held:
            add(slot, product)


def gather_terms(info, source_ref, total_ref, offset):
    values_ref, rows_ref, cols_ref, count = info
    blocks = source_ref.shape[1] // BLOCK

    def term(slot):
        source = source_ref[:, lanes(lax.rem(cols_ref[slot], blocks))]
        return lax.dot_general(
            source, values_ref[slot], (((1,), (1,)), ((), ())), preferred_element_type=jnp.float32
        )

    def add(slot, product):
        where = lanes(rows_ref[slot])
        total_ref[:, where] = total_ref[:, where] + product

    each_tile(offset, count, values_ref, term, add)


def near_kernel(values, rows, cols, count, parity, own, even, odd, total):
    total[...] = jnp.zeros_like(total)
    info = (values, rows, cols, count[0])
    even_offset = 3 - 2 * parity[0]
    gather_terms(info, own, total, 2)
    gather_terms(info, even, total, even_offset)
    gather_terms(info, odd, total, 4 - even_offset)


def far_kernel(values, rows, cols, count, parity, start, even, odd, hidden, total):
    total[...] = start[...]
    info = (values, rows, cols, count[0])
    even_offset = 4 - 4 * parity[0]
    gather_terms(info, even, total, even_offset)
    gather_terms(info, odd, total, 4 - even_offset)
    parts, _, width = hidden.shape
    for part in range(parts):
        hidden[part] = total[:, part * width : (part + 1) * width].astype(hidden.dtype)


def dense_kernel(hidden, cotangent, weight_t, weight, output, hidden_grad, grad_pre):
    parts, cols, width = hidden.shape
    full = parts * cols
    source = hidden[...].reshape(full, width)
    preact = jnp.dot(weight_t[...], source, preferred_element_type=jnp.float32)
    sigmoid = 1.0 / (1.0 + jnp.exp(-preact))
    output[...] = (preact * sigmoid).astype(output.dtype).reshape(output.shape)
    slope = sigmoid * (1.0 + preact * (1.0 - sigmoid))
    grad = cotangent[...].reshape(full, width).astype(jnp.float32) * slope
    grad = grad.astype(jnp.bfloat16)
    grad_pre[...] = grad
    back = jnp.dot(weight[...], grad, preferred_element_type=jnp.float32)
    hidden_grad[...] = back.astype(hidden_grad.dtype).reshape(hidden_grad.shape)


def spread_terms(info, grad_ref, total_ref, offset):
    values_ref, rows_ref, cols_ref, count = info
    parts, _, width = grad_ref.shape
    blocks = parts * width // BLOCK
    per_part = width // BLOCK

    def term(slot):
        row = rows_ref[slot]
        part = row // per_part
        source = grad_ref[part, :, lanes(row - part * per_part)]
        return jnp.dot(source, values_ref[slot], preferred_element_type=jnp.float32)

    def add(slot, product):
        where = lanes(lax.rem(cols_ref[slot], blocks))
        total_ref[:, where] = total_ref[:, where] + product

    each_tile(offset, count, values_ref, term, add)


def spread_far_kernel(values, rows, cols, count, parity, grad, even, odd, even_total, odd_total):
    info = (values, rows, cols, count[0])
    even_offset = 4 - 4 * parity[0]
    for offset, total, out in ((even_offset, even_total, even), (4 - even_offset, odd_total, odd)):
        total[...] = jnp.zeros_like(total)
        spread_terms(info, grad, total, offset)
        out[...] = total[...].astype(out.dtype)


def spread_near_kernel(values, rows, cols, count, parity, grad, even, odd, own):
    info = (values, rows, cols, count[0])
    even_offset = 3 - 2 * parity[0]
    for offset, total in ((even_offset, even), (4 - even_offset, odd), (2, own)):
        total[...] = jnp.zeros_like(total)
        spread_terms(info, grad, total, offset)


def call(kernel, args, specs, outs, scratch=(), flops=0):
    moved = sum(a.size * a.dtype.itemsize for a in args)
    moved += sum(o.size * o.dtype.itemsize for o in outs)
    return pl.pallas_call(
        kernel,
        out_shape=outs,
        in_specs=specs,
        out_specs=[VMEM] * len(outs),
        scratch_shapes=scratch,
        cost_estimate=pl.CostEstimate(flops=flops, bytes_accessed=moved, transcendentals=0),
        compiler_params=pltpu.CompilerParams(vmem_limit_bytes=24 << 20),
    )(*args)


def swapped(value):
    return lax.all_to_all(value, COLS, 0, 0, tiled=True)


def local(features, weight, tile_values, tile_rows, tile_cols, tile_count, cotangent):
    node_count, feat_cols = features.shape
    slots, tile, _ = tile_values.shape
    n_rows = lax.axis_size(ROWS)
    n_cols = lax.axis_size(COLS)
    width = node_count // n_cols
    full = feat_cols * n_cols
    even_pairs = swap_pairs(n_rows, 0)
    odd_pairs = swap_pairs(n_rows, 1)

    def even_swap(value):
        return lax.ppermute(value, ROWS, even_pairs)

    def odd_swap(value):
        return lax.ppermute(value, ROWS, odd_pairs)

    def pieces(value):
        return value.reshape(feat_cols, n_cols, width).transpose(1, 0, 2)

    parity = lax.rem(lax.axis_index("x"), 2).astype(jnp.int32).reshape(1)
    tables = (tile_values, tile_rows, tile_cols, tile_count, parity)
    table_specs = [VMEM, SMEM, SMEM, SMEM, SMEM]
    tile_flops = 2 * tile * tile * feat_cols
    wide = jax.ShapeDtypeStruct((feat_cols, node_count), jnp.float32)
    sent = jax.ShapeDtypeStruct((feat_cols, node_count), jnp.bfloat16)
    piece = jax.ShapeDtypeStruct((n_cols, feat_cols, width), jnp.bfloat16)
    total = pltpu.VMEM((feat_cols, node_count), jnp.float32)

    own = features.T
    even1 = even_swap(own)
    odd1 = odd_swap(own)
    weight_t = lax.all_gather(weight.T, COLS, axis=0, tiled=True)
    grad_out = swapped(pieces(cotangent.T))
    even1, odd1, weight_t = lax.optimization_barrier((even1, odd1, weight_t))
    odd2 = odd_swap(even1)
    even2 = even_swap(odd1)
    (near,) = call(
        near_kernel, tables + (own, even1, odd1), table_specs + [VMEM] * 3, [wide], flops=54 * tile_flops
    )
    (hidden,) = call(
        far_kernel,
        tables + (near, even2, odd2),
        table_specs + [VMEM] * 3,
        [piece],
        scratch=[total],
        flops=36 * tile_flops,
    )
    hidden = swapped(hidden)
    output, hidden_grad, grad_pre = call(
        dense_kernel,
        (hidden, grad_out, weight_t, weight_t.T),
        [VMEM] * 4,
        [piece, piece, jax.ShapeDtypeStruct((full, width), jnp.bfloat16)],
        flops=4 * full * full * width,
    )
    hidden_grad = swapped(hidden_grad)
    even_far, odd_far = call(
        spread_far_kernel,
        tables + (hidden_grad,),
        table_specs + [VMEM],
        [sent, sent],
        scratch=[total, total],
        flops=36 * tile_flops,
    )
    even_in = even_swap(even_far)
    odd_in = odd_swap(odd_far)
    even_near, odd_near, kept = call(
        spread_near_kernel,
        tables + (hidden_grad,),
        table_specs + [VMEM],
        [wide, wide, wide],
        flops=54 * tile_flops,
    )
    kept, grad_pre, hidden = lax.optimization_barrier((kept, grad_pre, hidden))
    weight_term = lax.dot_general(
        grad_pre,
        hidden.reshape(full, width),
        (((1,), (1,)), ((), ())),
        preferred_element_type=jnp.float32,
    )
    weight_term = swapped(weight_term.reshape(n_cols, feat_cols, full)).sum(0)
    even_near, odd_near, weight_term, output = lax.optimization_barrier(
        (even_near, odd_near, weight_term, output)
    )
    odd_last = (odd_near + even_in.astype(jnp.float32)).astype(jnp.bfloat16)
    even_last = (even_near + odd_in.astype(jnp.float32)).astype(jnp.bfloat16)
    odd_last, even_last, weight_term = lax.optimization_barrier((odd_last, even_last, weight_term))
    odd_last = odd_swap(odd_last)
    even_last = even_swap(even_last)
    weight_term = lax.all_gather(weight_term, "x").sum(0)
    halves = lax.all_gather(weight_term[:32], "z"), lax.all_gather(weight_term[32:], "z")
    weight_term = jnp.concatenate([half.sum(0) for half in halves], 0)
    weight_term = weight_term + lax.ppermute(weight_term, "yh", swap_pairs(2, 0))
    weight_grad = (weight_term * (1.0 / (node_count * n_rows) ** 0.5)).T

    output = swapped(output).transpose(1, 0, 2).reshape(feat_cols, node_count).T
    gathered = kept + even_last.astype(jnp.float32) + odd_last.astype(jnp.float32)
    feature_grad = gathered.astype(jnp.bfloat16).T
    return (output, feature_grad, weight_grad)


def solution(mesh):
    n_rows, n_cols = mesh.shape["rows"], mesh.shape["cols"]
    devices = mesh.devices.reshape(2, n_rows // 8, 4, 2, n_cols // 2)
    fine = Mesh(devices, ROWS + COLS)
    in_specs = (
        P(ROWS, COLS),
        P(None, COLS),
        P(ROWS, None, None),
        P(ROWS),
        P(ROWS),
        P(ROWS),
        P(ROWS, COLS),
    )
    out_specs = (P(ROWS, COLS), P(ROWS, COLS), P(None, COLS))
    return jax.shard_map(local, mesh=fine, in_specs=in_specs, out_specs=out_specs, check_vma=False)
```

time: 1380 us -> 225 us (0.16)
  the two profiles are of different devices: /device:TPU:1 before, /device:TPU:8 now
where the time goes in v1:
time: 225 us; the launch traced here: 224 us
  blocking collectives  103 us (46%)
  starting transfers between devices  68.5 us (30%)
  waiting for transfers between devices  20.1 us (9%)
  local copies, waits for them, and re-layouts  16.8 us (7%)
  Pallas kernels  7.75 us (3%)
  other arithmetic  5.57 us (2%)
    ppermute x4, starting transfers between devices, odd_swap(): return lax.ppermute(value, ROWS, odd_pairs)  37.1 us
    all_gather x1, blocking collectives, local(): lax.all_gather(weight_term[:32], 'z')  30.9 us
    all_gather x1, blocking collectives, local(): lax.all_gather(weight_term[32:], 'z')  28.8 us
    all_gather x1, blocking collectives, local(): weight_term = lax.all_gather(weight_term, 'x').sum(0)  20.5 us
    all_to_all x4, starting transfers between devices, swapped(): return lax.all_to_all(value, COLS, 0, 0, tiled=True)  18.2 us
    unnamed x38, local copies, waits for them, and re-layouts  12.3 us
    all_gather x1, blocking collectives, local(): weight_t = lax.all_gather(weight.T, COLS, axis=0, tiled=True)  11.5 us
    all_to_all x1, blocking collectives, swapped(): return lax.all_to_all(value, COLS, 0, 0, tiled=True)  11.2 us
  transfers between devices with their start and end apart: 13, of which 5 were waited for; matrix products, arithmetic and copies ran while one was open for 5% of the time, Pallas kernels for 2%

profile of v1, /device:TPU:8, one launch (start us, length us, event | category | flops | bytes accessed | tf_op | source)
XLA Modules:
  0.0 224.2 jit_solution(4687714260536026368)
XLA Ops:
  0.6 3.4 %collective-permute-start = (bf16[64,4096]{1,0:T(8,128)(2,1)}, bf16[64,4096]{1,0:T(8,128)(2,1)S(1)}, u32[]{:S(2)}, u32[]{:S(2)}) collective-permute-start(bf16[64,4096]{1,0:T(8,128)(2,1)} %bitcast.31), channel_id=1, source_target_pairs={{0,4},{4,0},{8,12},{12,8},{16,20},{20,16},{24,28},{28,24},{32,36},... | collective-permute-start | bytes 1572872 | tf_op jit(solution)/shard_map/ppermute | solution.py:160
  4.0 14.7 %collective-permute-start.1 = (bf16[64,4096]{1,0:T(8,128)(2,1)}, bf16[64,4096]{1,0:T(8,128)(2,1)S(1)}, u32[]{:S(2)}, u32[]{:S(2)}) collective-permute-start(bf16[64,4096]{1,0:T(8,128)(2,1)} %bitcast.32), channel_id=1, source_target_pairs={{4,8},{8,4},{12,16},{16,12},{20,24},{24,20},{28,32},{32,28},{36,40... | collective-permute-start | bytes 1572872 | tf_op jit(solution)/shard_map/ppermute | solution.py:163
  18.7 11.5 %all_gather.21.weight_t = bf16[256,256]{1,0:T(8,128)(2,1)S(1)} all-gather(bf16[64,256]{1,0:T(8,128)(2,1)} %bitcast.41), channel_id=1, replica_groups=mesh['yh'=2,'z'=16,'x'=4,'yl'=2,'core'=2] {'yl','core'}, dimensions={0}, use_global_device_ids=true | all-gather | bytes 163840 | tf_op jit(solution)/shard_map/all_gather | solution.py:180
  30.7 1.9 collective-permute-start.2
  32.6 9.3 %collective-permute-start.3 = (bf16[64,4096]{1,0:T(8,128)(2,1)S(1)}, bf16[64,4096]{1,0:T(8,128)(2,1)S(1)}, u32[]{:S(2)}, u32[]{:S(2)}) collective-permute-start(bf16[64,4096]{1,0:T(8,128)(2,1)S(1)} %collective-permute-done.even), channel_id=1, source_target_pairs={{4,8},{8,4},{12,16},{16,12},{20,24},{24,20},{28,32},{32,28},{36,40... | collective-permute-start | bytes 1572872 | tf_op jit(solution)/shard_map/ppermute | solution.py:163
  41.8 1.9 copy.25
  43.7 4.8 %all-to-all-start.1 = ((bf16[4,64,1024]{2,1,0:T(8,128)(2,1)}), bf16[4,64,1024]{2,1,0:T(8,128)(2,1)S(1)}, u32[]{:S(2)}, u32[]{:S(2)}) async-start(bf16[4,64,1024]{2,1,0:T(8,128)(2,1)} %bitcast.29), calls=%async_computation.1 | async-start | bytes 1048576 | tf_op jit(solution)/shard_map/all_to_all | solution.py:146
  49.2 1.8 copy-done
  53.3 1.9 shard_map.94.start
  55.3 1.5 shard_map.95
  57.6 2.9 %all-to-all-done.1.cotangent = bf16[4,64,1024]{2,1,0:T(8,128)(2,1)S(1)} async-done(((bf16[4,64,1024]{2,1,0:T(8,128)(2,1)}), bf16[4,64,1024]{2,1,0:T(8,128)(2,1)S(1)}, u32[]{:S(2)}, u32[]{:S(2)}) %all-to-all-start.1) | async-done | bytes 524320 | tf_op jit(solution)/shard_map/all_to_all | solution.py:146
  61.3 3.6 %all-to-all-start = ((bf16[4,64,1024]{2,1,0:T(8,128)(2,1)}), bf16[4,64,1024]{2,1,0:T(8,128)(2,1)S(1)}, u32[]{:S(2)}, u32[]{:S(2)}) async-start(bf16[4,64,1024]{2,1,0:T(8,128)(2,1)} %copy-done.2), calls=%async_computation | async-start | bytes 1048576 | tf_op jit(solution)/shard_map/all_to_all | solution.py:146
  65.7 6.4 %all-to-all-done.hidden = bf16[4,64,1024]{2,1,0:T(8,128)(2,1)S(1)} async-done(((bf16[4,64,1024]{2,1,0:T(8,128)(2,1)}), bf16[4,64,1024]{2,1,0:T(8,128)(2,1)S(1)}, u32[]{:S(2)}, u32[]{:S(2)}) %all-to-all-start) | async-done | bytes 524320 | tf_op jit(solution)/shard_map/all_to_all | solution.py:146
  75.7 11.2 %all_to_all.25.grad = bf16[4,64,1024]{2,1,0:T(8,128)(2,1)S(1)} all-to-all(bf16[4,64,1024]{2,1,0:T(8,128)(2,1)S(1)} %get-tuple-element.27), channel_id=1, replica_groups=mesh['yh'=2,'z'=16,'x'=4,'yl'=2,'core'=2] {'yl','core'}, dimensions={0} | all-to-all | bytes 1048576 | tf_op jit(solution)/shard_map/all_to_all | solution.py:146
  86.9 2.0 shard_map.98
  89.7 1.9 collective-permute-start.4
  91.6 1.5 shard_map.97
  96.1 1.0 fusion.2
  97.1 5.0 %all-to-all-start.3 = ((f32[4,64,256]{2,1,0:T(8,128)}), f32[4,64,256]{2,1,0:T(8,128)S(1)}, u32[]{:S(2)}, u32[]{:S(2)}) async-start(f32[4,64,256]{2,1,0:T(8,128)} %fusion.2), calls=%async_computation.3 | async-start | bytes 524288 | tf_op jit(solution)/shard_map/all_to_all | solution.py:146
  102.2 6.6 %collective-permute-start.5 = (bf16[64,4096]{1,0:T(8,128)(2,1)}, bf16[64,4096]{1,0:T(8,128)(2,1)}, u32[]{:S(2)}, u32[]{:S(2)}) collective-permute-start(bf16[64,4096]{1,0:T(8,128)(2,1)} %copy-done.18), channel_id=1, source_target_pairs={{4,8},{8,4},{12,16},{16,12},{20,24},{24,20},{28,32},{32,28},{36,40... | collective-permute-start | bytes 1572872 | tf_op jit(solution)/shard_map/ppermute | solution.py:163
  108.8 4.8 %all-to-all-start.4 = ((bf16[4,64,1024]{2,1,0:T(8,128)(2,1)}), bf16[4,64,1024]{2,1,0:T(8,128)(2,1)}, u32[]{:S(2)}, u32[]{:S(2)}) async-start(bf16[4,64,1024]{2,1,0:T(8,128)(2,1)} %copy-done.13), calls=%async_computation.4 | async-start | bytes 1048576 | tf_op jit(solution)/shard_map/all_to_all | solution.py:146
  113.6 1.9 add_convert_fusion.2
  115.6 8.6 %collective-permute-done.5 = bf16[64,4096]{1,0:T(8,128)(2,1)} collective-permute-done((bf16[64,4096]{1,0:T(8,128)(2,1)}, bf16[64,4096]{1,0:T(8,128)(2,1)}, u32[]{:S(2)}, u32[]{:S(2)}) %collective-permute-start.5) | collective-permute-done | bytes 524320 | tf_op jit(solution)/shard_map/ppermute | solution.py:163
  124.2 1.9 add_convert_fusion.1
  126.1 6.6 %collective-permute-start.7 = (bf16[64,4096]{1,0:T(8,128)(2,1)}, bf16[64,4096]{1,0:T(8,128)(2,1)S(1)}, u32[]{:S(2)}, u32[]{:S(2)}) collective-permute-start(bf16[64,4096]{1,0:T(8,128)(2,1)} %add_convert_fusion.2), channel_id=1, source_target_pairs={{4,8},{8,4},{12,16},{16,12},{20,24},{24,20},{28,32},{32,28},{36,40... | collective-permute-start | bytes 1572872 | tf_op jit(solution)/shard_map/ppermute | solution.py:163
  132.7 1.9 collective-permute-start.6
  134.6 20.5 %all-gather = f32[256,256]{1,0:T(8,128)S(1)} all-gather(f32[64,256]{1,0:T(8,128)S(1)} %reduce_sum.36), channel_id=2, replica_groups=mesh['yh'=2,'z'=16,'x'=4,'yl'=2,'core'=2] {'x'}, dimensions={0}, use_global_device_ids=true | all-gather | bytes 327680 | tf_op jit(solution)/shard_map/all_gather | solution.py:238
  155.2 28.8 %all-gather.2 = f32[512,256]{1,0:T(8,128)S(1)} all-gather(f32[32,256]{1,0:T(8,128)S(1)} %get-tuple-element.46), channel_id=4, replica_groups=mesh['yh'=2,'z'=16,'x'=4,'yl'=2,'core'=2] {'z'}, dimensions={0}, use_global_device_ids=true | all-gather | bytes 557056 | tf_op jit(solution)/shard_map/all_gather | solution.py:239
  184.0 30.9 %all-gather.1 = f32[512,256]{1,0:T(8,128)S(1)} all-gather(f32[32,256]{1,0:T(8,128)S(1)} %get-tuple-element.45), channel_id=3, replica_groups=mesh['yh'=2,'z'=16,'x'=4,'yl'=2,'core'=2] {'z'}, dimensions={0}, use_global_device_ids=true | all-gather | bytes 557056 | tf_op jit(solution)/shard_map/all_gather | solution.py:239
  214.9 4.1 %collective-permute-start.8 = (f32[64,256]{1,0:T(8,128)S(1)}, f32[64,256]{1,0:T(8,128)S(1)}, u32[]{:S(2)}, u32[]{:S(2)}) collective-permute-start(f32[64,256]{1,0:T(8,128)S(1)} %pad_maximum_fusion), channel_id=1, source_target_pairs={{0,256},{256,0},{1,257},{257,1},{2,258},{258,2},{3,259},{259,3},{4... | collective-permute-start | bytes 196616 | tf_op jit(solution)/shard_map/ppermute | solution.py:241
  219.1 1.9 copy.23
  220.9 1.7 collective-permute-done.8
  (56 shorter events, 14.2 us)
Async XLA Ops:
  0.6 29.6 %collective-permute-start = (bf16[64,4096]{1,0:T(8,128)(2,1)}, bf16[64,4096]{1,0:T(8,128)(2,1)S(1)}, u32[]{:S(2)}, u32[]{:S(2)}) collective-permute-start(bf16[64,4096]{1,0:T(8,128)(2,1)} %bitcast.31), channel_id=1, source_target_pairs={{0,4},{4,0},{8,12},{12,8},{16,20},{20,16},{24,28},{28,24},{32,36},... | collective-permute-start | bytes 1572872 | tf_op jit(solution)/shard_map/ppermute | solution.py:160
  4.0 26.6 %collective-permute-start.1 = (bf16[64,4096]{1,0:T(8,128)(2,1)}, bf16[64,4096]{1,0:T(8,128)(2,1)S(1)}, u32[]{:S(2)}, u32[]{:S(2)}) collective-permute-start(bf16[64,4096]{1,0:T(8,128)(2,1)} %bitcast.32), channel_id=1, source_target_pairs={{4,8},{8,4},{12,16},{16,12},{20,24},{24,20},{28,32},{32,28},{36,40... | collective-permute-start | bytes 1572872 | tf_op jit(solution)/shard_map/ppermute | solution.py:163
  30.7 24.6 %collective-permute-start.2 = (bf16[64,4096]{1,0:T(8,128)(2,1)S(1)}, bf16[64,4096]{1,0:T(8,128)(2,1)S(1)}, u32[]{:S(2)}, u32[]{:S(2)}) collective-permute-start(bf16[64,4096]{1,0:T(8,128)(2,1)S(1)} %collective-permute-done.1.odd), channel_id=1, source_target_pairs={{0,4},{4,0},{8,12},{12,8},{16,20},{20,16},{24,28},{28,24},{32,36},... | collective-permute-start | bytes 1572872 | tf_op jit(solution)/shard_map/ppermute | solution.py:160
  32.6 22.7 %collective-permute-start.3 = (bf16[64,4096]{1,0:T(8,128)(2,1)S(1)}, bf16[64,4096]{1,0:T(8,128)(2,1)S(1)}, u32[]{:S(2)}, u32[]{:S(2)}) collective-permute-start(bf16[64,4096]{1,0:T(8,128)(2,1)S(1)} %collective-permute-done.even), channel_id=1, source_target_pairs={{4,8},{8,4},{12,16},{16,12},{20,24},{24,20},{28,32},{32,28},{36,40... | collective-permute-start | bytes 1572872 | tf_op jit(solution)/shard_map/ppermute | solution.py:163
  43.7 16.8 %all-to-all-start.1 = ((bf16[4,64,1024]{2,1,0:T(8,128)(2,1)}), bf16[4,64,1024]{2,1,0:T(8,128)(2,1)S(1)}, u32[]{:S(2)}, u32[]{:S(2)}) async-start(bf16[4,64,1024]{2,1,0:T(8,128)(2,1)} %bitcast.29), calls=%async_computation.1 | async-start | bytes 1048576 | tf_op jit(solution)/shard_map/all_to_all | solution.py:146
  49.2 1.8 copy-start
  51.0 1.0 copy-start.11
  52.0 0.7 copy-start.14
  52.7 0.7 copy-start.16
  55.2 31.7 %copy-start.15 = (s32[88]{0:T(128)S(1)}, s32[88]{0:T(128)}, u32[]{:S(2)}) copy-start(s32[88]{0:T(128)} %rows.7) | copy-start | bytes 1060
  55.3 31.7 %copy-start.17 = (s32[88]{0:T(128)S(1)}, s32[88]{0:T(128)}, u32[]{:S(2)}) copy-start(s32[88]{0:T(128)} %cols.7) | copy-start | bytes 1060
  56.8 0.8 copy-start.2
  57.6 29.3 %copy-start.1 = (bf16[88,128,128]{2,1,0:T(8,128)(2,1)S(1)}, bf16[88,128,128]{2,1,0:T(8,128)(2,1)}, u32[]{:S(2)}) copy-start(bf16[88,128,128]{2,1,0:T(8,128)(2,1)} %values.7) | copy-start | bytes 8650756
  60.5 0.8 copy-start.3
  61.3 10.8 %all-to-all-start = ((bf16[4,64,1024]{2,1,0:T(8,128)(2,1)}), bf16[4,64,1024]{2,1,0:T(8,128)(2,1)S(1)}, u32[]{:S(2)}, u32[]{:S(2)}) async-start(bf16[4,64,1024]{2,1,0:T(8,128)(2,1)} %copy-done.2), calls=%async_computation | async-start | bytes 1048576 | tf_op jit(solution)/shard_map/all_to_all | solution.py:146
  72.1 1.0 copy-start.4
  73.1 0.9 copy-start.12
  74.9 0.8 copy-start.13
  88.9 0.8 copy-start.18
  89.7 23.9 %collective-permute-start.4 = (bf16[64,4096]{1,0:T(8,128)(2,1)}, bf16[64,4096]{1,0:T(8,128)(2,1)}, u32[]{:S(2)}, u32[]{:S(2)}) collective-permute-start(bf16[64,4096]{1,0:T(8,128)(2,1)} %get-tuple-element.38), channel_id=1, source_target_pairs={{0,4},{4,0},{8,12},{12,8},{16,20},{20,16},{24,28},{28,24},{32,36},... | collective-permute-start | bytes 1572872 | tf_op jit(solution)/shard_map/ppermute | solution.py:160
  93.1 1.0 copy-start.5
  94.1 1.0 copy-start.7
  95.1 1.0 copy-start.9
  96.1 17.5 %copy-start.10 = (f32[64,4096]{1,0:T(8,128)S(1)}, f32[64,4096]{1,0:T(8,128)}, u32[]{:S(2)}) copy-start(f32[64,4096]{1,0:T(8,128)} %copy-done.9) | copy-start | bytes 3145732
  96.1 28.1 %copy-start.8 = (f32[64,4096]{1,0:T(8,128)S(1)}, f32[64,4096]{1,0:T(8,128)}, u32[]{:S(2)}) copy-start(f32[64,4096]{1,0:T(8,128)} %copy-done.7) | copy-start | bytes 3145732
  97.1 11.6 %all-to-all-start.3 = ((f32[4,64,256]{2,1,0:T(8,128)}), f32[4,64,256]{2,1,0:T(8,128)S(1)}, u32[]{:S(2)}, u32[]{:S(2)}) async-start(f32[4,64,256]{2,1,0:T(8,128)} %fusion.2), calls=%async_computation.3 | async-start | bytes 524288 | tf_op jit(solution)/shard_map/all_to_all | solution.py:146
  102.2 22.0 %collective-permute-start.5 = (bf16[64,4096]{1,0:T(8,128)(2,1)}, bf16[64,4096]{1,0:T(8,128)(2,1)}, u32[]{:S(2)}, u32[]{:S(2)}) collective-permute-start(bf16[64,4096]{1,0:T(8,128)(2,1)} %copy-done.18), channel_id=1, source_target_pairs={{4,8},{8,4},{12,16},{16,12},{20,24},{24,20},{28,32},{32,28},{36,40... | collective-permute-start | bytes 1572872 | tf_op jit(solution)/shard_map/ppermute | solution.py:163
  108.8 110.2 %all-to-all-start.4 = ((bf16[4,64,1024]{2,1,0:T(8,128)(2,1)}), bf16[4,64,1024]{2,1,0:T(8,128)(2,1)}, u32[]{:S(2)}, u32[]{:S(2)}) async-start(bf16[4,64,1024]{2,1,0:T(8,128)(2,1)} %copy-done.13), calls=%async_computation.4 | async-start | bytes 1048576 | tf_op jit(solution)/shard_map/all_to_all | solution.py:146
  115.6 107.7 %copy-start.6 = (f32[64,4096]{1,0:T(8,128)S(1)}, f32[64,4096]{1,0:T(8,128)}, u32[]{:S(2)}) copy-start(f32[64,4096]{1,0:T(8,128)} %copy-done.5) | copy-start | bytes 3145732
  126.1 97.1 %collective-permute-start.7 = (bf16[64,4096]{1,0:T(8,128)(2,1)}, bf16[64,4096]{1,0:T(8,128)(2,1)S(1)}, u32[]{:S(2)}, u32[]{:S(2)}) collective-permute-start(bf16[64,4096]{1,0:T(8,128)(2,1)} %add_convert_fusion.2), channel_id=1, source_target_pairs={{4,8},{8,4},{12,16},{16,12},{20,24},{24,20},{28,32},{32,28},{36,40... | collective-permute-start | bytes 1572872 | tf_op jit(solution)/shard_map/ppermute | solution.py:163
  132.7 90.5 %collective-permute-start.6 = (bf16[64,4096]{1,0:T(8,128)(2,1)}, bf16[64,4096]{1,0:T(8,128)(2,1)S(1)}, u32[]{:S(2)}, u32[]{:S(2)}) collective-permute-start(bf16[64,4096]{1,0:T(8,128)(2,1)} %add_convert_fusion.1), channel_id=1, source_target_pairs={{0,4},{4,0},{8,12},{12,8},{16,20},{20,16},{24,28},{28,24},{32,36},... | collective-permute-start | bytes 1572872 | tf_op jit(solution)/shard_map/ppermute | solution.py:160
  214.9 7.7 %collective-permute-start.8 = (f32[64,256]{1,0:T(8,128)S(1)}, f32[64,256]{1,0:T(8,128)S(1)}, u32[]{:S(2)}, u32[]{:S(2)}) collective-permute-start(f32[64,256]{1,0:T(8,128)S(1)} %pad_maximum_fusion), channel_id=1, source_target_pairs={{0,256},{256,0},{1,257},{257,1},{2,258},{258,2},{3,259},{259,3},{4... | collective-permute-start | bytes 196616 | tf_op jit(solution)/shard_map/ppermute | solution.py:241

commit v2 on v1

--- a/solution.py
+++ b/solution.py
@@ -5,7 +5,7 @@
 from jax.experimental.pallas import tpu as pltpu
 from jax.sharding import Mesh, PartitionSpec as P
 
-ROWS = ("yh", "z", "x")
+ROWS = ("yh", "zh", "zl", "x")
 COLS = ("yl", "core")
 BLOCK = 128
 NEAR = 5
@@ -77,26 +77,31 @@
         hidden[part] = total[:, part * width : (part + 1) * width].astype(hidden.dtype)
 
 
-def dense_kernel(hidden, cotangent, weight_t, weight, output, hidden_grad, grad_pre):
+def dense_kernel(hidden, given, output, sent):
     parts, cols, width = hidden.shape
     full = parts * cols
     source = hidden[...].reshape(full, width)
-    preact = jnp.dot(weight_t[...], source, preferred_element_type=jnp.float32)
+    weight_t = given[:, :, width:].reshape(full, full)
+    preact = jnp.dot(weight_t, source, preferred_element_type=jnp.float32)
     sigmoid = 1.0 / (1.0 + jnp.exp(-preact))
     output[...] = (preact * sigmoid).astype(output.dtype).reshape(output.shape)
     slope = sigmoid * (1.0 + preact * (1.0 - sigmoid))
-    grad = cotangent[...].reshape(full, width).astype(jnp.float32) * slope
+    grad = given[:, :, :width].reshape(full, width).astype(jnp.float32) * slope
     grad = grad.astype(jnp.bfloat16)
-    grad_pre[...] = grad
-    back = jnp.dot(weight[...], grad, preferred_element_type=jnp.float32)
-    hidden_grad[...] = back.astype(hidden_grad.dtype).reshape(hidden_grad.shape)
+    back = lax.dot_general(
+        weight_t, grad, (((0,), (0,)), ((), ())), preferred_element_type=jnp.float32
+    )
+    sent[:, :, :width] = back.astype(sent.dtype).reshape(parts, cols, width)
+    weight_term = lax.dot_general(
+        grad, source, (((1,), (1,)), ((), ())), preferred_element_type=jnp.float32
+    )
+    sent[:, :, width:] = weight_term.astype(sent.dtype).reshape(parts, cols, full)
 
 
 def spread_terms(info, grad_ref, total_ref, offset):
     values_ref, rows_ref, cols_ref, count = info
-    parts, _, width = grad_ref.shape
-    blocks = parts * width // BLOCK
-    per_part = width // BLOCK
+    blocks = total_ref.shape[1] // BLOCK
+    per_part = blocks // grad_ref.shape[0]
 
     def term(slot):
         row = rows_ref[slot]
@@ -120,12 +125,25 @@
         out[...] = total[...].astype(out.dtype)
 
 
-def spread_near_kernel(values, rows, cols, count, parity, grad, even, odd, own):
+def spread_near_kernel(
+    values, rows, cols, count, parity, grad, from_odd, from_even, even, odd, even_total, odd_total
+):
     info = (values, rows, cols, count[0])
     even_offset = 3 - 2 * parity[0]
-    for offset, total in ((even_offset, even), (4 - even_offset, odd), (2, own)):
-        total[...] = jnp.zeros_like(total)
+    for offset, start, total, out in (
+        (even_offset, from_odd, even_total, even),
+        (4 - even_offset, from_even, odd_total, odd),
+    ):
+        total[...] = start[...].astype(total.dtype)
         spread_terms(info, grad, total, offset)
+        out[...] = total[...].astype(out.dtype)
+
+
+def spread_own_kernel(values, rows, cols, count, parity, grad, from_even, from_odd, out, total):
+    info = (values, rows, cols, count[0])
+    total[...] = from_even[...].astype(total.dtype) + from_odd[...].astype(total.dtype)
+    spread_terms(info, grad, total, 2)
+    out[...] = total[...].astype(out.dtype)
 
 
 def call(kernel, args, specs, outs, scratch=(), flops=0):
@@ -177,9 +195,9 @@
     own = features.T
     even1 = even_swap(own)
     odd1 = odd_swap(own)
-    weight_t = lax.all_gather(weight.T, COLS, axis=0, tiled=True)
-    grad_out = swapped(pieces(cotangent.T))
-    even1, odd1, weight_t = lax.optimization_barrier((even1, odd1, weight_t))
+    weight_t = jnp.broadcast_to(weight.T, (n_cols, feat_cols, full))
+    given = swapped(jnp.concatenate([pieces(cotangent.T), weight_t], 2))
+    odd1, given = lax.optimization_barrier((odd1, given))
     odd2 = odd_swap(even1)
     even2 = even_swap(odd1)
     (near,) = call(
@@ -193,18 +211,17 @@
         scratch=[total],
         flops=36 * tile_flops,
     )
-    hidden = swapped(hidden)
-    output, hidden_grad, grad_pre = call(
+    output, grads = call(
         dense_kernel,
-        (hidden, grad_out, weight_t, weight_t.T),
-        [VMEM] * 4,
-        [piece, piece, jax.ShapeDtypeStruct((full, width), jnp.bfloat16)],
-        flops=4 * full * full * width,
-    )
-    hidden_grad = swapped(hidden_grad)
+        (swapped(hidden), given),
+        [VMEM] * 2,
+        [piece, jax.ShapeDtypeStruct((n_cols, feat_cols, width + full), jnp.bfloat16)],
+        flops=6 * full * full * width,
+    )
+    grads = swapped(grads)
     even_far, odd_far = call(
         spread_far_kernel,
-        tables + (hidden_grad,),
+        tables + (grads,),
         table_specs + [VMEM],
         [sent, sent],
         scratch=[total, total],
@@ -212,44 +229,44 @@
     )
     even_in = even_swap(even_far)
     odd_in = odd_swap(odd_far)
-    even_near, odd_near, kept = call(
+
+    weight_grad = grads[:, :, width:].astype(jnp.float32).sum(0)
+    weight_grad, even_far, odd_far = lax.optimization_barrier((weight_grad, even_far, odd_far))
+    output = swapped(output)
+    weight_grad = lax.all_gather(weight_grad, "zl").sum(0)
+    even_in, odd_in, weight_grad = lax.optimization_barrier((even_in, odd_in, weight_grad))
+
+    even_near, odd_near = call(
         spread_near_kernel,
-        tables + (hidden_grad,),
-        table_specs + [VMEM],
-        [wide, wide, wide],
-        flops=54 * tile_flops,
-    )
-    kept, grad_pre, hidden = lax.optimization_barrier((kept, grad_pre, hidden))
-    weight_term = lax.dot_general(
-        grad_pre,
-        hidden.reshape(full, width),
-        (((1,), (1,)), ((), ())),
-        preferred_element_type=jnp.float32,
-    )
-    weight_term = swapped(weight_term.reshape(n_cols, feat_cols, full)).sum(0)
-    even_near, odd_near, weight_term, output = lax.optimization_barrier(
-        (even_near, odd_near, weight_term, output)
-    )
-    odd_last = (odd_near + even_in.astype(jnp.float32)).astype(jnp.bfloat16)
-    even_last = (even_near + odd_in.astype(jnp.float32)).astype(jnp.bfloat16)
-    odd_last, even_last, weight_term = lax.optimization_barrier((odd_last, even_last, weight_term))
-    odd_last = odd_swap(odd_last)
-    even_last = even_swap(even_last)
-    weight_term = lax.all_gather(weight_term, "x").sum(0)
-    halves = lax.all_gather(weight_term[:32], "z"), lax.all_gather(weight_term[32:], "z")
-    weight_term = jnp.concatenate([half.sum(0) for half in halves], 0)
-    weight_term = weight_term + lax.ppermute(weight_term, "yh", swap_pairs(2, 0))
-    weight_grad = (weight_term * (1.0 / (node_count * n_rows) ** 0.5)).T
-
-    output = swapped(output).transpose(1, 0, 2).reshape(feat_cols, node_count).T
-    gathered = kept + even_last.astype(jnp.float32) + odd_last.astype(jnp.float32)
-    feature_grad = gathered.astype(jnp.bfloat16).T
-    return (output, feature_grad, weight_grad)
+        tables + (grads, odd_in, even_in),
+        table_specs + [VMEM] * 3,
+        [sent, sent],
+        scratch=[total, total],
+        flops=36 * tile_flops,
+    )
+    even_last = even_swap(even_near)
+    odd_last = odd_swap(odd_near)
+    weight_grad, even_near, odd_near = lax.optimization_barrier((weight_grad, even_near, odd_near))
+    weight_grad = lax.all_gather(weight_grad, "zh").sum(0)
+    weight_grad = weight_grad + lax.ppermute(weight_grad, "yh", swap_pairs(2, 0))
+    (feature_grad,) = call(
+        spread_own_kernel,
+        tables + (grads, even_last, odd_last),
+        table_specs + [VMEM] * 3,
+        [sent],
+        scratch=[total],
+        flops=18 * tile_flops,
+    )
+    weight_grad, feature_grad = lax.optimization_barrier((weight_grad, feature_grad))
+    weight_grad = lax.all_gather(weight_grad, "x").sum(0)
+    weight_grad = (weight_grad * (1.0 / (node_count * n_rows) ** 0.5)).T
+    output = output.transpose(1, 0, 2).reshape(feat_cols, node_count).T
+    return (output, feature_grad.T, weight_grad)
 
 
 def solution(mesh):
     n_rows, n_cols = mesh.shape["rows"], mesh.shape["cols"]
-    devices = mesh.devices.reshape(2, n_rows // 8, 4, 2, n_cols // 2)
+    devices = mesh.devices.reshape(2, n_rows // 32, 4, 4, 2, n_cols // 2)
     fine = Mesh(devices, ROWS + COLS)
     in_specs = (
         P(ROWS, COLS),

time: 225 us -> 179 us (0.80)
  blocking collectives: 103 us -> 84.2 us
  local copies, waits for them, and re-layouts: 16.8 us -> 4.93 us
  starting transfers between devices: 68.5 us -> 57 us
  waiting for transfers between devices: 20.1 us -> 12.4 us
  Pallas kernels: 7.75 us -> 13 us
    all_gather x4 -> x3, blocking collectives: 91.7 us -> 47.1 us  [the longest x1 19.9 us: local(): weight_grad = lax.all_gather(weight_grad, 'zh').sum(0)]
    all_to_all x1 -> x3, blocking collectives: 11.2 us -> 37.1 us  [swapped(): return lax.all_to_all(value, COLS, 0, 0, tiled=True)]
    all_to_all x4 -> x1, starting transfers between devices: 18.2 us -> 5.95 us  [swapped(): return lax.all_to_all(value, COLS, 0, 0, tiled=True)]
    unnamed x38 -> x10, local copies, waits for them, and re-layouts: 12.3 us -> 1.06 us
    all_to_all x4 -> x1, waiting for transfers between devices: 9.33 us -> 0.01 us  [swapped(): return lax.all_to_all(value, COLS, 0, 0, tiled=True)]
    pallas_call x5 -> x6, Pallas kernels: 7.75 us -> 13 us  [call(): pl.pallas_call(kernel, out_shape=outs, in_specs=specs, out_specs=[VMEM] *...]
    convert_element_type x2 -> x0, other arithmetic: 3.86 us -> none  [the longest x1 1.94 us: local(): odd_last = (odd_near + even_in.astype(jnp.float32)).astype(jnp.bfloat16)]
    reduce_sum x4, other arithmetic: 0.11 us -> 3.24 us  [the longest x1 1.6 us: local(): weight_grad = lax.all_gather(weight_grad, 'zl').sum(0)]
  transfers between devices with their start and end apart: 13 -> 10, of which waited for: 5 -> 3; matrix products, arithmetic and copies ran while one was open for 5% -> 5% of each run, Pallas kernels for 2% -> 1%
where the time goes in v2:
time: 179 us; the launch traced here: 178 us
  blocking collectives  84.2 us (47%)
  starting transfers between devices  57 us (32%)
  Pallas kernels  13 us (7%)
  waiting for transfers between devices  12.4 us (7%)
  local copies, waits for them, and re-layouts  4.93 us (3%)
  other arithmetic  4.8 us (3%)
    ppermute x4, starting transfers between devices, odd_swap(): return lax.ppermute(value, ROWS, odd_pairs)  39.2 us
    all_to_all x3, blocking collectives, swapped(): return lax.all_to_all(value, COLS, 0, 0, tiled=True)  37.1 us
    all_gather x1, blocking collectives, local(): weight_grad = lax.all_gather(weight_grad, 'zh').sum(0)  19.9 us
    all_gather x1, blocking collectives, local(): weight_grad = lax.all_gather(weight_grad, 'zl').sum(0)  15 us
    pallas_call x6, Pallas kernels, call(): pl.pallas_call(kernel, out_shape=outs, in_specs=specs, out_specs=[VMEM] *...  13 us
    all_gather x1, blocking collectives, local(): weight_grad = lax.all_gather(weight_grad, 'x').sum(0)  12.2 us
    ppermute x4, starting transfers between devices, even_swap(): return lax.ppermute(value, ROWS, even_pairs)  8.72 us
    ppermute x4, waiting for transfers between devices, odd_swap(): return lax.ppermute(value, ROWS, odd_pairs)  8.26 us
  transfers between devices with their start and end apart: 10, of which 3 were waited for; matrix products, arithmetic and copies ran while one was open for 5% of the time, Pallas kernels for 1%

profile of v2, /device:TPU:8, one launch (start us, length us, event | category | flops | bytes accessed | tf_op | source)
XLA Modules:
  0.0 177.8 jit_solution(15341693336554438942)
XLA Ops:
  0.6 15.3 %collective-permute-start.1 = (bf16[64,4096]{1,0:T(8,128)(2,1)}, bf16[64,4096]{1,0:T(8,128)(2,1)}, u32[]{:S(2)}, u32[]{:S(2)}) collective-permute-start(bf16[64,4096]{1,0:T(8,128)(2,1)} %bitcast.22), channel_id=1, source_target_pairs={{4,8},{8,4},{12,16},{16,12},{20,24},{24,20},{28,32},{32,28},{36,40... | collective-permute-start | bytes 1572872 | tf_op jit(solution)/shard_map/ppermute | solution.py:181
  16.0 1.9 %collective-permute-start = (bf16[64,4096]{1,0:T(8,128)(2,1)}, bf16[64,4096]{1,0:T(8,128)(2,1)}, u32[]{:S(2)}, u32[]{:S(2)}) collective-permute-start(bf16[64,4096]{1,0:T(8,128)(2,1)} %bitcast.23), channel_id=1, source_target_pairs={{0,4},{4,0},{8,12},{12,8},{16,20},{20,16},{24,28},{28,24},{32,36},... | collective-permute-start | bytes 1572872 | tf_op jit(solution)/shard_map/ppermute | solution.py:178
  17.9 1.2 copy.17
  19.1 0.8 broadcast_in_dim.3
  20.0 13.3 %all_to_all.20.given = bf16[4,64,1280]{2,1,0:T(8,128)(2,1)S(1)} all-to-all(bf16[4,64,1280]{2,1,0:T(8,128)(2,1)S(1)} %pad_maximum_fusion), channel_id=1, replica_groups=mesh['yh'=2,'zh'=4,'zl'=4,'x'=4,'yl'=2,'core'=2] {'yl','core'}, dimensions={0} | all-to-all | bytes 1310720 | tf_op jit(solution)/shard_map/all_to_all | solution.py:164
  33.3 3.0 %collective-permute-start.2 = (bf16[64,4096]{1,0:T(8,128)(2,1)}, bf16[64,4096]{1,0:T(8,128)(2,1)}, u32[]{:S(2)}, u32[]{:S(2)}) collective-permute-start(bf16[64,4096]{1,0:T(8,128)(2,1)} %collective-permute-done.1.odd), channel_id=1, source_target_pairs={{0,4},{4,0},{8,12},{12,8},{16,20},{20,16},{24,28},{28,24},{32,36},... | collective-permute-start | bytes 1572872 | tf_op jit(solution)/shard_map/ppermute | solution.py:178
  36.3 7.7 %collective-permute-start.3 = (bf16[64,4096]{1,0:T(8,128)(2,1)}, bf16[64,4096]{1,0:T(8,128)(2,1)}, u32[]{:S(2)}, u32[]{:S(2)}) collective-permute-start(bf16[64,4096]{1,0:T(8,128)(2,1)} %collective-permute-done.even), channel_id=1, source_target_pairs={{4,8},{8,4},{12,16},{16,12},{20,24},{24,20},{28,32},{32,28},{36,40... | collective-permute-start | bytes 1572872 | tf_op jit(solution)/shard_map/ppermute | solution.py:181
  44.7 1.0 copy-done.1
  45.7 2.6 %shard_map.94.start = f32[64,4096]{1,0:T(8,128)S(1)} custom-call(bf16[88,128,128]{2,1,0:T(8,128)(2,1)S(1)} %copy-done, s32[88]{0:T(128)S(1)} %copy-done.3, s32[88]{0:T(128)S(1)} %copy-done.4, s32[1]{0:T(128)S(6)} %copy.18.count, s32[1]{0:T(128)} %bitcast.parity, bf16[64,4096]{1,0:T(8,128)(2,1)S(1)} %bitcast.24, bf16[64,4096]{1,0:T(8,128)(2,1)} %collective-permute-done.even, ...), custom_call_target="tpu_custom_call" | custom-call | flops 113246208 | bytes 5505736 | tf_op jit(solution)/shard_map/pallas_call | solution.py:152
  48.3 1.1 collective-permute-done.2.even
  49.4 8.2 %collective-permute-done.3.odd = bf16[64,4096]{1,0:T(8,128)(2,1)} collective-permute-done((bf16[64,4096]{1,0:T(8,128)(2,1)}, bf16[64,4096]{1,0:T(8,128)(2,1)}, u32[]{:S(2)}, u32[]{:S(2)}) %collective-permute-start.3) | collective-permute-done | bytes 524320 | tf_op jit(solution)/shard_map/ppermute | solution.py:181
  57.6 2.2 %shard_map.95 = bf16[4,64,1024]{2,1,0:T(8,128)(2,1)S(1)} custom-call(bf16[88,128,128]{2,1,0:T(8,128)(2,1)S(1)} %copy-done, s32[88]{0:T(128)S(1)} %copy-done.3, s32[88]{0:T(128)S(1)} %copy-done.4, s32[1]{0:T(128)S(6)} %copy.18.count, s32[1]{0:T(128)} %bitcast.parity, f32[64,4096]{1,0:T(8,128)S(1)} %shard_map.94.start, ...), custom_call_target="tpu_custom_call" | custom-call | flops 75497472 | bytes 5505736 | tf_op jit(solution)/shard_map/pallas_call | solution.py:152
  59.9 11.1 %all_to_all.21.hidden = bf16[4,64,1024]{2,1,0:T(8,128)(2,1)S(1)} all-to-all(bf16[4,64,1024]{2,1,0:T(8,128)(2,1)S(1)} %shard_map.95), channel_id=1, replica_groups=mesh['yh'=2,'zh'=4,'zl'=4,'x'=4,'yl'=2,'core'=2] {'yl','core'}, dimensions={0} | all-to-all | bytes 1048576 | tf_op jit(solution)/shard_map/all_to_all | solution.py:164
  71.0 1.0 shard_map.96
  72.1 12.7 %all_to_all.22.grad = bf16[4,64,1280]{2,1,0:T(8,128)(2,1)S(1)} all-to-all(bf16[4,64,1280]{2,1,0:T(8,128)(2,1)S(1)} %get-tuple-element.21), channel_id=1, replica_groups=mesh['yh'=2,'zh'=4,'zl'=4,'x'=4,'yl'=2,'core'=2] {'yl','core'}, dimensions={0} | all-to-all | bytes 1310720 | tf_op jit(solution)/shard_map/all_to_all | solution.py:164
  84.7 2.1 %shard_map.97 = (bf16[64,4096]{1,0:T(8,128)(2,1)}, bf16[64,4096]{1,0:T(8,128)(2,1)}) custom-call(bf16[88,128,128]{2,1,0:T(8,128)(2,1)S(1)} %copy-done, s32[88]{0:T(128)S(1)} %copy-done.3, s32[88]{0:T(128)S(1)} %copy-done.4, s32[1]{0:T(128)S(6)} %copy.18.count, s32[1]{0:T(128)} %bitcast.parity, bf16[4,64,1280]{2,1,0:T(8,128)(2,1)S(1)} %all_to_all.22.grad), custom_call_target="tpu_custom_call" | custom-call | flops 75497472 | bytes 4588232 | tf_op jit(solution)/shard_map/pallas_call | solution.py:152
  86.8 1.9 %collective-permute-start.4 = (bf16[64,4096]{1,0:T(8,128)(2,1)}, bf16[64,4096]{1,0:T(8,128)(2,1)}, u32[]{:S(2)}, u32[]{:S(2)}) collective-permute-start(bf16[64,4096]{1,0:T(8,128)(2,1)} %get-tuple-element.22), channel_id=1, source_target_pairs={{0,4},{4,0},{8,12},{12,8},{16,20},{20,16},{24,28},{28,24},{32,36},... | collective-permute-start | bytes 1572872 | tf_op jit(solution)/shard_map/ppermute | solution.py:178
  88.7 8.7 %collective-permute-start.5 = (bf16[64,4096]{1,0:T(8,128)(2,1)}, bf16[64,4096]{1,0:T(8,128)(2,1)}, u32[]{:S(2)}, u32[]{:S(2)}) collective-permute-start(bf16[64,4096]{1,0:T(8,128)(2,1)} %get-tuple-element.23), channel_id=1, source_target_pairs={{4,8},{8,4},{12,16},{16,12},{20,24},{24,20},{28,32},{32,28},{36,40... | collective-permute-start | bytes 1572872 | tf_op jit(solution)/shard_map/ppermute | solution.py:181
  97.5 15.0 %all-gather = f32[256,256]{1,0:T(8,128)} all-gather(f32[64,256]{1,0:T(8,128)S(1)} %convert_reduce_fusion), channel_id=2, replica_groups=mesh['yh'=2,'zh'=4,'zl'=4,'x'=4,'yl'=2,'core'=2] {'zl'}, dimensions={0}, use_global_device_ids=true | all-gather | bytes 327680 | tf_op jit(solution)/shard_map/all_gather | solution.py:236
  112.5 1.6 reduce_sum.37
  114.1 2.7 %shard_map.98 = (bf16[64,4096]{1,0:T(8,128)(2,1)}, bf16[64,4096]{1,0:T(8,128)(2,1)}) custom-call(bf16[88,128,128]{2,1,0:T(8,128)(2,1)S(1)} %copy-done, s32[88]{0:T(128)S(1)} %copy-done.3, s32[88]{0:T(128)S(1)} %copy-done.4, s32[1]{0:T(128)S(6)} %copy.18.count, s32[1]{0:T(128)} %bitcast.parity, bf16[4,64,1280]{2,1,0:T(8,128)(2,1)S(1)} %all_to_all.22.grad, ...), custom_call_target="tpu_custom_call" | custom-call | flops 75497472 | bytes 5636808 | tf_op jit(solution)/shard_map/pallas_call | solution.py:152
  116.9 1.9 %collective-permute-start.7 = (bf16[64,4096]{1,0:T(8,128)(2,1)}, bf16[64,4096]{1,0:T(8,128)(2,1)}, u32[]{:S(2)}, u32[]{:S(2)}) collective-permute-start(bf16[64,4096]{1,0:T(8,128)(2,1)} %get-tuple-element.28), channel_id=1, source_target_pairs={{0,4},{4,0},{8,12},{12,8},{16,20},{20,16},{24,28},{28,24},{32,36},... | collective-permute-start | bytes 1572872 | tf_op jit(solution)/shard_map/ppermute | solution.py:178
  118.8 7.4 %collective-permute-start.8 = (bf16[64,4096]{1,0:T(8,128)(2,1)}, bf16[64,4096]{1,0:T(8,128)(2,1)}, u32[]{:S(2)}, u32[]{:S(2)}) collective-permute-start(bf16[64,4096]{1,0:T(8,128)(2,1)} %get-tuple-element.29), channel_id=1, source_target_pairs={{4,8},{8,4},{12,16},{16,12},{20,24},{24,20},{28,32},{32,28},{36,40... | collective-permute-start | bytes 1572872 | tf_op jit(solution)/shard_map/ppermute | solution.py:181
  126.2 6.0 %all-to-all-start.2 = ((bf16[4,64,1024]{2,1,0:T(8,128)(2,1)}), bf16[4,64,1024]{2,1,0:T(8,128)(2,1)}, u32[]{:S(2)}, u32[]{:S(2)}) async-start(bf16[4,64,1024]{2,1,0:T(8,128)(2,1)} %copy-done.2), calls=%async_computation.2 | async-start | bytes 1048576 | tf_op jit(solution)/shard_map/all_to_all | solution.py:164
  132.2 19.9 %all-gather.1 = f32[256,256]{1,0:T(8,128)} all-gather(f32[64,256]{1,0:T(8,128)} %reduce_sum.37), channel_id=3, replica_groups=mesh['yh'=2,'zh'=4,'zl'=4,'x'=4,'yl'=2,'core'=2] {'zh'}, dimensions={0}, use_global_device_ids=true | all-gather | bytes 327680 | tf_op jit(solution)/shard_map/all_gather | solution.py:250
  152.0 1.6 reduce_sum.38
  153.6 3.1 %collective-permute-start.6 = (f32[64,256]{1,0:T(8,128)}, f32[64,256]{1,0:T(8,128)}, u32[]{:S(2)}, u32[]{:S(2)}) collective-permute-start(f32[64,256]{1,0:T(8,128)} %reduce_sum.38), channel_id=1, source_target_pairs={{0,256},{256,0},{1,257},{257,1},{2,258},{258,2},{3,259},{259,3},{4... | collective-permute-start | bytes 196616 | tf_op jit(solution)/shard_map/ppermute | solution.py:251
  156.8 1.9 %copy.15 = bf16[4,8,8,1024]{3,2,0,1:T(8,128)(2,1)} copy(bf16[4,8,8,1024]{3,2,1,0:T(8,128)(2,1)} %bitcast.14) | data formatting | bytes 1048576 | tf_op jit(solution)/shard_map/reshape | solution.py:263
  158.6 2.9 %collective-permute-done.6 = f32[64,256]{1,0:T(8,128)} collective-permute-done((f32[64,256]{1,0:T(8,128)}, f32[64,256]{1,0:T(8,128)}, u32[]{:S(2)}, u32[]{:S(2)}) %collective-permute-start.6) | collective-permute-done | bytes 65568 | tf_op jit(solution)/shard_map/ppermute | solution.py:251
  161.6 0.9 add.3
  162.5 2.5 %shard_map.99 = bf16[64,4096]{1,0:T(8,128)(2,1)} custom-call(bf16[88,128,128]{2,1,0:T(8,128)(2,1)S(1)} %copy-done, s32[88]{0:T(128)S(1)} %copy-done.3, s32[88]{0:T(128)S(1)} %copy-done.4, s32[1]{0:T(128)S(6)} %copy.18.count, s32[1]{0:T(128)} %bitcast.parity, bf16[4,64,1280]{2,1,0:T(8,128)(2,1)S(1)} %all_to_all.22.grad, ...), custom_call_target="tpu_custom_call" | custom-call | flops 37748736 | bytes 5112520 | tf_op jit(solution)/shard_map/pallas_call | solution.py:152
  164.9 12.2 %all-gather.2 = f32[256,256]{1,0:T(8,128)S(1)} all-gather(f32[64,256]{1,0:T(8,128)S(1)} %add.3), channel_id=4, replica_groups=mesh['yh'=2,'zh'=4,'zl'=4,'x'=4,'yl'=2,'core'=2] {'x'}, dimensions={0}, use_global_device_ids=true | all-gather | bytes 327680 | tf_op jit(solution)/shard_map/all_gather | solution.py:261
  (20 shorter events, 0.8 us)
Async XLA Ops:
  0.6 32.6 %collective-permute-start.1 = (bf16[64,4096]{1,0:T(8,128)(2,1)}, bf16[64,4096]{1,0:T(8,128)(2,1)}, u32[]{:S(2)}, u32[]{:S(2)}) collective-permute-start(bf16[64,4096]{1,0:T(8,128)(2,1)} %bitcast.22), channel_id=1, source_target_pairs={{4,8},{8,4},{12,16},{16,12},{20,24},{24,20},{28,32},{32,28},{36,40... | collective-permute-start | bytes 1572872 | tf_op jit(solution)/shard_map/ppermute | solution.py:181
  16.0 20.3 %collective-permute-start = (bf16[64,4096]{1,0:T(8,128)(2,1)}, bf16[64,4096]{1,0:T(8,128)(2,1)}, u32[]{:S(2)}, u32[]{:S(2)}) collective-permute-start(bf16[64,4096]{1,0:T(8,128)(2,1)} %bitcast.23), channel_id=1, source_target_pairs={{0,4},{4,0},{8,12},{12,8},{16,20},{20,16},{24,28},{28,24},{32,36},... | collective-permute-start | bytes 1572872 | tf_op jit(solution)/shard_map/ppermute | solution.py:178
  17.9 26.7 %copy-start = (bf16[88,128,128]{2,1,0:T(8,128)(2,1)S(1)}, bf16[88,128,128]{2,1,0:T(8,128)(2,1)}, u32[]{:S(2)}) copy-start(bf16[88,128,128]{2,1,0:T(8,128)(2,1)} %values.9) | copy-start | bytes 8650756
  19.9 24.7 %copy-start.3 = (s32[88]{0:T(128)S(1)}, s32[88]{0:T(128)}, u32[]{:S(2)}) copy-start(s32[88]{0:T(128)} %rows.9) | copy-start | bytes 1060
  19.9 24.7 %copy-start.4 = (s32[88]{0:T(128)S(1)}, s32[88]{0:T(128)}, u32[]{:S(2)}) copy-start(s32[88]{0:T(128)} %cols.9) | copy-start | bytes 1060
  33.3 16.1 %collective-permute-start.2 = (bf16[64,4096]{1,0:T(8,128)(2,1)}, bf16[64,4096]{1,0:T(8,128)(2,1)}, u32[]{:S(2)}, u32[]{:S(2)}) collective-permute-start(bf16[64,4096]{1,0:T(8,128)(2,1)} %collective-permute-done.1.odd), channel_id=1, source_target_pairs={{0,4},{4,0},{8,12},{12,8},{16,20},{20,16},{24,28},{28,24},{32,36},... | collective-permute-start | bytes 1572872 | tf_op jit(solution)/shard_map/ppermute | solution.py:178
  36.3 21.4 %collective-permute-start.3 = (bf16[64,4096]{1,0:T(8,128)(2,1)}, bf16[64,4096]{1,0:T(8,128)(2,1)}, u32[]{:S(2)}, u32[]{:S(2)}) collective-permute-start(bf16[64,4096]{1,0:T(8,128)(2,1)} %collective-permute-done.even), channel_id=1, source_target_pairs={{4,8},{8,4},{12,16},{16,12},{20,24},{24,20},{28,32},{32,28},{36,40... | collective-permute-start | bytes 1572872 | tf_op jit(solution)/shard_map/ppermute | solution.py:181
  44.6 1.0 copy-start.1
  72.0 14.7 %copy-start.2 = (bf16[4,64,1024]{2,1,0:T(8,128)(2,1)}, bf16[4,64,1024]{2,1,0:T(8,128)(2,1)S(1)}, u32[]{:S(2)}) copy-start(bf16[4,64,1024]{2,1,0:T(8,128)(2,1)S(1)} %get-tuple-element.20) | copy-start | bytes 1572868
  86.8 27.3 %collective-permute-start.4 = (bf16[64,4096]{1,0:T(8,128)(2,1)}, bf16[64,4096]{1,0:T(8,128)(2,1)}, u32[]{:S(2)}, u32[]{:S(2)}) collective-permute-start(bf16[64,4096]{1,0:T(8,128)(2,1)} %get-tuple-element.22), channel_id=1, source_target_pairs={{0,4},{4,0},{8,12},{12,8},{16,20},{20,16},{24,28},{28,24},{32,36},... | collective-permute-start | bytes 1572872 | tf_op jit(solution)/shard_map/ppermute | solution.py:178
  88.7 25.4 %collective-permute-start.5 = (bf16[64,4096]{1,0:T(8,128)(2,1)}, bf16[64,4096]{1,0:T(8,128)(2,1)}, u32[]{:S(2)}, u32[]{:S(2)}) collective-permute-start(bf16[64,4096]{1,0:T(8,128)(2,1)} %get-tuple-element.23), channel_id=1, source_target_pairs={{4,8},{8,4},{12,16},{16,12},{20,24},{24,20},{28,32},{32,28},{36,40... | collective-permute-start | bytes 1572872 | tf_op jit(solution)/shard_map/ppermute | solution.py:181
  116.9 45.6 %collective-permute-start.7 = (bf16[64,4096]{1,0:T(8,128)(2,1)}, bf16[64,4096]{1,0:T(8,128)(2,1)}, u32[]{:S(2)}, u32[]{:S(2)}) collective-permute-start(bf16[64,4096]{1,0:T(8,128)(2,1)} %get-tuple-element.28), channel_id=1, source_target_pairs={{0,4},{4,0},{8,12},{12,8},{16,20},{20,16},{24,28},{28,24},{32,36},... | collective-permute-start | bytes 1572872 | tf_op jit(solution)/shard_map/ppermute | solution.py:178
  118.8 43.7 %collective-permute-start.8 = (bf16[64,4096]{1,0:T(8,128)(2,1)}, bf16[64,4096]{1,0:T(8,128)(2,1)}, u32[]{:S(2)}, u32[]{:S(2)}) collective-permute-start(bf16[64,4096]{1,0:T(8,128)(2,1)} %get-tuple-element.29), channel_id=1, source_target_pairs={{4,8},{8,4},{12,16},{16,12},{20,24},{24,20},{28,32},{32,28},{36,40... | collective-permute-start | bytes 1572872 | tf_op jit(solution)/shard_map/ppermute | solution.py:181
  126.2 30.5 %all-to-all-start.2 = ((bf16[4,64,1024]{2,1,0:T(8,128)(2,1)}), bf16[4,64,1024]{2,1,0:T(8,128)(2,1)}, u32[]{:S(2)}, u32[]{:S(2)}) async-start(bf16[4,64,1024]{2,1,0:T(8,128)(2,1)} %copy-done.2), calls=%async_computation.2 | async-start | bytes 1048576 | tf_op jit(solution)/shard_map/all_to_all | solution.py:164
  153.6 8.0 %collective-permute-start.6 = (f32[64,256]{1,0:T(8,128)}, f32[64,256]{1,0:T(8,128)}, u32[]{:S(2)}, u32[]{:S(2)}) collective-permute-start(f32[64,256]{1,0:T(8,128)} %reduce_sum.38), channel_id=1, source_target_pairs={{0,256},{256,0},{1,257},{257,1},{2,258},{258,2},{3,259},{259,3},{4... | collective-permute-start | bytes 196616 | tf_op jit(solution)/shard_map/ppermute | solution.py:251

commit v3 on v2

--- a/solution.py
+++ b/solution.py
@@ -5,7 +5,7 @@
 from jax.experimental.pallas import tpu as pltpu
 from jax.sharding import Mesh, PartitionSpec as P
 
-ROWS = ("yh", "zh", "zl", "x")
+ROWS = ("yh", "z", "x")
 COLS = ("yl", "core")
 BLOCK = 128
 NEAR = 5
@@ -77,16 +77,16 @@
         hidden[part] = total[:, part * width : (part + 1) * width].astype(hidden.dtype)
 
 
-def dense_kernel(hidden, given, output, sent):
+def dense_kernel(hidden, grad_out, weight, output, sent):
     parts, cols, width = hidden.shape
     full = parts * cols
     source = hidden[...].reshape(full, width)
-    weight_t = given[:, :, width:].reshape(full, full)
+    weight_t = weight[...]
     preact = jnp.dot(weight_t, source, preferred_element_type=jnp.float32)
     sigmoid = 1.0 / (1.0 + jnp.exp(-preact))
     output[...] = (preact * sigmoid).astype(output.dtype).reshape(output.shape)
     slope = sigmoid * (1.0 + preact * (1.0 - sigmoid))
-    grad = given[:, :, :width].reshape(full, width).astype(jnp.float32) * slope
+    grad = grad_out[...].reshape(full, width).astype(jnp.float32) * slope
     grad = grad.astype(jnp.bfloat16)
     back = lax.dot_general(
         weight_t, grad, (((0,), (0,)), ((), ())), preferred_element_type=jnp.float32
@@ -195,11 +195,13 @@
     own = features.T
     even1 = even_swap(own)
     odd1 = odd_swap(own)
-    weight_t = jnp.broadcast_to(weight.T, (n_cols, feat_cols, full))
-    given = swapped(jnp.concatenate([pieces(cotangent.T), weight_t], 2))
-    odd1, given = lax.optimization_barrier((odd1, given))
+    grad_out = swapped(pieces(cotangent.T))
+    odd1, grad_out = lax.optimization_barrier((odd1, grad_out))
     odd2 = odd_swap(even1)
     even2 = even_swap(odd1)
+    weight_t, _ = lax.optimization_barrier((weight.T, grad_out))
+    weight_t = lax.all_gather(weight_t, COLS, axis=0, tiled=True)
+    own, weight_t = lax.optimization_barrier((own, weight_t))
     (near,) = call(
         near_kernel, tables + (own, even1, odd1), table_specs + [VMEM] * 3, [wide], flops=54 * tile_flops
     )
@@ -213,8 +215,8 @@
     )
     output, grads = call(
         dense_kernel,
-        (swapped(hidden), given),
-        [VMEM] * 2,
+        (swapped(hidden), grad_out, weight_t),
+        [VMEM] * 3,
         [piece, jax.ShapeDtypeStruct((n_cols, feat_cols, width + full), jnp.bfloat16)],
         flops=6 * full * full * width,
     )
@@ -231,11 +233,7 @@
     odd_in = odd_swap(odd_far)
 
     weight_grad = grads[:, :, width:].astype(jnp.float32).sum(0)
-    weight_grad, even_far, odd_far = lax.optimization_barrier((weight_grad, even_far, odd_far))
-    output = swapped(output)
-    weight_grad = lax.all_gather(weight_grad, "zl").sum(0)
-    even_in, odd_in, weight_grad = lax.optimization_barrier((even_in, odd_in, weight_grad))
-
+    weight_grad = lax.all_gather(weight_grad, "z")
     even_near, odd_near = call(
         spread_near_kernel,
         tables + (grads, odd_in, even_in),
@@ -246,9 +244,8 @@
     )
     even_last = even_swap(even_near)
     odd_last = odd_swap(odd_near)
-    weight_grad, even_near, odd_near = lax.optimization_barrier((weight_grad, even_near, odd_near))
-    weight_grad = lax.all_gather(weight_grad, "zh").sum(0)
-    weight_grad = weight_grad + lax.ppermute(weight_grad, "yh", swap_pairs(2, 0))
+    output, even_near, odd_near = lax.optimization_barrier((output, even_near, odd_near))
+    output = swapped(output)
     (feature_grad,) = call(
         spread_own_kernel,
         tables + (grads, even_last, odd_last),
@@ -258,6 +255,8 @@
         flops=18 * tile_flops,
     )
     weight_grad, feature_grad = lax.optimization_barrier((weight_grad, feature_grad))
+    weight_grad = weight_grad.sum(0)
+    weight_grad = weight_grad + lax.ppermute(weight_grad, "yh", swap_pairs(2, 0))
     weight_grad = lax.all_gather(weight_grad, "x").sum(0)
     weight_grad = (weight_grad * (1.0 / (node_count * n_rows) ** 0.5)).T
     output = output.transpose(1, 0, 2).reshape(feat_cols, node_count).T
@@ -266,7 +265,7 @@
 
 def solution(mesh):
     n_rows, n_cols = mesh.shape["rows"], mesh.shape["cols"]
-    devices = mesh.devices.reshape(2, n_rows // 32, 4, 4, 2, n_cols // 2)
+    devices = mesh.devices.reshape(2, n_rows // 8, 4, 2, n_cols // 2)
     fine = Mesh(devices, ROWS + COLS)
     in_specs = (
         P(ROWS, COLS),

time: 179 us -> 189 us (1.056)
  the two profiles are of different devices: /device:TPU:8 before, /device:TPU:2 now
where the time goes in v3:
time: 189 us
  starting transfers between devices  63.1 us (33%)
  blocking collectives  54.4 us (29%)
  waiting for transfers between devices  36.1 us (19%)
  between operations  14.9 us (8%)
  Pallas kernels  10.2 us (5%)
  local copies, waits for them, and re-layouts  7.14 us (4%)
  other arithmetic  2.6 us (1%)
    ppermute x4, starting transfers between devices, even_swap(): return lax.ppermute(value, ROWS, even_pairs)  44.1 us
    all_to_all x3, blocking collectives, swapped(): return lax.all_to_all(value, COLS, 0, 0, tiled=True)  35.4 us
    ppermute x4, waiting for transfers between devices, even_swap(): return lax.ppermute(value, ROWS, even_pairs)  15.5 us
    all_gather x1, waiting for transfers between devices, local(): weight_grad = lax.all_gather(weight_grad, 'z')  15.2 us
    all_gather x1, blocking collectives, local(): weight_grad = lax.all_gather(weight_grad, 'x').sum(0)  13.3 us
    pallas_call x6, Pallas kernels, call(): pl.pallas_call(kernel, out_shape=outs, in_specs=specs, out_specs=[VMEM] *...  10.2 us
    ppermute x4, starting transfers between devices, odd_swap(): return lax.ppermute(value, ROWS, odd_pairs)  9.95 us
    all_gather x1, blocking collectives, local(): weight_t = lax.all_gather(weight_t, COLS, axis=0, tiled=True)  5.64 us
  transfers between devices with their start and end apart: 11, of which 6 were waited for; matrix products, arithmetic and copies ran while one was open for 2% of the time, Pallas kernels for 4%

profile of v3, /device:TPU:2, one launch (start us, length us, event | category | flops | bytes accessed | tf_op | source)
XLA Modules:
  0.0 188.5 jit_solution(12217565044385270444)
XLA Ops:
  7.2 3.4 %collective-permute-start = (bf16[64,4096]{1,0:T(8,128)(2,1)}, bf16[64,4096]{1,0:T(8,128)(2,1)S(1)}, u32[]{:S(2)}, u32[]{:S(2)}) collective-permute-start(bf16[64,4096]{1,0:T(8,128)(2,1)} %bitcast.21), channel_id=1, source_target_pairs={{4,8},{8,4},{12,16},{16,12},{20,24},{24,20},{28,32},{32,28},{36,40... | collective-permute-start | bytes 1572872 | tf_op jit(solution)/shard_map/ppermute | solution.py:181
  10.6 15.3 %collective-permute-start.1 = (bf16[64,4096]{1,0:T(8,128)(2,1)}, bf16[64,4096]{1,0:T(8,128)(2,1)S(1)}, u32[]{:S(2)}, u32[]{:S(2)}) collective-permute-start(bf16[64,4096]{1,0:T(8,128)(2,1)} %bitcast.22), channel_id=1, source_target_pairs={{0,4},{4,0},{8,12},{12,8},{16,20},{20,16},{24,28},{28,24},{32,36},... | collective-permute-start | bytes 1572872 | tf_op jit(solution)/shard_map/ppermute | solution.py:178
  25.9 1.1 copy.17
  27.0 11.2 %all_to_all.20.grad_out = bf16[4,64,1024]{2,1,0:T(8,128)(2,1)S(1)} all-to-all(bf16[4,64,1024]{2,1,0:T(8,128)(2,1)S(1)} %bitcast.24), channel_id=1, replica_groups=mesh['yh'=2,'z'=16,'x'=4,'yl'=2,'core'=2] {'yl','core'}, dimensions={0} | all-to-all | bytes 1048576 | tf_op jit(solution)/shard_map/all_to_all | solution.py:164
  38.2 3.8 %collective-permute-start.2 = (bf16[64,4096]{1,0:T(8,128)(2,1)S(1)}, bf16[64,4096]{1,0:T(8,128)(2,1)S(1)}, u32[]{:S(2)}, u32[]{:S(2)}) collective-permute-start(bf16[64,4096]{1,0:T(8,128)(2,1)S(1)} %collective-permute-done.odd), channel_id=1, source_target_pairs={{0,4},{4,0},{8,12},{12,8},{16,20},{20,16},{24,28},{28,24},{32,36},... | collective-permute-start | bytes 1572872 | tf_op jit(solution)/shard_map/ppermute | solution.py:178
  42.0 1.9 %collective-permute-start.3 = (bf16[64,4096]{1,0:T(8,128)(2,1)S(1)}, bf16[64,4096]{1,0:T(8,128)(2,1)S(1)}, u32[]{:S(2)}, u32[]{:S(2)}) collective-permute-start(bf16[64,4096]{1,0:T(8,128)(2,1)S(1)} %collective-permute-done.1.even), channel_id=1, source_target_pairs={{4,8},{8,4},{12,16},{16,12},{20,24},{24,20},{28,32},{32,28},{36,40... | collective-permute-start | bytes 1572872 | tf_op jit(solution)/shard_map/ppermute | solution.py:181
  44.6 5.6 %all_gather.15.weight = bf16[256,256]{1,0:T(8,128)(2,1)S(1)} all-gather(bf16[64,256]{1,0:T(8,128)(2,1)} %bitcast.30), channel_id=1, replica_groups=mesh['yh'=2,'z'=16,'x'=4,'yl'=2,'core'=2] {'yl','core'}, dimensions={0}, use_global_device_ids=true | all-gather | bytes 163840 | tf_op jit(solution)/shard_map/all_gather | solution.py:203
  50.2 1.8 copy-done
  52.1 1.0 copy-done.2
  54.4 1.9 shard_map.94.start
  56.3 1.2 collective-permute-done.3.odd
  57.5 1.5 shard_map.95
  59.1 11.5 %all_to_all.21.hidden = bf16[4,64,1024]{2,1,0:T(8,128)(2,1)S(1)} all-to-all(bf16[4,64,1024]{2,1,0:T(8,128)(2,1)S(1)} %shard_map.95), channel_id=1, replica_groups=mesh['yh'=2,'z'=16,'x'=4,'yl'=2,'core'=2] {'yl','core'}, dimensions={0} | all-to-all | bytes 1048576 | tf_op jit(solution)/shard_map/all_to_all | solution.py:164
  70.6 1.0 shard_map.96
  71.7 12.7 %all_to_all.22.grad = bf16[4,64,1280]{2,1,0:T(8,128)(2,1)S(1)} all-to-all(bf16[4,64,1280]{2,1,0:T(8,128)(2,1)S(1)} %get-tuple-element.23), channel_id=1, replica_groups=mesh['yh'=2,'z'=16,'x'=4,'yl'=2,'core'=2] {'yl','core'}, dimensions={0} | all-to-all | bytes 1310720 | tf_op jit(solution)/shard_map/all_to_all | solution.py:164
  85.0 1.3 shard_map.97
  86.3 2.7 %collective-permute-start.4 = (bf16[64,4096]{1,0:T(8,128)(2,1)S(1)}, bf16[64,4096]{1,0:T(8,128)(2,1)S(1)}, u32[]{:S(2)}, u32[]{:S(2)}) collective-permute-start(bf16[64,4096]{1,0:T(8,128)(2,1)S(1)} %get-tuple-element.24), channel_id=1, source_target_pairs={{4,8},{8,4},{12,16},{16,12},{20,24},{24,20},{28,32},{32,28},{36,40... | collective-permute-start | bytes 1572872 | tf_op jit(solution)/shard_map/ppermute | solution.py:181
  89.0 15.2 %collective-permute-start.5 = (bf16[64,4096]{1,0:T(8,128)(2,1)S(1)}, bf16[64,4096]{1,0:T(8,128)(2,1)S(1)}, u32[]{:S(2)}, u32[]{:S(2)}) collective-permute-start(bf16[64,4096]{1,0:T(8,128)(2,1)S(1)} %get-tuple-element.25), channel_id=1, source_target_pairs={{0,4},{4,0},{8,12},{12,8},{16,20},{20,16},{24,28},{28,24},{32,36},... | collective-permute-start | bytes 1572872 | tf_op jit(solution)/shard_map/ppermute | solution.py:178
  104.2 11.3 %collective-permute-done.5.from_even = bf16[64,4096]{1,0:T(8,128)(2,1)S(1)} collective-permute-done((bf16[64,4096]{1,0:T(8,128)(2,1)S(1)}, bf16[64,4096]{1,0:T(8,128)(2,1)S(1)}, u32[]{:S(2)}, u32[]{:S(2)}) %collective-permute-start.5) | collective-permute-done | bytes 524320 | tf_op jit(solution)/shard_map/ppermute | solution.py:178
  115.5 2.1 %shard_map.98 = (bf16[64,4096]{1,0:T(8,128)(2,1)}, bf16[64,4096]{1,0:T(8,128)(2,1)}) custom-call(bf16[88,128,128]{2,1,0:T(8,128)(2,1)S(1)} %copy-done.1, s32[88]{0:T(128)S(1)} %copy-done.5, s32[88]{0:T(128)S(1)} %copy-done.7, s32[1]{0:T(128)S(6)} %copy.18.count, s32[1]{0:T(128)} %bitcast.parity, bf16[4,64,1280]{2,1,0:T(8,128)(2,1)S(1)} %all_to_all.22.grad, ...), custom_call_target="tpu_custom_call" | custom-call | flops 75497472 | bytes 5636808 | tf_op jit(solution)/shard_map/pallas_call | solution.py:152
  117.5 9.9 %collective-permute-start.6 = (bf16[64,4096]{1,0:T(8,128)(2,1)}, bf16[64,4096]{1,0:T(8,128)(2,1)}, u32[]{:S(2)}, u32[]{:S(2)}) collective-permute-start(bf16[64,4096]{1,0:T(8,128)(2,1)} %get-tuple-element.26), channel_id=1, source_target_pairs={{0,4},{4,0},{8,12},{12,8},{16,20},{20,16},{24,28},{28,24},{32,36},... | collective-permute-start | bytes 1572872 | tf_op jit(solution)/shard_map/ppermute | solution.py:178
  127.4 1.9 %collective-permute-start.7 = (bf16[64,4096]{1,0:T(8,128)(2,1)}, bf16[64,4096]{1,0:T(8,128)(2,1)}, u32[]{:S(2)}, u32[]{:S(2)}) collective-permute-start(bf16[64,4096]{1,0:T(8,128)(2,1)} %get-tuple-element.27), channel_id=1, source_target_pairs={{4,8},{8,4},{12,16},{16,12},{20,24},{24,20},{28,32},{32,28},{36,40... | collective-permute-start | bytes 1572872 | tf_op jit(solution)/shard_map/ppermute | solution.py:181
  129.4 4.2 %all-to-all-start.3 = ((bf16[4,64,1024]{2,1,0:T(8,128)(2,1)}), bf16[4,64,1024]{2,1,0:T(8,128)(2,1)}, u32[]{:S(2)}, u32[]{:S(2)}) async-start(bf16[4,64,1024]{2,1,0:T(8,128)(2,1)} %copy-done.3), calls=%async_computation.3 | async-start | bytes 1048576 | tf_op jit(solution)/shard_map/all_to_all | solution.py:164
  133.5 4.2 %collective-permute-done.6.from_even = bf16[64,4096]{1,0:T(8,128)(2,1)} collective-permute-done((bf16[64,4096]{1,0:T(8,128)(2,1)}, bf16[64,4096]{1,0:T(8,128)(2,1)}, u32[]{:S(2)}, u32[]{:S(2)}) %collective-permute-start.6) | collective-permute-done | bytes 524320 | tf_op jit(solution)/shard_map/ppermute | solution.py:178
  137.7 3.4 %collective-permute-done.7.from_odd = bf16[64,4096]{1,0:T(8,128)(2,1)} collective-permute-done((bf16[64,4096]{1,0:T(8,128)(2,1)}, bf16[64,4096]{1,0:T(8,128)(2,1)}, u32[]{:S(2)}, u32[]{:S(2)}) %collective-permute-start.7) | collective-permute-done | bytes 524320 | tf_op jit(solution)/shard_map/ppermute | solution.py:181
  141.1 2.5 %shard_map.99 = bf16[64,4096]{1,0:T(8,128)(2,1)} custom-call(bf16[88,128,128]{2,1,0:T(8,128)(2,1)S(1)} %copy-done.1, s32[88]{0:T(128)S(1)} %copy-done.5, s32[88]{0:T(128)S(1)} %copy-done.7, s32[1]{0:T(128)S(6)} %copy.18.count, s32[1]{0:T(128)} %bitcast.parity, bf16[4,64,1280]{2,1,0:T(8,128)(2,1)S(1)} %all_to_all.22.grad, ...), custom_call_target="tpu_custom_call" | custom-call | flops 37748736 | bytes 5112520 | tf_op jit(solution)/shard_map/pallas_call | solution.py:152
  143.6 15.2 %all-gather.4.cloned.1.call-done = f32[1024,256]{1,0:T(8,128)} async-done(((f32[64,256]{1,0:T(8,128)}), f32[1024,256]{1,0:T(8,128)}) %all-gather.4.cloned.1.call-update) | async-done | bytes 1048592 | tf_op jit(solution)/shard_map/all_gather | solution.py:236
  158.8 1.3 reduce_sum.28
  160.0 4.9 %collective-permute-start.8 = (f32[64,256]{1,0:T(8,128)S(1)}, f32[64,256]{1,0:T(8,128)S(1)}, u32[]{:S(2)}, u32[]{:S(2)}) collective-permute-start(f32[64,256]{1,0:T(8,128)S(1)} %reduce_sum.28), channel_id=1, source_target_pairs={{0,256},{256,0},{1,257},{257,1},{2,258},{258,2},{3,259},{259,3},{4... | collective-permute-start | bytes 196616 | tf_op jit(solution)/shard_map/ppermute | solution.py:259
  165.0 1.9 copy.15
  166.8 0.9 collective-permute-done.8
  167.7 13.3 %all-gather.1 = f32[256,256]{1,0:T(8,128)S(1)} all-gather(f32[64,256]{1,0:T(8,128)S(1)} %add.3), channel_id=3, replica_groups=mesh['yh'=2,'z'=16,'x'=4,'yl'=2,'core'=2] {'x'}, dimensions={0}, use_global_device_ids=true | all-gather | bytes 327680 | tf_op jit(solution)/shard_map/all_gather | solution.py:260
  (25 shorter events, 2.7 us)
Async XLA Ops:
  7.2 151.6 %all-gather.4.cloned.1.call-start = ((), (), s32[]{:S(2)}) async-start(), calls=%async_computation.4 | async-start | bytes 1114112 | tf_op jit(solution)/shard_map/all_gather | solution.py:236
  7.2 31.0 %collective-permute-start = (bf16[64,4096]{1,0:T(8,128)(2,1)}, bf16[64,4096]{1,0:T(8,128)(2,1)S(1)}, u32[]{:S(2)}, u32[]{:S(2)}) collective-permute-start(bf16[64,4096]{1,0:T(8,128)(2,1)} %bitcast.21), channel_id=1, source_target_pairs={{4,8},{8,4},{12,16},{16,12},{20,24},{24,20},{28,32},{32,28},{36,40... | collective-permute-start | bytes 1572872 | tf_op jit(solution)/shard_map/ppermute | solution.py:181
  10.6 31.4 %collective-permute-start.1 = (bf16[64,4096]{1,0:T(8,128)(2,1)}, bf16[64,4096]{1,0:T(8,128)(2,1)S(1)}, u32[]{:S(2)}, u32[]{:S(2)}) collective-permute-start(bf16[64,4096]{1,0:T(8,128)(2,1)} %bitcast.22), channel_id=1, source_target_pairs={{0,4},{4,0},{8,12},{12,8},{16,20},{20,16},{24,28},{28,24},{32,36},... | collective-permute-start | bytes 1572872 | tf_op jit(solution)/shard_map/ppermute | solution.py:178
  38.2 18.1 %collective-permute-start.2 = (bf16[64,4096]{1,0:T(8,128)(2,1)S(1)}, bf16[64,4096]{1,0:T(8,128)(2,1)S(1)}, u32[]{:S(2)}, u32[]{:S(2)}) collective-permute-start(bf16[64,4096]{1,0:T(8,128)(2,1)S(1)} %collective-permute-done.odd), channel_id=1, source_target_pairs={{0,4},{4,0},{8,12},{12,8},{16,20},{20,16},{24,28},{28,24},{32,36},... | collective-permute-start | bytes 1572872 | tf_op jit(solution)/shard_map/ppermute | solution.py:178
  42.0 15.5 %collective-permute-start.3 = (bf16[64,4096]{1,0:T(8,128)(2,1)S(1)}, bf16[64,4096]{1,0:T(8,128)(2,1)S(1)}, u32[]{:S(2)}, u32[]{:S(2)}) collective-permute-start(bf16[64,4096]{1,0:T(8,128)(2,1)S(1)} %collective-permute-done.1.even), channel_id=1, source_target_pairs={{4,8},{8,4},{12,16},{16,12},{20,24},{24,20},{28,32},{32,28},{36,40... | collective-permute-start | bytes 1572872 | tf_op jit(solution)/shard_map/ppermute | solution.py:181
  50.2 1.8 copy-start
  52.1 1.0 copy-start.2
  53.1 0.7 copy-start.4
  53.8 0.7 copy-start.6
  59.1 25.9 %copy-start.1 = (bf16[88,128,128]{2,1,0:T(8,128)(2,1)S(1)}, bf16[88,128,128]{2,1,0:T(8,128)(2,1)}, u32[]{:S(2)}) copy-start(bf16[88,128,128]{2,1,0:T(8,128)(2,1)} %values.9) | copy-start | bytes 8650756
  59.1 25.9 %copy-start.5 = (s32[88]{0:T(128)S(1)}, s32[88]{0:T(128)}, u32[]{:S(2)}) copy-start(s32[88]{0:T(128)} %rows.9) | copy-start | bytes 1060
  59.1 25.9 %copy-start.7 = (s32[88]{0:T(128)S(1)}, s32[88]{0:T(128)}, u32[]{:S(2)}) copy-start(s32[88]{0:T(128)} %cols.9) | copy-start | bytes 1060
  71.6 12.7 %copy-start.3 = (bf16[4,64,1024]{2,1,0:T(8,128)(2,1)}, bf16[4,64,1024]{2,1,0:T(8,128)(2,1)S(1)}, u32[]{:S(2)}) copy-start(bf16[4,64,1024]{2,1,0:T(8,128)(2,1)S(1)} %get-tuple-element.28) | copy-start | bytes 1572868
  86.3 17.9 %collective-permute-start.4 = (bf16[64,4096]{1,0:T(8,128)(2,1)S(1)}, bf16[64,4096]{1,0:T(8,128)(2,1)S(1)}, u32[]{:S(2)}, u32[]{:S(2)}) collective-permute-start(bf16[64,4096]{1,0:T(8,128)(2,1)S(1)} %get-tuple-element.24), channel_id=1, source_target_pairs={{4,8},{8,4},{12,16},{16,12},{20,24},{24,20},{28,32},{32,28},{36,40... | collective-permute-start | bytes 1572872 | tf_op jit(solution)/shard_map/ppermute | solution.py:181
  89.0 26.5 %collective-permute-start.5 = (bf16[64,4096]{1,0:T(8,128)(2,1)S(1)}, bf16[64,4096]{1,0:T(8,128)(2,1)S(1)}, u32[]{:S(2)}, u32[]{:S(2)}) collective-permute-start(bf16[64,4096]{1,0:T(8,128)(2,1)S(1)} %get-tuple-element.25), channel_id=1, source_target_pairs={{0,4},{4,0},{8,12},{12,8},{16,20},{20,16},{24,28},{28,24},{32,36},... | collective-permute-start | bytes 1572872 | tf_op jit(solution)/shard_map/ppermute | solution.py:178
  117.5 20.2 %collective-permute-start.6 = (bf16[64,4096]{1,0:T(8,128)(2,1)}, bf16[64,4096]{1,0:T(8,128)(2,1)}, u32[]{:S(2)}, u32[]{:S(2)}) collective-permute-start(bf16[64,4096]{1,0:T(8,128)(2,1)} %get-tuple-element.26), channel_id=1, source_target_pairs={{0,4},{4,0},{8,12},{12,8},{16,20},{20,16},{24,28},{28,24},{32,36},... | collective-permute-start | bytes 1572872 | tf_op jit(solution)/shard_map/ppermute | solution.py:178
  127.4 13.7 %collective-permute-start.7 = (bf16[64,4096]{1,0:T(8,128)(2,1)}, bf16[64,4096]{1,0:T(8,128)(2,1)}, u32[]{:S(2)}, u32[]{:S(2)}) collective-permute-start(bf16[64,4096]{1,0:T(8,128)(2,1)} %get-tuple-element.27), channel_id=1, source_target_pairs={{4,8},{8,4},{12,16},{16,12},{20,24},{24,20},{28,32},{32,28},{36,40... | collective-permute-start | bytes 1572872 | tf_op jit(solution)/shard_map/ppermute | solution.py:181
  129.4 35.6 %all-to-all-start.3 = ((bf16[4,64,1024]{2,1,0:T(8,128)(2,1)}), bf16[4,64,1024]{2,1,0:T(8,128)(2,1)}, u32[]{:S(2)}, u32[]{:S(2)}) async-start(bf16[4,64,1024]{2,1,0:T(8,128)(2,1)} %copy-done.3), calls=%async_computation.3 | async-start | bytes 1048576 | tf_op jit(solution)/shard_map/all_to_all | solution.py:164
  160.0 7.7 %collective-permute-start.8 = (f32[64,256]{1,0:T(8,128)S(1)}, f32[64,256]{1,0:T(8,128)S(1)}, u32[]{:S(2)}, u32[]{:S(2)}) collective-permute-start(f32[64,256]{1,0:T(8,128)S(1)} %reduce_sum.28), channel_id=1, source_target_pairs={{0,256},{256,0},{1,257},{257,1},{2,258},{258,2},{3,259},{259,3},{4... | collective-permute-start | bytes 196616 | tf_op jit(solution)/shard_map/ppermute | solution.py:259
Sparse Core Ops, SparseCore 0:
  85.1 73.5 all-gather.3

commit v4 on v3

v4 whole, which is shorter than its diff:
```python
import jax
import jax.numpy as jnp
from jax import lax
from jax.experimental import pallas as pl
from jax.experimental.pallas import tpu as pltpu
from jax.sharding import Mesh, PartitionSpec as P

ROWS = ("yh", "z", "x")
COLS = ("yl", "core")
BLOCK = 128
NEAR = 5
VMEM = pl.BlockSpec(memory_space=pltpu.VMEM)
SMEM = pl.BlockSpec(memory_space=pltpu.SMEM)
BATCH = 6


def swap_pairs(count, odd):
    pairs = []
    for first in range(odd, count, 2):
        second = (first + 1) % count
        pairs += [(first, second), (second, first)]
    return pairs


def lanes(index):
    return pl.ds(pl.multiple_of(index * BLOCK, BLOCK), BLOCK)


def wide_lanes(index, width):
    return pl.ds(pl.multiple_of(index * width, width), width)


def each_tile(offset, count, values_ref, term, add):
    slots = values_ref.shape[0]
    per_offset = -(-slots // NEAR)
    for first in range(0, per_offset, BATCH):
        held = []
        for k in range(first, min(first + BATCH, per_offset)):
            slot = k * NEAR + offset
            live = (slot < count).astype(jnp.float32)
            slot = jnp.minimum(slot, slots - 1)
            held.append((slot, term(slot) * live))
        for slot, product in held:
            add(slot, product)


def gather_terms(info, source_ref, total_ref, offset):
    values_ref, rows_ref, cols_ref, count = info
    blocks = source_ref.shape[1] // BLOCK

    def term(slot):
        source = source_ref[:, lanes(lax.rem(cols_ref[slot], blocks))]
        return lax.dot_general(
            source, values_ref[slot], (((1,), (1,)), ((), ())), preferred_element_type=jnp.float32
        )

    def add(slot, product):
        where = lanes(rows_ref[slot])
        total_ref[:, where] = total_ref[:, where] + product

    each_tile(offset, count, values_ref, term, add)


def near_kernel(values, rows, cols, count, place, own, even, odd, total):
    total[...] = jnp.zeros_like(total)
    info = (values, rows, cols, count[0])
    even_offset = 3 - 2 * place[0]
    gather_terms(info, own, total, 2)
    gather_terms(info, even, total, even_offset)
    gather_terms(info, odd, total, 4 - even_offset)


def pack_kernel(place, cotangent, weight, *packed):
    width = packed[0].shape[1] - weight.shape[1]
    for step, out in enumerate(packed):
        out[:, :width] = cotangent[:, wide_lanes(place[1] ^ step, width)]
        out[:, width:] = weight[...]


def far_kernel(values, rows, cols, count, place, start, even, odd, *rest):
    hidden, total = rest[:-1], rest[-1]
    total[...] = start[...]
    info = (values, rows, cols, count[0])
    even_offset = 4 - 4 * place[0]
    gather_terms(info, even, total, even_offset)
    gather_terms(info, odd, total, 4 - even_offset)
    for step, out in enumerate(hidden):
        width = out.shape[1]
        out[...] = total[:, wide_lanes(place[1] ^ step, width)].astype(out.dtype)


def dense_kernel(place, *refs):
    n = (len(refs) - 2) // 4
    hidden, given, output, sent = (refs[k * n : (k + 1) * n] for k in range(4))
    source_ref, back_ref = refs[4 * n :]
    cols, width = hidden[0].shape

    def group(step):
        return pl.ds(pl.multiple_of((place[1] ^ step) * cols, cols), cols)

    for step in range(n):
        source_ref[group(step), :] = hidden[step][...]
    source = source_ref[...]
    weight_t = jnp.concatenate([ref[:, width:] for ref in given], 0)
    preact = jnp.dot(weight_t, source, preferred_element_type=jnp.float32)
    sigmoid = 1.0 / (1.0 + jnp.exp(-preact))
    value = (preact * sigmoid).astype(jnp.bfloat16)
    slope = sigmoid * (1.0 + preact * (1.0 - sigmoid))
    grad = jnp.concatenate([ref[:, :width] for ref in given], 0).astype(jnp.float32) * slope
    grad = grad.astype(jnp.bfloat16)
    back = lax.dot_general(
        weight_t, grad, (((0,), (0,)), ((), ())), preferred_element_type=jnp.float32
    )
    back_ref[...] = back.astype(back_ref.dtype)
    weight_term = lax.dot_general(
        grad, source, (((1,), (1,)), ((), ())), preferred_element_type=jnp.float32
    ).astype(jnp.bfloat16)
    for step in range(n):
        here = slice(step * cols, (step + 1) * cols)
        output[step][...] = value[here]
        sent[step][:, :width] = back_ref[group(step), :]
        sent[step][:, width:] = weight_term[here]


def spread_terms(info, grad_ref, total_ref, offset):
    values_ref, rows_ref, cols_ref, count = info
    blocks = total_ref.shape[1] // BLOCK
    per_part = blocks // grad_ref.shape[0]

    def term(slot):
        row = rows_ref[slot]
        part = row // per_part
        source = grad_ref[part, :, lanes(row - part * per_part)]
        return jnp.dot(source, values_ref[slot], preferred_element_type=jnp.float32)

    def add(slot, product):
        where = lanes(lax.rem(cols_ref[slot], blocks))
        total_ref[:, where] = total_ref[:, where] + product

    each_tile(offset, count, values_ref, term, add)


def spread_far_kernel(values, rows, cols, count, place, *refs):
    n = len(refs) - 6
    sent = refs[:n]
    even, odd, grads, weight_sum, even_total, odd_total = refs[n:]
    width = grads.shape[2]
    for step, ref in enumerate(sent):
        grads[place[1] ^ step] = ref[:, :width]
    info = (values, rows, cols, count[0])
    even_offset = 4 - 4 * place[0]
    for offset, total, out in ((even_offset, even_total, even), (4 - even_offset, odd_total, odd)):
        total[...] = jnp.zeros_like(total)
        spread_terms(info, grads, total, offset)
        out[...] = total[...].astype(out.dtype)
    terms = [ref[:, width:].astype(jnp.float32) for ref in sent]
    weight_sum[...] = sum(terms[1:], terms[0])


def spread_near_kernel(
    values, rows, cols, count, place, grad, from_odd, from_even, even, odd, even_total, odd_total
):
    info = (values, rows, cols, count[0])
    even_offset = 3 - 2 * place[0]
    for offset, start, total, out in (
        (even_offset, from_odd, even_total, even),
        (4 - even_offset, from_even, odd_total, odd),
    ):
        total[...] = start[...].astype(total.dtype)
        spread_terms(info, grad, total, offset)
        out[...] = total[...].astype(out.dtype)


def spread_own_kernel(values, rows, cols, count, place, grad, from_even, from_odd, *refs):
    parts, (out, output, total) = refs[:-3], refs[-3:]
    info = (values, rows, cols, count[0])
    total[...] = from_even[...].astype(total.dtype) + from_odd[...].astype(total.dtype)
    spread_terms(info, grad, total, 2)
    out[...] = total[...].astype(out.dtype)
    for step, part in enumerate(parts):
        output[:, wide_lanes(place[1] ^ step, part.shape[1])] = part[...]


def call(kernel, args, specs, outs, scratch=(), flops=0):
    moved = sum(a.size * a.dtype.itemsize for a in args)
    moved += sum(o.size * o.dtype.itemsize for o in outs)
    return pl.pallas_call(
        kernel,
        out_shape=outs,
        in_specs=specs,
        out_specs=[VMEM] * len(outs),
        scratch_shapes=scratch,
        cost_estimate=pl.CostEstimate(flops=flops, bytes_accessed=moved, transcendentals=0),
        compiler_params=pltpu.CompilerParams(vmem_limit_bytes=24 << 20),
    )(*args)


def swapped(values):
    def pairs(step):
        return [(source, source ^ step) for source in range(len(values))]

    return [values[0]] + [
        lax.ppermute(value, COLS, pairs(step)) for step, value in enumerate(values) if step
    ]


def doubled(value, axis, step):
    count = lax.axis_size(axis)
    return value + lax.ppermute(value, axis, [(source, source ^ step) for source in range(count)])


def local(features, weight, tile_values, tile_rows, tile_cols, tile_count, cotangent):
    node_count, feat_cols = features.shape
    slots, tile, _ = tile_values.shape
    n_rows = lax.axis_size(ROWS)
    n_cols = lax.axis_size(COLS)
    width = node_count // n_cols
    full = feat_cols * n_cols
    even_pairs = swap_pairs(n_rows, 0)
    odd_pairs = swap_pairs(n_rows, 1)

    def even_swap(value):
        return lax.ppermute(value, ROWS, even_pairs)

    def odd_swap(value):
        return lax.ppermute(value, ROWS, odd_pairs)

    place = jnp.stack([lax.rem(lax.axis_index("x"), 2), lax.axis_index(COLS)]).astype(jnp.int32)
    tables = (tile_values, tile_rows, tile_cols, tile_count, place)
    table_specs = [VMEM, SMEM, SMEM, SMEM, SMEM]
    tile_flops = 2 * tile * tile * feat_cols

    def arrays(number, shape, dtype=jnp.bfloat16):
        return [jax.ShapeDtypeStruct(shape, dtype)] * number

    whole = (feat_cols, node_count)
    total = pltpu.VMEM(whole, jnp.float32)

    own = features.T
    even1 = even_swap(own)
    odd1 = odd_swap(own)
    given = call(
        pack_kernel,
        (place, cotangent.T, weight.T),
        [SMEM, VMEM, VMEM],
        arrays(n_cols, (feat_cols, width + full)),
    )
    even1, _ = lax.optimization_barrier((even1, given[0]))
    given = swapped(given)
    odd2 = odd_swap(even1)
    even2 = even_swap(odd1)
    (near,) = call(
        near_kernel,
        tables + (own, even1, odd1),
        table_specs + [VMEM] * 3,
        arrays(1, whole, jnp.float32),
        flops=54 * tile_flops,
    )
    hidden = call(
        far_kernel,
        tables + (near, even2, odd2),
        table_specs + [VMEM] * 3,
        arrays(n_cols, (feat_cols, width)),
        scratch=[total],
        flops=36 * tile_flops,
    )
    both = call(
        dense_kernel,
        (place, *swapped(hidden), *given),
        [SMEM] + [VMEM] * (2 * n_cols),
        arrays(n_cols, (feat_cols, width)) + arrays(n_cols, (feat_cols, width + full)),
        scratch=[pltpu.VMEM((full, width), jnp.bfloat16)] * 2,
        flops=6 * full * full * width,
    )
    output, sent = list(both[:n_cols]), swapped(both[n_cols:])
    even_far, odd_far, grads, weight_grad = call(
        spread_far_kernel,
        tables + tuple(sent),
        table_specs + [VMEM] * n_cols,
        arrays(2, whole) + arrays(1, (n_cols, feat_cols, width)) + arrays(1, (feat_cols, full), jnp.float32),
        scratch=[total, total],
        flops=36 * tile_flops,
    )
    even_in = even_swap(even_far)
    odd_in = odd_swap(odd_far)
    weight_grad = doubled(doubled(weight_grad, "z", 1), "z", 2)
    even_in, odd_in, weight_grad = lax.optimization_barrier((even_in, odd_in, weight_grad))
    even_near, odd_near = call(
        spread_near_kernel,
        tables + (grads, odd_in, even_in),
        table_specs + [VMEM] * 3,
        arrays(2, whole),
        scratch=[total, total],
        flops=36 * tile_flops,
    )
    even_last = even_swap(even_near)
    odd_last = odd_swap(odd_near)
    output[0], even_near = lax.optimization_barrier((output[0], even_near))
    output = swapped(output)
    weight_grad = doubled(weight_grad, "z", 4)
    feature_grad, output = call(
        spread_own_kernel,
        tables + (grads, even_last, odd_last, *output),
        table_specs + [VMEM] * (3 + n_cols),
        arrays(2, whole),
        scratch=[total],
        flops=18 * tile_flops,
    )
    weight_grad = doubled(weight_grad, "z", 8)
    weight_grad = doubled(weight_grad, "yh", 1)
    weight_grad = lax.all_gather(weight_grad, "x").sum(0)
    weight_grad = (weight_grad * (1.0 / (node_count * n_rows) ** 0.5)).T
    return (output.T, feature_grad.T, weight_grad)


def solution(mesh):
    n_rows, n_cols = mesh.shape["rows"], mesh.shape["cols"]
    devices = mesh.devices.reshape(2, n_rows // 8, 4, 2, n_cols // 2)
    fine = Mesh(devices, ROWS + COLS)
    in_specs = (
        P(ROWS, COLS),
        P(None, COLS),
        P(ROWS, None, None),
        P(ROWS),
        P(ROWS),
        P(ROWS),
        P(ROWS, COLS),
    )
    out_specs = (P(ROWS, COLS), P(ROWS, COLS), P(None, COLS))
    return jax.shard_map(local, mesh=fine, in_specs=in_specs, out_specs=out_specs, check_vma=False)
```

time: 189 us -> 182 us (0.963)
  the two profiles are of different devices: /device:TPU:2 before, /device:TPU:1 now
where the time goes in v4:
time: 182 us; the launch traced here: 180 us
  starting transfers between devices  99.5 us (55%)
  waiting for transfers between devices  46.5 us (26%)
  Pallas kernels  12.9 us (7%)
  blocking collectives  10.1 us (6%)
  local copies, waits for them, and re-layouts  5.97 us (3%)
  other arithmetic  3.2 us (2%)
    ppermute x4, starting transfers between devices, odd_swap(): return lax.ppermute(value, ROWS, odd_pairs)  36.6 us
    ppermute x12, starting transfers between devices, swapped(): lax.ppermute(value, COLS, pairs(step))  36.5 us
    ppermute x5, waiting for transfers between devices, doubled(): lax.ppermute(value, axis, [(source, source ^ step) for source in range(co...  25.2 us
    ppermute x5, starting transfers between devices, doubled(): lax.ppermute(value, axis, [(source, source ^ step) for source in range(co...  16.7 us
    pallas_call x7, Pallas kernels, call(): pl.pallas_call(kernel, out_shape=outs, in_specs=specs, out_specs=[VMEM] *...  12.9 us
    ppermute x4, waiting for transfers between devices, odd_swap(): return lax.ppermute(value, ROWS, odd_pairs)  11.2 us
    ppermute x12, waiting for transfers between devices, swapped(): lax.ppermute(value, COLS, pairs(step))  10.1 us
    all_gather x1, blocking collectives, local(): weight_grad = lax.all_gather(weight_grad, 'x').sum(0)  10.1 us
  transfers between devices with their start and end apart: 25, of which 10 were waited for; matrix products, arithmetic and copies ran while one was open for 2% of the time, Pallas kernels for 3%

profile of v4, /device:TPU:1, one launch (start us, length us, event | category | flops | bytes accessed | tf_op | source)
XLA Modules:
  0.0 179.9 jit_solution(9093251287659188949)
XLA Ops:
  0.6 4.0 %collective-permute-start = (bf16[64,4096]{1,0:T(8,128)(2,1)}, bf16[64,4096]{1,0:T(8,128)(2,1)S(1)}, u32[]{:S(2)}, u32[]{:S(2)}) collective-permute-start(bf16[64,4096]{1,0:T(8,128)(2,1)} %bitcast.10), channel_id=1, source_target_pairs={{0,4},{4,0},{8,12},{12,8},{16,20},{20,16},{24,28},{28,24},{32,36},... | collective-permute-start | bytes 1572872 | tf_op jit(solution)/shard_map/ppermute | solution.py:223
  4.6 15.3 %collective-permute-start.1 = (bf16[64,4096]{1,0:T(8,128)(2,1)}, bf16[64,4096]{1,0:T(8,128)(2,1)}, u32[]{:S(2)}, u32[]{:S(2)}) collective-permute-start(bf16[64,4096]{1,0:T(8,128)(2,1)} %bitcast.11), channel_id=1, source_target_pairs={{4,8},{8,4},{12,16},{16,12},{20,24},{24,20},{28,32},{32,28},{36,40... | collective-permute-start | bytes 1572872 | tf_op jit(solution)/shard_map/ppermute | solution.py:226
  22.4 9.1 %collective-permute-done.1.odd = bf16[64,4096]{1,0:T(8,128)(2,1)} collective-permute-done((bf16[64,4096]{1,0:T(8,128)(2,1)}, bf16[64,4096]{1,0:T(8,128)(2,1)}, u32[]{:S(2)}, u32[]{:S(2)}) %collective-permute-start.1) | collective-permute-done | bytes 524320 | tf_op jit(solution)/shard_map/ppermute | solution.py:226
  33.4 8.8 %collective-permute-start.3 = (bf16[64,4096]{1,0:T(8,128)(2,1)S(1)}, bf16[64,4096]{1,0:T(8,128)(2,1)S(1)}, u32[]{:S(2)}, u32[]{:S(2)}) collective-permute-start(bf16[64,4096]{1,0:T(8,128)(2,1)S(1)} %collective-permute-done.even), channel_id=1, source_target_pairs={{4,8},{8,4},{12,16},{16,12},{20,24},{24,20},{28,32},{32,28},{36,40... | collective-permute-start | bytes 1572872 | tf_op jit(solution)/shard_map/ppermute | solution.py:226
  42.2 4.1 %collective-permute-start.7 = (bf16[64,1280]{1,0:T(8,128)(2,1)S(1)}, bf16[64,1280]{1,0:T(8,128)(2,1)S(1)}, u32[]{:S(2)}, u32[]{:S(2)}) collective-permute-start(bf16[64,1280]{1,0:T(8,128)(2,1)S(1)} %get-tuple-element.38), channel_id=1, source_target_pairs={{0,1},{1,0},{2,3},{3,2},{4,5},{5,4},{6,7},{7,6},{8,9},{9,8},{10,11... | collective-permute-start | bytes 491528 | tf_op jit(solution)/shard_map/ppermute | solution.py:203
  46.3 2.3 %collective-permute-start.8 = (bf16[64,1280]{1,0:T(8,128)(2,1)S(1)}, bf16[64,1280]{1,0:T(8,128)(2,1)S(1)}, u32[]{:S(2)}, u32[]{:S(2)}) collective-permute-start(bf16[64,1280]{1,0:T(8,128)(2,1)S(1)} %get-tuple-element.39), channel_id=1, source_target_pairs={{0,2},{1,3},{2,0},{3,1},{4,6},{5,7},{6,4},{7,5},{8,10},{9,11},{10,... | collective-permute-start | bytes 491528 | tf_op jit(solution)/shard_map/ppermute | solution.py:203
  48.6 3.2 %collective-permute-start.9 = (bf16[64,1280]{1,0:T(8,128)(2,1)S(1)}, bf16[64,1280]{1,0:T(8,128)(2,1)S(1)}, u32[]{:S(2)}, u32[]{:S(2)}) collective-permute-start(bf16[64,1280]{1,0:T(8,128)(2,1)S(1)} %get-tuple-element.40), channel_id=1, source_target_pairs={{0,3},{1,2},{2,1},{3,0},{4,7},{5,6},{6,5},{7,4},{8,11},{9,10},{10,... | collective-permute-start | bytes 491528 | tf_op jit(solution)/shard_map/ppermute | solution.py:203
  56.6 2.4 %shard_map.95.start = f32[64,4096]{1,0:T(8,128)S(1)} custom-call(bf16[88,128,128]{2,1,0:T(8,128)(2,1)S(1)} %copy-done, s32[88]{0:T(128)S(1)} %copy-done.5, s32[88]{0:T(128)S(1)} %copy-done.7, s32[1]{0:T(128)S(6)} %copy.10.count, s32[2]{0:T(128)S(1)} %pad_add_fusion.place, bf16[64,4096]{1,0:T(8,128)(2,1)S(1)} %bitcast.12, ...), custom_call_target="tpu_custom_call" | custom-call | flops 113246208 | bytes 5505740 | tf_op jit(solution)/shard_map/pallas_call | solution.py:187
  60.6 2.1 %collective-permute-start.4 = (bf16[64,1024]{1,0:T(8,128)(2,1)S(1)}, bf16[64,1024]{1,0:T(8,128)(2,1)S(1)}, u32[]{:S(2)}, u32[]{:S(2)}) collective-permute-start(bf16[64,1024]{1,0:T(8,128)(2,1)S(1)} %get-tuple-element.35), channel_id=1, source_target_pairs={{0,1},{1,0},{2,3},{3,2},{4,5},{5,4},{6,7},{7,6},{8,9},{9,8},{10,11... | collective-permute-start | bytes 393224 | tf_op jit(solution)/shard_map/ppermute | solution.py:203
  62.7 2.3 %collective-permute-start.5 = (bf16[64,1024]{1,0:T(8,128)(2,1)S(1)}, bf16[64,1024]{1,0:T(8,128)(2,1)S(1)}, u32[]{:S(2)}, u32[]{:S(2)}) collective-permute-start(bf16[64,1024]{1,0:T(8,128)(2,1)S(1)} %get-tuple-element.36), channel_id=1, source_target_pairs={{0,2},{1,3},{2,0},{3,1},{4,6},{5,7},{6,4},{7,5},{8,10},{9,11},{10,... | collective-permute-start | bytes 393224 | tf_op jit(solution)/shard_map/ppermute | solution.py:203
  65.0 3.4 %collective-permute-start.6 = (bf16[64,1024]{1,0:T(8,128)(2,1)S(1)}, bf16[64,1024]{1,0:T(8,128)(2,1)S(1)}, u32[]{:S(2)}, u32[]{:S(2)}) collective-permute-start(bf16[64,1024]{1,0:T(8,128)(2,1)S(1)} %get-tuple-element.37), channel_id=1, source_target_pairs={{0,3},{1,2},{2,1},{3,0},{4,7},{5,6},{6,5},{7,4},{8,11},{9,10},{10,... | collective-permute-start | bytes 393224 | tf_op jit(solution)/shard_map/ppermute | solution.py:203
  69.4 3.4 %collective-permute-done.6.refs_3_ = bf16[64,1024]{1,0:T(8,128)(2,1)S(1)} collective-permute-done((bf16[64,1024]{1,0:T(8,128)(2,1)S(1)}, bf16[64,1024]{1,0:T(8,128)(2,1)S(1)}, u32[]{:S(2)}, u32[]{:S(2)}) %collective-permute-start.6) | collective-permute-done | bytes 131104 | tf_op jit(solution)/shard_map/ppermute | solution.py:203
  72.8 2.2 %shard_map.97 = (bf16[64,1024]{1,0:T(8,128)(2,1)S(1)}, bf16[64,1024]{1,0:T(8,128)(2,1)}, bf16[64,1024]{1,0:T(8,128)(2,1)}, bf16[64,1024]{1,0:T(8,128)(2,1)}, bf1...) custom-call(s32[2]{0:T(128)S(1)} %pad_add_fusion.place, ...), custom_call_target="tpu_custom_call" | custom-call | flops 402653184 | bytes 2359304 | tf_op jit(solution)/shard_map/pallas_call | solution.py:187
  75.0 2.3 %collective-permute-start.10 = (bf16[64,1280]{1,0:T(8,128)(2,1)S(1)}, bf16[64,1280]{1,0:T(8,128)(2,1)S(1)}, u32[]{:S(2)}, u32[]{:S(2)}) collective-permute-start(bf16[64,1280]{1,0:T(8,128)(2,1)S(1)} %get-tuple-element.42), channel_id=1, source_target_pairs={{0,1},{1,0},{2,3},{3,2},{4,5},{5,4},{6,7},{7,6},{8,9},{9,8},{10,11... | collective-permute-start | bytes 491528 | tf_op jit(solution)/shard_map/ppermute | solution.py:203
  77.3 2.9 %collective-permute-start.11 = (bf16[64,1280]{1,0:T(8,128)(2,1)S(1)}, bf16[64,1280]{1,0:T(8,128)(2,1)S(1)}, u32[]{:S(2)}, u32[]{:S(2)}) collective-permute-start(bf16[64,1280]{1,0:T(8,128)(2,1)S(1)} %get-tuple-element.43), channel_id=1, source_target_pairs={{0,2},{1,3},{2,0},{3,1},{4,6},{5,7},{6,4},{7,5},{8,10},{9,11},{10,... | collective-permute-start | bytes 491528 | tf_op jit(solution)/shard_map/ppermute | solution.py:203
  80.2 2.6 %collective-permute-start.12 = (bf16[64,1280]{1,0:T(8,128)(2,1)S(1)}, bf16[64,1280]{1,0:T(8,128)(2,1)S(1)}, u32[]{:S(2)}, u32[]{:S(2)}) collective-permute-start(bf16[64,1280]{1,0:T(8,128)(2,1)S(1)} %get-tuple-element.44), channel_id=1, source_target_pairs={{0,3},{1,2},{2,1},{3,0},{4,7},{5,6},{6,5},{7,4},{8,11},{9,10},{10,... | collective-permute-start | bytes 491528 | tf_op jit(solution)/shard_map/ppermute | solution.py:203
  82.9 2.1 %collective-permute-done.11.refs_2_ = bf16[64,1280]{1,0:T(8,128)(2,1)S(1)} collective-permute-done((bf16[64,1280]{1,0:T(8,128)(2,1)S(1)}, bf16[64,1280]{1,0:T(8,128)(2,1)S(1)}, u32[]{:S(2)}, u32[]{:S(2)}) %collective-permute-start.11) | collective-permute-done | bytes 163872 | tf_op jit(solution)/shard_map/ppermute | solution.py:203
  84.9 3.7 %collective-permute-done.12.refs_3_ = bf16[64,1280]{1,0:T(8,128)(2,1)S(1)} collective-permute-done((bf16[64,1280]{1,0:T(8,128)(2,1)S(1)}, bf16[64,1280]{1,0:T(8,128)(2,1)S(1)}, u32[]{:S(2)}, u32[]{:S(2)}) %collective-permute-start.12) | collective-permute-done | bytes 163872 | tf_op jit(solution)/shard_map/ppermute | solution.py:203
  92.0 5.1 %collective-permute-start.14 = (bf16[64,4096]{1,0:T(8,128)(2,1)S(1)}, bf16[64,4096]{1,0:T(8,128)(2,1)S(1)}, u32[]{:S(2)}, u32[]{:S(2)}) collective-permute-start(bf16[64,4096]{1,0:T(8,128)(2,1)S(1)} %get-tuple-element.47), channel_id=1, source_target_pairs={{4,8},{8,4},{12,16},{16,12},{20,24},{24,20},{28,32},{32,28},{36,40... | collective-permute-start | bytes 1572872 | tf_op jit(solution)/shard_map/ppermute | solution.py:226
  99.0 5.4 %collective-permute-done.15 = f32[64,256]{1,0:T(8,128)S(1)} collective-permute-done((f32[64,256]{1,0:T(8,128)S(1)}, f32[64,256]{1,0:T(8,128)S(1)}, u32[]{:S(2)}, u32[]{:S(2)}) %collective-permute-start.15) | collective-permute-done | bytes 65568 | tf_op jit(solution)/shard_map/ppermute | solution.py:209
  106.3 4.3 %collective-permute-done.16 = f32[64,256]{1,0:T(8,128)S(1)} collective-permute-done((f32[64,256]{1,0:T(8,128)S(1)}, f32[64,256]{1,0:T(8,128)S(1)}, u32[]{:S(2)}, u32[]{:S(2)}) %collective-permute-start.16) | collective-permute-done | bytes 65568 | tf_op jit(solution)/shard_map/ppermute | solution.py:209
  110.6 2.0 %collective-permute-done.14.from_odd = bf16[64,4096]{1,0:T(8,128)(2,1)S(1)} collective-permute-done((bf16[64,4096]{1,0:T(8,128)(2,1)S(1)}, bf16[64,4096]{1,0:T(8,128)(2,1)S(1)}, u32[]{:S(2)}, u32[]{:S(2)}) %collective-permute-start.14) | collective-permute-done | bytes 524320 | tf_op jit(solution)/shard_map/ppermute | solution.py:226
  112.7 2.1 %shard_map.99 = (bf16[64,4096]{1,0:T(8,128)(2,1)}, bf16[64,4096]{1,0:T(8,128)(2,1)}) custom-call(bf16[88,128,128]{2,1,0:T(8,128)(2,1)S(1)} %copy-done.1, s32[88]{0:T(128)S(1)} %copy-done.5, s32[88]{0:T(128)S(1)} %copy-done.7, s32[1]{0:T(128)S(6)} %copy.10.count, s32[2]{0:T(128)S(1)} %pad_add_fusion.place, bf16[4,64,1024]{2,1,0:T(8,128)(2,1)S(1)} %get-tuple-element.45.grad, ...), custom_call_target="tpu_custom_call" | custom-call | flops 75497472 | bytes 5505740 | tf_op jit(solution)/shard_map/pallas_call | solution.py:187
  114.8 7.5 %collective-permute-start.18 = (bf16[64,4096]{1,0:T(8,128)(2,1)}, bf16[64,4096]{1,0:T(8,128)(2,1)}, u32[]{:S(2)}, u32[]{:S(2)}) collective-permute-start(bf16[64,4096]{1,0:T(8,128)(2,1)} %get-tuple-element.52), channel_id=1, source_target_pairs={{4,8},{8,4},{12,16},{16,12},{20,24},{24,20},{28,32},{32,28},{36,40... | collective-permute-start | bytes 1572872 | tf_op jit(solution)/shard_map/ppermute | solution.py:226
  126.1 8.1 %collective-permute-done.22 = f32[64,256]{1,0:T(8,128)S(1)} collective-permute-done((f32[64,256]{1,0:T(8,128)S(1)}, f32[64,256]{1,0:T(8,128)S(1)}, u32[]{:S(2)}, u32[]{:S(2)}) %collective-permute-start.22) | collective-permute-done | bytes 65568 | tf_op jit(solution)/shard_map/ppermute | solution.py:209
  134.3 6.4 %collective-permute-start.23 = (f32[64,256]{1,0:T(8,128)S(1)}, f32[64,256]{1,0:T(8,128)S(1)}, u32[]{:S(2)}, u32[]{:S(2)}) collective-permute-start(f32[64,256]{1,0:T(8,128)S(1)} %add.21), channel_id=1, source_target_pairs={{0,128},{16,144},{32,160},{48,176},{64,192},{80,208},{96,224},{112... | collective-permute-start | bytes 196616 | tf_op jit(solution)/shard_map/ppermute | solution.py:209
  140.7 7.3 %collective-permute-done.23 = f32[64,256]{1,0:T(8,128)S(1)} collective-permute-done((f32[64,256]{1,0:T(8,128)S(1)}, f32[64,256]{1,0:T(8,128)S(1)}, u32[]{:S(2)}, u32[]{:S(2)}) %collective-permute-start.23) | collective-permute-done | bytes 65568 | tf_op jit(solution)/shard_map/ppermute | solution.py:209
  148.0 4.6 %collective-permute-start.24 = (f32[64,256]{1,0:T(8,128)S(1)}, f32[64,256]{1,0:T(8,128)S(1)}, u32[]{:S(2)}, u32[]{:S(2)}) collective-permute-start(f32[64,256]{1,0:T(8,128)S(1)} %add.22), channel_id=1, source_target_pairs={{0,256},{256,0},{1,257},{257,1},{2,258},{258,2},{3,259},{259,3},{4... | collective-permute-start | bytes 196616 | tf_op jit(solution)/shard_map/ppermute | solution.py:209
  152.6 5.8 %collective-permute-start.19 = (bf16[64,1024]{1,0:T(8,128)(2,1)}, bf16[64,1024]{1,0:T(8,128)(2,1)}, u32[]{:S(2)}, u32[]{:S(2)}) collective-permute-start(bf16[64,1024]{1,0:T(8,128)(2,1)} %get-tuple-element.55), channel_id=1, source_target_pairs={{0,1},{1,0},{2,3},{3,2},{4,5},{5,4},{6,7},{7,6},{8,9},{9,8},{10,11... | collective-permute-start | bytes 393224 | tf_op jit(solution)/shard_map/ppermute | solution.py:203
  160.3 3.5 %collective-permute-start.21 = (bf16[64,1024]{1,0:T(8,128)(2,1)}, bf16[64,1024]{1,0:T(8,128)(2,1)}, u32[]{:S(2)}, u32[]{:S(2)}) collective-permute-start(bf16[64,1024]{1,0:T(8,128)(2,1)} %get-tuple-element.57), channel_id=1, source_target_pairs={{0,3},{1,2},{2,1},{3,0},{4,7},{5,6},{6,5},{7,4},{8,11},{9,10},{10,... | collective-permute-start | bytes 393224 | tf_op jit(solution)/shard_map/ppermute | solution.py:203
  163.9 10.1 %all-gather = f32[256,256]{1,0:T(8,128)} all-gather(f32[64,256]{1,0:T(8,128)S(1)} %add.23), channel_id=2, replica_groups=mesh['yh'=2,'z'=16,'x'=4,'yl'=2,'core'=2] {'x'}, dimensions={0}, use_global_device_ids=true | all-gather | bytes 327680 | tf_op jit(solution)/shard_map/all_gather | solution.py:311
  177.1 2.8 %shard_map.100 = (bf16[64,4096]{1,0:T(8,128)(2,1)}, bf16[64,4096]{1,0:T(8,128)(2,1)}) custom-call(bf16[88,128,128]{2,1,0:T(8,128)(2,1)S(1)} %copy-done.1, s32[88]{0:T(128)S(1)} %copy-done.6, s32[88]{0:T(128)S(1)} %copy-done.8, s32[1]{0:T(128)S(6)} %copy.10.count, s32[2]{0:T(128)S(1)} %pad_add_fusion.place, bf16[4,64,1024]{2,1,0:T(8,128)(2,1)S(1)} %get-tuple-element.45.grad, ...), custom_call_target="tpu_custom_call" | custom-call | flops 37748736 | bytes 6030028 | tf_op jit(solution)/shard_map/pallas_call | solution.py:187
  (52 shorter events, 27.1 us)
Async XLA Ops:
  0.6 21.7 %collective-permute-start = (bf16[64,4096]{1,0:T(8,128)(2,1)}, bf16[64,4096]{1,0:T(8,128)(2,1)S(1)}, u32[]{:S(2)}, u32[]{:S(2)}) collective-permute-start(bf16[64,4096]{1,0:T(8,128)(2,1)} %bitcast.10), channel_id=1, source_target_pairs={{0,4},{4,0},{8,12},{12,8},{16,20},{20,16},{24,28},{28,24},{32,36},... | collective-permute-start | bytes 1572872 | tf_op jit(solution)/shard_map/ppermute | solution.py:223
  4.6 26.9 %collective-permute-start.1 = (bf16[64,4096]{1,0:T(8,128)(2,1)}, bf16[64,4096]{1,0:T(8,128)(2,1)}, u32[]{:S(2)}, u32[]{:S(2)}) collective-permute-start(bf16[64,4096]{1,0:T(8,128)(2,1)} %bitcast.11), channel_id=1, source_target_pairs={{4,8},{8,4},{12,16},{16,12},{20,24},{24,20},{28,32},{32,28},{36,40... | collective-permute-start | bytes 1572872 | tf_op jit(solution)/shard_map/ppermute | solution.py:226
  20.0 1.0 copy-start.3
  21.0 0.8 copy-start.4
  31.5 27.5 %collective-permute-start.2 = (bf16[64,4096]{1,0:T(8,128)(2,1)}, bf16[64,4096]{1,0:T(8,128)(2,1)S(1)}, u32[]{:S(2)}, u32[]{:S(2)}) collective-permute-start(bf16[64,4096]{1,0:T(8,128)(2,1)} %collective-permute-done.1.odd), channel_id=1, source_target_pairs={{0,4},{4,0},{8,12},{12,8},{16,20},{20,16},{24,28},{28,24},{32,36},... | collective-permute-start | bytes 1572872 | tf_op jit(solution)/shard_map/ppermute | solution.py:223
  33.4 25.6 %collective-permute-start.3 = (bf16[64,4096]{1,0:T(8,128)(2,1)S(1)}, bf16[64,4096]{1,0:T(8,128)(2,1)S(1)}, u32[]{:S(2)}, u32[]{:S(2)}) collective-permute-start(bf16[64,4096]{1,0:T(8,128)(2,1)S(1)} %collective-permute-done.even), channel_id=1, source_target_pairs={{4,8},{8,4},{12,16},{16,12},{20,24},{24,20},{28,32},{32,28},{36,40... | collective-permute-start | bytes 1572872 | tf_op jit(solution)/shard_map/ppermute | solution.py:226
  42.2 22.8 %collective-permute-start.7 = (bf16[64,1280]{1,0:T(8,128)(2,1)S(1)}, bf16[64,1280]{1,0:T(8,128)(2,1)S(1)}, u32[]{:S(2)}, u32[]{:S(2)}) collective-permute-start(bf16[64,1280]{1,0:T(8,128)(2,1)S(1)} %get-tuple-element.38), channel_id=1, source_target_pairs={{0,1},{1,0},{2,3},{3,2},{4,5},{5,4},{6,7},{7,6},{8,9},{9,8},{10,11... | collective-permute-start | bytes 491528 | tf_op jit(solution)/shard_map/ppermute | solution.py:203
  46.3 22.2 %collective-permute-start.8 = (bf16[64,1280]{1,0:T(8,128)(2,1)S(1)}, bf16[64,1280]{1,0:T(8,128)(2,1)S(1)}, u32[]{:S(2)}, u32[]{:S(2)}) collective-permute-start(bf16[64,1280]{1,0:T(8,128)(2,1)S(1)} %get-tuple-element.39), channel_id=1, source_target_pairs={{0,2},{1,3},{2,0},{3,1},{4,6},{5,7},{6,4},{7,5},{8,10},{9,11},{10,... | collective-permute-start | bytes 491528 | tf_op jit(solution)/shard_map/ppermute | solution.py:203
  48.6 19.9 %collective-permute-start.9 = (bf16[64,1280]{1,0:T(8,128)(2,1)S(1)}, bf16[64,1280]{1,0:T(8,128)(2,1)S(1)}, u32[]{:S(2)}, u32[]{:S(2)}) collective-permute-start(bf16[64,1280]{1,0:T(8,128)(2,1)S(1)} %get-tuple-element.40), channel_id=1, source_target_pairs={{0,3},{1,2},{2,1},{3,0},{4,7},{5,6},{6,5},{7,4},{8,11},{9,10},{10,... | collective-permute-start | bytes 491528 | tf_op jit(solution)/shard_map/ppermute | solution.py:203
  52.4 1.8 %copy-start = (bf16[88,128,128]{2,1,0:T(8,128)(2,1)S(1)}, bf16[88,128,128]{2,1,0:T(8,128)(2,1)}, u32[]{:S(2)}) copy-start(bf16[88,128,128]{2,1,0:T(8,128)(2,1)} %values.9) | copy-start | bytes 8650756
  54.2 1.0 copy-start.2
  59.0 29.7 %copy-start.1 = (bf16[88,128,128]{2,1,0:T(8,128)(2,1)S(1)}, bf16[88,128,128]{2,1,0:T(8,128)(2,1)}, u32[]{:S(2)}) copy-start(bf16[88,128,128]{2,1,0:T(8,128)(2,1)} %values.9) | copy-start | bytes 8650756
  60.6 7.9 %collective-permute-start.4 = (bf16[64,1024]{1,0:T(8,128)(2,1)S(1)}, bf16[64,1024]{1,0:T(8,128)(2,1)S(1)}, u32[]{:S(2)}, u32[]{:S(2)}) collective-permute-start(bf16[64,1024]{1,0:T(8,128)(2,1)S(1)} %get-tuple-element.35), channel_id=1, source_target_pairs={{0,1},{1,0},{2,3},{3,2},{4,5},{5,4},{6,7},{7,6},{8,9},{9,8},{10,11... | collective-permute-start | bytes 393224 | tf_op jit(solution)/shard_map/ppermute | solution.py:203
  62.7 6.7 %collective-permute-start.5 = (bf16[64,1024]{1,0:T(8,128)(2,1)S(1)}, bf16[64,1024]{1,0:T(8,128)(2,1)S(1)}, u32[]{:S(2)}, u32[]{:S(2)}) collective-permute-start(bf16[64,1024]{1,0:T(8,128)(2,1)S(1)} %get-tuple-element.36), channel_id=1, source_target_pairs={{0,2},{1,3},{2,0},{3,1},{4,6},{5,7},{6,4},{7,5},{8,10},{9,11},{10,... | collective-permute-start | bytes 393224 | tf_op jit(solution)/shard_map/ppermute | solution.py:203
  65.0 7.8 %collective-permute-start.6 = (bf16[64,1024]{1,0:T(8,128)(2,1)S(1)}, bf16[64,1024]{1,0:T(8,128)(2,1)S(1)}, u32[]{:S(2)}, u32[]{:S(2)}) collective-permute-start(bf16[64,1024]{1,0:T(8,128)(2,1)S(1)} %get-tuple-element.37), channel_id=1, source_target_pairs={{0,3},{1,2},{2,1},{3,0},{4,7},{5,6},{6,5},{7,4},{8,11},{9,10},{10,... | collective-permute-start | bytes 393224 | tf_op jit(solution)/shard_map/ppermute | solution.py:203
  75.0 7.9 %collective-permute-start.10 = (bf16[64,1280]{1,0:T(8,128)(2,1)S(1)}, bf16[64,1280]{1,0:T(8,128)(2,1)S(1)}, u32[]{:S(2)}, u32[]{:S(2)}) collective-permute-start(bf16[64,1280]{1,0:T(8,128)(2,1)S(1)} %get-tuple-element.42), channel_id=1, source_target_pairs={{0,1},{1,0},{2,3},{3,2},{4,5},{5,4},{6,7},{7,6},{8,9},{9,8},{10,11... | collective-permute-start | bytes 491528 | tf_op jit(solution)/shard_map/ppermute | solution.py:203
  77.3 7.7 %collective-permute-start.11 = (bf16[64,1280]{1,0:T(8,128)(2,1)S(1)}, bf16[64,1280]{1,0:T(8,128)(2,1)S(1)}, u32[]{:S(2)}, u32[]{:S(2)}) collective-permute-start(bf16[64,1280]{1,0:T(8,128)(2,1)S(1)} %get-tuple-element.43), channel_id=1, source_target_pairs={{0,2},{1,3},{2,0},{3,1},{4,6},{5,7},{6,4},{7,5},{8,10},{9,11},{10,... | collective-permute-start | bytes 491528 | tf_op jit(solution)/shard_map/ppermute | solution.py:203
  80.2 8.4 %collective-permute-start.12 = (bf16[64,1280]{1,0:T(8,128)(2,1)S(1)}, bf16[64,1280]{1,0:T(8,128)(2,1)S(1)}, u32[]{:S(2)}, u32[]{:S(2)}) collective-permute-start(bf16[64,1280]{1,0:T(8,128)(2,1)S(1)} %get-tuple-element.44), channel_id=1, source_target_pairs={{0,3},{1,2},{2,1},{3,0},{4,7},{5,6},{6,5},{7,4},{8,11},{9,10},{10,... | collective-permute-start | bytes 491528 | tf_op jit(solution)/shard_map/ppermute | solution.py:203
  90.0 20.6 %collective-permute-start.13 = (bf16[64,4096]{1,0:T(8,128)(2,1)S(1)}, bf16[64,4096]{1,0:T(8,128)(2,1)S(1)}, u32[]{:S(2)}, u32[]{:S(2)}) collective-permute-start(bf16[64,4096]{1,0:T(8,128)(2,1)S(1)} %get-tuple-element.46), channel_id=1, source_target_pairs={{0,4},{4,0},{8,12},{12,8},{16,20},{20,16},{24,28},{28,24},{32,36},... | collective-permute-start | bytes 1572872 | tf_op jit(solution)/shard_map/ppermute | solution.py:223
  92.0 20.7 %collective-permute-start.14 = (bf16[64,4096]{1,0:T(8,128)(2,1)S(1)}, bf16[64,4096]{1,0:T(8,128)(2,1)S(1)}, u32[]{:S(2)}, u32[]{:S(2)}) collective-permute-start(bf16[64,4096]{1,0:T(8,128)(2,1)S(1)} %get-tuple-element.47), channel_id=1, source_target_pairs={{4,8},{8,4},{12,16},{16,12},{20,24},{24,20},{28,32},{32,28},{36,40... | collective-permute-start | bytes 1572872 | tf_op jit(solution)/shard_map/ppermute | solution.py:226
  97.0 7.4 %collective-permute-start.15 = (f32[64,256]{1,0:T(8,128)S(1)}, f32[64,256]{1,0:T(8,128)S(1)}, u32[]{:S(2)}, u32[]{:S(2)}) collective-permute-start(f32[64,256]{1,0:T(8,128)S(1)} %get-tuple-element.48), channel_id=1, source_target_pairs={{0,16},{16,0},{32,48},{48,32},{64,80},{80,64},{96,112},{112,96},{1... | collective-permute-start | bytes 196616 | tf_op jit(solution)/shard_map/ppermute | solution.py:209
  104.4 6.2 %collective-permute-start.16 = (f32[64,256]{1,0:T(8,128)S(1)}, f32[64,256]{1,0:T(8,128)S(1)}, u32[]{:S(2)}, u32[]{:S(2)}) collective-permute-start(f32[64,256]{1,0:T(8,128)S(1)} %add.19), channel_id=1, source_target_pairs={{0,32},{16,48},{32,0},{48,16},{64,96},{80,112},{96,64},{112,80},{1... | collective-permute-start | bytes 196616 | tf_op jit(solution)/shard_map/ppermute | solution.py:209
  112.7 64.4 %copy-start.6 = (s32[88]{0:T(128)S(1)}, s32[88]{0:T(128)}, u32[]{:S(2)}) copy-start(s32[88]{0:T(128)} %rows.9) | copy-start | bytes 1060
  112.7 64.4 %copy-start.8 = (s32[88]{0:T(128)S(1)}, s32[88]{0:T(128)}, u32[]{:S(2)}) copy-start(s32[88]{0:T(128)} %cols.9) | copy-start | bytes 1060
  114.8 62.3 %collective-permute-start.18 = (bf16[64,4096]{1,0:T(8,128)(2,1)}, bf16[64,4096]{1,0:T(8,128)(2,1)}, u32[]{:S(2)}, u32[]{:S(2)}) collective-permute-start(bf16[64,4096]{1,0:T(8,128)(2,1)} %get-tuple-element.52), channel_id=1, source_target_pairs={{4,8},{8,4},{12,16},{16,12},{20,24},{24,20},{28,32},{32,28},{36,40... | collective-permute-start | bytes 1572872 | tf_op jit(solution)/shard_map/ppermute | solution.py:226
  122.3 54.8 %collective-permute-start.17 = (bf16[64,4096]{1,0:T(8,128)(2,1)}, bf16[64,4096]{1,0:T(8,128)(2,1)}, u32[]{:S(2)}, u32[]{:S(2)}) collective-permute-start(bf16[64,4096]{1,0:T(8,128)(2,1)} %get-tuple-element.51), channel_id=1, source_target_pairs={{0,4},{4,0},{8,12},{12,8},{16,20},{20,16},{24,28},{28,24},{32,36},... | collective-permute-start | bytes 1572872 | tf_op jit(solution)/shard_map/ppermute | solution.py:223
  124.2 10.0 %collective-permute-start.22 = (f32[64,256]{1,0:T(8,128)S(1)}, f32[64,256]{1,0:T(8,128)S(1)}, u32[]{:S(2)}, u32[]{:S(2)}) collective-permute-start(f32[64,256]{1,0:T(8,128)S(1)} %add.20), channel_id=1, source_target_pairs={{0,64},{16,80},{32,96},{48,112},{64,0},{80,16},{96,32},{112,48},{1... | collective-permute-start | bytes 196616 | tf_op jit(solution)/shard_map/ppermute | solution.py:209
  134.3 13.7 %collective-permute-start.23 = (f32[64,256]{1,0:T(8,128)S(1)}, f32[64,256]{1,0:T(8,128)S(1)}, u32[]{:S(2)}, u32[]{:S(2)}) collective-permute-start(f32[64,256]{1,0:T(8,128)S(1)} %add.21), channel_id=1, source_target_pairs={{0,128},{16,144},{32,160},{48,176},{64,192},{80,208},{96,224},{112... | collective-permute-start | bytes 196616 | tf_op jit(solution)/shard_map/ppermute | solution.py:209
  148.0 12.3 %collective-permute-start.24 = (f32[64,256]{1,0:T(8,128)S(1)}, f32[64,256]{1,0:T(8,128)S(1)}, u32[]{:S(2)}, u32[]{:S(2)}) collective-permute-start(f32[64,256]{1,0:T(8,128)S(1)} %add.22), channel_id=1, source_target_pairs={{0,256},{256,0},{1,257},{257,1},{2,258},{258,2},{3,259},{259,3},{4... | collective-permute-start | bytes 196616 | tf_op jit(solution)/shard_map/ppermute | solution.py:209
  152.6 24.5 %collective-permute-start.19 = (bf16[64,1024]{1,0:T(8,128)(2,1)}, bf16[64,1024]{1,0:T(8,128)(2,1)}, u32[]{:S(2)}, u32[]{:S(2)}) collective-permute-start(bf16[64,1024]{1,0:T(8,128)(2,1)} %get-tuple-element.55), channel_id=1, source_target_pairs={{0,1},{1,0},{2,3},{3,2},{4,5},{5,4},{6,7},{7,6},{8,9},{9,8},{10,11... | collective-permute-start | bytes 393224 | tf_op jit(solution)/shard_map/ppermute | solution.py:203
  158.4 18.7 %collective-permute-start.20 = (bf16[64,1024]{1,0:T(8,128)(2,1)}, bf16[64,1024]{1,0:T(8,128)(2,1)}, u32[]{:S(2)}, u32[]{:S(2)}) collective-permute-start(bf16[64,1024]{1,0:T(8,128)(2,1)} %get-tuple-element.56), channel_id=1, source_target_pairs={{0,2},{1,3},{2,0},{3,1},{4,6},{5,7},{6,4},{7,5},{8,10},{9,11},{10,... | collective-permute-start | bytes 393224 | tf_op jit(solution)/shard_map/ppermute | solution.py:203
  160.3 16.8 %collective-permute-start.21 = (bf16[64,1024]{1,0:T(8,128)(2,1)}, bf16[64,1024]{1,0:T(8,128)(2,1)}, u32[]{:S(2)}, u32[]{:S(2)}) collective-permute-start(bf16[64,1024]{1,0:T(8,128)(2,1)} %get-tuple-element.57), channel_id=1, source_target_pairs={{0,3},{1,2},{2,1},{3,0},{4,7},{5,6},{6,5},{7,4},{8,11},{9,10},{10,... | collective-permute-start | bytes 393224 | tf_op jit(solution)/shard_map/ppermute | solution.py:203
  (2 other events, 1.3 us)

commit v5 on v4

--- a/solution.py
+++ b/solution.py
@@ -1,3 +1,5 @@
+import functools
+
 import jax
 import jax.numpy as jnp
 from jax import lax
@@ -61,13 +63,16 @@
     each_tile(offset, count, values_ref, term, add)
 
 
-def near_kernel(values, rows, cols, count, place, own, even, odd, total):
+def first_kernel(values, rows, cols, count, place, own, even, total):
     total[...] = jnp.zeros_like(total)
     info = (values, rows, cols, count[0])
-    even_offset = 3 - 2 * place[0]
     gather_terms(info, own, total, 2)
-    gather_terms(info, even, total, even_offset)
-    gather_terms(info, odd, total, 4 - even_offset)
+    gather_terms(info, even, total, 3 - 2 * place[0])
+
+
+def second_kernel(values, rows, cols, count, place, start, odd, total):
+    total[...] = start[...]
+    gather_terms((values, rows, cols, count[0]), odd, total, 1 + 2 * place[0])
 
 
 def pack_kernel(place, cotangent, weight, *packed):
@@ -141,9 +146,9 @@
 
 
 def spread_far_kernel(values, rows, cols, count, place, *refs):
-    n = len(refs) - 6
+    n = len(refs) - 5
     sent = refs[:n]
-    even, odd, grads, weight_sum, even_total, odd_total = refs[n:]
+    even, odd, grads, even_total, odd_total = refs[n:]
     width = grads.shape[2]
     for step, ref in enumerate(sent):
         grads[place[1] ^ step] = ref[:, :width]
@@ -153,22 +158,12 @@
         total[...] = jnp.zeros_like(total)
         spread_terms(info, grads, total, offset)
         out[...] = total[...].astype(out.dtype)
-    terms = [ref[:, width:].astype(jnp.float32) for ref in sent]
-    weight_sum[...] = sum(terms[1:], terms[0])
-
-
-def spread_near_kernel(
-    values, rows, cols, count, place, grad, from_odd, from_even, even, odd, even_total, odd_total
-):
-    info = (values, rows, cols, count[0])
-    even_offset = 3 - 2 * place[0]
-    for offset, start, total, out in (
-        (even_offset, from_odd, even_total, even),
-        (4 - even_offset, from_even, odd_total, odd),
-    ):
-        total[...] = start[...].astype(total.dtype)
-        spread_terms(info, grad, total, offset)
-        out[...] = total[...].astype(out.dtype)
+
+
+def spread_near_kernel(offset, sign, values, rows, cols, count, place, grad, received, out, total):
+    total[...] = received[...].astype(total.dtype)
+    spread_terms((values, rows, cols, count[0]), grad, total, offset + sign * place[0])
+    out[...] = total[...].astype(out.dtype)
 
 
 def spread_own_kernel(values, rows, cols, count, place, grad, from_even, from_odd, *refs):
@@ -199,9 +194,10 @@
     def pairs(step):
         return [(source, source ^ step) for source in range(len(values))]
 
-    return [values[0]] + [
-        lax.ppermute(value, COLS, pairs(step)) for step, value in enumerate(values) if step
-    ]
+    moved = list(values)
+    for step in reversed(range(1, len(values))):
+        moved[step] = lax.ppermute(values[step], COLS, pairs(step))
+    return moved
 
 
 def doubled(value, axis, step):
@@ -248,13 +244,21 @@
     even1, _ = lax.optimization_barrier((even1, given[0]))
     given = swapped(given)
     odd2 = odd_swap(even1)
+    (first,) = call(
+        first_kernel,
+        tables + (own, even1),
+        table_specs + [VMEM] * 2,
+        arrays(1, whole, jnp.float32),
+        flops=36 * tile_flops,
+    )
+    odd1, first = lax.optimization_barrier((odd1, first))
     even2 = even_swap(odd1)
     (near,) = call(
-        near_kernel,
-        tables + (own, even1, odd1),
-        table_specs + [VMEM] * 3,
+        second_kernel,
+        tables + (first, odd1),
+        table_specs + [VMEM] * 2,
         arrays(1, whole, jnp.float32),
-        flops=54 * tile_flops,
+        flops=18 * tile_flops,
     )
     hidden = call(
         far_kernel,
@@ -273,31 +277,41 @@
         flops=6 * full * full * width,
     )
     output, sent = list(both[:n_cols]), swapped(both[n_cols:])
-    even_far, odd_far, grads, weight_grad = call(
+    terms = [value[:, width:].astype(jnp.float32) for value in sent]
+    weight_grad = doubled(sum(terms[1:], terms[0]), "z", 1)
+    even_far, odd_far, grads = call(
         spread_far_kernel,
         tables + tuple(sent),
         table_specs + [VMEM] * n_cols,
-        arrays(2, whole) + arrays(1, (n_cols, feat_cols, width)) + arrays(1, (feat_cols, full), jnp.float32),
+        arrays(2, whole) + arrays(1, (n_cols, feat_cols, width)),
         scratch=[total, total],
         flops=36 * tile_flops,
     )
     even_in = even_swap(even_far)
     odd_in = odd_swap(odd_far)
-    weight_grad = doubled(doubled(weight_grad, "z", 1), "z", 2)
-    even_in, odd_in, weight_grad = lax.optimization_barrier((even_in, odd_in, weight_grad))
-    even_near, odd_near = call(
-        spread_near_kernel,
-        tables + (grads, odd_in, even_in),
-        table_specs + [VMEM] * 3,
-        arrays(2, whole),
-        scratch=[total, total],
-        flops=36 * tile_flops,
-    )
+    weight_grad = doubled(doubled(weight_grad, "yh", 1), "z", 2)
+
+    def near_terms(offset, sign, received):
+        return call(
+            functools.partial(spread_near_kernel, offset, sign),
+            tables + (grads, received),
+            table_specs + [VMEM] * 2,
+            arrays(1, whole),
+            scratch=[total],
+            flops=18 * tile_flops,
+        )[0]
+
+    even_in, _ = lax.optimization_barrier((even_in, weight_grad))
+    odd_near = near_terms(1, 2, even_in)
+    odd_last = odd_swap(odd_near)
+    odd_in, _ = lax.optimization_barrier((odd_in, odd_near))
+    even_near = near_terms(3, -2, odd_in)
     even_last = even_swap(even_near)
-    odd_last = odd_swap(odd_near)
-    output[0], even_near = lax.optimization_barrier((output[0], even_near))
+    far = lax.ppermute(weight_grad, "z", [(source, source ^ 4) for source in range(n_rows // 8)])
+    far, _, output[0] = lax.optimization_barrier((far, even_near, output[0]))
+    weight_grad = weight_grad + far
+    weight_grad = doubled(weight_grad, "z", 8)
     output = swapped(output)
-    weight_grad = doubled(weight_grad, "z", 4)
     feature_grad, output = call(
         spread_own_kernel,
         tables + (grads, even_last, odd_last, *output),
@@ -306,8 +320,6 @@
         scratch=[total],
         flops=18 * tile_flops,
     )
-    weight_grad = doubled(weight_grad, "z", 8)
-    weight_grad = doubled(weight_grad, "yh", 1)
     weight_grad = lax.all_gather(weight_grad, "x").sum(0)
     weight_grad = (weight_grad * (1.0 / (node_count * n_rows) ** 0.5)).T
     return (output.T, feature_grad.T, weight_grad)

time: 182 us -> 181 us (level)
  waiting for transfers between devices: 46.5 us -> 38.8 us
  starting transfers between devices: 99.5 us -> 104 us
  Pallas kernels: 12.9 us -> 15 us
    ppermute x4, waiting for transfers between devices: 11.2 us -> 0.01 us  [odd_swap(): return lax.ppermute(value, ROWS, odd_pairs)]
    ppermute x12 -> x13, starting transfers between devices: 36.5 us -> 45.5 us  [the longest x12 43.6 us: swapped(): moved[step] = lax.ppermute(values[step], COLS, pairs(step))]
    ppermute x12 -> x13, waiting for transfers between devices: 10.1 us -> 18.7 us  [the longest x12 10.2 us: swapped(): moved[step] = lax.ppermute(values[step], COLS, pairs(step))]
    ppermute x5 -> x4, waiting for transfers between devices: 25.2 us -> 18.9 us  [doubled(): lax.ppermute(value, axis, [(source, source ^ step) for source in range(co...]
    ppermute x4, starting transfers between devices: 36.6 us -> 32.4 us  [odd_swap(): return lax.ppermute(value, ROWS, odd_pairs)]
    pallas_call x7 -> x9, Pallas kernels: 12.9 us -> 15 us  [call(): pl.pallas_call(kernel, out_shape=outs, in_specs=specs, out_specs=[VMEM] *...]
    ppermute x5 -> x4, starting transfers between devices: 16.7 us -> 16.4 us  [doubled(): lax.ppermute(value, axis, [(source, source ^ step) for source in range(co...]
  transfers between devices with their start and end apart: 25 -> 25, of which waited for: 10 -> 9; matrix products, arithmetic and copies ran while one was open for 2% -> 2% of each run, Pallas kernels for 3% -> 4%
where the time goes in v5:
time: 181 us; the launch traced here: 179 us
  starting transfers between devices  104 us (57%)
  waiting for transfers between devices  38.8 us (21%)
  Pallas kernels  15 us (8%)
  blocking collectives  10.1 us (6%)
  local copies, waits for them, and re-layouts  5.97 us (3%)
  other arithmetic  3.22 us (2%)
    ppermute x12, starting transfers between devices, swapped(): moved[step] = lax.ppermute(values[step], COLS, pairs(step))  43.6 us
    ppermute x4, starting transfers between devices, odd_swap(): return lax.ppermute(value, ROWS, odd_pairs)  32.4 us
    ppermute x4, waiting for transfers between devices, doubled(): lax.ppermute(value, axis, [(source, source ^ step) for source in range(co...  18.9 us
    ppermute x4, starting transfers between devices, doubled(): lax.ppermute(value, axis, [(source, source ^ step) for source in range(co...  16.4 us
    pallas_call x9, Pallas kernels, call(): pl.pallas_call(kernel, out_shape=outs, in_specs=specs, out_specs=[VMEM] *...  15 us
    ppermute x12, waiting for transfers between devices, swapped(): moved[step] = lax.ppermute(values[step], COLS, pairs(step))  10.2 us
    all_gather x1, blocking collectives, local(): weight_grad = lax.all_gather(weight_grad, 'x').sum(0)  10.1 us
    ppermute x4, starting transfers between devices, even_swap(): return lax.ppermute(value, ROWS, even_pairs)  9.7 us
  transfers between devices with their start and end apart: 25, of which 9 were waited for; matrix products, arithmetic and copies ran while one was open for 2% of the time, Pallas kernels for 4%

profile of v5, /device:TPU:1, one launch (start us, length us, event | category | flops | bytes accessed | tf_op | source)
XLA Modules:
  0.0 178.8 jit_solution(17722554426252606837)
XLA Ops:
  0.6 4.0 %collective-permute-start.1 = (bf16[64,4096]{1,0:T(8,128)(2,1)}, bf16[64,4096]{1,0:T(8,128)(2,1)S(1)}, u32[]{:S(2)}, u32[]{:S(2)}) collective-permute-start(bf16[64,4096]{1,0:T(8,128)(2,1)} %bitcast.10), channel_id=1, source_target_pairs={{0,4},{4,0},{8,12},{12,8},{16,20},{20,16},{24,28},{28,24},{32,36},... | collective-permute-start | bytes 1572872 | tf_op jit(solution)/shard_map/ppermute | solution.py:219
  4.6 15.3 %collective-permute-start = (bf16[64,4096]{1,0:T(8,128)(2,1)}, bf16[64,4096]{1,0:T(8,128)(2,1)}, u32[]{:S(2)}, u32[]{:S(2)}) collective-permute-start(bf16[64,4096]{1,0:T(8,128)(2,1)} %bitcast.11), channel_id=1, source_target_pairs={{4,8},{8,4},{12,16},{16,12},{20,24},{24,20},{28,32},{32,28},{36,40... | collective-permute-start | bytes 1572872 | tf_op jit(solution)/shard_map/ppermute | solution.py:222
  23.0 9.4 %collective-permute-start.3 = (bf16[64,4096]{1,0:T(8,128)(2,1)S(1)}, bf16[64,4096]{1,0:T(8,128)(2,1)S(1)}, u32[]{:S(2)}, u32[]{:S(2)}) collective-permute-start(bf16[64,4096]{1,0:T(8,128)(2,1)S(1)} %collective-permute-done.1.even), channel_id=1, source_target_pairs={{4,8},{8,4},{12,16},{16,12},{20,24},{24,20},{28,32},{32,28},{36,40... | collective-permute-start | bytes 1572872 | tf_op jit(solution)/shard_map/ppermute | solution.py:222
  40.0 3.6 %collective-permute-start.7 = (bf16[64,1280]{1,0:T(8,128)(2,1)S(1)}, bf16[64,1280]{1,0:T(8,128)(2,1)S(1)}, u32[]{:S(2)}, u32[]{:S(2)}) collective-permute-start(bf16[64,1280]{1,0:T(8,128)(2,1)S(1)} %get-tuple-element.39), channel_id=1, source_target_pairs={{0,1},{1,0},{2,3},{3,2},{4,5},{5,4},{6,7},{7,6},{8,9},{9,8},{10,11... | collective-permute-start | bytes 491528 | tf_op jit(solution)/shard_map/ppermute | solution.py:199
  43.6 2.3 %collective-permute-start.8 = (bf16[64,1280]{1,0:T(8,128)(2,1)S(1)}, bf16[64,1280]{1,0:T(8,128)(2,1)S(1)}, u32[]{:S(2)}, u32[]{:S(2)}) collective-permute-start(bf16[64,1280]{1,0:T(8,128)(2,1)S(1)} %get-tuple-element.40), channel_id=1, source_target_pairs={{0,2},{1,3},{2,0},{3,1},{4,6},{5,7},{6,4},{7,5},{8,10},{9,11},{10,... | collective-permute-start | bytes 491528 | tf_op jit(solution)/shard_map/ppermute | solution.py:199
  46.0 3.2 %collective-permute-start.9 = (bf16[64,1280]{1,0:T(8,128)(2,1)S(1)}, bf16[64,1280]{1,0:T(8,128)(2,1)S(1)}, u32[]{:S(2)}, u32[]{:S(2)}) collective-permute-start(bf16[64,1280]{1,0:T(8,128)(2,1)S(1)} %get-tuple-element.41), channel_id=1, source_target_pairs={{0,3},{1,2},{2,1},{3,0},{4,7},{5,6},{6,5},{7,4},{8,11},{9,10},{10,... | collective-permute-start | bytes 491528 | tf_op jit(solution)/shard_map/ppermute | solution.py:199
  53.4 4.6 %collective-permute-start.4 = (bf16[64,1024]{1,0:T(8,128)(2,1)S(1)}, bf16[64,1024]{1,0:T(8,128)(2,1)S(1)}, u32[]{:S(2)}, u32[]{:S(2)}) collective-permute-start(bf16[64,1024]{1,0:T(8,128)(2,1)S(1)} %get-tuple-element.36), channel_id=1, source_target_pairs={{0,1},{1,0},{2,3},{3,2},{4,5},{5,4},{6,7},{7,6},{8,9},{9,8},{10,11... | collective-permute-start | bytes 393224 | tf_op jit(solution)/shard_map/ppermute | solution.py:199
  58.0 2.3 %collective-permute-start.5 = (bf16[64,1024]{1,0:T(8,128)(2,1)S(1)}, bf16[64,1024]{1,0:T(8,128)(2,1)S(1)}, u32[]{:S(2)}, u32[]{:S(2)}) collective-permute-start(bf16[64,1024]{1,0:T(8,128)(2,1)S(1)} %get-tuple-element.37), channel_id=1, source_target_pairs={{0,2},{1,3},{2,0},{3,1},{4,6},{5,7},{6,4},{7,5},{8,10},{9,11},{10,... | collective-permute-start | bytes 393224 | tf_op jit(solution)/shard_map/ppermute | solution.py:199
  60.3 3.2 %collective-permute-start.6 = (bf16[64,1024]{1,0:T(8,128)(2,1)S(1)}, bf16[64,1024]{1,0:T(8,128)(2,1)S(1)}, u32[]{:S(2)}, u32[]{:S(2)}) collective-permute-start(bf16[64,1024]{1,0:T(8,128)(2,1)S(1)} %get-tuple-element.38), channel_id=1, source_target_pairs={{0,3},{1,2},{2,1},{3,0},{4,7},{5,6},{6,5},{7,4},{8,11},{9,10},{10,... | collective-permute-start | bytes 393224 | tf_op jit(solution)/shard_map/ppermute | solution.py:199
  65.0 3.0 %collective-permute-done.6.refs_3_ = bf16[64,1024]{1,0:T(8,128)(2,1)S(1)} collective-permute-done((bf16[64,1024]{1,0:T(8,128)(2,1)S(1)}, bf16[64,1024]{1,0:T(8,128)(2,1)S(1)}, u32[]{:S(2)}, u32[]{:S(2)}) %collective-permute-start.6) | collective-permute-done | bytes 131104 | tf_op jit(solution)/shard_map/ppermute | solution.py:199
  68.0 2.2 %shard_map.98 = (bf16[64,1024]{1,0:T(8,128)(2,1)S(1)}, bf16[64,1024]{1,0:T(8,128)(2,1)}, bf16[64,1024]{1,0:T(8,128)(2,1)}, bf16[64,1024]{1,0:T(8,128)(2,1)}, bf1...) custom-call(s32[2]{0:T(128)S(1)} %pad_add_fusion.place, ...), custom_call_target="tpu_custom_call" | custom-call | flops 402653184 | bytes 2359304 | tf_op jit(solution)/shard_map/pallas_call | solution.py:182
  70.1 2.3 %collective-permute-start.10 = (bf16[64,1280]{1,0:T(8,128)(2,1)S(1)}, bf16[64,1280]{1,0:T(8,128)(2,1)S(1)}, u32[]{:S(2)}, u32[]{:S(2)}) collective-permute-start(bf16[64,1280]{1,0:T(8,128)(2,1)S(1)} %get-tuple-element.43), channel_id=1, source_target_pairs={{0,1},{1,0},{2,3},{3,2},{4,5},{5,4},{6,7},{7,6},{8,9},{9,8},{10,11... | collective-permute-start | bytes 491528 | tf_op jit(solution)/shard_map/ppermute | solution.py:199
  72.4 2.6 %collective-permute-start.11 = (bf16[64,1280]{1,0:T(8,128)(2,1)S(1)}, bf16[64,1280]{1,0:T(8,128)(2,1)S(1)}, u32[]{:S(2)}, u32[]{:S(2)}) collective-permute-start(bf16[64,1280]{1,0:T(8,128)(2,1)S(1)} %get-tuple-element.44), channel_id=1, source_target_pairs={{0,2},{1,3},{2,0},{3,1},{4,6},{5,7},{6,4},{7,5},{8,10},{9,11},{10,... | collective-permute-start | bytes 491528 | tf_op jit(solution)/shard_map/ppermute | solution.py:199
  75.0 3.0 %collective-permute-start.12 = (bf16[64,1280]{1,0:T(8,128)(2,1)S(1)}, bf16[64,1280]{1,0:T(8,128)(2,1)S(1)}, u32[]{:S(2)}, u32[]{:S(2)}) collective-permute-start(bf16[64,1280]{1,0:T(8,128)(2,1)S(1)} %get-tuple-element.45), channel_id=1, source_target_pairs={{0,3},{1,2},{2,1},{3,0},{4,7},{5,6},{6,5},{7,4},{8,11},{9,10},{10,... | collective-permute-start | bytes 491528 | tf_op jit(solution)/shard_map/ppermute | solution.py:199
  78.0 2.1 %collective-permute-done.11.refs_2_ = bf16[64,1280]{1,0:T(8,128)(2,1)S(1)} collective-permute-done((bf16[64,1280]{1,0:T(8,128)(2,1)S(1)}, bf16[64,1280]{1,0:T(8,128)(2,1)S(1)}, u32[]{:S(2)}, u32[]{:S(2)}) %collective-permute-start.11) | collective-permute-done | bytes 163872 | tf_op jit(solution)/shard_map/ppermute | solution.py:199
  80.1 3.7 %collective-permute-done.12.refs_3_ = bf16[64,1280]{1,0:T(8,128)(2,1)S(1)} collective-permute-done((bf16[64,1280]{1,0:T(8,128)(2,1)S(1)}, bf16[64,1280]{1,0:T(8,128)(2,1)S(1)}, u32[]{:S(2)}, u32[]{:S(2)}) %collective-permute-start.12) | collective-permute-done | bytes 163872 | tf_op jit(solution)/shard_map/ppermute | solution.py:199
  85.1 1.9 %collective-permute-start.14 = (bf16[64,4096]{1,0:T(8,128)(2,1)S(1)}, bf16[64,4096]{1,0:T(8,128)(2,1)S(1)}, u32[]{:S(2)}, u32[]{:S(2)}) collective-permute-start(bf16[64,4096]{1,0:T(8,128)(2,1)S(1)} %get-tuple-element.48), channel_id=1, source_target_pairs={{0,4},{4,0},{8,12},{12,8},{16,20},{20,16},{24,28},{28,24},{32,36},... | collective-permute-start | bytes 1572872 | tf_op jit(solution)/shard_map/ppermute | solution.py:219
  87.1 2.9 %collective-permute-start.13 = (bf16[64,4096]{1,0:T(8,128)(2,1)S(1)}, bf16[64,4096]{1,0:T(8,128)(2,1)S(1)}, u32[]{:S(2)}, u32[]{:S(2)}) collective-permute-start(bf16[64,4096]{1,0:T(8,128)(2,1)S(1)} %get-tuple-element.47), channel_id=1, source_target_pairs={{4,8},{8,4},{12,16},{16,12},{20,24},{24,20},{28,32},{32,28},{36,40... | collective-permute-start | bytes 1572872 | tf_op jit(solution)/shard_map/ppermute | solution.py:222
  90.0 1.9 %collective-permute-start.15 = (f32[64,256]{1,0:T(8,128)S(1)}, f32[64,256]{1,0:T(8,128)S(1)}, u32[]{:S(2)}, u32[]{:S(2)}) collective-permute-start(f32[64,256]{1,0:T(8,128)S(1)} %convert_add_fusion), channel_id=1, source_target_pairs={{0,16},{16,0},{32,48},{48,32},{64,80},{80,64},{96,112},{112,96},{1... | collective-permute-start | bytes 196616 | tf_op jit(solution)/shard_map/ppermute | solution.py:205
  91.9 3.4 %collective-permute-done.15 = f32[64,256]{1,0:T(8,128)S(1)} collective-permute-done((f32[64,256]{1,0:T(8,128)S(1)}, f32[64,256]{1,0:T(8,128)S(1)}, u32[]{:S(2)}, u32[]{:S(2)}) %collective-permute-start.15) | collective-permute-done | bytes 65568 | tf_op jit(solution)/shard_map/ppermute | solution.py:205
  95.3 3.0 %collective-permute-start.16 = (f32[64,256]{1,0:T(8,128)S(1)}, f32[64,256]{1,0:T(8,128)S(1)}, u32[]{:S(2)}, u32[]{:S(2)}) collective-permute-start(f32[64,256]{1,0:T(8,128)S(1)} %add.31), channel_id=1, source_target_pairs={{0,256},{256,0},{1,257},{257,1},{2,258},{258,2},{3,259},{259,3},{4... | collective-permute-start | bytes 196616 | tf_op jit(solution)/shard_map/ppermute | solution.py:205
  98.4 11.6 %collective-permute-done.16 = f32[64,256]{1,0:T(8,128)S(1)} collective-permute-done((f32[64,256]{1,0:T(8,128)S(1)}, f32[64,256]{1,0:T(8,128)S(1)}, u32[]{:S(2)}, u32[]{:S(2)}) %collective-permute-start.16) | collective-permute-done | bytes 65568 | tf_op jit(solution)/shard_map/ppermute | solution.py:205
  110.0 1.9 %collective-permute-start.17 = (f32[64,256]{1,0:T(8,128)S(1)}, f32[64,256]{1,0:T(8,128)S(1)}, u32[]{:S(2)}, u32[]{:S(2)}) collective-permute-start(f32[64,256]{1,0:T(8,128)S(1)} %add.32), channel_id=1, source_target_pairs={{0,32},{16,48},{32,0},{48,16},{64,96},{80,112},{96,64},{112,80},{1... | collective-permute-start | bytes 196616 | tf_op jit(solution)/shard_map/ppermute | solution.py:205
  111.9 4.0 %collective-permute-done.17 = f32[64,256]{1,0:T(8,128)S(1)} collective-permute-done((f32[64,256]{1,0:T(8,128)S(1)}, f32[64,256]{1,0:T(8,128)S(1)}, u32[]{:S(2)}, u32[]{:S(2)}) %collective-permute-start.17) | collective-permute-done | bytes 65568 | tf_op jit(solution)/shard_map/ppermute | solution.py:205
  121.3 4.8 %collective-permute-start.19 = (bf16[64,4096]{1,0:T(8,128)(2,1)}, bf16[64,4096]{1,0:T(8,128)(2,1)}, u32[]{:S(2)}, u32[]{:S(2)}) collective-permute-start(bf16[64,4096]{1,0:T(8,128)(2,1)} %shard_map.100), channel_id=1, source_target_pairs={{4,8},{8,4},{12,16},{16,12},{20,24},{24,20},{28,32},{32,28},{36,40... | collective-permute-start | bytes 1572872 | tf_op jit(solution)/shard_map/ppermute | solution.py:222
  128.1 8.5 %collective-permute-done.20 = f32[64,256]{1,0:T(8,128)S(1)} collective-permute-done((f32[64,256]{1,0:T(8,128)S(1)}, f32[64,256]{1,0:T(8,128)S(1)}, u32[]{:S(2)}, u32[]{:S(2)}) %collective-permute-start.20) | collective-permute-done | bytes 65568 | tf_op jit(solution)/shard_map/ppermute | solution.py:310
  136.5 9.5 %collective-permute-start.24 = (f32[64,256]{1,0:T(8,128)S(1)}, f32[64,256]{1,0:T(8,128)S(1)}, u32[]{:S(2)}, u32[]{:S(2)}) collective-permute-start(f32[64,256]{1,0:T(8,128)S(1)} %add.34), channel_id=1, source_target_pairs={{0,128},{16,144},{32,160},{48,176},{64,192},{80,208},{96,224},{112... | collective-permute-start | bytes 196616 | tf_op jit(solution)/shard_map/ppermute | solution.py:205
  146.0 11.2 %collective-permute-start.21 = (bf16[64,1024]{1,0:T(8,128)(2,1)}, bf16[64,1024]{1,0:T(8,128)(2,1)}, u32[]{:S(2)}, u32[]{:S(2)}) collective-permute-start(bf16[64,1024]{1,0:T(8,128)(2,1)} %get-tuple-element.53), channel_id=1, source_target_pairs={{0,1},{1,0},{2,3},{3,2},{4,5},{5,4},{6,7},{7,6},{8,9},{9,8},{10,11... | collective-permute-start | bytes 393224 | tf_op jit(solution)/shard_map/ppermute | solution.py:199
  157.2 2.3 %collective-permute-start.22 = (bf16[64,1024]{1,0:T(8,128)(2,1)}, bf16[64,1024]{1,0:T(8,128)(2,1)}, u32[]{:S(2)}, u32[]{:S(2)}) collective-permute-start(bf16[64,1024]{1,0:T(8,128)(2,1)} %get-tuple-element.54), channel_id=1, source_target_pairs={{0,2},{1,3},{2,0},{3,1},{4,6},{5,7},{6,4},{7,5},{8,10},{9,11},{10,... | collective-permute-start | bytes 393224 | tf_op jit(solution)/shard_map/ppermute | solution.py:199
  159.6 3.1 %collective-permute-start.23 = (bf16[64,1024]{1,0:T(8,128)(2,1)}, bf16[64,1024]{1,0:T(8,128)(2,1)}, u32[]{:S(2)}, u32[]{:S(2)}) collective-permute-start(bf16[64,1024]{1,0:T(8,128)(2,1)} %get-tuple-element.55), channel_id=1, source_target_pairs={{0,3},{1,2},{2,1},{3,0},{4,7},{5,6},{6,5},{7,4},{8,11},{9,10},{10,... | collective-permute-start | bytes 393224 | tf_op jit(solution)/shard_map/ppermute | solution.py:199
  162.8 10.1 %all-gather = f32[256,256]{1,0:T(8,128)} all-gather(f32[64,256]{1,0:T(8,128)S(1)} %add.35), channel_id=2, replica_groups=mesh['yh'=2,'z'=16,'x'=4,'yl'=2,'core'=2] {'x'}, dimensions={0}, use_global_device_ids=true | all-gather | bytes 327680 | tf_op jit(solution)/shard_map/all_gather | solution.py:323
  176.0 2.8 %shard_map.102 = (bf16[64,4096]{1,0:T(8,128)(2,1)}, bf16[64,4096]{1,0:T(8,128)(2,1)}) custom-call(bf16[88,128,128]{2,1,0:T(8,128)(2,1)S(1)} %copy-done.1, s32[88]{0:T(128)S(1)} %copy-done.6, s32[88]{0:T(128)S(1)} %copy-done.8, s32[1]{0:T(128)S(6)} %copy.10.count, s32[2]{0:T(128)S(1)} %pad_add_fusion.place, bf16[4,64,1024]{2,1,0:T(8,128)(2,1)S(1)} %get-tuple-element.46.grad, ...), custom_call_target="tpu_custom_call" | custom-call | flops 37748736 | bytes 6030028 | tf_op jit(solution)/shard_map/pallas_call | solution.py:182
  (55 shorter events, 27.7 us)
Async XLA Ops:
  0.6 22.4 %collective-permute-start.1 = (bf16[64,4096]{1,0:T(8,128)(2,1)}, bf16[64,4096]{1,0:T(8,128)(2,1)S(1)}, u32[]{:S(2)}, u32[]{:S(2)}) collective-permute-start(bf16[64,4096]{1,0:T(8,128)(2,1)} %bitcast.10), channel_id=1, source_target_pairs={{0,4},{4,0},{8,12},{12,8},{16,20},{20,16},{24,28},{28,24},{32,36},... | collective-permute-start | bytes 1572872 | tf_op jit(solution)/shard_map/ppermute | solution.py:219
  4.6 33.5 %collective-permute-start = (bf16[64,4096]{1,0:T(8,128)(2,1)}, bf16[64,4096]{1,0:T(8,128)(2,1)}, u32[]{:S(2)}, u32[]{:S(2)}) collective-permute-start(bf16[64,4096]{1,0:T(8,128)(2,1)} %bitcast.11), channel_id=1, source_target_pairs={{4,8},{8,4},{12,16},{16,12},{20,24},{24,20},{28,32},{32,28},{36,40... | collective-permute-start | bytes 1572872 | tf_op jit(solution)/shard_map/ppermute | solution.py:222
  20.6 1.0 copy-start.3
  21.7 0.8 copy-start.4
  23.0 27.7 %collective-permute-start.3 = (bf16[64,4096]{1,0:T(8,128)(2,1)S(1)}, bf16[64,4096]{1,0:T(8,128)(2,1)S(1)}, u32[]{:S(2)}, u32[]{:S(2)}) collective-permute-start(bf16[64,4096]{1,0:T(8,128)(2,1)S(1)} %collective-permute-done.1.even), channel_id=1, source_target_pairs={{4,8},{8,4},{12,16},{16,12},{20,24},{24,20},{28,32},{32,28},{36,40... | collective-permute-start | bytes 1572872 | tf_op jit(solution)/shard_map/ppermute | solution.py:222
  32.4 1.8 %copy-start = (bf16[88,128,128]{2,1,0:T(8,128)(2,1)S(1)}, bf16[88,128,128]{2,1,0:T(8,128)(2,1)}, u32[]{:S(2)}) copy-start(bf16[88,128,128]{2,1,0:T(8,128)(2,1)} %values.13) | copy-start | bytes 8650756
  34.2 1.0 copy-start.2
  38.1 13.8 %collective-permute-start.2 = (bf16[64,4096]{1,0:T(8,128)(2,1)}, bf16[64,4096]{1,0:T(8,128)(2,1)S(1)}, u32[]{:S(2)}, u32[]{:S(2)}) collective-permute-start(bf16[64,4096]{1,0:T(8,128)(2,1)} %collective-permute-done.odd), channel_id=1, source_target_pairs={{0,4},{4,0},{8,12},{12,8},{16,20},{20,16},{24,28},{28,24},{32,36},... | collective-permute-start | bytes 1572872 | tf_op jit(solution)/shard_map/ppermute | solution.py:219
  40.0 20.3 %collective-permute-start.7 = (bf16[64,1280]{1,0:T(8,128)(2,1)S(1)}, bf16[64,1280]{1,0:T(8,128)(2,1)S(1)}, u32[]{:S(2)}, u32[]{:S(2)}) collective-permute-start(bf16[64,1280]{1,0:T(8,128)(2,1)S(1)} %get-tuple-element.39), channel_id=1, source_target_pairs={{0,1},{1,0},{2,3},{3,2},{4,5},{5,4},{6,7},{7,6},{8,9},{9,8},{10,11... | collective-permute-start | bytes 491528 | tf_op jit(solution)/shard_map/ppermute | solution.py:199
  43.6 19.8 %collective-permute-start.8 = (bf16[64,1280]{1,0:T(8,128)(2,1)S(1)}, bf16[64,1280]{1,0:T(8,128)(2,1)S(1)}, u32[]{:S(2)}, u32[]{:S(2)}) collective-permute-start(bf16[64,1280]{1,0:T(8,128)(2,1)S(1)} %get-tuple-element.40), channel_id=1, source_target_pairs={{0,2},{1,3},{2,0},{3,1},{4,6},{5,7},{6,4},{7,5},{8,10},{9,11},{10,... | collective-permute-start | bytes 491528 | tf_op jit(solution)/shard_map/ppermute | solution.py:199
  46.0 17.5 %collective-permute-start.9 = (bf16[64,1280]{1,0:T(8,128)(2,1)S(1)}, bf16[64,1280]{1,0:T(8,128)(2,1)S(1)}, u32[]{:S(2)}, u32[]{:S(2)}) collective-permute-start(bf16[64,1280]{1,0:T(8,128)(2,1)S(1)} %get-tuple-element.41), channel_id=1, source_target_pairs={{0,3},{1,2},{2,1},{3,0},{4,7},{5,6},{6,5},{7,4},{8,11},{9,10},{10,... | collective-permute-start | bytes 491528 | tf_op jit(solution)/shard_map/ppermute | solution.py:199
  50.7 33.1 %copy-start.1 = (bf16[88,128,128]{2,1,0:T(8,128)(2,1)S(1)}, bf16[88,128,128]{2,1,0:T(8,128)(2,1)}, u32[]{:S(2)}) copy-start(bf16[88,128,128]{2,1,0:T(8,128)(2,1)} %values.13) | copy-start | bytes 8650756
  53.4 10.1 %collective-permute-start.4 = (bf16[64,1024]{1,0:T(8,128)(2,1)S(1)}, bf16[64,1024]{1,0:T(8,128)(2,1)S(1)}, u32[]{:S(2)}, u32[]{:S(2)}) collective-permute-start(bf16[64,1024]{1,0:T(8,128)(2,1)S(1)} %get-tuple-element.36), channel_id=1, source_target_pairs={{0,1},{1,0},{2,3},{3,2},{4,5},{5,4},{6,7},{7,6},{8,9},{9,8},{10,11... | collective-permute-start | bytes 393224 | tf_op jit(solution)/shard_map/ppermute | solution.py:199
  58.0 7.0 %collective-permute-start.5 = (bf16[64,1024]{1,0:T(8,128)(2,1)S(1)}, bf16[64,1024]{1,0:T(8,128)(2,1)S(1)}, u32[]{:S(2)}, u32[]{:S(2)}) collective-permute-start(bf16[64,1024]{1,0:T(8,128)(2,1)S(1)} %get-tuple-element.37), channel_id=1, source_target_pairs={{0,2},{1,3},{2,0},{3,1},{4,6},{5,7},{6,4},{7,5},{8,10},{9,11},{10,... | collective-permute-start | bytes 393224 | tf_op jit(solution)/shard_map/ppermute | solution.py:199
  60.3 7.6 %collective-permute-start.6 = (bf16[64,1024]{1,0:T(8,128)(2,1)S(1)}, bf16[64,1024]{1,0:T(8,128)(2,1)S(1)}, u32[]{:S(2)}, u32[]{:S(2)}) collective-permute-start(bf16[64,1024]{1,0:T(8,128)(2,1)S(1)} %get-tuple-element.38), channel_id=1, source_target_pairs={{0,3},{1,2},{2,1},{3,0},{4,7},{5,6},{6,5},{7,4},{8,11},{9,10},{10,... | collective-permute-start | bytes 393224 | tf_op jit(solution)/shard_map/ppermute | solution.py:199
  70.1 7.9 %collective-permute-start.10 = (bf16[64,1280]{1,0:T(8,128)(2,1)S(1)}, bf16[64,1280]{1,0:T(8,128)(2,1)S(1)}, u32[]{:S(2)}, u32[]{:S(2)}) collective-permute-start(bf16[64,1280]{1,0:T(8,128)(2,1)S(1)} %get-tuple-element.43), channel_id=1, source_target_pairs={{0,1},{1,0},{2,3},{3,2},{4,5},{5,4},{6,7},{7,6},{8,9},{9,8},{10,11... | collective-permute-start | bytes 491528 | tf_op jit(solution)/shard_map/ppermute | solution.py:199
  72.4 7.7 %collective-permute-start.11 = (bf16[64,1280]{1,0:T(8,128)(2,1)S(1)}, bf16[64,1280]{1,0:T(8,128)(2,1)S(1)}, u32[]{:S(2)}, u32[]{:S(2)}) collective-permute-start(bf16[64,1280]{1,0:T(8,128)(2,1)S(1)} %get-tuple-element.44), channel_id=1, source_target_pairs={{0,2},{1,3},{2,0},{3,1},{4,6},{5,7},{6,4},{7,5},{8,10},{9,11},{10,... | collective-permute-start | bytes 491528 | tf_op jit(solution)/shard_map/ppermute | solution.py:199
  75.0 8.7 %collective-permute-start.12 = (bf16[64,1280]{1,0:T(8,128)(2,1)S(1)}, bf16[64,1280]{1,0:T(8,128)(2,1)S(1)}, u32[]{:S(2)}, u32[]{:S(2)}) collective-permute-start(bf16[64,1280]{1,0:T(8,128)(2,1)S(1)} %get-tuple-element.45), channel_id=1, source_target_pairs={{0,3},{1,2},{2,1},{3,0},{4,7},{5,6},{6,5},{7,4},{8,11},{9,10},{10,... | collective-permute-start | bytes 491528 | tf_op jit(solution)/shard_map/ppermute | solution.py:199
  85.1 30.7 %collective-permute-start.14 = (bf16[64,4096]{1,0:T(8,128)(2,1)S(1)}, bf16[64,4096]{1,0:T(8,128)(2,1)S(1)}, u32[]{:S(2)}, u32[]{:S(2)}) collective-permute-start(bf16[64,4096]{1,0:T(8,128)(2,1)S(1)} %get-tuple-element.48), channel_id=1, source_target_pairs={{0,4},{4,0},{8,12},{12,8},{16,20},{20,16},{24,28},{28,24},{32,36},... | collective-permute-start | bytes 1572872 | tf_op jit(solution)/shard_map/ppermute | solution.py:219
  87.1 30.6 %collective-permute-start.13 = (bf16[64,4096]{1,0:T(8,128)(2,1)S(1)}, bf16[64,4096]{1,0:T(8,128)(2,1)S(1)}, u32[]{:S(2)}, u32[]{:S(2)}) collective-permute-start(bf16[64,4096]{1,0:T(8,128)(2,1)S(1)} %get-tuple-element.47), channel_id=1, source_target_pairs={{4,8},{8,4},{12,16},{16,12},{20,24},{24,20},{28,32},{32,28},{36,40... | collective-permute-start | bytes 1572872 | tf_op jit(solution)/shard_map/ppermute | solution.py:222
  90.0 5.3 %collective-permute-start.15 = (f32[64,256]{1,0:T(8,128)S(1)}, f32[64,256]{1,0:T(8,128)S(1)}, u32[]{:S(2)}, u32[]{:S(2)}) collective-permute-start(f32[64,256]{1,0:T(8,128)S(1)} %convert_add_fusion), channel_id=1, source_target_pairs={{0,16},{16,0},{32,48},{48,32},{64,80},{80,64},{96,112},{112,96},{1... | collective-permute-start | bytes 196616 | tf_op jit(solution)/shard_map/ppermute | solution.py:205
  95.3 14.6 %collective-permute-start.16 = (f32[64,256]{1,0:T(8,128)S(1)}, f32[64,256]{1,0:T(8,128)S(1)}, u32[]{:S(2)}, u32[]{:S(2)}) collective-permute-start(f32[64,256]{1,0:T(8,128)S(1)} %add.31), channel_id=1, source_target_pairs={{0,256},{256,0},{1,257},{257,1},{2,258},{258,2},{3,259},{259,3},{4... | collective-permute-start | bytes 196616 | tf_op jit(solution)/shard_map/ppermute | solution.py:205
  110.0 5.9 %collective-permute-start.17 = (f32[64,256]{1,0:T(8,128)S(1)}, f32[64,256]{1,0:T(8,128)S(1)}, u32[]{:S(2)}, u32[]{:S(2)}) collective-permute-start(f32[64,256]{1,0:T(8,128)S(1)} %add.32), channel_id=1, source_target_pairs={{0,32},{16,48},{32,0},{48,16},{64,96},{80,112},{96,64},{112,80},{1... | collective-permute-start | bytes 196616 | tf_op jit(solution)/shard_map/ppermute | solution.py:205
  117.6 58.3 %copy-start.6 = (s32[88]{0:T(128)S(1)}, s32[88]{0:T(128)}, u32[]{:S(2)}) copy-start(s32[88]{0:T(128)} %rows.13) | copy-start | bytes 1060
  117.6 58.4 %copy-start.8 = (s32[88]{0:T(128)S(1)}, s32[88]{0:T(128)}, u32[]{:S(2)}) copy-start(s32[88]{0:T(128)} %cols.13) | copy-start | bytes 1060
  119.4 56.6 %collective-permute-start.18 = (bf16[64,4096]{1,0:T(8,128)(2,1)}, bf16[64,4096]{1,0:T(8,128)(2,1)}, u32[]{:S(2)}, u32[]{:S(2)}) collective-permute-start(bf16[64,4096]{1,0:T(8,128)(2,1)} %shard_map.101), channel_id=1, source_target_pairs={{0,4},{4,0},{8,12},{12,8},{16,20},{20,16},{24,28},{28,24},{32,36},... | collective-permute-start | bytes 1572872 | tf_op jit(solution)/shard_map/ppermute | solution.py:219
  121.3 54.7 %collective-permute-start.19 = (bf16[64,4096]{1,0:T(8,128)(2,1)}, bf16[64,4096]{1,0:T(8,128)(2,1)}, u32[]{:S(2)}, u32[]{:S(2)}) collective-permute-start(bf16[64,4096]{1,0:T(8,128)(2,1)} %shard_map.100), channel_id=1, source_target_pairs={{4,8},{8,4},{12,16},{16,12},{20,24},{24,20},{28,32},{32,28},{36,40... | collective-permute-start | bytes 1572872 | tf_op jit(solution)/shard_map/ppermute | solution.py:222
  126.1 10.4 %collective-permute-start.20 = (f32[64,256]{1,0:T(8,128)S(1)}, f32[64,256]{1,0:T(8,128)S(1)}, u32[]{:S(2)}, u32[]{:S(2)}) collective-permute-start(f32[64,256]{1,0:T(8,128)S(1)} %add.33), channel_id=1, source_target_pairs={{0,64},{16,80},{32,96},{48,112},{64,0},{80,16},{96,32},{112,48},{1... | collective-permute-start | bytes 196616 | tf_op jit(solution)/shard_map/ppermute | solution.py:310
  136.5 23.0 %collective-permute-start.24 = (f32[64,256]{1,0:T(8,128)S(1)}, f32[64,256]{1,0:T(8,128)S(1)}, u32[]{:S(2)}, u32[]{:S(2)}) collective-permute-start(f32[64,256]{1,0:T(8,128)S(1)} %add.34), channel_id=1, source_target_pairs={{0,128},{16,144},{32,160},{48,176},{64,192},{80,208},{96,224},{112... | collective-permute-start | bytes 196616 | tf_op jit(solution)/shard_map/ppermute | solution.py:205
  146.0 29.9 %collective-permute-start.21 = (bf16[64,1024]{1,0:T(8,128)(2,1)}, bf16[64,1024]{1,0:T(8,128)(2,1)}, u32[]{:S(2)}, u32[]{:S(2)}) collective-permute-start(bf16[64,1024]{1,0:T(8,128)(2,1)} %get-tuple-element.53), channel_id=1, source_target_pairs={{0,1},{1,0},{2,3},{3,2},{4,5},{5,4},{6,7},{7,6},{8,9},{9,8},{10,11... | collective-permute-start | bytes 393224 | tf_op jit(solution)/shard_map/ppermute | solution.py:199
  157.2 18.7 %collective-permute-start.22 = (bf16[64,1024]{1,0:T(8,128)(2,1)}, bf16[64,1024]{1,0:T(8,128)(2,1)}, u32[]{:S(2)}, u32[]{:S(2)}) collective-permute-start(bf16[64,1024]{1,0:T(8,128)(2,1)} %get-tuple-element.54), channel_id=1, source_target_pairs={{0,2},{1,3},{2,0},{3,1},{4,6},{5,7},{6,4},{7,5},{8,10},{9,11},{10,... | collective-permute-start | bytes 393224 | tf_op jit(solution)/shard_map/ppermute | solution.py:199
  159.6 16.4 %collective-permute-start.23 = (bf16[64,1024]{1,0:T(8,128)(2,1)}, bf16[64,1024]{1,0:T(8,128)(2,1)}, u32[]{:S(2)}, u32[]{:S(2)}) collective-permute-start(bf16[64,1024]{1,0:T(8,128)(2,1)} %get-tuple-element.55), channel_id=1, source_target_pairs={{0,3},{1,2},{2,1},{3,0},{4,7},{5,6},{6,5},{7,4},{8,11},{9,10},{10,... | collective-permute-start | bytes 393224 | tf_op jit(solution)/shard_map/ppermute | solution.py:199
  (2 other events, 1.3 us)

commit v6 on v5

--- a/solution.py
+++ b/solution.py
@@ -14,6 +14,7 @@
 VMEM = pl.BlockSpec(memory_space=pltpu.VMEM)
 SMEM = pl.BlockSpec(memory_space=pltpu.SMEM)
 BATCH = 6
+PARTNERS = (0, 3, 2, 1)
 
 
 def swap_pairs(count, odd):
@@ -78,7 +79,7 @@
 def pack_kernel(place, cotangent, weight, *packed):
     width = packed[0].shape[1] - weight.shape[1]
     for step, out in enumerate(packed):
-        out[:, :width] = cotangent[:, wide_lanes(place[1] ^ step, width)]
+        out[:, :width] = cotangent[:, wide_lanes(place[1] ^ PARTNERS[step], width)]
         out[:, width:] = weight[...]
 
 
@@ -91,17 +92,17 @@
     gather_terms(info, odd, total, 4 - even_offset)
     for step, out in enumerate(hidden):
         width = out.shape[1]
-        out[...] = total[:, wide_lanes(place[1] ^ step, width)].astype(out.dtype)
+        out[...] = total[:, wide_lanes(place[1] ^ PARTNERS[step], width)].astype(out.dtype)
 
 
 def dense_kernel(place, *refs):
     n = (len(refs) - 2) // 4
-    hidden, given, output, sent = (refs[k * n : (k + 1) * n] for k in range(4))
+    hidden, given, sent, output = (refs[k * n : (k + 1) * n] for k in range(4))
     source_ref, back_ref = refs[4 * n :]
     cols, width = hidden[0].shape
 
     def group(step):
-        return pl.ds(pl.multiple_of((place[1] ^ step) * cols, cols), cols)
+        return pl.ds(pl.multiple_of((place[1] ^ PARTNERS[step]) * cols, cols), cols)
 
     for step in range(n):
         source_ref[group(step), :] = hidden[step][...]
@@ -151,7 +152,7 @@
     even, odd, grads, even_total, odd_total = refs[n:]
     width = grads.shape[2]
     for step, ref in enumerate(sent):
-        grads[place[1] ^ step] = ref[:, :width]
+        grads[place[1] ^ PARTNERS[step]] = ref[:, :width]
     info = (values, rows, cols, count[0])
     even_offset = 4 - 4 * place[0]
     for offset, total, out in ((even_offset, even_total, even), (4 - even_offset, odd_total, odd)):
@@ -173,7 +174,7 @@
     spread_terms(info, grad, total, 2)
     out[...] = total[...].astype(out.dtype)
     for step, part in enumerate(parts):
-        output[:, wide_lanes(place[1] ^ step, part.shape[1])] = part[...]
+        output[:, wide_lanes(place[1] ^ PARTNERS[step], part.shape[1])] = part[...]
 
 
 def call(kernel, args, specs, outs, scratch=(), flops=0):
@@ -192,17 +193,21 @@
 
 def swapped(values):
     def pairs(step):
-        return [(source, source ^ step) for source in range(len(values))]
-
-    moved = list(values)
-    for step in reversed(range(1, len(values))):
-        moved[step] = lax.ppermute(values[step], COLS, pairs(step))
-    return moved
-
-
-def doubled(value, axis, step):
+        return [(source, source ^ PARTNERS[step]) for source in range(len(values))]
+
+    return [values[0]] + [
+        lax.ppermute(value, COLS, pairs(step)) for step, value in enumerate(values) if step
+    ]
+
+
+def summed(value, axis):
+    copies = jnp.broadcast_to(value, (lax.axis_size(axis), *value.shape))
+    return lax.all_to_all(copies, axis, 0, 0, tiled=True).sum(0)
+
+
+def paired(value, axis, step):
     count = lax.axis_size(axis)
-    return value + lax.ppermute(value, axis, [(source, source ^ step) for source in range(count)])
+    return lax.ppermute(value, axis, [(source, source ^ step) for source in range(count)])
 
 
 def local(features, weight, tile_values, tile_rows, tile_cols, tile_count, cotangent):
@@ -272,13 +277,13 @@
         dense_kernel,
         (place, *swapped(hidden), *given),
         [SMEM] + [VMEM] * (2 * n_cols),
-        arrays(n_cols, (feat_cols, width)) + arrays(n_cols, (feat_cols, width + full)),
+        arrays(n_cols, (feat_cols, width + full)) + arrays(n_cols, (feat_cols, width)),
         scratch=[pltpu.VMEM((full, width), jnp.bfloat16)] * 2,
         flops=6 * full * full * width,
     )
-    output, sent = list(both[:n_cols]), swapped(both[n_cols:])
+    output, sent = both[n_cols:], swapped(both[:n_cols])
     terms = [value[:, width:].astype(jnp.float32) for value in sent]
-    weight_grad = doubled(sum(terms[1:], terms[0]), "z", 1)
+    weight_grad = sum(terms[1:], terms[0])
     even_far, odd_far, grads = call(
         spread_far_kernel,
         tables + tuple(sent),
@@ -289,7 +294,9 @@
     )
     even_in = even_swap(even_far)
     odd_in = odd_swap(odd_far)
-    weight_grad = doubled(doubled(weight_grad, "yh", 1), "z", 2)
+    weight_grad, _ = lax.optimization_barrier((weight_grad, even_far))
+    weight_grad = weight_grad + paired(weight_grad, "z", 1)
+    weight_grad = weight_grad + paired(weight_grad, "z", 2)
 
     def near_terms(offset, sign, received):
         return call(
@@ -307,11 +314,12 @@
     odd_in, _ = lax.optimization_barrier((odd_in, odd_near))
     even_near = near_terms(3, -2, odd_in)
     even_last = even_swap(even_near)
-    far = lax.ppermute(weight_grad, "z", [(source, source ^ 4) for source in range(n_rows // 8)])
-    far, _, output[0] = lax.optimization_barrier((far, even_near, output[0]))
-    weight_grad = weight_grad + far
-    weight_grad = doubled(weight_grad, "z", 8)
+    moved = paired(weight_grad, "yh", 1)
+    moved, _, *output = lax.optimization_barrier((moved, even_near, *output))
     output = swapped(output)
+    weight_grad = weight_grad + moved
+    moved = [paired(weight_grad, "z", step) for step in (4, 12, 8)]
+    weight_grad = weight_grad + moved[0] + moved[1] + moved[2]
     feature_grad, output = call(
         spread_own_kernel,
         tables + (grads, even_last, odd_last, *output),
@@ -320,7 +328,8 @@
         scratch=[total],
         flops=18 * tile_flops,
     )
-    weight_grad = lax.all_gather(weight_grad, "x").sum(0)
+    weight_grad, feature_grad = lax.optimization_barrier((weight_grad, feature_grad))
+    weight_grad = summed(weight_grad, "x")
     weight_grad = (weight_grad * (1.0 / (node_count * n_rows) ** 0.5)).T
     return (output.T, feature_grad.T, weight_grad)
 

time: 181 us -> 166 us (0.917)
  Pallas kernels: 15 us -> 11.6 us
  waiting for transfers between devices: 38.8 us -> 35.5 us
  starting transfers between devices: 104 us -> 101 us
  other arithmetic: 3.22 us -> 0.8 us
    all_gather x1 -> x0, blocking collectives: 10.1 us -> none  [local(): weight_grad = lax.all_gather(weight_grad, 'x').sum(0)]
    all_to_all x0 -> x1, blocking collectives: none -> 8.78 us  [summed(): return lax.all_to_all(copies, axis, 0, 0, tiled=True).sum(0)]
    ppermute x17 -> x18, waiting for transfers between devices: 37.7 us -> 29.3 us  [the longest x6 20.3 us: paired(): lax.ppermute(value, axis, [(source, source ^ step) for source in range(co...]
    ppermute x17 -> x18, starting transfers between devices: 61.9 us -> 57.1 us  [the longest x12 35 us: swapped(): lax.ppermute(value, COLS, pairs(step))]
    ppermute x4, waiting for transfers between devices: 0.01 us -> 4.77 us  [odd_swap(): return lax.ppermute(value, ROWS, odd_pairs)]
    pallas_call x9, Pallas kernels: 15 us -> 11.6 us  [call(): pl.pallas_call(kernel, out_shape=outs, in_specs=specs, out_specs=[VMEM] *...]
    unnamed x18 -> x14, local copies, waits for them, and re-layouts: 5.97 us -> 5.97 us
  transfers between devices with their start and end apart: 25 -> 26, of which waited for: 9 -> 9; matrix products, arithmetic and copies ran while one was open for 2% -> 0% of each run, Pallas kernels for 4% -> 3%
where the time goes in v6:
time: 166 us; the launch traced here: 165 us
  starting transfers between devices  101 us (61%)
  waiting for transfers between devices  35.5 us (21%)
  Pallas kernels  11.6 us (7%)
  blocking collectives  8.78 us (5%)
  local copies, waits for them, and re-layouts  5.98 us (4%)
  between operations  1.69 us (1%)
    ppermute x12, starting transfers between devices, swapped(): lax.ppermute(value, COLS, pairs(step))  35 us
    ppermute x4, starting transfers between devices, odd_swap(): return lax.ppermute(value, ROWS, odd_pairs)  34.1 us
    ppermute x6, starting transfers between devices, paired(): lax.ppermute(value, axis, [(source, source ^ step) for source in range(co...  22.1 us
    ppermute x6, waiting for transfers between devices, paired(): lax.ppermute(value, axis, [(source, source ^ step) for source in range(co...  20.3 us
    pallas_call x9, Pallas kernels, call(): pl.pallas_call(kernel, out_shape=outs, in_specs=specs, out_specs=[VMEM] *...  11.6 us
    ppermute x4, starting transfers between devices, even_swap(): return lax.ppermute(value, ROWS, even_pairs)  9.71 us
    ppermute x12, waiting for transfers between devices, swapped(): lax.ppermute(value, COLS, pairs(step))  8.94 us
    all_to_all x1, blocking collectives, summed(): return lax.all_to_all(copies, axis, 0, 0, tiled=True).sum(0)  8.78 us
  transfers between devices with their start and end apart: 26, of which 9 were waited for; matrix products, arithmetic and copies ran while one was open for 0% of the time, Pallas kernels for 3%

profile of v6, /device:TPU:1, one launch (start us, length us, event | category | flops | bytes accessed | tf_op | source)
XLA Modules:
  0.0 165.4 jit_solution(10315103079916147998)
XLA Ops:
  0.6 4.0 %collective-permute-start.1 = (bf16[64,4096]{1,0:T(8,128)(2,1)}, bf16[64,4096]{1,0:T(8,128)(2,1)S(1)}, u32[]{:S(2)}, u32[]{:S(2)}) collective-permute-start(bf16[64,4096]{1,0:T(8,128)(2,1)} %bitcast.9), channel_id=1, source_target_pairs={{0,4},{4,0},{8,12},{12,8},{16,20},{20,16},{24,28},{28,24},{32,36},... | collective-permute-start | bytes 1572872 | tf_op jit(solution)/shard_map/ppermute | solution.py:224
  4.6 15.3 %collective-permute-start = (bf16[64,4096]{1,0:T(8,128)(2,1)}, bf16[64,4096]{1,0:T(8,128)(2,1)S(1)}, u32[]{:S(2)}, u32[]{:S(2)}) collective-permute-start(bf16[64,4096]{1,0:T(8,128)(2,1)} %bitcast.10), channel_id=1, source_target_pairs={{4,8},{8,4},{12,16},{16,12},{20,24},{24,20},{28,32},{32,28},{36,40... | collective-permute-start | bytes 1572872 | tf_op jit(solution)/shard_map/ppermute | solution.py:227
  23.0 9.3 %collective-permute-start.3 = (bf16[64,4096]{1,0:T(8,128)(2,1)S(1)}, bf16[64,4096]{1,0:T(8,128)(2,1)S(1)}, u32[]{:S(2)}, u32[]{:S(2)}) collective-permute-start(bf16[64,4096]{1,0:T(8,128)(2,1)S(1)} %collective-permute-done.1.even), channel_id=1, source_target_pairs={{4,8},{8,4},{12,16},{16,12},{20,24},{24,20},{28,32},{32,28},{36,40... | collective-permute-start | bytes 1572872 | tf_op jit(solution)/shard_map/ppermute | solution.py:227
  38.0 1.9 %collective-permute-start.2 = (bf16[64,4096]{1,0:T(8,128)(2,1)S(1)}, bf16[64,4096]{1,0:T(8,128)(2,1)S(1)}, u32[]{:S(2)}, u32[]{:S(2)}) collective-permute-start(bf16[64,4096]{1,0:T(8,128)(2,1)S(1)} %collective-permute-done.odd), channel_id=1, source_target_pairs={{0,4},{4,0},{8,12},{12,8},{16,20},{20,16},{24,28},{28,24},{32,36},... | collective-permute-start | bytes 1572872 | tf_op jit(solution)/shard_map/ppermute | solution.py:224
  39.9 4.0 %collective-permute-start.7 = (bf16[64,1280]{1,0:T(8,128)(2,1)S(1)}, bf16[64,1280]{1,0:T(8,128)(2,1)S(1)}, u32[]{:S(2)}, u32[]{:S(2)}) collective-permute-start(bf16[64,1280]{1,0:T(8,128)(2,1)S(1)} %get-tuple-element.45), channel_id=1, source_target_pairs={{0,3},{1,2},{2,1},{3,0},{4,7},{5,6},{6,5},{7,4},{8,11},{9,10},{10,... | collective-permute-start | bytes 491528 | tf_op jit(solution)/shard_map/ppermute | solution.py:199
  43.9 3.0 %collective-permute-start.8 = (bf16[64,1280]{1,0:T(8,128)(2,1)S(1)}, bf16[64,1280]{1,0:T(8,128)(2,1)S(1)}, u32[]{:S(2)}, u32[]{:S(2)}) collective-permute-start(bf16[64,1280]{1,0:T(8,128)(2,1)S(1)} %get-tuple-element.46), channel_id=1, source_target_pairs={{0,2},{1,3},{2,0},{3,1},{4,6},{5,7},{6,4},{7,5},{8,10},{9,11},{10,... | collective-permute-start | bytes 491528 | tf_op jit(solution)/shard_map/ppermute | solution.py:199
  46.9 1.9 %collective-permute-start.9 = (bf16[64,1280]{1,0:T(8,128)(2,1)S(1)}, bf16[64,1280]{1,0:T(8,128)(2,1)S(1)}, u32[]{:S(2)}, u32[]{:S(2)}) collective-permute-start(bf16[64,1280]{1,0:T(8,128)(2,1)S(1)} %get-tuple-element.47), channel_id=1, source_target_pairs={{0,1},{1,0},{2,3},{3,2},{4,5},{5,4},{6,7},{7,6},{8,9},{9,8},{10,11... | collective-permute-start | bytes 491528 | tf_op jit(solution)/shard_map/ppermute | solution.py:199
  53.0 4.9 %collective-permute-start.4 = (bf16[64,1024]{1,0:T(8,128)(2,1)S(1)}, bf16[64,1024]{1,0:T(8,128)(2,1)S(1)}, u32[]{:S(2)}, u32[]{:S(2)}) collective-permute-start(bf16[64,1024]{1,0:T(8,128)(2,1)S(1)} %get-tuple-element.42), channel_id=1, source_target_pairs={{0,3},{1,2},{2,1},{3,0},{4,7},{5,6},{6,5},{7,4},{8,11},{9,10},{10,... | collective-permute-start | bytes 393224 | tf_op jit(solution)/shard_map/ppermute | solution.py:199
  58.0 3.0 %collective-permute-start.5 = (bf16[64,1024]{1,0:T(8,128)(2,1)S(1)}, bf16[64,1024]{1,0:T(8,128)(2,1)S(1)}, u32[]{:S(2)}, u32[]{:S(2)}) collective-permute-start(bf16[64,1024]{1,0:T(8,128)(2,1)S(1)} %get-tuple-element.43), channel_id=1, source_target_pairs={{0,2},{1,3},{2,0},{3,1},{4,6},{5,7},{6,4},{7,5},{8,10},{9,11},{10,... | collective-permute-start | bytes 393224 | tf_op jit(solution)/shard_map/ppermute | solution.py:199
  61.0 1.9 %collective-permute-start.6 = (bf16[64,1024]{1,0:T(8,128)(2,1)S(1)}, bf16[64,1024]{1,0:T(8,128)(2,1)S(1)}, u32[]{:S(2)}, u32[]{:S(2)}) collective-permute-start(bf16[64,1024]{1,0:T(8,128)(2,1)S(1)} %get-tuple-element.44), channel_id=1, source_target_pairs={{0,1},{1,0},{2,3},{3,2},{4,5},{5,4},{6,7},{7,6},{8,9},{9,8},{10,11... | collective-permute-start | bytes 393224 | tf_op jit(solution)/shard_map/ppermute | solution.py:199
  62.9 2.3 %collective-permute-done.5.refs_2_ = bf16[64,1024]{1,0:T(8,128)(2,1)S(1)} collective-permute-done((bf16[64,1024]{1,0:T(8,128)(2,1)S(1)}, bf16[64,1024]{1,0:T(8,128)(2,1)S(1)}, u32[]{:S(2)}, u32[]{:S(2)}) %collective-permute-start.5) | collective-permute-done | bytes 131104 | tf_op jit(solution)/shard_map/ppermute | solution.py:199
  66.8 2.8 %collective-permute-start.10 = (bf16[64,1280]{1,0:T(8,128)(2,1)S(1)}, bf16[64,1280]{1,0:T(8,128)(2,1)S(1)}, u32[]{:S(2)}, u32[]{:S(2)}) collective-permute-start(bf16[64,1280]{1,0:T(8,128)(2,1)S(1)} %get-tuple-element.49), channel_id=1, source_target_pairs={{0,3},{1,2},{2,1},{3,0},{4,7},{5,6},{6,5},{7,4},{8,11},{9,10},{10,... | collective-permute-start | bytes 491528 | tf_op jit(solution)/shard_map/ppermute | solution.py:199
  69.7 2.9 %collective-permute-start.11 = (bf16[64,1280]{1,0:T(8,128)(2,1)S(1)}, bf16[64,1280]{1,0:T(8,128)(2,1)S(1)}, u32[]{:S(2)}, u32[]{:S(2)}) collective-permute-start(bf16[64,1280]{1,0:T(8,128)(2,1)S(1)} %get-tuple-element.50), channel_id=1, source_target_pairs={{0,2},{1,3},{2,0},{3,1},{4,6},{5,7},{6,4},{7,5},{8,10},{9,11},{10,... | collective-permute-start | bytes 491528 | tf_op jit(solution)/shard_map/ppermute | solution.py:199
  72.6 2.1 %collective-permute-start.12 = (bf16[64,1280]{1,0:T(8,128)(2,1)S(1)}, bf16[64,1280]{1,0:T(8,128)(2,1)S(1)}, u32[]{:S(2)}, u32[]{:S(2)}) collective-permute-start(bf16[64,1280]{1,0:T(8,128)(2,1)S(1)} %get-tuple-element.51), channel_id=1, source_target_pairs={{0,1},{1,0},{2,3},{3,2},{4,5},{5,4},{6,7},{7,6},{8,9},{9,8},{10,11... | collective-permute-start | bytes 491528 | tf_op jit(solution)/shard_map/ppermute | solution.py:199
  75.3 3.5 %collective-permute-done.11.refs_2_ = bf16[64,1280]{1,0:T(8,128)(2,1)S(1)} collective-permute-done((bf16[64,1280]{1,0:T(8,128)(2,1)S(1)}, bf16[64,1280]{1,0:T(8,128)(2,1)S(1)}, u32[]{:S(2)}, u32[]{:S(2)}) %collective-permute-start.11) | collective-permute-done | bytes 163872 | tf_op jit(solution)/shard_map/ppermute | solution.py:199
  80.2 1.9 %collective-permute-start.14 = (bf16[64,4096]{1,0:T(8,128)(2,1)S(1)}, bf16[64,4096]{1,0:T(8,128)(2,1)S(1)}, u32[]{:S(2)}, u32[]{:S(2)}) collective-permute-start(bf16[64,4096]{1,0:T(8,128)(2,1)S(1)} %get-tuple-element.54), channel_id=1, source_target_pairs={{0,4},{4,0},{8,12},{12,8},{16,20},{20,16},{24,28},{28,24},{32,36},... | collective-permute-start | bytes 1572872 | tf_op jit(solution)/shard_map/ppermute | solution.py:224
  82.1 2.6 %collective-permute-start.13 = (bf16[64,4096]{1,0:T(8,128)(2,1)S(1)}, bf16[64,4096]{1,0:T(8,128)(2,1)S(1)}, u32[]{:S(2)}, u32[]{:S(2)}) collective-permute-start(bf16[64,4096]{1,0:T(8,128)(2,1)S(1)} %get-tuple-element.53), channel_id=1, source_target_pairs={{4,8},{8,4},{12,16},{16,12},{20,24},{24,20},{28,32},{32,28},{36,40... | collective-permute-start | bytes 1572872 | tf_op jit(solution)/shard_map/ppermute | solution.py:227
  84.7 1.9 %collective-permute-start.15 = (f32[64,256]{1,0:T(8,128)S(1)}, f32[64,256]{1,0:T(8,128)S(1)}, u32[]{:S(2)}, u32[]{:S(2)}) collective-permute-start(f32[64,256]{1,0:T(8,128)S(1)} %convert_add_fusion), channel_id=1, source_target_pairs={{0,16},{16,0},{32,48},{48,32},{64,80},{80,64},{96,112},{112,96},{1... | collective-permute-start | bytes 196616 | tf_op jit(solution)/shard_map/ppermute | solution.py:210
  86.6 3.4 %collective-permute-done.15 = f32[64,256]{1,0:T(8,128)S(1)} collective-permute-done((f32[64,256]{1,0:T(8,128)S(1)}, f32[64,256]{1,0:T(8,128)S(1)}, u32[]{:S(2)}, u32[]{:S(2)}) %collective-permute-start.15) | collective-permute-done | bytes 65568 | tf_op jit(solution)/shard_map/ppermute | solution.py:210
  90.0 2.1 %collective-permute-start.16 = (f32[64,256]{1,0:T(8,128)S(1)}, f32[64,256]{1,0:T(8,128)S(1)}, u32[]{:S(2)}, u32[]{:S(2)}) collective-permute-start(f32[64,256]{1,0:T(8,128)S(1)} %add.34), channel_id=1, source_target_pairs={{0,32},{16,48},{32,0},{48,16},{64,96},{80,112},{96,64},{112,80},{1... | collective-permute-start | bytes 196616 | tf_op jit(solution)/shard_map/ppermute | solution.py:210
  92.1 4.6 %collective-permute-done.16 = f32[64,256]{1,0:T(8,128)S(1)} collective-permute-done((f32[64,256]{1,0:T(8,128)S(1)}, f32[64,256]{1,0:T(8,128)S(1)}, u32[]{:S(2)}, u32[]{:S(2)}) %collective-permute-start.16) | collective-permute-done | bytes 65568 | tf_op jit(solution)/shard_map/ppermute | solution.py:210
  97.6 4.8 %collective-permute-done.13.received = bf16[64,4096]{1,0:T(8,128)(2,1)S(1)} collective-permute-done((bf16[64,4096]{1,0:T(8,128)(2,1)S(1)}, bf16[64,4096]{1,0:T(8,128)(2,1)S(1)}, u32[]{:S(2)}, u32[]{:S(2)}) %collective-permute-start.13) | collective-permute-done | bytes 524320 | tf_op jit(solution)/shard_map/ppermute | solution.py:227
  105.3 7.0 %collective-permute-start.18 = (bf16[64,4096]{1,0:T(8,128)(2,1)S(1)}, bf16[64,4096]{1,0:T(8,128)(2,1)S(1)}, u32[]{:S(2)}, u32[]{:S(2)}) collective-permute-start(bf16[64,4096]{1,0:T(8,128)(2,1)S(1)} %shard_map.100), channel_id=1, source_target_pairs={{4,8},{8,4},{12,16},{16,12},{20,24},{24,20},{28,32},{32,28},{36,40... | collective-permute-start | bytes 1572872 | tf_op jit(solution)/shard_map/ppermute | solution.py:227
  114.2 12.4 %collective-permute-done.19 = f32[64,256]{1,0:T(8,128)S(1)} collective-permute-done((f32[64,256]{1,0:T(8,128)S(1)}, f32[64,256]{1,0:T(8,128)S(1)}, u32[]{:S(2)}, u32[]{:S(2)}) %collective-permute-start.19) | collective-permute-done | bytes 65568 | tf_op jit(solution)/shard_map/ppermute | solution.py:210
  126.6 1.9 %collective-permute-start.25 = (f32[64,256]{1,0:T(8,128)S(1)}, f32[64,256]{1,0:T(8,128)S(1)}, u32[]{:S(2)}, u32[]{:S(2)}) collective-permute-start(f32[64,256]{1,0:T(8,128)S(1)} %add.36), channel_id=1, source_target_pairs={{0,128},{16,144},{32,160},{48,176},{64,192},{80,208},{96,224},{112... | collective-permute-start | bytes 196616 | tf_op jit(solution)/shard_map/ppermute | solution.py:210
  128.5 1.9 %collective-permute-start.24 = (f32[64,256]{1,0:T(8,128)S(1)}, f32[64,256]{1,0:T(8,128)S(1)}, u32[]{:S(2)}, u32[]{:S(2)}) collective-permute-start(f32[64,256]{1,0:T(8,128)S(1)} %add.36), channel_id=1, source_target_pairs={{0,192},{16,208},{32,224},{48,240},{64,128},{80,144},{96,160},{112... | collective-permute-start | bytes 196616 | tf_op jit(solution)/shard_map/ppermute | solution.py:210
  130.4 12.3 %collective-permute-start.23 = (f32[64,256]{1,0:T(8,128)S(1)}, f32[64,256]{1,0:T(8,128)S(1)}, u32[]{:S(2)}, u32[]{:S(2)}) collective-permute-start(f32[64,256]{1,0:T(8,128)S(1)} %add.36), channel_id=1, source_target_pairs={{0,64},{16,80},{32,96},{48,112},{64,0},{80,16},{96,32},{112,48},{1... | collective-permute-start | bytes 196616 | tf_op jit(solution)/shard_map/ppermute | solution.py:210
  142.8 3.8 %collective-permute-start.20 = (bf16[64,1024]{1,0:T(8,128)(2,1)S(1)}, bf16[64,1024]{1,0:T(8,128)(2,1)S(1)}, u32[]{:S(2)}, u32[]{:S(2)}) collective-permute-start(bf16[64,1024]{1,0:T(8,128)(2,1)S(1)} %get-tuple-element.63), channel_id=1, source_target_pairs={{0,3},{1,2},{2,1},{3,0},{4,7},{5,6},{6,5},{7,4},{8,11},{9,10},{10,... | collective-permute-start | bytes 393224 | tf_op jit(solution)/shard_map/ppermute | solution.py:199
  146.6 2.7 %collective-permute-start.21 = (bf16[64,1024]{1,0:T(8,128)(2,1)S(1)}, bf16[64,1024]{1,0:T(8,128)(2,1)S(1)}, u32[]{:S(2)}, u32[]{:S(2)}) collective-permute-start(bf16[64,1024]{1,0:T(8,128)(2,1)S(1)} %get-tuple-element.64), channel_id=1, source_target_pairs={{0,2},{1,3},{2,0},{3,1},{4,6},{5,7},{6,4},{7,5},{8,10},{9,11},{10,... | collective-permute-start | bytes 393224 | tf_op jit(solution)/shard_map/ppermute | solution.py:199
  151.3 2.6 %collective-permute-done.21.refs_2_ = bf16[64,1024]{1,0:T(8,128)(2,1)S(1)} collective-permute-done((bf16[64,1024]{1,0:T(8,128)(2,1)S(1)}, bf16[64,1024]{1,0:T(8,128)(2,1)S(1)}, u32[]{:S(2)}, u32[]{:S(2)}) %collective-permute-start.21) | collective-permute-done | bytes 131104 | tf_op jit(solution)/shard_map/ppermute | solution.py:199
  153.9 2.0 %shard_map.102 = (bf16[64,4096]{1,0:T(8,128)(2,1)}, bf16[64,4096]{1,0:T(8,128)(2,1)}) custom-call(bf16[88,128,128]{2,1,0:T(8,128)(2,1)S(1)} %copy-done.1, s32[88]{0:T(128)S(1)} %copy-done.5, s32[88]{0:T(128)S(1)} %copy-done.6, s32[1]{0:T(128)S(6)} %copy.10.count, s32[2]{0:T(128)S(1)} %pad_add_fusion.place, bf16[4,64,1024]{2,1,0:T(8,128)(2,1)S(1)} %get-tuple-element.52.grad, ...), custom_call_target="tpu_custom_call" | custom-call | flops 37748736 | bytes 6030028 | tf_op jit(solution)/shard_map/pallas_call | solution.py:183
  155.9 8.8 %all_to_all.5 = f32[4,64,256]{2,1,0:T(8,128)S(1)} all-to-all(f32[4,64,256]{2,1,0:T(8,128)S(1)} %broadcast_in_dim.3), channel_id=1, replica_groups=mesh['yh'=2,'z'=16,'x'=4,'yl'=2,'core'=2] {'x'}, dimensions={0} | all-to-all | bytes 524288 | tf_op jit(solution)/shard_map/all_to_all | solution.py:205
  (53 shorter events, 24.3 us)
Async XLA Ops:
  0.6 22.4 %collective-permute-start.1 = (bf16[64,4096]{1,0:T(8,128)(2,1)}, bf16[64,4096]{1,0:T(8,128)(2,1)S(1)}, u32[]{:S(2)}, u32[]{:S(2)}) collective-permute-start(bf16[64,4096]{1,0:T(8,128)(2,1)} %bitcast.9), channel_id=1, source_target_pairs={{0,4},{4,0},{8,12},{12,8},{16,20},{20,16},{24,28},{28,24},{32,36},... | collective-permute-start | bytes 1572872 | tf_op jit(solution)/shard_map/ppermute | solution.py:224
  4.6 33.4 %collective-permute-start = (bf16[64,4096]{1,0:T(8,128)(2,1)}, bf16[64,4096]{1,0:T(8,128)(2,1)S(1)}, u32[]{:S(2)}, u32[]{:S(2)}) collective-permute-start(bf16[64,4096]{1,0:T(8,128)(2,1)} %bitcast.10), channel_id=1, source_target_pairs={{4,8},{8,4},{12,16},{16,12},{20,24},{24,20},{28,32},{32,28},{36,40... | collective-permute-start | bytes 1572872 | tf_op jit(solution)/shard_map/ppermute | solution.py:227
  20.6 1.0 copy-start.3
  21.7 0.8 copy-start.4
  23.0 26.9 %collective-permute-start.3 = (bf16[64,4096]{1,0:T(8,128)(2,1)S(1)}, bf16[64,4096]{1,0:T(8,128)(2,1)S(1)}, u32[]{:S(2)}, u32[]{:S(2)}) collective-permute-start(bf16[64,4096]{1,0:T(8,128)(2,1)S(1)} %collective-permute-done.1.even), channel_id=1, source_target_pairs={{4,8},{8,4},{12,16},{16,12},{20,24},{24,20},{28,32},{32,28},{36,40... | collective-permute-start | bytes 1572872 | tf_op jit(solution)/shard_map/ppermute | solution.py:227
  32.3 1.8 %copy-start = (bf16[88,128,128]{2,1,0:T(8,128)(2,1)S(1)}, bf16[88,128,128]{2,1,0:T(8,128)(2,1)}, u32[]{:S(2)}) copy-start(bf16[88,128,128]{2,1,0:T(8,128)(2,1)} %values.13) | copy-start | bytes 8650756
  34.1 1.0 copy-start.2
  35.2 0.7 copy-start.5
  38.0 13.5 %collective-permute-start.2 = (bf16[64,4096]{1,0:T(8,128)(2,1)S(1)}, bf16[64,4096]{1,0:T(8,128)(2,1)S(1)}, u32[]{:S(2)}, u32[]{:S(2)}) collective-permute-start(bf16[64,4096]{1,0:T(8,128)(2,1)S(1)} %collective-permute-done.odd), channel_id=1, source_target_pairs={{0,4},{4,0},{8,12},{12,8},{16,20},{20,16},{24,28},{28,24},{32,36},... | collective-permute-start | bytes 1572872 | tf_op jit(solution)/shard_map/ppermute | solution.py:224
  39.9 21.1 %collective-permute-start.7 = (bf16[64,1280]{1,0:T(8,128)(2,1)S(1)}, bf16[64,1280]{1,0:T(8,128)(2,1)S(1)}, u32[]{:S(2)}, u32[]{:S(2)}) collective-permute-start(bf16[64,1280]{1,0:T(8,128)(2,1)S(1)} %get-tuple-element.45), channel_id=1, source_target_pairs={{0,3},{1,2},{2,1},{3,0},{4,7},{5,6},{6,5},{7,4},{8,11},{9,10},{10,... | collective-permute-start | bytes 491528 | tf_op jit(solution)/shard_map/ppermute | solution.py:199
  43.9 19.0 %collective-permute-start.8 = (bf16[64,1280]{1,0:T(8,128)(2,1)S(1)}, bf16[64,1280]{1,0:T(8,128)(2,1)S(1)}, u32[]{:S(2)}, u32[]{:S(2)}) collective-permute-start(bf16[64,1280]{1,0:T(8,128)(2,1)S(1)} %get-tuple-element.46), channel_id=1, source_target_pairs={{0,2},{1,3},{2,0},{3,1},{4,6},{5,7},{6,4},{7,5},{8,10},{9,11},{10,... | collective-permute-start | bytes 491528 | tf_op jit(solution)/shard_map/ppermute | solution.py:199
  46.9 16.0 %collective-permute-start.9 = (bf16[64,1280]{1,0:T(8,128)(2,1)S(1)}, bf16[64,1280]{1,0:T(8,128)(2,1)S(1)}, u32[]{:S(2)}, u32[]{:S(2)}) collective-permute-start(bf16[64,1280]{1,0:T(8,128)(2,1)S(1)} %get-tuple-element.47), channel_id=1, source_target_pairs={{0,1},{1,0},{2,3},{3,2},{4,5},{5,4},{6,7},{7,6},{8,9},{9,8},{10,11... | collective-permute-start | bytes 491528 | tf_op jit(solution)/shard_map/ppermute | solution.py:199
  49.9 28.9 %copy-start.1 = (bf16[88,128,128]{2,1,0:T(8,128)(2,1)S(1)}, bf16[88,128,128]{2,1,0:T(8,128)(2,1)}, u32[]{:S(2)}) copy-start(bf16[88,128,128]{2,1,0:T(8,128)(2,1)} %values.13) | copy-start | bytes 8650756
  53.0 9.9 %collective-permute-start.4 = (bf16[64,1024]{1,0:T(8,128)(2,1)S(1)}, bf16[64,1024]{1,0:T(8,128)(2,1)S(1)}, u32[]{:S(2)}, u32[]{:S(2)}) collective-permute-start(bf16[64,1024]{1,0:T(8,128)(2,1)S(1)} %get-tuple-element.42), channel_id=1, source_target_pairs={{0,3},{1,2},{2,1},{3,0},{4,7},{5,6},{6,5},{7,4},{8,11},{9,10},{10,... | collective-permute-start | bytes 393224 | tf_op jit(solution)/shard_map/ppermute | solution.py:199
  58.0 7.2 %collective-permute-start.5 = (bf16[64,1024]{1,0:T(8,128)(2,1)S(1)}, bf16[64,1024]{1,0:T(8,128)(2,1)S(1)}, u32[]{:S(2)}, u32[]{:S(2)}) collective-permute-start(bf16[64,1024]{1,0:T(8,128)(2,1)S(1)} %get-tuple-element.43), channel_id=1, source_target_pairs={{0,2},{1,3},{2,0},{3,1},{4,6},{5,7},{6,4},{7,5},{8,10},{9,11},{10,... | collective-permute-start | bytes 393224 | tf_op jit(solution)/shard_map/ppermute | solution.py:199
  61.0 4.2 %collective-permute-start.6 = (bf16[64,1024]{1,0:T(8,128)(2,1)S(1)}, bf16[64,1024]{1,0:T(8,128)(2,1)S(1)}, u32[]{:S(2)}, u32[]{:S(2)}) collective-permute-start(bf16[64,1024]{1,0:T(8,128)(2,1)S(1)} %get-tuple-element.44), channel_id=1, source_target_pairs={{0,1},{1,0},{2,3},{3,2},{4,5},{5,4},{6,7},{7,6},{8,9},{9,8},{10,11... | collective-permute-start | bytes 393224 | tf_op jit(solution)/shard_map/ppermute | solution.py:199
  66.8 8.5 %collective-permute-start.10 = (bf16[64,1280]{1,0:T(8,128)(2,1)S(1)}, bf16[64,1280]{1,0:T(8,128)(2,1)S(1)}, u32[]{:S(2)}, u32[]{:S(2)}) collective-permute-start(bf16[64,1280]{1,0:T(8,128)(2,1)S(1)} %get-tuple-element.49), channel_id=1, source_target_pairs={{0,3},{1,2},{2,1},{3,0},{4,7},{5,6},{6,5},{7,4},{8,11},{9,10},{10,... | collective-permute-start | bytes 491528 | tf_op jit(solution)/shard_map/ppermute | solution.py:199
  69.7 9.1 %collective-permute-start.11 = (bf16[64,1280]{1,0:T(8,128)(2,1)S(1)}, bf16[64,1280]{1,0:T(8,128)(2,1)S(1)}, u32[]{:S(2)}, u32[]{:S(2)}) collective-permute-start(bf16[64,1280]{1,0:T(8,128)(2,1)S(1)} %get-tuple-element.50), channel_id=1, source_target_pairs={{0,2},{1,3},{2,0},{3,1},{4,6},{5,7},{6,4},{7,5},{8,10},{9,11},{10,... | collective-permute-start | bytes 491528 | tf_op jit(solution)/shard_map/ppermute | solution.py:199
  72.6 6.2 %collective-permute-start.12 = (bf16[64,1280]{1,0:T(8,128)(2,1)S(1)}, bf16[64,1280]{1,0:T(8,128)(2,1)S(1)}, u32[]{:S(2)}, u32[]{:S(2)}) collective-permute-start(bf16[64,1280]{1,0:T(8,128)(2,1)S(1)} %get-tuple-element.51), channel_id=1, source_target_pairs={{0,1},{1,0},{2,3},{3,2},{4,5},{5,4},{6,7},{7,6},{8,9},{9,8},{10,11... | collective-permute-start | bytes 491528 | tf_op jit(solution)/shard_map/ppermute | solution.py:199
  80.2 16.5 %collective-permute-start.14 = (bf16[64,4096]{1,0:T(8,128)(2,1)S(1)}, bf16[64,4096]{1,0:T(8,128)(2,1)S(1)}, u32[]{:S(2)}, u32[]{:S(2)}) collective-permute-start(bf16[64,4096]{1,0:T(8,128)(2,1)S(1)} %get-tuple-element.54), channel_id=1, source_target_pairs={{0,4},{4,0},{8,12},{12,8},{16,20},{20,16},{24,28},{28,24},{32,36},... | collective-permute-start | bytes 1572872 | tf_op jit(solution)/shard_map/ppermute | solution.py:224
  82.1 20.3 %collective-permute-start.13 = (bf16[64,4096]{1,0:T(8,128)(2,1)S(1)}, bf16[64,4096]{1,0:T(8,128)(2,1)S(1)}, u32[]{:S(2)}, u32[]{:S(2)}) collective-permute-start(bf16[64,4096]{1,0:T(8,128)(2,1)S(1)} %get-tuple-element.53), channel_id=1, source_target_pairs={{4,8},{8,4},{12,16},{16,12},{20,24},{24,20},{28,32},{32,28},{36,40... | collective-permute-start | bytes 1572872 | tf_op jit(solution)/shard_map/ppermute | solution.py:227
  84.7 5.3 %collective-permute-start.15 = (f32[64,256]{1,0:T(8,128)S(1)}, f32[64,256]{1,0:T(8,128)S(1)}, u32[]{:S(2)}, u32[]{:S(2)}) collective-permute-start(f32[64,256]{1,0:T(8,128)S(1)} %convert_add_fusion), channel_id=1, source_target_pairs={{0,16},{16,0},{32,48},{48,32},{64,80},{80,64},{96,112},{112,96},{1... | collective-permute-start | bytes 196616 | tf_op jit(solution)/shard_map/ppermute | solution.py:210
  90.0 6.6 %collective-permute-start.16 = (f32[64,256]{1,0:T(8,128)S(1)}, f32[64,256]{1,0:T(8,128)S(1)}, u32[]{:S(2)}, u32[]{:S(2)}) collective-permute-start(f32[64,256]{1,0:T(8,128)S(1)} %add.34), channel_id=1, source_target_pairs={{0,32},{16,48},{32,0},{48,16},{64,96},{80,112},{96,64},{112,80},{1... | collective-permute-start | bytes 196616 | tf_op jit(solution)/shard_map/ppermute | solution.py:210
  103.3 50.5 %collective-permute-start.17 = (bf16[64,4096]{1,0:T(8,128)(2,1)S(1)}, bf16[64,4096]{1,0:T(8,128)(2,1)S(1)}, u32[]{:S(2)}, u32[]{:S(2)}) collective-permute-start(bf16[64,4096]{1,0:T(8,128)(2,1)S(1)} %shard_map.101), channel_id=1, source_target_pairs={{0,4},{4,0},{8,12},{12,8},{16,20},{20,16},{24,28},{28,24},{32,36},... | collective-permute-start | bytes 1572872 | tf_op jit(solution)/shard_map/ppermute | solution.py:224
  105.3 48.6 %collective-permute-start.18 = (bf16[64,4096]{1,0:T(8,128)(2,1)S(1)}, bf16[64,4096]{1,0:T(8,128)(2,1)S(1)}, u32[]{:S(2)}, u32[]{:S(2)}) collective-permute-start(bf16[64,4096]{1,0:T(8,128)(2,1)S(1)} %shard_map.100), channel_id=1, source_target_pairs={{4,8},{8,4},{12,16},{16,12},{20,24},{24,20},{28,32},{32,28},{36,40... | collective-permute-start | bytes 1572872 | tf_op jit(solution)/shard_map/ppermute | solution.py:227
  112.3 14.3 %collective-permute-start.19 = (f32[64,256]{1,0:T(8,128)S(1)}, f32[64,256]{1,0:T(8,128)S(1)}, u32[]{:S(2)}, u32[]{:S(2)}) collective-permute-start(f32[64,256]{1,0:T(8,128)S(1)} %add.35), channel_id=1, source_target_pairs={{0,256},{256,0},{1,257},{257,1},{2,258},{258,2},{3,259},{259,3},{4... | collective-permute-start | bytes 196616 | tf_op jit(solution)/shard_map/ppermute | solution.py:210
  126.6 16.2 %collective-permute-start.25 = (f32[64,256]{1,0:T(8,128)S(1)}, f32[64,256]{1,0:T(8,128)S(1)}, u32[]{:S(2)}, u32[]{:S(2)}) collective-permute-start(f32[64,256]{1,0:T(8,128)S(1)} %add.36), channel_id=1, source_target_pairs={{0,128},{16,144},{32,160},{48,176},{64,192},{80,208},{96,224},{112... | collective-permute-start | bytes 196616 | tf_op jit(solution)/shard_map/ppermute | solution.py:210
  128.5 18.1 %collective-permute-start.24 = (f32[64,256]{1,0:T(8,128)S(1)}, f32[64,256]{1,0:T(8,128)S(1)}, u32[]{:S(2)}, u32[]{:S(2)}) collective-permute-start(f32[64,256]{1,0:T(8,128)S(1)} %add.36), channel_id=1, source_target_pairs={{0,192},{16,208},{32,224},{48,240},{64,128},{80,144},{96,160},{112... | collective-permute-start | bytes 196616 | tf_op jit(solution)/shard_map/ppermute | solution.py:210
  130.4 18.9 %collective-permute-start.23 = (f32[64,256]{1,0:T(8,128)S(1)}, f32[64,256]{1,0:T(8,128)S(1)}, u32[]{:S(2)}, u32[]{:S(2)}) collective-permute-start(f32[64,256]{1,0:T(8,128)S(1)} %add.36), channel_id=1, source_target_pairs={{0,64},{16,80},{32,96},{48,112},{64,0},{80,16},{96,32},{112,48},{1... | collective-permute-start | bytes 196616 | tf_op jit(solution)/shard_map/ppermute | solution.py:210
  142.8 8.5 %collective-permute-start.20 = (bf16[64,1024]{1,0:T(8,128)(2,1)S(1)}, bf16[64,1024]{1,0:T(8,128)(2,1)S(1)}, u32[]{:S(2)}, u32[]{:S(2)}) collective-permute-start(bf16[64,1024]{1,0:T(8,128)(2,1)S(1)} %get-tuple-element.63), channel_id=1, source_target_pairs={{0,3},{1,2},{2,1},{3,0},{4,7},{5,6},{6,5},{7,4},{8,11},{9,10},{10,... | collective-permute-start | bytes 393224 | tf_op jit(solution)/shard_map/ppermute | solution.py:199
  146.6 7.2 %collective-permute-start.21 = (bf16[64,1024]{1,0:T(8,128)(2,1)S(1)}, bf16[64,1024]{1,0:T(8,128)(2,1)S(1)}, u32[]{:S(2)}, u32[]{:S(2)}) collective-permute-start(bf16[64,1024]{1,0:T(8,128)(2,1)S(1)} %get-tuple-element.64), channel_id=1, source_target_pairs={{0,2},{1,3},{2,0},{3,1},{4,6},{5,7},{6,4},{7,5},{8,10},{9,11},{10,... | collective-permute-start | bytes 393224 | tf_op jit(solution)/shard_map/ppermute | solution.py:199
  149.3 4.5 %collective-permute-start.22 = (bf16[64,1024]{1,0:T(8,128)(2,1)S(1)}, bf16[64,1024]{1,0:T(8,128)(2,1)S(1)}, u32[]{:S(2)}, u32[]{:S(2)}) collective-permute-start(bf16[64,1024]{1,0:T(8,128)(2,1)S(1)} %get-tuple-element.65), channel_id=1, source_target_pairs={{0,1},{1,0},{2,3},{3,2},{4,5},{5,4},{6,7},{7,6},{8,9},{9,8},{10,11... | collective-permute-start | bytes 393224 | tf_op jit(solution)/shard_map/ppermute | solution.py:199
  (1 other events, 0.7 us)

commit v7 on v6

--- a/solution.py
+++ b/solution.py
@@ -295,8 +295,8 @@
     even_in = even_swap(even_far)
     odd_in = odd_swap(odd_far)
     weight_grad, _ = lax.optimization_barrier((weight_grad, even_far))
+    weight_grad = weight_grad + paired(weight_grad, "yh", 1)
     weight_grad = weight_grad + paired(weight_grad, "z", 1)
-    weight_grad = weight_grad + paired(weight_grad, "z", 2)
 
     def near_terms(offset, sign, received):
         return call(
@@ -311,13 +311,12 @@
     even_in, _ = lax.optimization_barrier((even_in, weight_grad))
     odd_near = near_terms(1, 2, even_in)
     odd_last = odd_swap(odd_near)
-    odd_in, _ = lax.optimization_barrier((odd_in, odd_near))
+    weight_grad = weight_grad + paired(weight_grad, "z", 2)
+    output = swapped(output)
+    odd_in, *_ = lax.optimization_barrier((odd_in, odd_near, weight_grad, *output))
     even_near = near_terms(3, -2, odd_in)
     even_last = even_swap(even_near)
-    moved = paired(weight_grad, "yh", 1)
-    moved, _, *output = lax.optimization_barrier((moved, even_near, *output))
-    output = swapped(output)
-    weight_grad = weight_grad + moved
+    weight_grad, _ = lax.optimization_barrier((weight_grad, even_near))
     moved = [paired(weight_grad, "z", step) for step in (4, 12, 8)]
     weight_grad = weight_grad + moved[0] + moved[1] + moved[2]
     feature_grad, output = call(

time: 166 us -> 167 us (level)
  waiting for transfers between devices: 35.5 us -> 40.4 us
  starting transfers between devices: 101 us -> 96.5 us
    ppermute x4, starting transfers between devices: 34.1 us -> 29.2 us  [odd_swap(): return lax.ppermute(value, ROWS, odd_pairs)]
    ppermute x4, waiting for transfers between devices: 4.77 us -> 7.98 us  [odd_swap(): return lax.ppermute(value, ROWS, odd_pairs)]
    ppermute x6, waiting for transfers between devices: 20.3 us -> 23.2 us  [paired(): lax.ppermute(value, axis, [(source, source ^ step) for source in range(co...]
  transfers between devices with their start and end apart: 26 -> 26, of which waited for: 9 -> 10; matrix products, arithmetic and copies ran while one was open for 0% -> 0% of each run, Pallas kernels for 3% -> 3%
where the time goes in v7:
time: 167 us; the launch traced here: 165 us
  starting transfers between devices  96.5 us (58%)
  waiting for transfers between devices  40.4 us (24%)
  Pallas kernels  11.6 us (7%)
  blocking collectives  7.92 us (5%)
  local copies, waits for them, and re-layouts  5.98 us (4%)
  between operations  1.68 us (1%)
    ppermute x12, starting transfers between devices, swapped(): lax.ppermute(value, COLS, pairs(step))  35.6 us
    ppermute x4, starting transfers between devices, odd_swap(): return lax.ppermute(value, ROWS, odd_pairs)  29.2 us
    ppermute x6, waiting for transfers between devices, paired(): lax.ppermute(value, axis, [(source, source ^ step) for source in range(co...  23.2 us
    ppermute x6, starting transfers between devices, paired(): lax.ppermute(value, axis, [(source, source ^ step) for source in range(co...  21.9 us
    pallas_call x9, Pallas kernels, call(): pl.pallas_call(kernel, out_shape=outs, in_specs=specs, out_specs=[VMEM] *...  11.6 us
    ppermute x4, starting transfers between devices, even_swap(): return lax.ppermute(value, ROWS, even_pairs)  9.71 us
    ppermute x4, waiting for transfers between devices, odd_swap(): return lax.ppermute(value, ROWS, odd_pairs)  7.98 us
    all_to_all x1, blocking collectives, summed(): return lax.all_to_all(copies, axis, 0, 0, tiled=True).sum(0)  7.92 us
  transfers between devices with their start and end apart: 26, of which 10 were waited for; matrix products, arithmetic and copies ran while one was open for 0% of the time, Pallas kernels for 3%

profile of v7, /device:TPU:1, one launch (start us, length us, event | category | flops | bytes accessed | tf_op | source)
XLA Modules:
  0.0 164.8 jit_solution(15270609041860504750)
XLA Ops:
  0.6 4.0 %collective-permute-start.1 = (bf16[64,4096]{1,0:T(8,128)(2,1)}, bf16[64,4096]{1,0:T(8,128)(2,1)S(1)}, u32[]{:S(2)}, u32[]{:S(2)}) collective-permute-start(bf16[64,4096]{1,0:T(8,128)(2,1)} %bitcast.9), channel_id=1, source_target_pairs={{0,4},{4,0},{8,12},{12,8},{16,20},{20,16},{24,28},{28,24},{32,36},... | collective-permute-start | bytes 1572872 | tf_op jit(solution)/shard_map/ppermute | solution.py:224
  4.6 15.3 %collective-permute-start = (bf16[64,4096]{1,0:T(8,128)(2,1)}, bf16[64,4096]{1,0:T(8,128)(2,1)S(1)}, u32[]{:S(2)}, u32[]{:S(2)}) collective-permute-start(bf16[64,4096]{1,0:T(8,128)(2,1)} %bitcast.10), channel_id=1, source_target_pairs={{4,8},{8,4},{12,16},{16,12},{20,24},{24,20},{28,32},{32,28},{36,40... | collective-permute-start | bytes 1572872 | tf_op jit(solution)/shard_map/ppermute | solution.py:227
  23.0 9.3 %collective-permute-start.3 = (bf16[64,4096]{1,0:T(8,128)(2,1)S(1)}, bf16[64,4096]{1,0:T(8,128)(2,1)S(1)}, u32[]{:S(2)}, u32[]{:S(2)}) collective-permute-start(bf16[64,4096]{1,0:T(8,128)(2,1)S(1)} %collective-permute-done.1.even), channel_id=1, source_target_pairs={{4,8},{8,4},{12,16},{16,12},{20,24},{24,20},{28,32},{32,28},{36,40... | collective-permute-start | bytes 1572872 | tf_op jit(solution)/shard_map/ppermute | solution.py:227
  38.0 1.9 %collective-permute-start.2 = (bf16[64,4096]{1,0:T(8,128)(2,1)S(1)}, bf16[64,4096]{1,0:T(8,128)(2,1)S(1)}, u32[]{:S(2)}, u32[]{:S(2)}) collective-permute-start(bf16[64,4096]{1,0:T(8,128)(2,1)S(1)} %collective-permute-done.odd), channel_id=1, source_target_pairs={{0,4},{4,0},{8,12},{12,8},{16,20},{20,16},{24,28},{28,24},{32,36},... | collective-permute-start | bytes 1572872 | tf_op jit(solution)/shard_map/ppermute | solution.py:224
  39.9 4.0 %collective-permute-start.7 = (bf16[64,1280]{1,0:T(8,128)(2,1)S(1)}, bf16[64,1280]{1,0:T(8,128)(2,1)S(1)}, u32[]{:S(2)}, u32[]{:S(2)}) collective-permute-start(bf16[64,1280]{1,0:T(8,128)(2,1)S(1)} %get-tuple-element.41), channel_id=1, source_target_pairs={{0,3},{1,2},{2,1},{3,0},{4,7},{5,6},{6,5},{7,4},{8,11},{9,10},{10,... | collective-permute-start | bytes 491528 | tf_op jit(solution)/shard_map/ppermute | solution.py:199
  43.9 3.0 %collective-permute-start.8 = (bf16[64,1280]{1,0:T(8,128)(2,1)S(1)}, bf16[64,1280]{1,0:T(8,128)(2,1)S(1)}, u32[]{:S(2)}, u32[]{:S(2)}) collective-permute-start(bf16[64,1280]{1,0:T(8,128)(2,1)S(1)} %get-tuple-element.42), channel_id=1, source_target_pairs={{0,2},{1,3},{2,0},{3,1},{4,6},{5,7},{6,4},{7,5},{8,10},{9,11},{10,... | collective-permute-start | bytes 491528 | tf_op jit(solution)/shard_map/ppermute | solution.py:199
  46.9 1.9 %collective-permute-start.9 = (bf16[64,1280]{1,0:T(8,128)(2,1)S(1)}, bf16[64,1280]{1,0:T(8,128)(2,1)S(1)}, u32[]{:S(2)}, u32[]{:S(2)}) collective-permute-start(bf16[64,1280]{1,0:T(8,128)(2,1)S(1)} %get-tuple-element.43), channel_id=1, source_target_pairs={{0,1},{1,0},{2,3},{3,2},{4,5},{5,4},{6,7},{7,6},{8,9},{9,8},{10,11... | collective-permute-start | bytes 491528 | tf_op jit(solution)/shard_map/ppermute | solution.py:199
  53.0 4.9 %collective-permute-start.4 = (bf16[64,1024]{1,0:T(8,128)(2,1)S(1)}, bf16[64,1024]{1,0:T(8,128)(2,1)S(1)}, u32[]{:S(2)}, u32[]{:S(2)}) collective-permute-start(bf16[64,1024]{1,0:T(8,128)(2,1)S(1)} %get-tuple-element.38), channel_id=1, source_target_pairs={{0,3},{1,2},{2,1},{3,0},{4,7},{5,6},{6,5},{7,4},{8,11},{9,10},{10,... | collective-permute-start | bytes 393224 | tf_op jit(solution)/shard_map/ppermute | solution.py:199
  58.0 3.0 %collective-permute-start.5 = (bf16[64,1024]{1,0:T(8,128)(2,1)S(1)}, bf16[64,1024]{1,0:T(8,128)(2,1)S(1)}, u32[]{:S(2)}, u32[]{:S(2)}) collective-permute-start(bf16[64,1024]{1,0:T(8,128)(2,1)S(1)} %get-tuple-element.39), channel_id=1, source_target_pairs={{0,2},{1,3},{2,0},{3,1},{4,6},{5,7},{6,4},{7,5},{8,10},{9,11},{10,... | collective-permute-start | bytes 393224 | tf_op jit(solution)/shard_map/ppermute | solution.py:199
  61.0 1.9 %collective-permute-start.6 = (bf16[64,1024]{1,0:T(8,128)(2,1)S(1)}, bf16[64,1024]{1,0:T(8,128)(2,1)S(1)}, u32[]{:S(2)}, u32[]{:S(2)}) collective-permute-start(bf16[64,1024]{1,0:T(8,128)(2,1)S(1)} %get-tuple-element.40), channel_id=1, source_target_pairs={{0,1},{1,0},{2,3},{3,2},{4,5},{5,4},{6,7},{7,6},{8,9},{9,8},{10,11... | collective-permute-start | bytes 393224 | tf_op jit(solution)/shard_map/ppermute | solution.py:199
  62.9 2.3 %collective-permute-done.5.refs_2_ = bf16[64,1024]{1,0:T(8,128)(2,1)S(1)} collective-permute-done((bf16[64,1024]{1,0:T(8,128)(2,1)S(1)}, bf16[64,1024]{1,0:T(8,128)(2,1)S(1)}, u32[]{:S(2)}, u32[]{:S(2)}) %collective-permute-start.5) | collective-permute-done | bytes 131104 | tf_op jit(solution)/shard_map/ppermute | solution.py:199
  66.8 2.8 %collective-permute-start.10 = (bf16[64,1280]{1,0:T(8,128)(2,1)S(1)}, bf16[64,1280]{1,0:T(8,128)(2,1)S(1)}, u32[]{:S(2)}, u32[]{:S(2)}) collective-permute-start(bf16[64,1280]{1,0:T(8,128)(2,1)S(1)} %get-tuple-element.45), channel_id=1, source_target_pairs={{0,3},{1,2},{2,1},{3,0},{4,7},{5,6},{6,5},{7,4},{8,11},{9,10},{10,... | collective-permute-start | bytes 491528 | tf_op jit(solution)/shard_map/ppermute | solution.py:199
  69.7 2.9 %collective-permute-start.11 = (bf16[64,1280]{1,0:T(8,128)(2,1)S(1)}, bf16[64,1280]{1,0:T(8,128)(2,1)S(1)}, u32[]{:S(2)}, u32[]{:S(2)}) collective-permute-start(bf16[64,1280]{1,0:T(8,128)(2,1)S(1)} %get-tuple-element.46), channel_id=1, source_target_pairs={{0,2},{1,3},{2,0},{3,1},{4,6},{5,7},{6,4},{7,5},{8,10},{9,11},{10,... | collective-permute-start | bytes 491528 | tf_op jit(solution)/shard_map/ppermute | solution.py:199
  72.6 2.1 %collective-permute-start.12 = (bf16[64,1280]{1,0:T(8,128)(2,1)S(1)}, bf16[64,1280]{1,0:T(8,128)(2,1)S(1)}, u32[]{:S(2)}, u32[]{:S(2)}) collective-permute-start(bf16[64,1280]{1,0:T(8,128)(2,1)S(1)} %get-tuple-element.47), channel_id=1, source_target_pairs={{0,1},{1,0},{2,3},{3,2},{4,5},{5,4},{6,7},{7,6},{8,9},{9,8},{10,11... | collective-permute-start | bytes 491528 | tf_op jit(solution)/shard_map/ppermute | solution.py:199
  75.3 3.5 %collective-permute-done.11.refs_2_ = bf16[64,1280]{1,0:T(8,128)(2,1)S(1)} collective-permute-done((bf16[64,1280]{1,0:T(8,128)(2,1)S(1)}, bf16[64,1280]{1,0:T(8,128)(2,1)S(1)}, u32[]{:S(2)}, u32[]{:S(2)}) %collective-permute-start.11) | collective-permute-done | bytes 163872 | tf_op jit(solution)/shard_map/ppermute | solution.py:199
  80.2 2.1 %collective-permute-start.13 = (bf16[64,4096]{1,0:T(8,128)(2,1)S(1)}, bf16[64,4096]{1,0:T(8,128)(2,1)S(1)}, u32[]{:S(2)}, u32[]{:S(2)}) collective-permute-start(bf16[64,4096]{1,0:T(8,128)(2,1)S(1)} %get-tuple-element.49), channel_id=1, source_target_pairs={{4,8},{8,4},{12,16},{16,12},{20,24},{24,20},{28,32},{32,28},{36,40... | collective-permute-start | bytes 1572872 | tf_op jit(solution)/shard_map/ppermute | solution.py:227
  82.2 1.9 %collective-permute-start.14 = (bf16[64,4096]{1,0:T(8,128)(2,1)S(1)}, bf16[64,4096]{1,0:T(8,128)(2,1)S(1)}, u32[]{:S(2)}, u32[]{:S(2)}) collective-permute-start(bf16[64,4096]{1,0:T(8,128)(2,1)S(1)} %get-tuple-element.50), channel_id=1, source_target_pairs={{0,4},{4,0},{8,12},{12,8},{16,20},{20,16},{24,28},{28,24},{32,36},... | collective-permute-start | bytes 1572872 | tf_op jit(solution)/shard_map/ppermute | solution.py:224
  84.2 1.9 %collective-permute-start.15 = (f32[64,256]{1,0:T(8,128)S(1)}, f32[64,256]{1,0:T(8,128)S(1)}, u32[]{:S(2)}, u32[]{:S(2)}) collective-permute-start(f32[64,256]{1,0:T(8,128)S(1)} %convert_add_fusion), channel_id=1, source_target_pairs={{0,256},{256,0},{1,257},{257,1},{2,258},{258,2},{3,259},{259,3},{4... | collective-permute-start | bytes 196616 | tf_op jit(solution)/shard_map/ppermute | solution.py:210
  86.1 16.5 %collective-permute-done.15 = f32[64,256]{1,0:T(8,128)S(1)} collective-permute-done((f32[64,256]{1,0:T(8,128)S(1)}, f32[64,256]{1,0:T(8,128)S(1)}, u32[]{:S(2)}, u32[]{:S(2)}) %collective-permute-start.15) | collective-permute-done | bytes 65568 | tf_op jit(solution)/shard_map/ppermute | solution.py:210
  102.7 1.9 %collective-permute-start.16 = (f32[64,256]{1,0:T(8,128)S(1)}, f32[64,256]{1,0:T(8,128)S(1)}, u32[]{:S(2)}, u32[]{:S(2)}) collective-permute-start(f32[64,256]{1,0:T(8,128)S(1)} %add.34), channel_id=1, source_target_pairs={{0,16},{16,0},{32,48},{48,32},{64,80},{80,64},{96,112},{112,96},{1... | collective-permute-start | bytes 196616 | tf_op jit(solution)/shard_map/ppermute | solution.py:210
  104.6 3.1 %collective-permute-done.16 = f32[64,256]{1,0:T(8,128)S(1)} collective-permute-done((f32[64,256]{1,0:T(8,128)S(1)}, f32[64,256]{1,0:T(8,128)S(1)}, u32[]{:S(2)}, u32[]{:S(2)}) %collective-permute-start.16) | collective-permute-done | bytes 65568 | tf_op jit(solution)/shard_map/ppermute | solution.py:210
  109.6 4.0 %collective-permute-start.18 = (bf16[64,1024]{1,0:T(8,128)(2,1)S(1)}, bf16[64,1024]{1,0:T(8,128)(2,1)S(1)}, u32[]{:S(2)}, u32[]{:S(2)}) collective-permute-start(bf16[64,1024]{1,0:T(8,128)(2,1)S(1)} %get-tuple-element.54), channel_id=1, source_target_pairs={{0,3},{1,2},{2,1},{3,0},{4,7},{5,6},{6,5},{7,4},{8,11},{9,10},{10,... | collective-permute-start | bytes 393224 | tf_op jit(solution)/shard_map/ppermute | solution.py:199
  113.7 3.0 %collective-permute-start.19 = (bf16[64,1024]{1,0:T(8,128)(2,1)S(1)}, bf16[64,1024]{1,0:T(8,128)(2,1)S(1)}, u32[]{:S(2)}, u32[]{:S(2)}) collective-permute-start(bf16[64,1024]{1,0:T(8,128)(2,1)S(1)} %get-tuple-element.55), channel_id=1, source_target_pairs={{0,2},{1,3},{2,0},{3,1},{4,6},{5,7},{6,4},{7,5},{8,10},{9,11},{10,... | collective-permute-start | bytes 393224 | tf_op jit(solution)/shard_map/ppermute | solution.py:199
  116.6 2.0 %collective-permute-start.20 = (bf16[64,1024]{1,0:T(8,128)(2,1)S(1)}, bf16[64,1024]{1,0:T(8,128)(2,1)S(1)}, u32[]{:S(2)}, u32[]{:S(2)}) collective-permute-start(bf16[64,1024]{1,0:T(8,128)(2,1)S(1)} %get-tuple-element.56), channel_id=1, source_target_pairs={{0,1},{1,0},{2,3},{3,2},{4,5},{5,4},{6,7},{7,6},{8,9},{9,8},{10,11... | collective-permute-start | bytes 393224 | tf_op jit(solution)/shard_map/ppermute | solution.py:199
  121.9 1.9 %collective-permute-start.21 = (bf16[64,4096]{1,0:T(8,128)(2,1)S(1)}, bf16[64,4096]{1,0:T(8,128)(2,1)S(1)}, u32[]{:S(2)}, u32[]{:S(2)}) collective-permute-start(bf16[64,4096]{1,0:T(8,128)(2,1)S(1)} %shard_map.101), channel_id=1, source_target_pairs={{0,4},{4,0},{8,12},{12,8},{16,20},{20,16},{24,28},{28,24},{32,36},... | collective-permute-start | bytes 1572872 | tf_op jit(solution)/shard_map/ppermute | solution.py:224
  123.8 2.6 %collective-permute-start.22 = (bf16[64,4096]{1,0:T(8,128)(2,1)S(1)}, bf16[64,4096]{1,0:T(8,128)(2,1)S(1)}, u32[]{:S(2)}, u32[]{:S(2)}) collective-permute-start(bf16[64,4096]{1,0:T(8,128)(2,1)S(1)} %shard_map.100), channel_id=1, source_target_pairs={{4,8},{8,4},{12,16},{16,12},{20,24},{24,20},{28,32},{32,28},{36,40... | collective-permute-start | bytes 1572872 | tf_op jit(solution)/shard_map/ppermute | solution.py:227
  126.4 1.9 %collective-permute-start.25 = (f32[64,256]{1,0:T(8,128)S(1)}, f32[64,256]{1,0:T(8,128)S(1)}, u32[]{:S(2)}, u32[]{:S(2)}) collective-permute-start(f32[64,256]{1,0:T(8,128)S(1)} %add.36), channel_id=1, source_target_pairs={{0,128},{16,144},{32,160},{48,176},{64,192},{80,208},{96,224},{112... | collective-permute-start | bytes 196616 | tf_op jit(solution)/shard_map/ppermute | solution.py:210
  128.3 2.1 %collective-permute-start.24 = (f32[64,256]{1,0:T(8,128)S(1)}, f32[64,256]{1,0:T(8,128)S(1)}, u32[]{:S(2)}, u32[]{:S(2)}) collective-permute-start(f32[64,256]{1,0:T(8,128)S(1)} %add.36), channel_id=1, source_target_pairs={{0,192},{16,208},{32,224},{48,240},{64,128},{80,144},{96,160},{112... | collective-permute-start | bytes 196616 | tf_op jit(solution)/shard_map/ppermute | solution.py:210
  130.4 12.2 %collective-permute-start.23 = (f32[64,256]{1,0:T(8,128)S(1)}, f32[64,256]{1,0:T(8,128)S(1)}, u32[]{:S(2)}, u32[]{:S(2)}) collective-permute-start(f32[64,256]{1,0:T(8,128)S(1)} %add.36), channel_id=1, source_target_pairs={{0,64},{16,80},{32,96},{48,112},{64,0},{80,16},{96,32},{112,48},{1... | collective-permute-start | bytes 196616 | tf_op jit(solution)/shard_map/ppermute | solution.py:210
  146.2 8.0 %collective-permute-done.22.from_odd = bf16[64,4096]{1,0:T(8,128)(2,1)S(1)} collective-permute-done((bf16[64,4096]{1,0:T(8,128)(2,1)S(1)}, bf16[64,4096]{1,0:T(8,128)(2,1)S(1)}, u32[]{:S(2)}, u32[]{:S(2)}) %collective-permute-start.22) | collective-permute-done | bytes 524320 | tf_op jit(solution)/shard_map/ppermute | solution.py:227
  154.2 2.0 %shard_map.102 = (bf16[64,4096]{1,0:T(8,128)(2,1)}, bf16[64,4096]{1,0:T(8,128)(2,1)}) custom-call(bf16[88,128,128]{2,1,0:T(8,128)(2,1)S(1)} %copy-done.1, s32[88]{0:T(128)S(1)} %copy-done.5, s32[88]{0:T(128)S(1)} %copy-done.6, s32[1]{0:T(128)S(6)} %copy.10.count, s32[2]{0:T(128)S(1)} %pad_add_fusion.place, bf16[4,64,1024]{2,1,0:T(8,128)(2,1)S(1)} %get-tuple-element.48.grad, ...), custom_call_target="tpu_custom_call" | custom-call | flops 37748736 | bytes 6030028 | tf_op jit(solution)/shard_map/pallas_call | solution.py:183
  156.2 7.9 %all_to_all.5 = f32[4,64,256]{2,1,0:T(8,128)S(1)} all-to-all(f32[4,64,256]{2,1,0:T(8,128)S(1)} %broadcast_in_dim.3), channel_id=1, replica_groups=mesh['yh'=2,'z'=16,'x'=4,'yl'=2,'core'=2] {'x'}, dimensions={0} | all-to-all | bytes 524288 | tf_op jit(solution)/shard_map/all_to_all | solution.py:205
  (53 shorter events, 25.3 us)
Async XLA Ops:
  0.6 22.4 %collective-permute-start.1 = (bf16[64,4096]{1,0:T(8,128)(2,1)}, bf16[64,4096]{1,0:T(8,128)(2,1)S(1)}, u32[]{:S(2)}, u32[]{:S(2)}) collective-permute-start(bf16[64,4096]{1,0:T(8,128)(2,1)} %bitcast.9), channel_id=1, source_target_pairs={{0,4},{4,0},{8,12},{12,8},{16,20},{20,16},{24,28},{28,24},{32,36},... | collective-permute-start | bytes 1572872 | tf_op jit(solution)/shard_map/ppermute | solution.py:224
  4.6 33.4 %collective-permute-start = (bf16[64,4096]{1,0:T(8,128)(2,1)}, bf16[64,4096]{1,0:T(8,128)(2,1)S(1)}, u32[]{:S(2)}, u32[]{:S(2)}) collective-permute-start(bf16[64,4096]{1,0:T(8,128)(2,1)} %bitcast.10), channel_id=1, source_target_pairs={{4,8},{8,4},{12,16},{16,12},{20,24},{24,20},{28,32},{32,28},{36,40... | collective-permute-start | bytes 1572872 | tf_op jit(solution)/shard_map/ppermute | solution.py:227
  20.6 1.0 copy-start.3
  21.7 0.8 copy-start.4
  23.0 26.9 %collective-permute-start.3 = (bf16[64,4096]{1,0:T(8,128)(2,1)S(1)}, bf16[64,4096]{1,0:T(8,128)(2,1)S(1)}, u32[]{:S(2)}, u32[]{:S(2)}) collective-permute-start(bf16[64,4096]{1,0:T(8,128)(2,1)S(1)} %collective-permute-done.1.even), channel_id=1, source_target_pairs={{4,8},{8,4},{12,16},{16,12},{20,24},{24,20},{28,32},{32,28},{36,40... | collective-permute-start | bytes 1572872 | tf_op jit(solution)/shard_map/ppermute | solution.py:227
  32.3 1.8 %copy-start = (bf16[88,128,128]{2,1,0:T(8,128)(2,1)S(1)}, bf16[88,128,128]{2,1,0:T(8,128)(2,1)}, u32[]{:S(2)}) copy-start(bf16[88,128,128]{2,1,0:T(8,128)(2,1)} %values.13) | copy-start | bytes 8650756
  34.1 1.0 copy-start.2
  35.2 0.7 copy-start.5
  38.0 13.5 %collective-permute-start.2 = (bf16[64,4096]{1,0:T(8,128)(2,1)S(1)}, bf16[64,4096]{1,0:T(8,128)(2,1)S(1)}, u32[]{:S(2)}, u32[]{:S(2)}) collective-permute-start(bf16[64,4096]{1,0:T(8,128)(2,1)S(1)} %collective-permute-done.odd), channel_id=1, source_target_pairs={{0,4},{4,0},{8,12},{12,8},{16,20},{20,16},{24,28},{28,24},{32,36},... | collective-permute-start | bytes 1572872 | tf_op jit(solution)/shard_map/ppermute | solution.py:224
  39.9 21.0 %collective-permute-start.7 = (bf16[64,1280]{1,0:T(8,128)(2,1)S(1)}, bf16[64,1280]{1,0:T(8,128)(2,1)S(1)}, u32[]{:S(2)}, u32[]{:S(2)}) collective-permute-start(bf16[64,1280]{1,0:T(8,128)(2,1)S(1)} %get-tuple-element.41), channel_id=1, source_target_pairs={{0,3},{1,2},{2,1},{3,0},{4,7},{5,6},{6,5},{7,4},{8,11},{9,10},{10,... | collective-permute-start | bytes 491528 | tf_op jit(solution)/shard_map/ppermute | solution.py:199
  43.9 19.0 %collective-permute-start.8 = (bf16[64,1280]{1,0:T(8,128)(2,1)S(1)}, bf16[64,1280]{1,0:T(8,128)(2,1)S(1)}, u32[]{:S(2)}, u32[]{:S(2)}) collective-permute-start(bf16[64,1280]{1,0:T(8,128)(2,1)S(1)} %get-tuple-element.42), channel_id=1, source_target_pairs={{0,2},{1,3},{2,0},{3,1},{4,6},{5,7},{6,4},{7,5},{8,10},{9,11},{10,... | collective-permute-start | bytes 491528 | tf_op jit(solution)/shard_map/ppermute | solution.py:199
  46.9 16.0 %collective-permute-start.9 = (bf16[64,1280]{1,0:T(8,128)(2,1)S(1)}, bf16[64,1280]{1,0:T(8,128)(2,1)S(1)}, u32[]{:S(2)}, u32[]{:S(2)}) collective-permute-start(bf16[64,1280]{1,0:T(8,128)(2,1)S(1)} %get-tuple-element.43), channel_id=1, source_target_pairs={{0,1},{1,0},{2,3},{3,2},{4,5},{5,4},{6,7},{7,6},{8,9},{9,8},{10,11... | collective-permute-start | bytes 491528 | tf_op jit(solution)/shard_map/ppermute | solution.py:199
  49.9 28.9 %copy-start.1 = (bf16[88,128,128]{2,1,0:T(8,128)(2,1)S(1)}, bf16[88,128,128]{2,1,0:T(8,128)(2,1)}, u32[]{:S(2)}) copy-start(bf16[88,128,128]{2,1,0:T(8,128)(2,1)} %values.13) | copy-start | bytes 8650756
  53.0 9.9 %collective-permute-start.4 = (bf16[64,1024]{1,0:T(8,128)(2,1)S(1)}, bf16[64,1024]{1,0:T(8,128)(2,1)S(1)}, u32[]{:S(2)}, u32[]{:S(2)}) collective-permute-start(bf16[64,1024]{1,0:T(8,128)(2,1)S(1)} %get-tuple-element.38), channel_id=1, source_target_pairs={{0,3},{1,2},{2,1},{3,0},{4,7},{5,6},{6,5},{7,4},{8,11},{9,10},{10,... | collective-permute-start | bytes 393224 | tf_op jit(solution)/shard_map/ppermute | solution.py:199
  58.0 7.2 %collective-permute-start.5 = (bf16[64,1024]{1,0:T(8,128)(2,1)S(1)}, bf16[64,1024]{1,0:T(8,128)(2,1)S(1)}, u32[]{:S(2)}, u32[]{:S(2)}) collective-permute-start(bf16[64,1024]{1,0:T(8,128)(2,1)S(1)} %get-tuple-element.39), channel_id=1, source_target_pairs={{0,2},{1,3},{2,0},{3,1},{4,6},{5,7},{6,4},{7,5},{8,10},{9,11},{10,... | collective-permute-start | bytes 393224 | tf_op jit(solution)/shard_map/ppermute | solution.py:199
  61.0 4.2 %collective-permute-start.6 = (bf16[64,1024]{1,0:T(8,128)(2,1)S(1)}, bf16[64,1024]{1,0:T(8,128)(2,1)S(1)}, u32[]{:S(2)}, u32[]{:S(2)}) collective-permute-start(bf16[64,1024]{1,0:T(8,128)(2,1)S(1)} %get-tuple-element.40), channel_id=1, source_target_pairs={{0,1},{1,0},{2,3},{3,2},{4,5},{5,4},{6,7},{7,6},{8,9},{9,8},{10,11... | collective-permute-start | bytes 393224 | tf_op jit(solution)/shard_map/ppermute | solution.py:199
  66.8 8.5 %collective-permute-start.10 = (bf16[64,1280]{1,0:T(8,128)(2,1)S(1)}, bf16[64,1280]{1,0:T(8,128)(2,1)S(1)}, u32[]{:S(2)}, u32[]{:S(2)}) collective-permute-start(bf16[64,1280]{1,0:T(8,128)(2,1)S(1)} %get-tuple-element.45), channel_id=1, source_target_pairs={{0,3},{1,2},{2,1},{3,0},{4,7},{5,6},{6,5},{7,4},{8,11},{9,10},{10,... | collective-permute-start | bytes 491528 | tf_op jit(solution)/shard_map/ppermute | solution.py:199
  69.7 9.1 %collective-permute-start.11 = (bf16[64,1280]{1,0:T(8,128)(2,1)S(1)}, bf16[64,1280]{1,0:T(8,128)(2,1)S(1)}, u32[]{:S(2)}, u32[]{:S(2)}) collective-permute-start(bf16[64,1280]{1,0:T(8,128)(2,1)S(1)} %get-tuple-element.46), channel_id=1, source_target_pairs={{0,2},{1,3},{2,0},{3,1},{4,6},{5,7},{6,4},{7,5},{8,10},{9,11},{10,... | collective-permute-start | bytes 491528 | tf_op jit(solution)/shard_map/ppermute | solution.py:199
  72.6 6.2 %collective-permute-start.12 = (bf16[64,1280]{1,0:T(8,128)(2,1)S(1)}, bf16[64,1280]{1,0:T(8,128)(2,1)S(1)}, u32[]{:S(2)}, u32[]{:S(2)}) collective-permute-start(bf16[64,1280]{1,0:T(8,128)(2,1)S(1)} %get-tuple-element.47), channel_id=1, source_target_pairs={{0,1},{1,0},{2,3},{3,2},{4,5},{5,4},{6,7},{7,6},{8,9},{9,8},{10,11... | collective-permute-start | bytes 491528 | tf_op jit(solution)/shard_map/ppermute | solution.py:199
  80.2 40.8 %collective-permute-start.13 = (bf16[64,4096]{1,0:T(8,128)(2,1)S(1)}, bf16[64,4096]{1,0:T(8,128)(2,1)S(1)}, u32[]{:S(2)}, u32[]{:S(2)}) collective-permute-start(bf16[64,4096]{1,0:T(8,128)(2,1)S(1)} %get-tuple-element.49), channel_id=1, source_target_pairs={{4,8},{8,4},{12,16},{16,12},{20,24},{24,20},{28,32},{32,28},{36,40... | collective-permute-start | bytes 1572872 | tf_op jit(solution)/shard_map/ppermute | solution.py:227
  82.2 36.4 %collective-permute-start.14 = (bf16[64,4096]{1,0:T(8,128)(2,1)S(1)}, bf16[64,4096]{1,0:T(8,128)(2,1)S(1)}, u32[]{:S(2)}, u32[]{:S(2)}) collective-permute-start(bf16[64,4096]{1,0:T(8,128)(2,1)S(1)} %get-tuple-element.50), channel_id=1, source_target_pairs={{0,4},{4,0},{8,12},{12,8},{16,20},{20,16},{24,28},{28,24},{32,36},... | collective-permute-start | bytes 1572872 | tf_op jit(solution)/shard_map/ppermute | solution.py:224
  84.2 18.5 %collective-permute-start.15 = (f32[64,256]{1,0:T(8,128)S(1)}, f32[64,256]{1,0:T(8,128)S(1)}, u32[]{:S(2)}, u32[]{:S(2)}) collective-permute-start(f32[64,256]{1,0:T(8,128)S(1)} %convert_add_fusion), channel_id=1, source_target_pairs={{0,256},{256,0},{1,257},{257,1},{2,258},{258,2},{3,259},{259,3},{4... | collective-permute-start | bytes 196616 | tf_op jit(solution)/shard_map/ppermute | solution.py:210
  102.7 5.0 %collective-permute-start.16 = (f32[64,256]{1,0:T(8,128)S(1)}, f32[64,256]{1,0:T(8,128)S(1)}, u32[]{:S(2)}, u32[]{:S(2)}) collective-permute-start(f32[64,256]{1,0:T(8,128)S(1)} %add.34), channel_id=1, source_target_pairs={{0,16},{16,0},{32,48},{48,32},{64,80},{80,64},{96,112},{112,96},{1... | collective-permute-start | bytes 196616 | tf_op jit(solution)/shard_map/ppermute | solution.py:210
  107.7 8.9 %collective-permute-start.17 = (f32[64,256]{1,0:T(8,128)S(1)}, f32[64,256]{1,0:T(8,128)S(1)}, u32[]{:S(2)}, u32[]{:S(2)}) collective-permute-start(f32[64,256]{1,0:T(8,128)S(1)} %add.35), channel_id=1, source_target_pairs={{0,32},{16,48},{32,0},{48,16},{64,96},{80,112},{96,64},{112,80},{1... | collective-permute-start | bytes 196616 | tf_op jit(solution)/shard_map/ppermute | solution.py:210
  109.6 10.0 %collective-permute-start.18 = (bf16[64,1024]{1,0:T(8,128)(2,1)S(1)}, bf16[64,1024]{1,0:T(8,128)(2,1)S(1)}, u32[]{:S(2)}, u32[]{:S(2)}) collective-permute-start(bf16[64,1024]{1,0:T(8,128)(2,1)S(1)} %get-tuple-element.54), channel_id=1, source_target_pairs={{0,3},{1,2},{2,1},{3,0},{4,7},{5,6},{6,5},{7,4},{8,11},{9,10},{10,... | collective-permute-start | bytes 393224 | tf_op jit(solution)/shard_map/ppermute | solution.py:199
  113.7 7.2 %collective-permute-start.19 = (bf16[64,1024]{1,0:T(8,128)(2,1)S(1)}, bf16[64,1024]{1,0:T(8,128)(2,1)S(1)}, u32[]{:S(2)}, u32[]{:S(2)}) collective-permute-start(bf16[64,1024]{1,0:T(8,128)(2,1)S(1)} %get-tuple-element.55), channel_id=1, source_target_pairs={{0,2},{1,3},{2,0},{3,1},{4,6},{5,7},{6,4},{7,5},{8,10},{9,11},{10,... | collective-permute-start | bytes 393224 | tf_op jit(solution)/shard_map/ppermute | solution.py:199
  116.6 4.3 %collective-permute-start.20 = (bf16[64,1024]{1,0:T(8,128)(2,1)S(1)}, bf16[64,1024]{1,0:T(8,128)(2,1)S(1)}, u32[]{:S(2)}, u32[]{:S(2)}) collective-permute-start(bf16[64,1024]{1,0:T(8,128)(2,1)S(1)} %get-tuple-element.56), channel_id=1, source_target_pairs={{0,1},{1,0},{2,3},{3,2},{4,5},{5,4},{6,7},{7,6},{8,9},{9,8},{10,11... | collective-permute-start | bytes 393224 | tf_op jit(solution)/shard_map/ppermute | solution.py:199
  121.9 24.3 %collective-permute-start.21 = (bf16[64,4096]{1,0:T(8,128)(2,1)S(1)}, bf16[64,4096]{1,0:T(8,128)(2,1)S(1)}, u32[]{:S(2)}, u32[]{:S(2)}) collective-permute-start(bf16[64,4096]{1,0:T(8,128)(2,1)S(1)} %shard_map.101), channel_id=1, source_target_pairs={{0,4},{4,0},{8,12},{12,8},{16,20},{20,16},{24,28},{28,24},{32,36},... | collective-permute-start | bytes 1572872 | tf_op jit(solution)/shard_map/ppermute | solution.py:224
  123.8 30.4 %collective-permute-start.22 = (bf16[64,4096]{1,0:T(8,128)(2,1)S(1)}, bf16[64,4096]{1,0:T(8,128)(2,1)S(1)}, u32[]{:S(2)}, u32[]{:S(2)}) collective-permute-start(bf16[64,4096]{1,0:T(8,128)(2,1)S(1)} %shard_map.100), channel_id=1, source_target_pairs={{4,8},{8,4},{12,16},{16,12},{20,24},{24,20},{28,32},{32,28},{36,40... | collective-permute-start | bytes 1572872 | tf_op jit(solution)/shard_map/ppermute | solution.py:227
  126.4 16.2 %collective-permute-start.25 = (f32[64,256]{1,0:T(8,128)S(1)}, f32[64,256]{1,0:T(8,128)S(1)}, u32[]{:S(2)}, u32[]{:S(2)}) collective-permute-start(f32[64,256]{1,0:T(8,128)S(1)} %add.36), channel_id=1, source_target_pairs={{0,128},{16,144},{32,160},{48,176},{64,192},{80,208},{96,224},{112... | collective-permute-start | bytes 196616 | tf_op jit(solution)/shard_map/ppermute | solution.py:210
  128.3 16.0 %collective-permute-start.24 = (f32[64,256]{1,0:T(8,128)S(1)}, f32[64,256]{1,0:T(8,128)S(1)}, u32[]{:S(2)}, u32[]{:S(2)}) collective-permute-start(f32[64,256]{1,0:T(8,128)S(1)} %add.36), channel_id=1, source_target_pairs={{0,192},{16,208},{32,224},{48,240},{64,128},{80,144},{96,160},{112... | collective-permute-start | bytes 196616 | tf_op jit(solution)/shard_map/ppermute | solution.py:210
  130.4 15.8 %collective-permute-start.23 = (f32[64,256]{1,0:T(8,128)S(1)}, f32[64,256]{1,0:T(8,128)S(1)}, u32[]{:S(2)}, u32[]{:S(2)}) collective-permute-start(f32[64,256]{1,0:T(8,128)S(1)} %add.36), channel_id=1, source_target_pairs={{0,64},{16,80},{32,96},{48,112},{64,0},{80,16},{96,32},{112,48},{1... | collective-permute-start | bytes 196616 | tf_op jit(solution)/shard_map/ppermute | solution.py:210
  (1 other events, 0.7 us)

commit v8 on v6

--- a/solution.py
+++ b/solution.py
@@ -311,12 +311,12 @@
     even_in, _ = lax.optimization_barrier((even_in, weight_grad))
     odd_near = near_terms(1, 2, even_in)
     odd_last = odd_swap(odd_near)
-    odd_in, _ = lax.optimization_barrier((odd_in, odd_near))
+    output = swapped(output)
+    odd_in, *_ = lax.optimization_barrier((odd_in, odd_near, *output))
     even_near = near_terms(3, -2, odd_in)
     even_last = even_swap(even_near)
     moved = paired(weight_grad, "yh", 1)
-    moved, _, *output = lax.optimization_barrier((moved, even_near, *output))
-    output = swapped(output)
+    moved, _ = lax.optimization_barrier((moved, even_near))
     weight_grad = weight_grad + moved
     moved = [paired(weight_grad, "z", step) for step in (4, 12, 8)]
     weight_grad = weight_grad + moved[0] + moved[1] + moved[2]

time: 166 us -> 164 us (0.988)
  waiting for transfers between devices: 35.5 us -> 28.9 us
  starting transfers between devices: 101 us -> 106 us
    ppermute x4, waiting for transfers between devices: 4.77 us -> 0.01 us  [odd_swap(): return lax.ppermute(value, ROWS, odd_pairs)]
    ppermute x4, starting transfers between devices: 34.1 us -> 37.7 us  [odd_swap(): return lax.ppermute(value, ROWS, odd_pairs)]
    ppermute x6, waiting for transfers between devices: 20.3 us -> 16.8 us  [paired(): lax.ppermute(value, axis, [(source, source ^ step) for source in range(co...]
where the time goes in v8:
time: 164 us; the launch traced here: 163 us
  starting transfers between devices  106 us (65%)
  waiting for transfers between devices  28.9 us (18%)
  Pallas kernels  11.6 us (7%)
  blocking collectives  7.92 us (5%)
  local copies, waits for them, and re-layouts  5.98 us (4%)
  between operations  1.7 us (1%)
    ppermute x4, starting transfers between devices, odd_swap(): return lax.ppermute(value, ROWS, odd_pairs)  37.7 us
    ppermute x12, starting transfers between devices, swapped(): lax.ppermute(value, COLS, pairs(step))  36.3 us
    ppermute x6, starting transfers between devices, paired(): lax.ppermute(value, axis, [(source, source ^ step) for source in range(co...  22.1 us
    ppermute x6, waiting for transfers between devices, paired(): lax.ppermute(value, axis, [(source, source ^ step) for source in range(co...  16.8 us
    pallas_call x9, Pallas kernels, call(): pl.pallas_call(kernel, out_shape=outs, in_specs=specs, out_specs=[VMEM] *...  11.6 us
    ppermute x12, waiting for transfers between devices, swapped(): lax.ppermute(value, COLS, pairs(step))  10.5 us
    ppermute x4, starting transfers between devices, even_swap(): return lax.ppermute(value, ROWS, even_pairs)  9.72 us
    all_to_all x1, blocking collectives, summed(): return lax.all_to_all(copies, axis, 0, 0, tiled=True).sum(0)  7.92 us
  transfers between devices with their start and end apart: 26, of which 9 were waited for; matrix products, arithmetic and copies ran while one was open for 0% of the time, Pallas kernels for 3%

profile of v8, /device:TPU:1, one launch (start us, length us, event | category | flops | bytes accessed | tf_op | source)
XLA Modules:
  0.0 162.7 jit_solution(7092290249709843766)
XLA Ops:
  0.6 4.0 %collective-permute-start.1 = (bf16[64,4096]{1,0:T(8,128)(2,1)}, bf16[64,4096]{1,0:T(8,128)(2,1)S(1)}, u32[]{:S(2)}, u32[]{:S(2)}) collective-permute-start(bf16[64,4096]{1,0:T(8,128)(2,1)} %bitcast.9), channel_id=1, source_target_pairs={{0,4},{4,0},{8,12},{12,8},{16,20},{20,16},{24,28},{28,24},{32,36},... | collective-permute-start | bytes 1572872 | tf_op jit(solution)/shard_map/ppermute | solution.py:224
  4.6 15.3 %collective-permute-start = (bf16[64,4096]{1,0:T(8,128)(2,1)}, bf16[64,4096]{1,0:T(8,128)(2,1)S(1)}, u32[]{:S(2)}, u32[]{:S(2)}) collective-permute-start(bf16[64,4096]{1,0:T(8,128)(2,1)} %bitcast.10), channel_id=1, source_target_pairs={{4,8},{8,4},{12,16},{16,12},{20,24},{24,20},{28,32},{32,28},{36,40... | collective-permute-start | bytes 1572872 | tf_op jit(solution)/shard_map/ppermute | solution.py:227
  23.0 9.3 %collective-permute-start.3 = (bf16[64,4096]{1,0:T(8,128)(2,1)S(1)}, bf16[64,4096]{1,0:T(8,128)(2,1)S(1)}, u32[]{:S(2)}, u32[]{:S(2)}) collective-permute-start(bf16[64,4096]{1,0:T(8,128)(2,1)S(1)} %collective-permute-done.1.even), channel_id=1, source_target_pairs={{4,8},{8,4},{12,16},{16,12},{20,24},{24,20},{28,32},{32,28},{36,40... | collective-permute-start | bytes 1572872 | tf_op jit(solution)/shard_map/ppermute | solution.py:227
  38.0 1.9 %collective-permute-start.2 = (bf16[64,4096]{1,0:T(8,128)(2,1)S(1)}, bf16[64,4096]{1,0:T(8,128)(2,1)S(1)}, u32[]{:S(2)}, u32[]{:S(2)}) collective-permute-start(bf16[64,4096]{1,0:T(8,128)(2,1)S(1)} %collective-permute-done.odd), channel_id=1, source_target_pairs={{0,4},{4,0},{8,12},{12,8},{16,20},{20,16},{24,28},{28,24},{32,36},... | collective-permute-start | bytes 1572872 | tf_op jit(solution)/shard_map/ppermute | solution.py:224
  39.9 4.0 %collective-permute-start.7 = (bf16[64,1280]{1,0:T(8,128)(2,1)S(1)}, bf16[64,1280]{1,0:T(8,128)(2,1)S(1)}, u32[]{:S(2)}, u32[]{:S(2)}) collective-permute-start(bf16[64,1280]{1,0:T(8,128)(2,1)S(1)} %get-tuple-element.41), channel_id=1, source_target_pairs={{0,3},{1,2},{2,1},{3,0},{4,7},{5,6},{6,5},{7,4},{8,11},{9,10},{10,... | collective-permute-start | bytes 491528 | tf_op jit(solution)/shard_map/ppermute | solution.py:199
  43.9 3.0 %collective-permute-start.8 = (bf16[64,1280]{1,0:T(8,128)(2,1)S(1)}, bf16[64,1280]{1,0:T(8,128)(2,1)S(1)}, u32[]{:S(2)}, u32[]{:S(2)}) collective-permute-start(bf16[64,1280]{1,0:T(8,128)(2,1)S(1)} %get-tuple-element.42), channel_id=1, source_target_pairs={{0,2},{1,3},{2,0},{3,1},{4,6},{5,7},{6,4},{7,5},{8,10},{9,11},{10,... | collective-permute-start | bytes 491528 | tf_op jit(solution)/shard_map/ppermute | solution.py:199
  46.9 1.9 %collective-permute-start.9 = (bf16[64,1280]{1,0:T(8,128)(2,1)S(1)}, bf16[64,1280]{1,0:T(8,128)(2,1)S(1)}, u32[]{:S(2)}, u32[]{:S(2)}) collective-permute-start(bf16[64,1280]{1,0:T(8,128)(2,1)S(1)} %get-tuple-element.43), channel_id=1, source_target_pairs={{0,1},{1,0},{2,3},{3,2},{4,5},{5,4},{6,7},{7,6},{8,9},{9,8},{10,11... | collective-permute-start | bytes 491528 | tf_op jit(solution)/shard_map/ppermute | solution.py:199
  53.0 4.9 %collective-permute-start.4 = (bf16[64,1024]{1,0:T(8,128)(2,1)S(1)}, bf16[64,1024]{1,0:T(8,128)(2,1)S(1)}, u32[]{:S(2)}, u32[]{:S(2)}) collective-permute-start(bf16[64,1024]{1,0:T(8,128)(2,1)S(1)} %get-tuple-element.38), channel_id=1, source_target_pairs={{0,3},{1,2},{2,1},{3,0},{4,7},{5,6},{6,5},{7,4},{8,11},{9,10},{10,... | collective-permute-start | bytes 393224 | tf_op jit(solution)/shard_map/ppermute | solution.py:199
  58.0 3.0 %collective-permute-start.5 = (bf16[64,1024]{1,0:T(8,128)(2,1)S(1)}, bf16[64,1024]{1,0:T(8,128)(2,1)S(1)}, u32[]{:S(2)}, u32[]{:S(2)}) collective-permute-start(bf16[64,1024]{1,0:T(8,128)(2,1)S(1)} %get-tuple-element.39), channel_id=1, source_target_pairs={{0,2},{1,3},{2,0},{3,1},{4,6},{5,7},{6,4},{7,5},{8,10},{9,11},{10,... | collective-permute-start | bytes 393224 | tf_op jit(solution)/shard_map/ppermute | solution.py:199
  60.9 1.9 %collective-permute-start.6 = (bf16[64,1024]{1,0:T(8,128)(2,1)S(1)}, bf16[64,1024]{1,0:T(8,128)(2,1)S(1)}, u32[]{:S(2)}, u32[]{:S(2)}) collective-permute-start(bf16[64,1024]{1,0:T(8,128)(2,1)S(1)} %get-tuple-element.40), channel_id=1, source_target_pairs={{0,1},{1,0},{2,3},{3,2},{4,5},{5,4},{6,7},{7,6},{8,9},{9,8},{10,11... | collective-permute-start | bytes 393224 | tf_op jit(solution)/shard_map/ppermute | solution.py:199
  62.9 2.3 %collective-permute-done.5.refs_2_ = bf16[64,1024]{1,0:T(8,128)(2,1)S(1)} collective-permute-done((bf16[64,1024]{1,0:T(8,128)(2,1)S(1)}, bf16[64,1024]{1,0:T(8,128)(2,1)S(1)}, u32[]{:S(2)}, u32[]{:S(2)}) %collective-permute-start.5) | collective-permute-done | bytes 131104 | tf_op jit(solution)/shard_map/ppermute | solution.py:199
  66.8 2.8 %collective-permute-start.10 = (bf16[64,1280]{1,0:T(8,128)(2,1)S(1)}, bf16[64,1280]{1,0:T(8,128)(2,1)S(1)}, u32[]{:S(2)}, u32[]{:S(2)}) collective-permute-start(bf16[64,1280]{1,0:T(8,128)(2,1)S(1)} %get-tuple-element.45), channel_id=1, source_target_pairs={{0,3},{1,2},{2,1},{3,0},{4,7},{5,6},{6,5},{7,4},{8,11},{9,10},{10,... | collective-permute-start | bytes 491528 | tf_op jit(solution)/shard_map/ppermute | solution.py:199
  69.6 2.9 %collective-permute-start.11 = (bf16[64,1280]{1,0:T(8,128)(2,1)S(1)}, bf16[64,1280]{1,0:T(8,128)(2,1)S(1)}, u32[]{:S(2)}, u32[]{:S(2)}) collective-permute-start(bf16[64,1280]{1,0:T(8,128)(2,1)S(1)} %get-tuple-element.46), channel_id=1, source_target_pairs={{0,2},{1,3},{2,0},{3,1},{4,6},{5,7},{6,4},{7,5},{8,10},{9,11},{10,... | collective-permute-start | bytes 491528 | tf_op jit(solution)/shard_map/ppermute | solution.py:199
  72.6 2.1 %collective-permute-start.12 = (bf16[64,1280]{1,0:T(8,128)(2,1)S(1)}, bf16[64,1280]{1,0:T(8,128)(2,1)S(1)}, u32[]{:S(2)}, u32[]{:S(2)}) collective-permute-start(bf16[64,1280]{1,0:T(8,128)(2,1)S(1)} %get-tuple-element.47), channel_id=1, source_target_pairs={{0,1},{1,0},{2,3},{3,2},{4,5},{5,4},{6,7},{7,6},{8,9},{9,8},{10,11... | collective-permute-start | bytes 491528 | tf_op jit(solution)/shard_map/ppermute | solution.py:199
  75.3 3.5 %collective-permute-done.11.refs_2_ = bf16[64,1280]{1,0:T(8,128)(2,1)S(1)} collective-permute-done((bf16[64,1280]{1,0:T(8,128)(2,1)S(1)}, bf16[64,1280]{1,0:T(8,128)(2,1)S(1)}, u32[]{:S(2)}, u32[]{:S(2)}) %collective-permute-start.11) | collective-permute-done | bytes 163872 | tf_op jit(solution)/shard_map/ppermute | solution.py:199
  80.2 1.9 %collective-permute-start.14 = (bf16[64,4096]{1,0:T(8,128)(2,1)S(1)}, bf16[64,4096]{1,0:T(8,128)(2,1)S(1)}, u32[]{:S(2)}, u32[]{:S(2)}) collective-permute-start(bf16[64,4096]{1,0:T(8,128)(2,1)S(1)} %get-tuple-element.50), channel_id=1, source_target_pairs={{0,4},{4,0},{8,12},{12,8},{16,20},{20,16},{24,28},{28,24},{32,36},... | collective-permute-start | bytes 1572872 | tf_op jit(solution)/shard_map/ppermute | solution.py:224
  82.1 2.6 %collective-permute-start.13 = (bf16[64,4096]{1,0:T(8,128)(2,1)S(1)}, bf16[64,4096]{1,0:T(8,128)(2,1)S(1)}, u32[]{:S(2)}, u32[]{:S(2)}) collective-permute-start(bf16[64,4096]{1,0:T(8,128)(2,1)S(1)} %get-tuple-element.49), channel_id=1, source_target_pairs={{4,8},{8,4},{12,16},{16,12},{20,24},{24,20},{28,32},{32,28},{36,40... | collective-permute-start | bytes 1572872 | tf_op jit(solution)/shard_map/ppermute | solution.py:227
  84.7 1.9 %collective-permute-start.15 = (f32[64,256]{1,0:T(8,128)S(1)}, f32[64,256]{1,0:T(8,128)S(1)}, u32[]{:S(2)}, u32[]{:S(2)}) collective-permute-start(f32[64,256]{1,0:T(8,128)S(1)} %convert_add_fusion), channel_id=1, source_target_pairs={{0,16},{16,0},{32,48},{48,32},{64,80},{80,64},{96,112},{112,96},{1... | collective-permute-start | bytes 196616 | tf_op jit(solution)/shard_map/ppermute | solution.py:210
  86.6 3.4 %collective-permute-done.15 = f32[64,256]{1,0:T(8,128)S(1)} collective-permute-done((f32[64,256]{1,0:T(8,128)S(1)}, f32[64,256]{1,0:T(8,128)S(1)}, u32[]{:S(2)}, u32[]{:S(2)}) %collective-permute-start.15) | collective-permute-done | bytes 65568 | tf_op jit(solution)/shard_map/ppermute | solution.py:210
  90.0 2.1 %collective-permute-start.16 = (f32[64,256]{1,0:T(8,128)S(1)}, f32[64,256]{1,0:T(8,128)S(1)}, u32[]{:S(2)}, u32[]{:S(2)}) collective-permute-start(f32[64,256]{1,0:T(8,128)S(1)} %add.34), channel_id=1, source_target_pairs={{0,32},{16,48},{32,0},{48,16},{64,96},{80,112},{96,64},{112,80},{1... | collective-permute-start | bytes 196616 | tf_op jit(solution)/shard_map/ppermute | solution.py:210
  92.1 5.4 %collective-permute-start.17 = (bf16[64,1024]{1,0:T(8,128)(2,1)S(1)}, bf16[64,1024]{1,0:T(8,128)(2,1)S(1)}, u32[]{:S(2)}, u32[]{:S(2)}) collective-permute-start(bf16[64,1024]{1,0:T(8,128)(2,1)S(1)} %get-tuple-element.54), channel_id=1, source_target_pairs={{0,3},{1,2},{2,1},{3,0},{4,7},{5,6},{6,5},{7,4},{8,11},{9,10},{10,... | collective-permute-start | bytes 393224 | tf_op jit(solution)/shard_map/ppermute | solution.py:199
  97.5 2.0 %collective-permute-start.18 = (bf16[64,1024]{1,0:T(8,128)(2,1)S(1)}, bf16[64,1024]{1,0:T(8,128)(2,1)S(1)}, u32[]{:S(2)}, u32[]{:S(2)}) collective-permute-start(bf16[64,1024]{1,0:T(8,128)(2,1)S(1)} %get-tuple-element.55), channel_id=1, source_target_pairs={{0,2},{1,3},{2,0},{3,1},{4,6},{5,7},{6,4},{7,5},{8,10},{9,11},{10,... | collective-permute-start | bytes 393224 | tf_op jit(solution)/shard_map/ppermute | solution.py:199
  99.6 2.2 %collective-permute-start.19 = (bf16[64,1024]{1,0:T(8,128)(2,1)S(1)}, bf16[64,1024]{1,0:T(8,128)(2,1)S(1)}, u32[]{:S(2)}, u32[]{:S(2)}) collective-permute-start(bf16[64,1024]{1,0:T(8,128)(2,1)S(1)} %get-tuple-element.56), channel_id=1, source_target_pairs={{0,1},{1,0},{2,3},{3,2},{4,5},{5,4},{6,7},{7,6},{8,9},{9,8},{10,11... | collective-permute-start | bytes 393224 | tf_op jit(solution)/shard_map/ppermute | solution.py:199
  104.1 2.8 %collective-permute-done.18.refs_2_ = bf16[64,1024]{1,0:T(8,128)(2,1)S(1)} collective-permute-done((bf16[64,1024]{1,0:T(8,128)(2,1)S(1)}, bf16[64,1024]{1,0:T(8,128)(2,1)S(1)}, u32[]{:S(2)}, u32[]{:S(2)}) %collective-permute-start.18) | collective-permute-done | bytes 131104 | tf_op jit(solution)/shard_map/ppermute | solution.py:199
  107.9 1.9 %collective-permute-start.20 = (bf16[64,4096]{1,0:T(8,128)(2,1)S(1)}, bf16[64,4096]{1,0:T(8,128)(2,1)S(1)}, u32[]{:S(2)}, u32[]{:S(2)}) collective-permute-start(bf16[64,4096]{1,0:T(8,128)(2,1)S(1)} %shard_map.101), channel_id=1, source_target_pairs={{0,4},{4,0},{8,12},{12,8},{16,20},{20,16},{24,28},{28,24},{32,36},... | collective-permute-start | bytes 1572872 | tf_op jit(solution)/shard_map/ppermute | solution.py:224
  109.8 10.6 %collective-permute-start.21 = (bf16[64,4096]{1,0:T(8,128)(2,1)S(1)}, bf16[64,4096]{1,0:T(8,128)(2,1)S(1)}, u32[]{:S(2)}, u32[]{:S(2)}) collective-permute-start(bf16[64,4096]{1,0:T(8,128)(2,1)S(1)} %shard_map.100), channel_id=1, source_target_pairs={{4,8},{8,4},{12,16},{16,12},{20,24},{24,20},{28,32},{32,28},{36,40... | collective-permute-start | bytes 1572872 | tf_op jit(solution)/shard_map/ppermute | solution.py:227
  120.4 1.9 %collective-permute-start.22 = (f32[64,256]{1,0:T(8,128)S(1)}, f32[64,256]{1,0:T(8,128)S(1)}, u32[]{:S(2)}, u32[]{:S(2)}) collective-permute-start(f32[64,256]{1,0:T(8,128)S(1)} %add.35), channel_id=1, source_target_pairs={{0,256},{256,0},{1,257},{257,1},{2,258},{258,2},{3,259},{259,3},{4... | collective-permute-start | bytes 196616 | tf_op jit(solution)/shard_map/ppermute | solution.py:210
  122.3 11.8 %collective-permute-done.22 = f32[64,256]{1,0:T(8,128)S(1)} collective-permute-done((f32[64,256]{1,0:T(8,128)S(1)}, f32[64,256]{1,0:T(8,128)S(1)}, u32[]{:S(2)}, u32[]{:S(2)}) %collective-permute-start.22) | collective-permute-done | bytes 65568 | tf_op jit(solution)/shard_map/ppermute | solution.py:210
  134.2 1.9 %collective-permute-start.25 = (f32[64,256]{1,0:T(8,128)S(1)}, f32[64,256]{1,0:T(8,128)S(1)}, u32[]{:S(2)}, u32[]{:S(2)}) collective-permute-start(f32[64,256]{1,0:T(8,128)S(1)} %add.36), channel_id=1, source_target_pairs={{0,128},{16,144},{32,160},{48,176},{64,192},{80,208},{96,224},{112... | collective-permute-start | bytes 196616 | tf_op jit(solution)/shard_map/ppermute | solution.py:210
  138.1 12.3 %collective-permute-start.23 = (f32[64,256]{1,0:T(8,128)S(1)}, f32[64,256]{1,0:T(8,128)S(1)}, u32[]{:S(2)}, u32[]{:S(2)}) collective-permute-start(f32[64,256]{1,0:T(8,128)S(1)} %add.36), channel_id=1, source_target_pairs={{0,64},{16,80},{32,96},{48,112},{64,0},{80,16},{96,32},{112,48},{1... | collective-permute-start | bytes 196616 | tf_op jit(solution)/shard_map/ppermute | solution.py:210
  152.1 2.0 %shard_map.102 = (bf16[64,4096]{1,0:T(8,128)(2,1)}, bf16[64,4096]{1,0:T(8,128)(2,1)}) custom-call(bf16[88,128,128]{2,1,0:T(8,128)(2,1)S(1)} %copy-done.1, s32[88]{0:T(128)S(1)} %copy-done.5, s32[88]{0:T(128)S(1)} %copy-done.6, s32[1]{0:T(128)S(6)} %copy.10.count, s32[2]{0:T(128)S(1)} %pad_add_fusion.place, bf16[4,64,1024]{2,1,0:T(8,128)(2,1)S(1)} %get-tuple-element.48.grad, ...), custom_call_target="tpu_custom_call" | custom-call | flops 37748736 | bytes 6030028 | tf_op jit(solution)/shard_map/pallas_call | solution.py:183
  154.1 7.9 %all_to_all.5 = f32[4,64,256]{2,1,0:T(8,128)S(1)} all-to-all(f32[4,64,256]{2,1,0:T(8,128)S(1)} %broadcast_in_dim.3), channel_id=1, replica_groups=mesh['yh'=2,'z'=16,'x'=4,'yl'=2,'core'=2] {'x'}, dimensions={0} | all-to-all | bytes 524288 | tf_op jit(solution)/shard_map/all_to_all | solution.py:205
  (53 shorter events, 23.4 us)
Async XLA Ops:
  0.6 22.4 %collective-permute-start.1 = (bf16[64,4096]{1,0:T(8,128)(2,1)}, bf16[64,4096]{1,0:T(8,128)(2,1)S(1)}, u32[]{:S(2)}, u32[]{:S(2)}) collective-permute-start(bf16[64,4096]{1,0:T(8,128)(2,1)} %bitcast.9), channel_id=1, source_target_pairs={{0,4},{4,0},{8,12},{12,8},{16,20},{20,16},{24,28},{28,24},{32,36},... | collective-permute-start | bytes 1572872 | tf_op jit(solution)/shard_map/ppermute | solution.py:224
  4.6 33.4 %collective-permute-start = (bf16[64,4096]{1,0:T(8,128)(2,1)}, bf16[64,4096]{1,0:T(8,128)(2,1)S(1)}, u32[]{:S(2)}, u32[]{:S(2)}) collective-permute-start(bf16[64,4096]{1,0:T(8,128)(2,1)} %bitcast.10), channel_id=1, source_target_pairs={{4,8},{8,4},{12,16},{16,12},{20,24},{24,20},{28,32},{32,28},{36,40... | collective-permute-start | bytes 1572872 | tf_op jit(solution)/shard_map/ppermute | solution.py:227
  20.6 1.0 copy-start.3
  21.7 0.8 copy-start.4
  23.0 26.9 %collective-permute-start.3 = (bf16[64,4096]{1,0:T(8,128)(2,1)S(1)}, bf16[64,4096]{1,0:T(8,128)(2,1)S(1)}, u32[]{:S(2)}, u32[]{:S(2)}) collective-permute-start(bf16[64,4096]{1,0:T(8,128)(2,1)S(1)} %collective-permute-done.1.even), channel_id=1, source_target_pairs={{4,8},{8,4},{12,16},{16,12},{20,24},{24,20},{28,32},{32,28},{36,40... | collective-permute-start | bytes 1572872 | tf_op jit(solution)/shard_map/ppermute | solution.py:227
  32.3 1.8 %copy-start = (bf16[88,128,128]{2,1,0:T(8,128)(2,1)S(1)}, bf16[88,128,128]{2,1,0:T(8,128)(2,1)}, u32[]{:S(2)}) copy-start(bf16[88,128,128]{2,1,0:T(8,128)(2,1)} %values.13) | copy-start | bytes 8650756
  34.1 1.0 copy-start.2
  35.2 0.7 copy-start.5
  38.0 13.5 %collective-permute-start.2 = (bf16[64,4096]{1,0:T(8,128)(2,1)S(1)}, bf16[64,4096]{1,0:T(8,128)(2,1)S(1)}, u32[]{:S(2)}, u32[]{:S(2)}) collective-permute-start(bf16[64,4096]{1,0:T(8,128)(2,1)S(1)} %collective-permute-done.odd), channel_id=1, source_target_pairs={{0,4},{4,0},{8,12},{12,8},{16,20},{20,16},{24,28},{28,24},{32,36},... | collective-permute-start | bytes 1572872 | tf_op jit(solution)/shard_map/ppermute | solution.py:224
  39.9 21.0 %collective-permute-start.7 = (bf16[64,1280]{1,0:T(8,128)(2,1)S(1)}, bf16[64,1280]{1,0:T(8,128)(2,1)S(1)}, u32[]{:S(2)}, u32[]{:S(2)}) collective-permute-start(bf16[64,1280]{1,0:T(8,128)(2,1)S(1)} %get-tuple-element.41), channel_id=1, source_target_pairs={{0,3},{1,2},{2,1},{3,0},{4,7},{5,6},{6,5},{7,4},{8,11},{9,10},{10,... | collective-permute-start | bytes 491528 | tf_op jit(solution)/shard_map/ppermute | solution.py:199
  43.9 19.0 %collective-permute-start.8 = (bf16[64,1280]{1,0:T(8,128)(2,1)S(1)}, bf16[64,1280]{1,0:T(8,128)(2,1)S(1)}, u32[]{:S(2)}, u32[]{:S(2)}) collective-permute-start(bf16[64,1280]{1,0:T(8,128)(2,1)S(1)} %get-tuple-element.42), channel_id=1, source_target_pairs={{0,2},{1,3},{2,0},{3,1},{4,6},{5,7},{6,4},{7,5},{8,10},{9,11},{10,... | collective-permute-start | bytes 491528 | tf_op jit(solution)/shard_map/ppermute | solution.py:199
  46.9 16.0 %collective-permute-start.9 = (bf16[64,1280]{1,0:T(8,128)(2,1)S(1)}, bf16[64,1280]{1,0:T(8,128)(2,1)S(1)}, u32[]{:S(2)}, u32[]{:S(2)}) collective-permute-start(bf16[64,1280]{1,0:T(8,128)(2,1)S(1)} %get-tuple-element.43), channel_id=1, source_target_pairs={{0,1},{1,0},{2,3},{3,2},{4,5},{5,4},{6,7},{7,6},{8,9},{9,8},{10,11... | collective-permute-start | bytes 491528 | tf_op jit(solution)/shard_map/ppermute | solution.py:199
  49.9 28.9 %copy-start.1 = (bf16[88,128,128]{2,1,0:T(8,128)(2,1)S(1)}, bf16[88,128,128]{2,1,0:T(8,128)(2,1)}, u32[]{:S(2)}) copy-start(bf16[88,128,128]{2,1,0:T(8,128)(2,1)} %values.13) | copy-start | bytes 8650756
  53.0 9.9 %collective-permute-start.4 = (bf16[64,1024]{1,0:T(8,128)(2,1)S(1)}, bf16[64,1024]{1,0:T(8,128)(2,1)S(1)}, u32[]{:S(2)}, u32[]{:S(2)}) collective-permute-start(bf16[64,1024]{1,0:T(8,128)(2,1)S(1)} %get-tuple-element.38), channel_id=1, source_target_pairs={{0,3},{1,2},{2,1},{3,0},{4,7},{5,6},{6,5},{7,4},{8,11},{9,10},{10,... | collective-permute-start | bytes 393224 | tf_op jit(solution)/shard_map/ppermute | solution.py:199
  58.0 7.2 %collective-permute-start.5 = (bf16[64,1024]{1,0:T(8,128)(2,1)S(1)}, bf16[64,1024]{1,0:T(8,128)(2,1)S(1)}, u32[]{:S(2)}, u32[]{:S(2)}) collective-permute-start(bf16[64,1024]{1,0:T(8,128)(2,1)S(1)} %get-tuple-element.39), channel_id=1, source_target_pairs={{0,2},{1,3},{2,0},{3,1},{4,6},{5,7},{6,4},{7,5},{8,10},{9,11},{10,... | collective-permute-start | bytes 393224 | tf_op jit(solution)/shard_map/ppermute | solution.py:199
  60.9 4.2 %collective-permute-start.6 = (bf16[64,1024]{1,0:T(8,128)(2,1)S(1)}, bf16[64,1024]{1,0:T(8,128)(2,1)S(1)}, u32[]{:S(2)}, u32[]{:S(2)}) collective-permute-start(bf16[64,1024]{1,0:T(8,128)(2,1)S(1)} %get-tuple-element.40), channel_id=1, source_target_pairs={{0,1},{1,0},{2,3},{3,2},{4,5},{5,4},{6,7},{7,6},{8,9},{9,8},{10,11... | collective-permute-start | bytes 393224 | tf_op jit(solution)/shard_map/ppermute | solution.py:199
  66.8 8.5 %collective-permute-start.10 = (bf16[64,1280]{1,0:T(8,128)(2,1)S(1)}, bf16[64,1280]{1,0:T(8,128)(2,1)S(1)}, u32[]{:S(2)}, u32[]{:S(2)}) collective-permute-start(bf16[64,1280]{1,0:T(8,128)(2,1)S(1)} %get-tuple-element.45), channel_id=1, source_target_pairs={{0,3},{1,2},{2,1},{3,0},{4,7},{5,6},{6,5},{7,4},{8,11},{9,10},{10,... | collective-permute-start | bytes 491528 | tf_op jit(solution)/shard_map/ppermute | solution.py:199
  69.6 9.1 %collective-permute-start.11 = (bf16[64,1280]{1,0:T(8,128)(2,1)S(1)}, bf16[64,1280]{1,0:T(8,128)(2,1)S(1)}, u32[]{:S(2)}, u32[]{:S(2)}) collective-permute-start(bf16[64,1280]{1,0:T(8,128)(2,1)S(1)} %get-tuple-element.46), channel_id=1, source_target_pairs={{0,2},{1,3},{2,0},{3,1},{4,6},{5,7},{6,4},{7,5},{8,10},{9,11},{10,... | collective-permute-start | bytes 491528 | tf_op jit(solution)/shard_map/ppermute | solution.py:199
  72.6 6.2 %collective-permute-start.12 = (bf16[64,1280]{1,0:T(8,128)(2,1)S(1)}, bf16[64,1280]{1,0:T(8,128)(2,1)S(1)}, u32[]{:S(2)}, u32[]{:S(2)}) collective-permute-start(bf16[64,1280]{1,0:T(8,128)(2,1)S(1)} %get-tuple-element.47), channel_id=1, source_target_pairs={{0,1},{1,0},{2,3},{3,2},{4,5},{5,4},{6,7},{7,6},{8,9},{9,8},{10,11... | collective-permute-start | bytes 491528 | tf_op jit(solution)/shard_map/ppermute | solution.py:199
  80.2 21.6 %collective-permute-start.14 = (bf16[64,4096]{1,0:T(8,128)(2,1)S(1)}, bf16[64,4096]{1,0:T(8,128)(2,1)S(1)}, u32[]{:S(2)}, u32[]{:S(2)}) collective-permute-start(bf16[64,4096]{1,0:T(8,128)(2,1)S(1)} %get-tuple-element.50), channel_id=1, source_target_pairs={{0,4},{4,0},{8,12},{12,8},{16,20},{20,16},{24,28},{28,24},{32,36},... | collective-permute-start | bytes 1572872 | tf_op jit(solution)/shard_map/ppermute | solution.py:224
  82.1 24.8 %collective-permute-start.13 = (bf16[64,4096]{1,0:T(8,128)(2,1)S(1)}, bf16[64,4096]{1,0:T(8,128)(2,1)S(1)}, u32[]{:S(2)}, u32[]{:S(2)}) collective-permute-start(bf16[64,4096]{1,0:T(8,128)(2,1)S(1)} %get-tuple-element.49), channel_id=1, source_target_pairs={{4,8},{8,4},{12,16},{16,12},{20,24},{24,20},{28,32},{32,28},{36,40... | collective-permute-start | bytes 1572872 | tf_op jit(solution)/shard_map/ppermute | solution.py:227
  84.7 5.3 %collective-permute-start.15 = (f32[64,256]{1,0:T(8,128)S(1)}, f32[64,256]{1,0:T(8,128)S(1)}, u32[]{:S(2)}, u32[]{:S(2)}) collective-permute-start(f32[64,256]{1,0:T(8,128)S(1)} %convert_add_fusion), channel_id=1, source_target_pairs={{0,16},{16,0},{32,48},{48,32},{64,80},{80,64},{96,112},{112,96},{1... | collective-permute-start | bytes 196616 | tf_op jit(solution)/shard_map/ppermute | solution.py:210
  90.0 9.5 %collective-permute-start.16 = (f32[64,256]{1,0:T(8,128)S(1)}, f32[64,256]{1,0:T(8,128)S(1)}, u32[]{:S(2)}, u32[]{:S(2)}) collective-permute-start(f32[64,256]{1,0:T(8,128)S(1)} %add.34), channel_id=1, source_target_pairs={{0,32},{16,48},{32,0},{48,16},{64,96},{80,112},{96,64},{112,80},{1... | collective-permute-start | bytes 196616 | tf_op jit(solution)/shard_map/ppermute | solution.py:210
  92.1 12.0 %collective-permute-start.17 = (bf16[64,1024]{1,0:T(8,128)(2,1)S(1)}, bf16[64,1024]{1,0:T(8,128)(2,1)S(1)}, u32[]{:S(2)}, u32[]{:S(2)}) collective-permute-start(bf16[64,1024]{1,0:T(8,128)(2,1)S(1)} %get-tuple-element.54), channel_id=1, source_target_pairs={{0,3},{1,2},{2,1},{3,0},{4,7},{5,6},{6,5},{7,4},{8,11},{9,10},{10,... | collective-permute-start | bytes 393224 | tf_op jit(solution)/shard_map/ppermute | solution.py:199
  97.5 9.4 %collective-permute-start.18 = (bf16[64,1024]{1,0:T(8,128)(2,1)S(1)}, bf16[64,1024]{1,0:T(8,128)(2,1)S(1)}, u32[]{:S(2)}, u32[]{:S(2)}) collective-permute-start(bf16[64,1024]{1,0:T(8,128)(2,1)S(1)} %get-tuple-element.55), channel_id=1, source_target_pairs={{0,2},{1,3},{2,0},{3,1},{4,6},{5,7},{6,4},{7,5},{8,10},{9,11},{10,... | collective-permute-start | bytes 393224 | tf_op jit(solution)/shard_map/ppermute | solution.py:199
  99.6 7.4 %collective-permute-start.19 = (bf16[64,1024]{1,0:T(8,128)(2,1)S(1)}, bf16[64,1024]{1,0:T(8,128)(2,1)S(1)}, u32[]{:S(2)}, u32[]{:S(2)}) collective-permute-start(bf16[64,1024]{1,0:T(8,128)(2,1)S(1)} %get-tuple-element.56), channel_id=1, source_target_pairs={{0,1},{1,0},{2,3},{3,2},{4,5},{5,4},{6,7},{7,6},{8,9},{9,8},{10,11... | collective-permute-start | bytes 393224 | tf_op jit(solution)/shard_map/ppermute | solution.py:199
  107.9 44.2 %collective-permute-start.20 = (bf16[64,4096]{1,0:T(8,128)(2,1)S(1)}, bf16[64,4096]{1,0:T(8,128)(2,1)S(1)}, u32[]{:S(2)}, u32[]{:S(2)}) collective-permute-start(bf16[64,4096]{1,0:T(8,128)(2,1)S(1)} %shard_map.101), channel_id=1, source_target_pairs={{0,4},{4,0},{8,12},{12,8},{16,20},{20,16},{24,28},{28,24},{32,36},... | collective-permute-start | bytes 1572872 | tf_op jit(solution)/shard_map/ppermute | solution.py:224
  109.8 42.3 %collective-permute-start.21 = (bf16[64,4096]{1,0:T(8,128)(2,1)S(1)}, bf16[64,4096]{1,0:T(8,128)(2,1)S(1)}, u32[]{:S(2)}, u32[]{:S(2)}) collective-permute-start(bf16[64,4096]{1,0:T(8,128)(2,1)S(1)} %shard_map.100), channel_id=1, source_target_pairs={{4,8},{8,4},{12,16},{16,12},{20,24},{24,20},{28,32},{32,28},{36,40... | collective-permute-start | bytes 1572872 | tf_op jit(solution)/shard_map/ppermute | solution.py:227
  120.4 13.8 %collective-permute-start.22 = (f32[64,256]{1,0:T(8,128)S(1)}, f32[64,256]{1,0:T(8,128)S(1)}, u32[]{:S(2)}, u32[]{:S(2)}) collective-permute-start(f32[64,256]{1,0:T(8,128)S(1)} %add.35), channel_id=1, source_target_pairs={{0,256},{256,0},{1,257},{257,1},{2,258},{258,2},{3,259},{259,3},{4... | collective-permute-start | bytes 196616 | tf_op jit(solution)/shard_map/ppermute | solution.py:210
  134.2 16.2 %collective-permute-start.25 = (f32[64,256]{1,0:T(8,128)S(1)}, f32[64,256]{1,0:T(8,128)S(1)}, u32[]{:S(2)}, u32[]{:S(2)}) collective-permute-start(f32[64,256]{1,0:T(8,128)S(1)} %add.36), channel_id=1, source_target_pairs={{0,128},{16,144},{32,160},{48,176},{64,192},{80,208},{96,224},{112... | collective-permute-start | bytes 196616 | tf_op jit(solution)/shard_map/ppermute | solution.py:210
  136.1 14.3 %collective-permute-start.24 = (f32[64,256]{1,0:T(8,128)S(1)}, f32[64,256]{1,0:T(8,128)S(1)}, u32[]{:S(2)}, u32[]{:S(2)}) collective-permute-start(f32[64,256]{1,0:T(8,128)S(1)} %add.36), channel_id=1, source_target_pairs={{0,192},{16,208},{32,224},{48,240},{64,128},{80,144},{96,160},{112... | collective-permute-start | bytes 196616 | tf_op jit(solution)/shard_map/ppermute | solution.py:210
  138.1 14.0 %collective-permute-start.23 = (f32[64,256]{1,0:T(8,128)S(1)}, f32[64,256]{1,0:T(8,128)S(1)}, u32[]{:S(2)}, u32[]{:S(2)}) collective-permute-start(f32[64,256]{1,0:T(8,128)S(1)} %add.36), channel_id=1, source_target_pairs={{0,64},{16,80},{32,96},{48,112},{64,0},{80,16},{96,32},{112,48},{1... | collective-permute-start | bytes 196616 | tf_op jit(solution)/shard_map/ppermute | solution.py:210
  (1 other events, 0.7 us)

commit v9 on v8

--- a/solution.py
+++ b/solution.py
@@ -201,8 +201,8 @@
 
 
 def summed(value, axis):
-    copies = jnp.broadcast_to(value, (lax.axis_size(axis), *value.shape))
-    return lax.all_to_all(copies, axis, 0, 0, tiled=True).sum(0)
+    copies = jnp.broadcast_to(value.astype(jnp.bfloat16), (lax.axis_size(axis), *value.shape))
+    return lax.all_to_all(copies, axis, 0, 0, tiled=True).astype(jnp.float32).sum(0)
 
 
 def paired(value, axis, step):
@@ -315,11 +315,9 @@
     odd_in, *_ = lax.optimization_barrier((odd_in, odd_near, *output))
     even_near = near_terms(3, -2, odd_in)
     even_last = even_swap(even_near)
-    moved = paired(weight_grad, "yh", 1)
-    moved, _ = lax.optimization_barrier((moved, even_near))
-    weight_grad = weight_grad + moved
+    weight_grad, _ = lax.optimization_barrier((weight_grad, even_near))
     moved = [paired(weight_grad, "z", step) for step in (4, 12, 8)]
-    weight_grad = weight_grad + moved[0] + moved[1] + moved[2]
+    weight_grad = (weight_grad + moved[2]) + (moved[0] + moved[1])
     feature_grad, output = call(
         spread_own_kernel,
         tables + (grads, even_last, odd_last, *output),
@@ -329,7 +327,7 @@
         flops=18 * tile_flops,
     )
     weight_grad, feature_grad = lax.optimization_barrier((weight_grad, feature_grad))
-    weight_grad = summed(weight_grad, "x")
+    weight_grad = summed(weight_grad, ("yh", "x"))
     weight_grad = (weight_grad * (1.0 / (node_count * n_rows) ** 0.5)).T
     return (output.T, feature_grad.T, weight_grad)
 

time: 164 us -> 159 us (0.970)
  waiting for transfers between devices: 28.9 us -> 21.4 us
  blocking collectives: 7.92 us -> 11.8 us
  starting transfers between devices: 106 us -> 104 us
    ppermute x6 -> x5, waiting for transfers between devices: 16.8 us -> 9.34 us  [paired(): lax.ppermute(value, axis, [(source, source ^ step) for source in range(co...]
    all_to_all x1, blocking collectives: 7.92 us -> 11.8 us  [summed(): lax.all_to_all(copies, axis, 0, 0, tiled=True).astype(jnp.float32).sum(0)]
    ppermute x6 -> x5, starting transfers between devices: 22.1 us -> 20.2 us  [paired(): lax.ppermute(value, axis, [(source, source ^ step) for source in range(co...]
  transfers between devices with their start and end apart: 26 -> 25, of which waited for: 9 -> 8; matrix products, arithmetic and copies ran while one was open for 0% -> 0% of each run, Pallas kernels for 3% -> 4%
where the time goes in v9:
time: 159 us; the launch traced here: 157 us
  starting transfers between devices  104 us (65%)
  waiting for transfers between devices  21.4 us (13%)
  blocking collectives  11.8 us (7%)
  Pallas kernels  11.6 us (7%)
  local copies, waits for them, and re-layouts  5.98 us (4%)
  between operations  1.67 us (1%)
    ppermute x4, starting transfers between devices, odd_swap(): return lax.ppermute(value, ROWS, odd_pairs)  37.7 us
    ppermute x12, starting transfers between devices, swapped(): lax.ppermute(value, COLS, pairs(step))  36.3 us
    ppermute x5, starting transfers between devices, paired(): lax.ppermute(value, axis, [(source, source ^ step) for source in range(co...  20.2 us
    all_to_all x1, blocking collectives, summed(): lax.all_to_all(copies, axis, 0, 0, tiled=True).astype(jnp.float32).sum(0)  11.8 us
    pallas_call x9, Pallas kernels, call(): pl.pallas_call(kernel, out_shape=outs, in_specs=specs, out_specs=[VMEM] *...  11.6 us
    ppermute x12, waiting for transfers between devices, swapped(): lax.ppermute(value, COLS, pairs(step))  10.5 us
    ppermute x4, starting transfers between devices, even_swap(): return lax.ppermute(value, ROWS, even_pairs)  9.71 us
    ppermute x5, waiting for transfers between devices, paired(): lax.ppermute(value, axis, [(source, source ^ step) for source in range(co...  9.34 us
  transfers between devices with their start and end apart: 25, of which 8 were waited for; matrix products, arithmetic and copies ran while one was open for 0% of the time, Pallas kernels for 4%

profile of v9, /device:TPU:1, one launch (start us, length us, event | category | flops | bytes accessed | tf_op | source)
XLA Modules:
  0.0 157.2 jit_solution(10647662521276326781)
XLA Ops:
  0.6 4.0 %collective-permute-start.1 = (bf16[64,4096]{1,0:T(8,128)(2,1)}, bf16[64,4096]{1,0:T(8,128)(2,1)S(1)}, u32[]{:S(2)}, u32[]{:S(2)}) collective-permute-start(bf16[64,4096]{1,0:T(8,128)(2,1)} %bitcast.9), channel_id=1, source_target_pairs={{0,4},{4,0},{8,12},{12,8},{16,20},{20,16},{24,28},{28,24},{32,36},... | collective-permute-start | bytes 1572872 | tf_op jit(solution)/shard_map/ppermute | solution.py:224
  4.6 15.3 %collective-permute-start = (bf16[64,4096]{1,0:T(8,128)(2,1)}, bf16[64,4096]{1,0:T(8,128)(2,1)S(1)}, u32[]{:S(2)}, u32[]{:S(2)}) collective-permute-start(bf16[64,4096]{1,0:T(8,128)(2,1)} %bitcast.10), channel_id=1, source_target_pairs={{4,8},{8,4},{12,16},{16,12},{20,24},{24,20},{28,32},{32,28},{36,40... | collective-permute-start | bytes 1572872 | tf_op jit(solution)/shard_map/ppermute | solution.py:227
  23.0 9.3 %collective-permute-start.3 = (bf16[64,4096]{1,0:T(8,128)(2,1)S(1)}, bf16[64,4096]{1,0:T(8,128)(2,1)S(1)}, u32[]{:S(2)}, u32[]{:S(2)}) collective-permute-start(bf16[64,4096]{1,0:T(8,128)(2,1)S(1)} %collective-permute-done.1.even), channel_id=1, source_target_pairs={{4,8},{8,4},{12,16},{16,12},{20,24},{24,20},{28,32},{32,28},{36,40... | collective-permute-start | bytes 1572872 | tf_op jit(solution)/shard_map/ppermute | solution.py:227
  38.0 1.9 %collective-permute-start.2 = (bf16[64,4096]{1,0:T(8,128)(2,1)S(1)}, bf16[64,4096]{1,0:T(8,128)(2,1)S(1)}, u32[]{:S(2)}, u32[]{:S(2)}) collective-permute-start(bf16[64,4096]{1,0:T(8,128)(2,1)S(1)} %collective-permute-done.odd), channel_id=1, source_target_pairs={{0,4},{4,0},{8,12},{12,8},{16,20},{20,16},{24,28},{28,24},{32,36},... | collective-permute-start | bytes 1572872 | tf_op jit(solution)/shard_map/ppermute | solution.py:224
  39.9 4.0 %collective-permute-start.7 = (bf16[64,1280]{1,0:T(8,128)(2,1)S(1)}, bf16[64,1280]{1,0:T(8,128)(2,1)S(1)}, u32[]{:S(2)}, u32[]{:S(2)}) collective-permute-start(bf16[64,1280]{1,0:T(8,128)(2,1)S(1)} %get-tuple-element.41), channel_id=1, source_target_pairs={{0,3},{1,2},{2,1},{3,0},{4,7},{5,6},{6,5},{7,4},{8,11},{9,10},{10,... | collective-permute-start | bytes 491528 | tf_op jit(solution)/shard_map/ppermute | solution.py:199
  43.9 3.0 %collective-permute-start.8 = (bf16[64,1280]{1,0:T(8,128)(2,1)S(1)}, bf16[64,1280]{1,0:T(8,128)(2,1)S(1)}, u32[]{:S(2)}, u32[]{:S(2)}) collective-permute-start(bf16[64,1280]{1,0:T(8,128)(2,1)S(1)} %get-tuple-element.42), channel_id=1, source_target_pairs={{0,2},{1,3},{2,0},{3,1},{4,6},{5,7},{6,4},{7,5},{8,10},{9,11},{10,... | collective-permute-start | bytes 491528 | tf_op jit(solution)/shard_map/ppermute | solution.py:199
  46.9 1.9 %collective-permute-start.9 = (bf16[64,1280]{1,0:T(8,128)(2,1)S(1)}, bf16[64,1280]{1,0:T(8,128)(2,1)S(1)}, u32[]{:S(2)}, u32[]{:S(2)}) collective-permute-start(bf16[64,1280]{1,0:T(8,128)(2,1)S(1)} %get-tuple-element.43), channel_id=1, source_target_pairs={{0,1},{1,0},{2,3},{3,2},{4,5},{5,4},{6,7},{7,6},{8,9},{9,8},{10,11... | collective-permute-start | bytes 491528 | tf_op jit(solution)/shard_map/ppermute | solution.py:199
  53.0 4.9 %collective-permute-start.4 = (bf16[64,1024]{1,0:T(8,128)(2,1)S(1)}, bf16[64,1024]{1,0:T(8,128)(2,1)S(1)}, u32[]{:S(2)}, u32[]{:S(2)}) collective-permute-start(bf16[64,1024]{1,0:T(8,128)(2,1)S(1)} %get-tuple-element.38), channel_id=1, source_target_pairs={{0,3},{1,2},{2,1},{3,0},{4,7},{5,6},{6,5},{7,4},{8,11},{9,10},{10,... | collective-permute-start | bytes 393224 | tf_op jit(solution)/shard_map/ppermute | solution.py:199
  58.0 3.0 %collective-permute-start.5 = (bf16[64,1024]{1,0:T(8,128)(2,1)S(1)}, bf16[64,1024]{1,0:T(8,128)(2,1)S(1)}, u32[]{:S(2)}, u32[]{:S(2)}) collective-permute-start(bf16[64,1024]{1,0:T(8,128)(2,1)S(1)} %get-tuple-element.39), channel_id=1, source_target_pairs={{0,2},{1,3},{2,0},{3,1},{4,6},{5,7},{6,4},{7,5},{8,10},{9,11},{10,... | collective-permute-start | bytes 393224 | tf_op jit(solution)/shard_map/ppermute | solution.py:199
  61.0 1.9 %collective-permute-start.6 = (bf16[64,1024]{1,0:T(8,128)(2,1)S(1)}, bf16[64,1024]{1,0:T(8,128)(2,1)S(1)}, u32[]{:S(2)}, u32[]{:S(2)}) collective-permute-start(bf16[64,1024]{1,0:T(8,128)(2,1)S(1)} %get-tuple-element.40), channel_id=1, source_target_pairs={{0,1},{1,0},{2,3},{3,2},{4,5},{5,4},{6,7},{7,6},{8,9},{9,8},{10,11... | collective-permute-start | bytes 393224 | tf_op jit(solution)/shard_map/ppermute | solution.py:199
  62.9 2.3 %collective-permute-done.5.refs_2_ = bf16[64,1024]{1,0:T(8,128)(2,1)S(1)} collective-permute-done((bf16[64,1024]{1,0:T(8,128)(2,1)S(1)}, bf16[64,1024]{1,0:T(8,128)(2,1)S(1)}, u32[]{:S(2)}, u32[]{:S(2)}) %collective-permute-start.5) | collective-permute-done | bytes 131104 | tf_op jit(solution)/shard_map/ppermute | solution.py:199
  66.8 2.8 %collective-permute-start.10 = (bf16[64,1280]{1,0:T(8,128)(2,1)S(1)}, bf16[64,1280]{1,0:T(8,128)(2,1)S(1)}, u32[]{:S(2)}, u32[]{:S(2)}) collective-permute-start(bf16[64,1280]{1,0:T(8,128)(2,1)S(1)} %get-tuple-element.45), channel_id=1, source_target_pairs={{0,3},{1,2},{2,1},{3,0},{4,7},{5,6},{6,5},{7,4},{8,11},{9,10},{10,... | collective-permute-start | bytes 491528 | tf_op jit(solution)/shard_map/ppermute | solution.py:199
  69.7 2.9 %collective-permute-start.11 = (bf16[64,1280]{1,0:T(8,128)(2,1)S(1)}, bf16[64,1280]{1,0:T(8,128)(2,1)S(1)}, u32[]{:S(2)}, u32[]{:S(2)}) collective-permute-start(bf16[64,1280]{1,0:T(8,128)(2,1)S(1)} %get-tuple-element.46), channel_id=1, source_target_pairs={{0,2},{1,3},{2,0},{3,1},{4,6},{5,7},{6,4},{7,5},{8,10},{9,11},{10,... | collective-permute-start | bytes 491528 | tf_op jit(solution)/shard_map/ppermute | solution.py:199
  72.6 2.1 %collective-permute-start.12 = (bf16[64,1280]{1,0:T(8,128)(2,1)S(1)}, bf16[64,1280]{1,0:T(8,128)(2,1)S(1)}, u32[]{:S(2)}, u32[]{:S(2)}) collective-permute-start(bf16[64,1280]{1,0:T(8,128)(2,1)S(1)} %get-tuple-element.47), channel_id=1, source_target_pairs={{0,1},{1,0},{2,3},{3,2},{4,5},{5,4},{6,7},{7,6},{8,9},{9,8},{10,11... | collective-permute-start | bytes 491528 | tf_op jit(solution)/shard_map/ppermute | solution.py:199
  75.3 3.5 %collective-permute-done.11.refs_2_ = bf16[64,1280]{1,0:T(8,128)(2,1)S(1)} collective-permute-done((bf16[64,1280]{1,0:T(8,128)(2,1)S(1)}, bf16[64,1280]{1,0:T(8,128)(2,1)S(1)}, u32[]{:S(2)}, u32[]{:S(2)}) %collective-permute-start.11) | collective-permute-done | bytes 163872 | tf_op jit(solution)/shard_map/ppermute | solution.py:199
  80.2 1.9 %collective-permute-start.14 = (bf16[64,4096]{1,0:T(8,128)(2,1)S(1)}, bf16[64,4096]{1,0:T(8,128)(2,1)S(1)}, u32[]{:S(2)}, u32[]{:S(2)}) collective-permute-start(bf16[64,4096]{1,0:T(8,128)(2,1)S(1)} %get-tuple-element.50), channel_id=1, source_target_pairs={{0,4},{4,0},{8,12},{12,8},{16,20},{20,16},{24,28},{28,24},{32,36},... | collective-permute-start | bytes 1572872 | tf_op jit(solution)/shard_map/ppermute | solution.py:224
  82.1 2.6 %collective-permute-start.13 = (bf16[64,4096]{1,0:T(8,128)(2,1)S(1)}, bf16[64,4096]{1,0:T(8,128)(2,1)S(1)}, u32[]{:S(2)}, u32[]{:S(2)}) collective-permute-start(bf16[64,4096]{1,0:T(8,128)(2,1)S(1)} %get-tuple-element.49), channel_id=1, source_target_pairs={{4,8},{8,4},{12,16},{16,12},{20,24},{24,20},{28,32},{32,28},{36,40... | collective-permute-start | bytes 1572872 | tf_op jit(solution)/shard_map/ppermute | solution.py:227
  84.7 1.9 %collective-permute-start.15 = (f32[64,256]{1,0:T(8,128)S(1)}, f32[64,256]{1,0:T(8,128)S(1)}, u32[]{:S(2)}, u32[]{:S(2)}) collective-permute-start(f32[64,256]{1,0:T(8,128)S(1)} %convert_add_fusion), channel_id=1, source_target_pairs={{0,16},{16,0},{32,48},{48,32},{64,80},{80,64},{96,112},{112,96},{1... | collective-permute-start | bytes 196616 | tf_op jit(solution)/shard_map/ppermute | solution.py:210
  86.6 3.4 %collective-permute-done.15 = f32[64,256]{1,0:T(8,128)S(1)} collective-permute-done((f32[64,256]{1,0:T(8,128)S(1)}, f32[64,256]{1,0:T(8,128)S(1)}, u32[]{:S(2)}, u32[]{:S(2)}) %collective-permute-start.15) | collective-permute-done | bytes 65568 | tf_op jit(solution)/shard_map/ppermute | solution.py:210
  90.0 2.1 %collective-permute-start.16 = (f32[64,256]{1,0:T(8,128)S(1)}, f32[64,256]{1,0:T(8,128)S(1)}, u32[]{:S(2)}, u32[]{:S(2)}) collective-permute-start(f32[64,256]{1,0:T(8,128)S(1)} %add.31), channel_id=1, source_target_pairs={{0,32},{16,48},{32,0},{48,16},{64,96},{80,112},{96,64},{112,80},{1... | collective-permute-start | bytes 196616 | tf_op jit(solution)/shard_map/ppermute | solution.py:210
  92.1 5.4 %collective-permute-start.17 = (bf16[64,1024]{1,0:T(8,128)(2,1)S(1)}, bf16[64,1024]{1,0:T(8,128)(2,1)S(1)}, u32[]{:S(2)}, u32[]{:S(2)}) collective-permute-start(bf16[64,1024]{1,0:T(8,128)(2,1)S(1)} %get-tuple-element.54), channel_id=1, source_target_pairs={{0,3},{1,2},{2,1},{3,0},{4,7},{5,6},{6,5},{7,4},{8,11},{9,10},{10,... | collective-permute-start | bytes 393224 | tf_op jit(solution)/shard_map/ppermute | solution.py:199
  97.5 2.0 %collective-permute-start.18 = (bf16[64,1024]{1,0:T(8,128)(2,1)S(1)}, bf16[64,1024]{1,0:T(8,128)(2,1)S(1)}, u32[]{:S(2)}, u32[]{:S(2)}) collective-permute-start(bf16[64,1024]{1,0:T(8,128)(2,1)S(1)} %get-tuple-element.55), channel_id=1, source_target_pairs={{0,2},{1,3},{2,0},{3,1},{4,6},{5,7},{6,4},{7,5},{8,10},{9,11},{10,... | collective-permute-start | bytes 393224 | tf_op jit(solution)/shard_map/ppermute | solution.py:199
  99.6 2.2 %collective-permute-start.19 = (bf16[64,1024]{1,0:T(8,128)(2,1)S(1)}, bf16[64,1024]{1,0:T(8,128)(2,1)S(1)}, u32[]{:S(2)}, u32[]{:S(2)}) collective-permute-start(bf16[64,1024]{1,0:T(8,128)(2,1)S(1)} %get-tuple-element.56), channel_id=1, source_target_pairs={{0,1},{1,0},{2,3},{3,2},{4,5},{5,4},{6,7},{7,6},{8,9},{9,8},{10,11... | collective-permute-start | bytes 393224 | tf_op jit(solution)/shard_map/ppermute | solution.py:199
  104.1 2.8 %collective-permute-done.18.refs_2_ = bf16[64,1024]{1,0:T(8,128)(2,1)S(1)} collective-permute-done((bf16[64,1024]{1,0:T(8,128)(2,1)S(1)}, bf16[64,1024]{1,0:T(8,128)(2,1)S(1)}, u32[]{:S(2)}, u32[]{:S(2)}) %collective-permute-start.18) | collective-permute-done | bytes 131104 | tf_op jit(solution)/shard_map/ppermute | solution.py:199
  107.9 1.9 %collective-permute-start.20 = (bf16[64,4096]{1,0:T(8,128)(2,1)S(1)}, bf16[64,4096]{1,0:T(8,128)(2,1)S(1)}, u32[]{:S(2)}, u32[]{:S(2)}) collective-permute-start(bf16[64,4096]{1,0:T(8,128)(2,1)S(1)} %shard_map.101), channel_id=1, source_target_pairs={{0,4},{4,0},{8,12},{12,8},{16,20},{20,16},{24,28},{28,24},{32,36},... | collective-permute-start | bytes 1572872 | tf_op jit(solution)/shard_map/ppermute | solution.py:224
  109.8 10.6 %collective-permute-start.21 = (bf16[64,4096]{1,0:T(8,128)(2,1)S(1)}, bf16[64,4096]{1,0:T(8,128)(2,1)S(1)}, u32[]{:S(2)}, u32[]{:S(2)}) collective-permute-start(bf16[64,4096]{1,0:T(8,128)(2,1)S(1)} %shard_map.100), channel_id=1, source_target_pairs={{4,8},{8,4},{12,16},{16,12},{20,24},{24,20},{28,32},{32,28},{36,40... | collective-permute-start | bytes 1572872 | tf_op jit(solution)/shard_map/ppermute | solution.py:227
  120.4 2.5 %collective-permute-start.24 = (f32[64,256]{1,0:T(8,128)S(1)}, f32[64,256]{1,0:T(8,128)S(1)}, u32[]{:S(2)}, u32[]{:S(2)}) collective-permute-start(f32[64,256]{1,0:T(8,128)S(1)} %add.32), channel_id=1, source_target_pairs={{0,192},{16,208},{32,224},{48,240},{64,128},{80,144},{96,160},{112... | collective-permute-start | bytes 196616 | tf_op jit(solution)/shard_map/ppermute | solution.py:210
  122.9 1.9 %collective-permute-start.23 = (f32[64,256]{1,0:T(8,128)S(1)}, f32[64,256]{1,0:T(8,128)S(1)}, u32[]{:S(2)}, u32[]{:S(2)}) collective-permute-start(f32[64,256]{1,0:T(8,128)S(1)} %add.32), channel_id=1, source_target_pairs={{0,64},{16,80},{32,96},{48,112},{64,0},{80,16},{96,32},{112,48},{1... | collective-permute-start | bytes 196616 | tf_op jit(solution)/shard_map/ppermute | solution.py:210
  124.8 11.8 %collective-permute-start.22 = (f32[64,256]{1,0:T(8,128)S(1)}, f32[64,256]{1,0:T(8,128)S(1)}, u32[]{:S(2)}, u32[]{:S(2)}) collective-permute-start(f32[64,256]{1,0:T(8,128)S(1)} %add.32), channel_id=1, source_target_pairs={{0,128},{16,144},{32,160},{48,176},{64,192},{80,208},{96,224},{112... | collective-permute-start | bytes 196616 | tf_op jit(solution)/shard_map/ppermute | solution.py:210
  136.6 6.0 %collective-permute-done.24 = f32[64,256]{1,0:T(8,128)S(1)} collective-permute-done((f32[64,256]{1,0:T(8,128)S(1)}, f32[64,256]{1,0:T(8,128)S(1)}, u32[]{:S(2)}, u32[]{:S(2)}) %collective-permute-start.24) | collective-permute-done | bytes 65568 | tf_op jit(solution)/shard_map/ppermute | solution.py:210
  142.6 2.0 %shard_map.102 = (bf16[64,4096]{1,0:T(8,128)(2,1)}, bf16[64,4096]{1,0:T(8,128)(2,1)}) custom-call(bf16[88,128,128]{2,1,0:T(8,128)(2,1)S(1)} %copy-done.1, s32[88]{0:T(128)S(1)} %copy-done.5, s32[88]{0:T(128)S(1)} %copy-done.6, s32[1]{0:T(128)S(6)} %copy.10.count, s32[2]{0:T(128)S(1)} %pad_add_fusion.place, bf16[4,64,1024]{2,1,0:T(8,128)(2,1)S(1)} %get-tuple-element.48.grad, ...), custom_call_target="tpu_custom_call" | custom-call | flops 37748736 | bytes 6030028 | tf_op jit(solution)/shard_map/pallas_call | solution.py:183
  144.7 11.8 %all_to_all.5 = bf16[8,64,256]{2,1,0:T(8,128)(2,1)S(1)} all-to-all(bf16[8,64,256]{2,1,0:T(8,128)(2,1)S(1)} %broadcast_in_dim.3), channel_id=1, replica_groups=mesh['yh'=2,'z'=16,'x'=4,'yl'=2,'core'=2] {'yh','x'}, dimensions={0} | all-to-all | bytes 524288 | tf_op jit(solution)/shard_map/all_to_all | solution.py:205
  (50 shorter events, 19.9 us)
Async XLA Ops:
  0.6 22.4 %collective-permute-start.1 = (bf16[64,4096]{1,0:T(8,128)(2,1)}, bf16[64,4096]{1,0:T(8,128)(2,1)S(1)}, u32[]{:S(2)}, u32[]{:S(2)}) collective-permute-start(bf16[64,4096]{1,0:T(8,128)(2,1)} %bitcast.9), channel_id=1, source_target_pairs={{0,4},{4,0},{8,12},{12,8},{16,20},{20,16},{24,28},{28,24},{32,36},... | collective-permute-start | bytes 1572872 | tf_op jit(solution)/shard_map/ppermute | solution.py:224
  4.6 33.4 %collective-permute-start = (bf16[64,4096]{1,0:T(8,128)(2,1)}, bf16[64,4096]{1,0:T(8,128)(2,1)S(1)}, u32[]{:S(2)}, u32[]{:S(2)}) collective-permute-start(bf16[64,4096]{1,0:T(8,128)(2,1)} %bitcast.10), channel_id=1, source_target_pairs={{4,8},{8,4},{12,16},{16,12},{20,24},{24,20},{28,32},{32,28},{36,40... | collective-permute-start | bytes 1572872 | tf_op jit(solution)/shard_map/ppermute | solution.py:227
  20.6 1.0 copy-start.3
  21.7 0.8 copy-start.4
  23.0 26.9 %collective-permute-start.3 = (bf16[64,4096]{1,0:T(8,128)(2,1)S(1)}, bf16[64,4096]{1,0:T(8,128)(2,1)S(1)}, u32[]{:S(2)}, u32[]{:S(2)}) collective-permute-start(bf16[64,4096]{1,0:T(8,128)(2,1)S(1)} %collective-permute-done.1.even), channel_id=1, source_target_pairs={{4,8},{8,4},{12,16},{16,12},{20,24},{24,20},{28,32},{32,28},{36,40... | collective-permute-start | bytes 1572872 | tf_op jit(solution)/shard_map/ppermute | solution.py:227
  32.3 1.8 %copy-start = (bf16[88,128,128]{2,1,0:T(8,128)(2,1)S(1)}, bf16[88,128,128]{2,1,0:T(8,128)(2,1)}, u32[]{:S(2)}) copy-start(bf16[88,128,128]{2,1,0:T(8,128)(2,1)} %values.13) | copy-start | bytes 8650756
  34.1 1.0 copy-start.2
  35.2 0.7 copy-start.5
  35.8 0.7 copy-start.6
  38.0 13.5 %collective-permute-start.2 = (bf16[64,4096]{1,0:T(8,128)(2,1)S(1)}, bf16[64,4096]{1,0:T(8,128)(2,1)S(1)}, u32[]{:S(2)}, u32[]{:S(2)}) collective-permute-start(bf16[64,4096]{1,0:T(8,128)(2,1)S(1)} %collective-permute-done.odd), channel_id=1, source_target_pairs={{0,4},{4,0},{8,12},{12,8},{16,20},{20,16},{24,28},{28,24},{32,36},... | collective-permute-start | bytes 1572872 | tf_op jit(solution)/shard_map/ppermute | solution.py:224
  39.9 21.0 %collective-permute-start.7 = (bf16[64,1280]{1,0:T(8,128)(2,1)S(1)}, bf16[64,1280]{1,0:T(8,128)(2,1)S(1)}, u32[]{:S(2)}, u32[]{:S(2)}) collective-permute-start(bf16[64,1280]{1,0:T(8,128)(2,1)S(1)} %get-tuple-element.41), channel_id=1, source_target_pairs={{0,3},{1,2},{2,1},{3,0},{4,7},{5,6},{6,5},{7,4},{8,11},{9,10},{10,... | collective-permute-start | bytes 491528 | tf_op jit(solution)/shard_map/ppermute | solution.py:199
  43.9 19.0 %collective-permute-start.8 = (bf16[64,1280]{1,0:T(8,128)(2,1)S(1)}, bf16[64,1280]{1,0:T(8,128)(2,1)S(1)}, u32[]{:S(2)}, u32[]{:S(2)}) collective-permute-start(bf16[64,1280]{1,0:T(8,128)(2,1)S(1)} %get-tuple-element.42), channel_id=1, source_target_pairs={{0,2},{1,3},{2,0},{3,1},{4,6},{5,7},{6,4},{7,5},{8,10},{9,11},{10,... | collective-permute-start | bytes 491528 | tf_op jit(solution)/shard_map/ppermute | solution.py:199
  46.9 16.0 %collective-permute-start.9 = (bf16[64,1280]{1,0:T(8,128)(2,1)S(1)}, bf16[64,1280]{1,0:T(8,128)(2,1)S(1)}, u32[]{:S(2)}, u32[]{:S(2)}) collective-permute-start(bf16[64,1280]{1,0:T(8,128)(2,1)S(1)} %get-tuple-element.43), channel_id=1, source_target_pairs={{0,1},{1,0},{2,3},{3,2},{4,5},{5,4},{6,7},{7,6},{8,9},{9,8},{10,11... | collective-permute-start | bytes 491528 | tf_op jit(solution)/shard_map/ppermute | solution.py:199
  49.9 28.9 %copy-start.1 = (bf16[88,128,128]{2,1,0:T(8,128)(2,1)S(1)}, bf16[88,128,128]{2,1,0:T(8,128)(2,1)}, u32[]{:S(2)}) copy-start(bf16[88,128,128]{2,1,0:T(8,128)(2,1)} %values.13) | copy-start | bytes 8650756
  53.0 9.9 %collective-permute-start.4 = (bf16[64,1024]{1,0:T(8,128)(2,1)S(1)}, bf16[64,1024]{1,0:T(8,128)(2,1)S(1)}, u32[]{:S(2)}, u32[]{:S(2)}) collective-permute-start(bf16[64,1024]{1,0:T(8,128)(2,1)S(1)} %get-tuple-element.38), channel_id=1, source_target_pairs={{0,3},{1,2},{2,1},{3,0},{4,7},{5,6},{6,5},{7,4},{8,11},{9,10},{10,... | collective-permute-start | bytes 393224 | tf_op jit(solution)/shard_map/ppermute | solution.py:199
  58.0 7.2 %collective-permute-start.5 = (bf16[64,1024]{1,0:T(8,128)(2,1)S(1)}, bf16[64,1024]{1,0:T(8,128)(2,1)S(1)}, u32[]{:S(2)}, u32[]{:S(2)}) collective-permute-start(bf16[64,1024]{1,0:T(8,128)(2,1)S(1)} %get-tuple-element.39), channel_id=1, source_target_pairs={{0,2},{1,3},{2,0},{3,1},{4,6},{5,7},{6,4},{7,5},{8,10},{9,11},{10,... | collective-permute-start | bytes 393224 | tf_op jit(solution)/shard_map/ppermute | solution.py:199
  61.0 4.2 %collective-permute-start.6 = (bf16[64,1024]{1,0:T(8,128)(2,1)S(1)}, bf16[64,1024]{1,0:T(8,128)(2,1)S(1)}, u32[]{:S(2)}, u32[]{:S(2)}) collective-permute-start(bf16[64,1024]{1,0:T(8,128)(2,1)S(1)} %get-tuple-element.40), channel_id=1, source_target_pairs={{0,1},{1,0},{2,3},{3,2},{4,5},{5,4},{6,7},{7,6},{8,9},{9,8},{10,11... | collective-permute-start | bytes 393224 | tf_op jit(solution)/shard_map/ppermute | solution.py:199
  66.8 8.5 %collective-permute-start.10 = (bf16[64,1280]{1,0:T(8,128)(2,1)S(1)}, bf16[64,1280]{1,0:T(8,128)(2,1)S(1)}, u32[]{:S(2)}, u32[]{:S(2)}) collective-permute-start(bf16[64,1280]{1,0:T(8,128)(2,1)S(1)} %get-tuple-element.45), channel_id=1, source_target_pairs={{0,3},{1,2},{2,1},{3,0},{4,7},{5,6},{6,5},{7,4},{8,11},{9,10},{10,... | collective-permute-start | bytes 491528 | tf_op jit(solution)/shard_map/ppermute | solution.py:199
  69.7 9.1 %collective-permute-start.11 = (bf16[64,1280]{1,0:T(8,128)(2,1)S(1)}, bf16[64,1280]{1,0:T(8,128)(2,1)S(1)}, u32[]{:S(2)}, u32[]{:S(2)}) collective-permute-start(bf16[64,1280]{1,0:T(8,128)(2,1)S(1)} %get-tuple-element.46), channel_id=1, source_target_pairs={{0,2},{1,3},{2,0},{3,1},{4,6},{5,7},{6,4},{7,5},{8,10},{9,11},{10,... | collective-permute-start | bytes 491528 | tf_op jit(solution)/shard_map/ppermute | solution.py:199
  72.6 6.2 %collective-permute-start.12 = (bf16[64,1280]{1,0:T(8,128)(2,1)S(1)}, bf16[64,1280]{1,0:T(8,128)(2,1)S(1)}, u32[]{:S(2)}, u32[]{:S(2)}) collective-permute-start(bf16[64,1280]{1,0:T(8,128)(2,1)S(1)} %get-tuple-element.47), channel_id=1, source_target_pairs={{0,1},{1,0},{2,3},{3,2},{4,5},{5,4},{6,7},{7,6},{8,9},{9,8},{10,11... | collective-permute-start | bytes 491528 | tf_op jit(solution)/shard_map/ppermute | solution.py:199
  80.2 21.6 %collective-permute-start.14 = (bf16[64,4096]{1,0:T(8,128)(2,1)S(1)}, bf16[64,4096]{1,0:T(8,128)(2,1)S(1)}, u32[]{:S(2)}, u32[]{:S(2)}) collective-permute-start(bf16[64,4096]{1,0:T(8,128)(2,1)S(1)} %get-tuple-element.50), channel_id=1, source_target_pairs={{0,4},{4,0},{8,12},{12,8},{16,20},{20,16},{24,28},{28,24},{32,36},... | collective-permute-start | bytes 1572872 | tf_op jit(solution)/shard_map/ppermute | solution.py:224
  82.1 24.8 %collective-permute-start.13 = (bf16[64,4096]{1,0:T(8,128)(2,1)S(1)}, bf16[64,4096]{1,0:T(8,128)(2,1)S(1)}, u32[]{:S(2)}, u32[]{:S(2)}) collective-permute-start(bf16[64,4096]{1,0:T(8,128)(2,1)S(1)} %get-tuple-element.49), channel_id=1, source_target_pairs={{4,8},{8,4},{12,16},{16,12},{20,24},{24,20},{28,32},{32,28},{36,40... | collective-permute-start | bytes 1572872 | tf_op jit(solution)/shard_map/ppermute | solution.py:227
  84.7 5.3 %collective-permute-start.15 = (f32[64,256]{1,0:T(8,128)S(1)}, f32[64,256]{1,0:T(8,128)S(1)}, u32[]{:S(2)}, u32[]{:S(2)}) collective-permute-start(f32[64,256]{1,0:T(8,128)S(1)} %convert_add_fusion), channel_id=1, source_target_pairs={{0,16},{16,0},{32,48},{48,32},{64,80},{80,64},{96,112},{112,96},{1... | collective-permute-start | bytes 196616 | tf_op jit(solution)/shard_map/ppermute | solution.py:210
  90.0 9.5 %collective-permute-start.16 = (f32[64,256]{1,0:T(8,128)S(1)}, f32[64,256]{1,0:T(8,128)S(1)}, u32[]{:S(2)}, u32[]{:S(2)}) collective-permute-start(f32[64,256]{1,0:T(8,128)S(1)} %add.31), channel_id=1, source_target_pairs={{0,32},{16,48},{32,0},{48,16},{64,96},{80,112},{96,64},{112,80},{1... | collective-permute-start | bytes 196616 | tf_op jit(solution)/shard_map/ppermute | solution.py:210
  92.1 12.0 %collective-permute-start.17 = (bf16[64,1024]{1,0:T(8,128)(2,1)S(1)}, bf16[64,1024]{1,0:T(8,128)(2,1)S(1)}, u32[]{:S(2)}, u32[]{:S(2)}) collective-permute-start(bf16[64,1024]{1,0:T(8,128)(2,1)S(1)} %get-tuple-element.54), channel_id=1, source_target_pairs={{0,3},{1,2},{2,1},{3,0},{4,7},{5,6},{6,5},{7,4},{8,11},{9,10},{10,... | collective-permute-start | bytes 393224 | tf_op jit(solution)/shard_map/ppermute | solution.py:199
  97.5 9.4 %collective-permute-start.18 = (bf16[64,1024]{1,0:T(8,128)(2,1)S(1)}, bf16[64,1024]{1,0:T(8,128)(2,1)S(1)}, u32[]{:S(2)}, u32[]{:S(2)}) collective-permute-start(bf16[64,1024]{1,0:T(8,128)(2,1)S(1)} %get-tuple-element.55), channel_id=1, source_target_pairs={{0,2},{1,3},{2,0},{3,1},{4,6},{5,7},{6,4},{7,5},{8,10},{9,11},{10,... | collective-permute-start | bytes 393224 | tf_op jit(solution)/shard_map/ppermute | solution.py:199
  99.6 7.4 %collective-permute-start.19 = (bf16[64,1024]{1,0:T(8,128)(2,1)S(1)}, bf16[64,1024]{1,0:T(8,128)(2,1)S(1)}, u32[]{:S(2)}, u32[]{:S(2)}) collective-permute-start(bf16[64,1024]{1,0:T(8,128)(2,1)S(1)} %get-tuple-element.56), channel_id=1, source_target_pairs={{0,1},{1,0},{2,3},{3,2},{4,5},{5,4},{6,7},{7,6},{8,9},{9,8},{10,11... | collective-permute-start | bytes 393224 | tf_op jit(solution)/shard_map/ppermute | solution.py:199
  107.9 34.7 %collective-permute-start.20 = (bf16[64,4096]{1,0:T(8,128)(2,1)S(1)}, bf16[64,4096]{1,0:T(8,128)(2,1)S(1)}, u32[]{:S(2)}, u32[]{:S(2)}) collective-permute-start(bf16[64,4096]{1,0:T(8,128)(2,1)S(1)} %shard_map.101), channel_id=1, source_target_pairs={{0,4},{4,0},{8,12},{12,8},{16,20},{20,16},{24,28},{28,24},{32,36},... | collective-permute-start | bytes 1572872 | tf_op jit(solution)/shard_map/ppermute | solution.py:224
  109.8 32.8 %collective-permute-start.21 = (bf16[64,4096]{1,0:T(8,128)(2,1)S(1)}, bf16[64,4096]{1,0:T(8,128)(2,1)S(1)}, u32[]{:S(2)}, u32[]{:S(2)}) collective-permute-start(bf16[64,4096]{1,0:T(8,128)(2,1)S(1)} %shard_map.100), channel_id=1, source_target_pairs={{4,8},{8,4},{12,16},{16,12},{20,24},{24,20},{28,32},{32,28},{36,40... | collective-permute-start | bytes 1572872 | tf_op jit(solution)/shard_map/ppermute | solution.py:227
  120.4 22.2 %collective-permute-start.24 = (f32[64,256]{1,0:T(8,128)S(1)}, f32[64,256]{1,0:T(8,128)S(1)}, u32[]{:S(2)}, u32[]{:S(2)}) collective-permute-start(f32[64,256]{1,0:T(8,128)S(1)} %add.32), channel_id=1, source_target_pairs={{0,192},{16,208},{32,224},{48,240},{64,128},{80,144},{96,160},{112... | collective-permute-start | bytes 196616 | tf_op jit(solution)/shard_map/ppermute | solution.py:210
  122.9 19.7 %collective-permute-start.23 = (f32[64,256]{1,0:T(8,128)S(1)}, f32[64,256]{1,0:T(8,128)S(1)}, u32[]{:S(2)}, u32[]{:S(2)}) collective-permute-start(f32[64,256]{1,0:T(8,128)S(1)} %add.32), channel_id=1, source_target_pairs={{0,64},{16,80},{32,96},{48,112},{64,0},{80,16},{96,32},{112,48},{1... | collective-permute-start | bytes 196616 | tf_op jit(solution)/shard_map/ppermute | solution.py:210
  124.8 17.8 %collective-permute-start.22 = (f32[64,256]{1,0:T(8,128)S(1)}, f32[64,256]{1,0:T(8,128)S(1)}, u32[]{:S(2)}, u32[]{:S(2)}) collective-permute-start(f32[64,256]{1,0:T(8,128)S(1)} %add.32), channel_id=1, source_target_pairs={{0,128},{16,144},{32,160},{48,176},{64,192},{80,208},{96,224},{112... | collective-permute-start | bytes 196616 | tf_op jit(solution)/shard_map/ppermute | solution.py:210

commit v10 on v9

--- a/solution.py
+++ b/solution.py
@@ -47,12 +47,13 @@
             add(slot, product)
 
 
-def gather_terms(info, source_ref, total_ref, offset):
+def gather_terms(info, source_refs, total_ref, offset):
     values_ref, rows_ref, cols_ref, count = info
-    blocks = source_ref.shape[1] // BLOCK
+    blocks = total_ref.shape[1] // BLOCK
 
     def term(slot):
-        source = source_ref[:, lanes(lax.rem(cols_ref[slot], blocks))]
+        where = lanes(lax.rem(cols_ref[slot], blocks))
+        source = jnp.concatenate([ref[:, where] for ref in source_refs], 0)
         return lax.dot_general(
             source, values_ref[slot], (((1,), (1,)), ((), ())), preferred_element_type=jnp.float32
         )
@@ -64,16 +65,16 @@
     each_tile(offset, count, values_ref, term, add)
 
 
-def first_kernel(values, rows, cols, count, place, own, even, total):
+def first_kernel(values, rows, cols, count, place, own_a, own_b, even_a, even_b, total):
     total[...] = jnp.zeros_like(total)
     info = (values, rows, cols, count[0])
-    gather_terms(info, own, total, 2)
-    gather_terms(info, even, total, 3 - 2 * place[0])
-
-
-def second_kernel(values, rows, cols, count, place, start, odd, total):
+    gather_terms(info, [own_a, own_b], total, 2)
+    gather_terms(info, [even_a, even_b], total, 3 - 2 * place[0])
+
+
+def second_kernel(values, rows, cols, count, place, start, odd_a, odd_b, total):
     total[...] = start[...]
-    gather_terms((values, rows, cols, count[0]), odd, total, 1 + 2 * place[0])
+    gather_terms((values, rows, cols, count[0]), [odd_a, odd_b], total, 1 + 2 * place[0])
 
 
 def pack_kernel(place, cotangent, weight, *packed):
@@ -83,13 +84,13 @@
         out[:, width:] = weight[...]
 
 
-def far_kernel(values, rows, cols, count, place, start, even, odd, *rest):
+def far_kernel(values, rows, cols, count, place, start, even_a, even_b, odd_a, odd_b, *rest):
     hidden, total = rest[:-1], rest[-1]
     total[...] = start[...]
     info = (values, rows, cols, count[0])
     even_offset = 4 - 4 * place[0]
-    gather_terms(info, even, total, even_offset)
-    gather_terms(info, odd, total, 4 - even_offset)
+    gather_terms(info, [even_a, even_b], total, even_offset)
+    gather_terms(info, [odd_a, odd_b], total, 4 - even_offset)
     for step, out in enumerate(hidden):
         width = out.shape[1]
         out[...] = total[:, wide_lanes(place[1] ^ PARTNERS[step], width)].astype(out.dtype)
@@ -238,37 +239,40 @@
     total = pltpu.VMEM(whole, jnp.float32)
 
     own = features.T
-    even1 = even_swap(own)
-    odd1 = odd_swap(own)
+    half = feat_cols // 2
+    even1, odd1 = [], []
+    own = (own[:half], own[half:])
+    for piece in own:
+        even1.append(even_swap(piece))
+        odd1.append(odd_swap(piece))
     given = call(
         pack_kernel,
         (place, cotangent.T, weight.T),
         [SMEM, VMEM, VMEM],
         arrays(n_cols, (feat_cols, width + full)),
     )
-    even1, _ = lax.optimization_barrier((even1, given[0]))
+    even1[0], _ = lax.optimization_barrier((even1[0], given[0]))
     given = swapped(given)
-    odd2 = odd_swap(even1)
+    odd2 = [odd_swap(piece) for piece in even1]
+    even2 = [even_swap(piece) for piece in odd1]
     (first,) = call(
         first_kernel,
-        tables + (own, even1),
-        table_specs + [VMEM] * 2,
+        tables + (*own, *even1),
+        table_specs + [VMEM] * 4,
         arrays(1, whole, jnp.float32),
         flops=36 * tile_flops,
     )
-    odd1, first = lax.optimization_barrier((odd1, first))
-    even2 = even_swap(odd1)
     (near,) = call(
         second_kernel,
-        tables + (first, odd1),
-        table_specs + [VMEM] * 2,
+        tables + (first, *odd1),
+        table_specs + [VMEM] * 3,
         arrays(1, whole, jnp.float32),
         flops=18 * tile_flops,
     )
     hidden = call(
         far_kernel,
-        tables + (near, even2, odd2),
-        table_specs + [VMEM] * 3,
+        tables + (near, *even2, *odd2),
+        table_specs + [VMEM] * 5,
         arrays(n_cols, (feat_cols, width)),
         scratch=[total],
         flops=36 * tile_flops,

time: 159 us -> 169 us (1.063)
  starting transfers between devices: 104 us -> 111 us
  waiting for transfers between devices: 21.4 us -> 25.5 us
    ppermute x5, waiting for transfers between devices: 9.34 us -> 14.8 us  [paired(): lax.ppermute(value, axis, [(source, source ^ step) for source in range(co...]
    ppermute x4 -> x6, starting transfers between devices: 9.71 us -> 15 us  [even_swap(): return lax.ppermute(value, ROWS, even_pairs)]
    ppermute x4 -> x6, starting transfers between devices: 37.7 us -> 42.4 us  [odd_swap(): return lax.ppermute(value, ROWS, odd_pairs)]
    ppermute x12, starting transfers between devices: 36.3 us -> 33.6 us  [swapped(): lax.ppermute(value, COLS, pairs(step))]
    unnamed x14 -> x12, local copies, waits for them, and re-layouts: 5.97 us -> 4.92 us
  transfers between devices with their start and end apart: 25 -> 29, of which waited for: 8 -> 8; matrix products, arithmetic and copies ran while one was open for 0% -> 0% of each run, Pallas kernels for 4% -> 3%
where the time goes in v10:
time: 169 us; the launch traced here: 167 us
  starting transfers between devices  111 us (66%)
  waiting for transfers between devices  25.5 us (15%)
  Pallas kernels  11.6 us (7%)
  blocking collectives  10.6 us (6%)
  local copies, waits for them, and re-layouts  6.01 us (4%)
  between operations  1.75 us (1%)
    ppermute x6, starting transfers between devices, odd_swap(): return lax.ppermute(value, ROWS, odd_pairs)  42.4 us
    ppermute x12, starting transfers between devices, swapped(): lax.ppermute(value, COLS, pairs(step))  33.6 us
    ppermute x5, starting transfers between devices, paired(): lax.ppermute(value, axis, [(source, source ^ step) for source in range(co...  20 us
    ppermute x6, starting transfers between devices, even_swap(): return lax.ppermute(value, ROWS, even_pairs)  15 us
    ppermute x5, waiting for transfers between devices, paired(): lax.ppermute(value, axis, [(source, source ^ step) for source in range(co...  14.8 us
    pallas_call x9, Pallas kernels, call(): pl.pallas_call(kernel, out_shape=outs, in_specs=specs, out_specs=[VMEM] *...  11.6 us
    all_to_all x1, blocking collectives, summed(): lax.all_to_all(copies, axis, 0, 0, tiled=True).astype(jnp.float32).sum(0)  10.6 us
    ppermute x12, waiting for transfers between devices, swapped(): lax.ppermute(value, COLS, pairs(step))  9.72 us
  transfers between devices with their start and end apart: 29, of which 8 were waited for; matrix products, arithmetic and copies ran while one was open for 0% of the time, Pallas kernels for 3%

profile of v10, /device:TPU:1, one launch (start us, length us, event | category | flops | bytes accessed | tf_op | source)
XLA Modules:
  0.0 167.3 jit_solution(7752408221376507852)
XLA Ops:
  1.7 3.9 %collective-permute-start = (bf16[32,4096]{1,0:T(8,128)(2,1)S(1)}, bf16[32,4096]{1,0:T(8,128)(2,1)S(1)}, u32[]{:S(2)}, u32[]{:S(2)}) collective-permute-start(bf16[32,4096]{1,0:T(8,128)(2,1)S(1)} %get-tuple-element.60.own_a), channel_id=1, source_target_pairs={{0,4},{4,0},{8,12},{12,8},{16,20},{20,16},{24,28},{28,24},{32,36},... | collective-permute-start | bytes 786440 | tf_op jit(solution)/shard_map/ppermute | solution.py:225
  5.7 15.3 %collective-permute-start.2 = (bf16[32,4096]{1,0:T(8,128)(2,1)S(1)}, bf16[32,4096]{1,0:T(8,128)(2,1)S(1)}, u32[]{:S(2)}, u32[]{:S(2)}) collective-permute-start(bf16[32,4096]{1,0:T(8,128)(2,1)S(1)} %get-tuple-element.60.own_a), channel_id=1, source_target_pairs={{4,8},{8,4},{12,16},{16,12},{20,24},{24,20},{28,32},{32,28},{36,40... | collective-permute-start | bytes 786440 | tf_op jit(solution)/shard_map/ppermute | solution.py:228
  20.9 1.9 %collective-permute-start.3 = (bf16[32,4096]{1,0:T(8,128)(2,1)S(1)}, bf16[32,4096]{1,0:T(8,128)(2,1)S(1)}, u32[]{:S(2)}, u32[]{:S(2)}) collective-permute-start(bf16[32,4096]{1,0:T(8,128)(2,1)S(1)} %get-tuple-element.59.own_b), channel_id=1, source_target_pairs={{4,8},{8,4},{12,16},{16,12},{20,24},{24,20},{28,32},{32,28},{36,40... | collective-permute-start | bytes 786440 | tf_op jit(solution)/shard_map/ppermute | solution.py:228
  22.9 1.9 %collective-permute-start.1 = (bf16[32,4096]{1,0:T(8,128)(2,1)S(1)}, bf16[32,4096]{1,0:T(8,128)(2,1)S(1)}, u32[]{:S(2)}, u32[]{:S(2)}) collective-permute-start(bf16[32,4096]{1,0:T(8,128)(2,1)S(1)} %get-tuple-element.59.own_b), channel_id=1, source_target_pairs={{0,4},{4,0},{8,12},{12,8},{16,20},{20,16},{24,28},{28,24},{32,36},... | collective-permute-start | bytes 786440 | tf_op jit(solution)/shard_map/ppermute | solution.py:225
  27.3 9.1 %collective-permute-start.6 = (bf16[32,4096]{1,0:T(8,128)(2,1)S(1)}, bf16[32,4096]{1,0:T(8,128)(2,1)S(1)}, u32[]{:S(2)}, u32[]{:S(2)}) collective-permute-start(bf16[32,4096]{1,0:T(8,128)(2,1)S(1)} %collective-permute-done.even_a), channel_id=1, source_target_pairs={{4,8},{8,4},{12,16},{16,12},{20,24},{24,20},{28,32},{32,28},{36,40... | collective-permute-start | bytes 786440 | tf_op jit(solution)/shard_map/ppermute | solution.py:228
  36.4 1.9 %collective-permute-start.4 = (bf16[32,4096]{1,0:T(8,128)(2,1)S(1)}, bf16[32,4096]{1,0:T(8,128)(2,1)S(1)}, u32[]{:S(2)}, u32[]{:S(2)}) collective-permute-start(bf16[32,4096]{1,0:T(8,128)(2,1)S(1)} %collective-permute-done.2.odd_a), channel_id=1, source_target_pairs={{0,4},{4,0},{8,12},{12,8},{16,20},{20,16},{24,28},{28,24},{32,36},... | collective-permute-start | bytes 786440 | tf_op jit(solution)/shard_map/ppermute | solution.py:225
  38.3 3.4 %collective-permute-start.5 = (bf16[32,4096]{1,0:T(8,128)(2,1)S(1)}, bf16[32,4096]{1,0:T(8,128)(2,1)S(1)}, u32[]{:S(2)}, u32[]{:S(2)}) collective-permute-start(bf16[32,4096]{1,0:T(8,128)(2,1)S(1)} %collective-permute-done.3.odd_b), channel_id=1, source_target_pairs={{0,4},{4,0},{8,12},{12,8},{16,20},{20,16},{24,28},{28,24},{32,36},... | collective-permute-start | bytes 786440 | tf_op jit(solution)/shard_map/ppermute | solution.py:225
  41.7 1.9 %collective-permute-start.7 = (bf16[32,4096]{1,0:T(8,128)(2,1)S(1)}, bf16[32,4096]{1,0:T(8,128)(2,1)S(1)}, u32[]{:S(2)}, u32[]{:S(2)}) collective-permute-start(bf16[32,4096]{1,0:T(8,128)(2,1)S(1)} %collective-permute-done.1.even_b), channel_id=1, source_target_pairs={{4,8},{8,4},{12,16},{16,12},{20,24},{24,20},{28,32},{32,28},{36,40... | collective-permute-start | bytes 786440 | tf_op jit(solution)/shard_map/ppermute | solution.py:228
  43.6 4.5 %collective-permute-start.11 = (bf16[64,1280]{1,0:T(8,128)(2,1)S(1)}, bf16[64,1280]{1,0:T(8,128)(2,1)S(1)}, u32[]{:S(2)}, u32[]{:S(2)}) collective-permute-start(bf16[64,1280]{1,0:T(8,128)(2,1)S(1)} %get-tuple-element.37), channel_id=1, source_target_pairs={{0,3},{1,2},{2,1},{3,0},{4,7},{5,6},{6,5},{7,4},{8,11},{9,10},{10,... | collective-permute-start | bytes 491528 | tf_op jit(solution)/shard_map/ppermute | solution.py:200
  48.2 3.0 %collective-permute-start.12 = (bf16[64,1280]{1,0:T(8,128)(2,1)S(1)}, bf16[64,1280]{1,0:T(8,128)(2,1)S(1)}, u32[]{:S(2)}, u32[]{:S(2)}) collective-permute-start(bf16[64,1280]{1,0:T(8,128)(2,1)S(1)} %get-tuple-element.38), channel_id=1, source_target_pairs={{0,2},{1,3},{2,0},{3,1},{4,6},{5,7},{6,4},{7,5},{8,10},{9,11},{10,... | collective-permute-start | bytes 491528 | tf_op jit(solution)/shard_map/ppermute | solution.py:200
  51.2 1.9 %collective-permute-start.13 = (bf16[64,1280]{1,0:T(8,128)(2,1)S(1)}, bf16[64,1280]{1,0:T(8,128)(2,1)S(1)}, u32[]{:S(2)}, u32[]{:S(2)}) collective-permute-start(bf16[64,1280]{1,0:T(8,128)(2,1)S(1)} %get-tuple-element.39), channel_id=1, source_target_pairs={{0,1},{1,0},{2,3},{3,2},{4,5},{5,4},{6,7},{7,6},{8,9},{9,8},{10,11... | collective-permute-start | bytes 491528 | tf_op jit(solution)/shard_map/ppermute | solution.py:200
  61.1 2.4 %collective-permute-start.10 = (bf16[64,1024]{1,0:T(8,128)(2,1)S(1)}, bf16[64,1024]{1,0:T(8,128)(2,1)S(1)}, u32[]{:S(2)}, u32[]{:S(2)}) collective-permute-start(bf16[64,1024]{1,0:T(8,128)(2,1)S(1)} %get-tuple-element.36), channel_id=1, source_target_pairs={{0,1},{1,0},{2,3},{3,2},{4,5},{5,4},{6,7},{7,6},{8,9},{9,8},{10,11... | collective-permute-start | bytes 393224 | tf_op jit(solution)/shard_map/ppermute | solution.py:200
  63.5 2.2 %collective-permute-start.8 = (bf16[64,1024]{1,0:T(8,128)(2,1)S(1)}, bf16[64,1024]{1,0:T(8,128)(2,1)S(1)}, u32[]{:S(2)}, u32[]{:S(2)}) collective-permute-start(bf16[64,1024]{1,0:T(8,128)(2,1)S(1)} %get-tuple-element.34), channel_id=1, source_target_pairs={{0,3},{1,2},{2,1},{3,0},{4,7},{5,6},{6,5},{7,4},{8,11},{9,10},{10,... | collective-permute-start | bytes 393224 | tf_op jit(solution)/shard_map/ppermute | solution.py:200
  65.7 3.0 %collective-permute-start.9 = (bf16[64,1024]{1,0:T(8,128)(2,1)S(1)}, bf16[64,1024]{1,0:T(8,128)(2,1)S(1)}, u32[]{:S(2)}, u32[]{:S(2)}) collective-permute-start(bf16[64,1024]{1,0:T(8,128)(2,1)S(1)} %get-tuple-element.35), channel_id=1, source_target_pairs={{0,2},{1,3},{2,0},{3,1},{4,6},{5,7},{6,4},{7,5},{8,10},{9,11},{10,... | collective-permute-start | bytes 393224 | tf_op jit(solution)/shard_map/ppermute | solution.py:200
  68.7 2.2 %collective-permute-done.8.refs_1_ = bf16[64,1024]{1,0:T(8,128)(2,1)S(1)} collective-permute-done((bf16[64,1024]{1,0:T(8,128)(2,1)S(1)}, bf16[64,1024]{1,0:T(8,128)(2,1)S(1)}, u32[]{:S(2)}, u32[]{:S(2)}) %collective-permute-start.8) | collective-permute-done | bytes 131104 | tf_op jit(solution)/shard_map/ppermute | solution.py:200
  70.9 2.2 %collective-permute-done.9.refs_2_ = bf16[64,1024]{1,0:T(8,128)(2,1)S(1)} collective-permute-done((bf16[64,1024]{1,0:T(8,128)(2,1)S(1)}, bf16[64,1024]{1,0:T(8,128)(2,1)S(1)}, u32[]{:S(2)}, u32[]{:S(2)}) %collective-permute-start.9) | collective-permute-done | bytes 131104 | tf_op jit(solution)/shard_map/ppermute | solution.py:200
  74.8 3.2 %collective-permute-start.14 = (bf16[64,1280]{1,0:T(8,128)(2,1)S(1)}, bf16[64,1280]{1,0:T(8,128)(2,1)S(1)}, u32[]{:S(2)}, u32[]{:S(2)}) collective-permute-start(bf16[64,1280]{1,0:T(8,128)(2,1)S(1)} %get-tuple-element.41), channel_id=1, source_target_pairs={{0,3},{1,2},{2,1},{3,0},{4,7},{5,6},{6,5},{7,4},{8,11},{9,10},{10,... | collective-permute-start | bytes 491528 | tf_op jit(solution)/shard_map/ppermute | solution.py:200
  78.0 2.8 %collective-permute-start.15 = (bf16[64,1280]{1,0:T(8,128)(2,1)S(1)}, bf16[64,1280]{1,0:T(8,128)(2,1)S(1)}, u32[]{:S(2)}, u32[]{:S(2)}) collective-permute-start(bf16[64,1280]{1,0:T(8,128)(2,1)S(1)} %get-tuple-element.42), channel_id=1, source_target_pairs={{0,2},{1,3},{2,0},{3,1},{4,6},{5,7},{6,4},{7,5},{8,10},{9,11},{10,... | collective-permute-start | bytes 491528 | tf_op jit(solution)/shard_map/ppermute | solution.py:200
  80.8 1.9 %collective-permute-start.16 = (bf16[64,1280]{1,0:T(8,128)(2,1)S(1)}, bf16[64,1280]{1,0:T(8,128)(2,1)S(1)}, u32[]{:S(2)}, u32[]{:S(2)}) collective-permute-start(bf16[64,1280]{1,0:T(8,128)(2,1)S(1)} %get-tuple-element.43), channel_id=1, source_target_pairs={{0,1},{1,0},{2,3},{3,2},{4,5},{5,4},{6,7},{7,6},{8,9},{9,8},{10,11... | collective-permute-start | bytes 491528 | tf_op jit(solution)/shard_map/ppermute | solution.py:200
  83.3 3.5 %collective-permute-done.15.refs_2_ = bf16[64,1280]{1,0:T(8,128)(2,1)S(1)} collective-permute-done((bf16[64,1280]{1,0:T(8,128)(2,1)S(1)}, bf16[64,1280]{1,0:T(8,128)(2,1)S(1)}, u32[]{:S(2)}, u32[]{:S(2)}) %collective-permute-start.15) | collective-permute-done | bytes 163872 | tf_op jit(solution)/shard_map/ppermute | solution.py:200
  90.1 9.3 %collective-permute-start.17 = (bf16[64,4096]{1,0:T(8,128)(2,1)S(1)}, bf16[64,4096]{1,0:T(8,128)(2,1)S(1)}, u32[]{:S(2)}, u32[]{:S(2)}) collective-permute-start(bf16[64,4096]{1,0:T(8,128)(2,1)S(1)} %get-tuple-element.45), channel_id=1, source_target_pairs={{4,8},{8,4},{12,16},{16,12},{20,24},{24,20},{28,32},{32,28},{36,40... | collective-permute-start | bytes 1572872 | tf_op jit(solution)/shard_map/ppermute | solution.py:228
  99.4 1.9 %collective-permute-start.19 = (f32[64,256]{1,0:T(8,128)S(1)}, f32[64,256]{1,0:T(8,128)S(1)}, u32[]{:S(2)}, u32[]{:S(2)}) collective-permute-start(f32[64,256]{1,0:T(8,128)S(1)} %convert_add_fusion), channel_id=1, source_target_pairs={{0,16},{16,0},{32,48},{48,32},{64,80},{80,64},{96,112},{112,96},{1... | collective-permute-start | bytes 196616 | tf_op jit(solution)/shard_map/ppermute | solution.py:211
  101.3 6.6 %collective-permute-done.19 = f32[64,256]{1,0:T(8,128)S(1)} collective-permute-done((f32[64,256]{1,0:T(8,128)S(1)}, f32[64,256]{1,0:T(8,128)S(1)}, u32[]{:S(2)}, u32[]{:S(2)}) %collective-permute-start.19) | collective-permute-done | bytes 65568 | tf_op jit(solution)/shard_map/ppermute | solution.py:211
  109.9 3.7 %collective-permute-start.21 = (bf16[64,1024]{1,0:T(8,128)(2,1)S(1)}, bf16[64,1024]{1,0:T(8,128)(2,1)S(1)}, u32[]{:S(2)}, u32[]{:S(2)}) collective-permute-start(bf16[64,1024]{1,0:T(8,128)(2,1)S(1)} %get-tuple-element.50), channel_id=1, source_target_pairs={{0,3},{1,2},{2,1},{3,0},{4,7},{5,6},{6,5},{7,4},{8,11},{9,10},{10,... | collective-permute-start | bytes 393224 | tf_op jit(solution)/shard_map/ppermute | solution.py:200
  113.6 3.0 %collective-permute-start.22 = (bf16[64,1024]{1,0:T(8,128)(2,1)S(1)}, bf16[64,1024]{1,0:T(8,128)(2,1)S(1)}, u32[]{:S(2)}, u32[]{:S(2)}) collective-permute-start(bf16[64,1024]{1,0:T(8,128)(2,1)S(1)} %get-tuple-element.51), channel_id=1, source_target_pairs={{0,2},{1,3},{2,0},{3,1},{4,6},{5,7},{6,4},{7,5},{8,10},{9,11},{10,... | collective-permute-start | bytes 393224 | tf_op jit(solution)/shard_map/ppermute | solution.py:200
  123.7 4.9 %collective-permute-start.25 = (bf16[64,4096]{1,0:T(8,128)(2,1)S(1)}, bf16[64,4096]{1,0:T(8,128)(2,1)S(1)}, u32[]{:S(2)}, u32[]{:S(2)}) collective-permute-start(bf16[64,4096]{1,0:T(8,128)(2,1)S(1)} %shard_map.100), channel_id=1, source_target_pairs={{4,8},{8,4},{12,16},{16,12},{20,24},{24,20},{28,32},{32,28},{36,40... | collective-permute-start | bytes 1572872 | tf_op jit(solution)/shard_map/ppermute | solution.py:228
  128.6 2.1 %collective-permute-start.26 = (f32[64,256]{1,0:T(8,128)S(1)}, f32[64,256]{1,0:T(8,128)S(1)}, u32[]{:S(2)}, u32[]{:S(2)}) collective-permute-start(f32[64,256]{1,0:T(8,128)S(1)} %add.32), channel_id=1, source_target_pairs={{0,128},{16,144},{32,160},{48,176},{64,192},{80,208},{96,224},{112... | collective-permute-start | bytes 196616 | tf_op jit(solution)/shard_map/ppermute | solution.py:211
  130.7 5.7 %collective-permute-start.27 = (f32[64,256]{1,0:T(8,128)S(1)}, f32[64,256]{1,0:T(8,128)S(1)}, u32[]{:S(2)}, u32[]{:S(2)}) collective-permute-start(f32[64,256]{1,0:T(8,128)S(1)} %add.32), channel_id=1, source_target_pairs={{0,64},{16,80},{32,96},{48,112},{64,0},{80,16},{96,32},{112,48},{1... | collective-permute-start | bytes 196616 | tf_op jit(solution)/shard_map/ppermute | solution.py:211
  136.4 8.3 %collective-permute-start.28 = (f32[64,256]{1,0:T(8,128)S(1)}, f32[64,256]{1,0:T(8,128)S(1)}, u32[]{:S(2)}, u32[]{:S(2)}) collective-permute-start(f32[64,256]{1,0:T(8,128)S(1)} %add.32), channel_id=1, source_target_pairs={{0,192},{16,208},{32,224},{48,240},{64,128},{80,144},{96,160},{112... | collective-permute-start | bytes 196616 | tf_op jit(solution)/shard_map/ppermute | solution.py:211
  144.8 8.1 %collective-permute-done.27 = f32[64,256]{1,0:T(8,128)S(1)} collective-permute-done((f32[64,256]{1,0:T(8,128)S(1)}, f32[64,256]{1,0:T(8,128)S(1)}, u32[]{:S(2)}, u32[]{:S(2)}) %collective-permute-start.27) | collective-permute-done | bytes 65568 | tf_op jit(solution)/shard_map/ppermute | solution.py:211
  154.0 2.0 %shard_map.102 = (bf16[64,4096]{1,0:T(8,128)(2,1)}, bf16[64,4096]{1,0:T(8,128)(2,1)}) custom-call(bf16[88,128,128]{2,1,0:T(8,128)(2,1)S(1)} %copy-done.1, s32[88]{0:T(128)S(1)} %copy-done.4, s32[88]{0:T(128)S(1)} %copy-done.5, s32[1]{0:T(128)S(6)} %copy.10.count, s32[2]{0:T(128)S(1)} %pad_add_fusion.place, bf16[4,64,1024]{2,1,0:T(8,128)(2,1)S(1)} %get-tuple-element.44.grad, ...), custom_call_target="tpu_custom_call" | custom-call | flops 37748736 | bytes 6030028 | tf_op jit(solution)/shard_map/pallas_call | solution.py:184
  156.0 10.6 %all_to_all.5 = bf16[8,64,256]{2,1,0:T(8,128)(2,1)S(1)} all-to-all(bf16[8,64,256]{2,1,0:T(8,128)(2,1)S(1)} %broadcast_in_dim.3), channel_id=1, replica_groups=mesh['yh'=2,'z'=16,'x'=4,'yl'=2,'core'=2] {'yh','x'}, dimensions={0} | all-to-all | bytes 524288 | tf_op jit(solution)/shard_map/all_to_all | solution.py:206
  (57 shorter events, 26.9 us)
Async XLA Ops:
  1.7 25.6 %collective-permute-start = (bf16[32,4096]{1,0:T(8,128)(2,1)S(1)}, bf16[32,4096]{1,0:T(8,128)(2,1)S(1)}, u32[]{:S(2)}, u32[]{:S(2)}) collective-permute-start(bf16[32,4096]{1,0:T(8,128)(2,1)S(1)} %get-tuple-element.60.own_a), channel_id=1, source_target_pairs={{0,4},{4,0},{8,12},{12,8},{16,20},{20,16},{24,28},{28,24},{32,36},... | collective-permute-start | bytes 786440 | tf_op jit(solution)/shard_map/ppermute | solution.py:225
  5.7 30.7 %collective-permute-start.2 = (bf16[32,4096]{1,0:T(8,128)(2,1)S(1)}, bf16[32,4096]{1,0:T(8,128)(2,1)S(1)}, u32[]{:S(2)}, u32[]{:S(2)}) collective-permute-start(bf16[32,4096]{1,0:T(8,128)(2,1)S(1)} %get-tuple-element.60.own_a), channel_id=1, source_target_pairs={{4,8},{8,4},{12,16},{16,12},{20,24},{24,20},{28,32},{32,28},{36,40... | collective-permute-start | bytes 786440 | tf_op jit(solution)/shard_map/ppermute | solution.py:228
  20.9 17.4 %collective-permute-start.3 = (bf16[32,4096]{1,0:T(8,128)(2,1)S(1)}, bf16[32,4096]{1,0:T(8,128)(2,1)S(1)}, u32[]{:S(2)}, u32[]{:S(2)}) collective-permute-start(bf16[32,4096]{1,0:T(8,128)(2,1)S(1)} %get-tuple-element.59.own_b), channel_id=1, source_target_pairs={{4,8},{8,4},{12,16},{16,12},{20,24},{24,20},{28,32},{32,28},{36,40... | collective-permute-start | bytes 786440 | tf_op jit(solution)/shard_map/ppermute | solution.py:228
  22.9 18.8 %collective-permute-start.1 = (bf16[32,4096]{1,0:T(8,128)(2,1)S(1)}, bf16[32,4096]{1,0:T(8,128)(2,1)S(1)}, u32[]{:S(2)}, u32[]{:S(2)}) collective-permute-start(bf16[32,4096]{1,0:T(8,128)(2,1)S(1)} %get-tuple-element.59.own_b), channel_id=1, source_target_pairs={{0,4},{4,0},{8,12},{12,8},{16,20},{20,16},{24,28},{28,24},{32,36},... | collective-permute-start | bytes 786440 | tf_op jit(solution)/shard_map/ppermute | solution.py:225
  24.9 1.0 copy-start.2
  27.3 20.9 %collective-permute-start.6 = (bf16[32,4096]{1,0:T(8,128)(2,1)S(1)}, bf16[32,4096]{1,0:T(8,128)(2,1)S(1)}, u32[]{:S(2)}, u32[]{:S(2)}) collective-permute-start(bf16[32,4096]{1,0:T(8,128)(2,1)S(1)} %collective-permute-done.even_a), channel_id=1, source_target_pairs={{4,8},{8,4},{12,16},{16,12},{20,24},{24,20},{28,32},{32,28},{36,40... | collective-permute-start | bytes 786440 | tf_op jit(solution)/shard_map/ppermute | solution.py:228
  36.4 14.8 %collective-permute-start.4 = (bf16[32,4096]{1,0:T(8,128)(2,1)S(1)}, bf16[32,4096]{1,0:T(8,128)(2,1)S(1)}, u32[]{:S(2)}, u32[]{:S(2)}) collective-permute-start(bf16[32,4096]{1,0:T(8,128)(2,1)S(1)} %collective-permute-done.2.odd_a), channel_id=1, source_target_pairs={{0,4},{4,0},{8,12},{12,8},{16,20},{20,16},{24,28},{28,24},{32,36},... | collective-permute-start | bytes 786440 | tf_op jit(solution)/shard_map/ppermute | solution.py:225
  38.3 21.2 %collective-permute-start.5 = (bf16[32,4096]{1,0:T(8,128)(2,1)S(1)}, bf16[32,4096]{1,0:T(8,128)(2,1)S(1)}, u32[]{:S(2)}, u32[]{:S(2)}) collective-permute-start(bf16[32,4096]{1,0:T(8,128)(2,1)S(1)} %collective-permute-done.3.odd_b), channel_id=1, source_target_pairs={{0,4},{4,0},{8,12},{12,8},{16,20},{20,16},{24,28},{28,24},{32,36},... | collective-permute-start | bytes 786440 | tf_op jit(solution)/shard_map/ppermute | solution.py:225
  41.7 17.8 %collective-permute-start.7 = (bf16[32,4096]{1,0:T(8,128)(2,1)S(1)}, bf16[32,4096]{1,0:T(8,128)(2,1)S(1)}, u32[]{:S(2)}, u32[]{:S(2)}) collective-permute-start(bf16[32,4096]{1,0:T(8,128)(2,1)S(1)} %collective-permute-done.1.even_b), channel_id=1, source_target_pairs={{4,8},{8,4},{12,16},{16,12},{20,24},{24,20},{28,32},{32,28},{36,40... | collective-permute-start | bytes 786440 | tf_op jit(solution)/shard_map/ppermute | solution.py:228
  43.6 22.1 %collective-permute-start.11 = (bf16[64,1280]{1,0:T(8,128)(2,1)S(1)}, bf16[64,1280]{1,0:T(8,128)(2,1)S(1)}, u32[]{:S(2)}, u32[]{:S(2)}) collective-permute-start(bf16[64,1280]{1,0:T(8,128)(2,1)S(1)} %get-tuple-element.37), channel_id=1, source_target_pairs={{0,3},{1,2},{2,1},{3,0},{4,7},{5,6},{6,5},{7,4},{8,11},{9,10},{10,... | collective-permute-start | bytes 491528 | tf_op jit(solution)/shard_map/ppermute | solution.py:200
  48.2 20.5 %collective-permute-start.12 = (bf16[64,1280]{1,0:T(8,128)(2,1)S(1)}, bf16[64,1280]{1,0:T(8,128)(2,1)S(1)}, u32[]{:S(2)}, u32[]{:S(2)}) collective-permute-start(bf16[64,1280]{1,0:T(8,128)(2,1)S(1)} %get-tuple-element.38), channel_id=1, source_target_pairs={{0,2},{1,3},{2,0},{3,1},{4,6},{5,7},{6,4},{7,5},{8,10},{9,11},{10,... | collective-permute-start | bytes 491528 | tf_op jit(solution)/shard_map/ppermute | solution.py:200
  51.2 17.5 %collective-permute-start.13 = (bf16[64,1280]{1,0:T(8,128)(2,1)S(1)}, bf16[64,1280]{1,0:T(8,128)(2,1)S(1)}, u32[]{:S(2)}, u32[]{:S(2)}) collective-permute-start(bf16[64,1280]{1,0:T(8,128)(2,1)S(1)} %get-tuple-element.39), channel_id=1, source_target_pairs={{0,1},{1,0},{2,3},{3,2},{4,5},{5,4},{6,7},{7,6},{8,9},{9,8},{10,11... | collective-permute-start | bytes 491528 | tf_op jit(solution)/shard_map/ppermute | solution.py:200
  53.8 1.8 %copy-start = (bf16[88,128,128]{2,1,0:T(8,128)(2,1)S(1)}, bf16[88,128,128]{2,1,0:T(8,128)(2,1)}, u32[]{:S(2)}) copy-start(bf16[88,128,128]{2,1,0:T(8,128)(2,1)} %values.13) | copy-start | bytes 8650756
  59.5 27.3 %copy-start.1 = (bf16[88,128,128]{2,1,0:T(8,128)(2,1)S(1)}, bf16[88,128,128]{2,1,0:T(8,128)(2,1)}, u32[]{:S(2)}) copy-start(bf16[88,128,128]{2,1,0:T(8,128)(2,1)} %values.13) | copy-start | bytes 8650756
  61.1 7.6 %collective-permute-start.10 = (bf16[64,1024]{1,0:T(8,128)(2,1)S(1)}, bf16[64,1024]{1,0:T(8,128)(2,1)S(1)}, u32[]{:S(2)}, u32[]{:S(2)}) collective-permute-start(bf16[64,1024]{1,0:T(8,128)(2,1)S(1)} %get-tuple-element.36), channel_id=1, source_target_pairs={{0,1},{1,0},{2,3},{3,2},{4,5},{5,4},{6,7},{7,6},{8,9},{9,8},{10,11... | collective-permute-start | bytes 393224 | tf_op jit(solution)/shard_map/ppermute | solution.py:200
  63.5 7.4 %collective-permute-start.8 = (bf16[64,1024]{1,0:T(8,128)(2,1)S(1)}, bf16[64,1024]{1,0:T(8,128)(2,1)S(1)}, u32[]{:S(2)}, u32[]{:S(2)}) collective-permute-start(bf16[64,1024]{1,0:T(8,128)(2,1)S(1)} %get-tuple-element.34), channel_id=1, source_target_pairs={{0,3},{1,2},{2,1},{3,0},{4,7},{5,6},{6,5},{7,4},{8,11},{9,10},{10,... | collective-permute-start | bytes 393224 | tf_op jit(solution)/shard_map/ppermute | solution.py:200
  65.7 7.4 %collective-permute-start.9 = (bf16[64,1024]{1,0:T(8,128)(2,1)S(1)}, bf16[64,1024]{1,0:T(8,128)(2,1)S(1)}, u32[]{:S(2)}, u32[]{:S(2)}) collective-permute-start(bf16[64,1024]{1,0:T(8,128)(2,1)S(1)} %get-tuple-element.35), channel_id=1, source_target_pairs={{0,2},{1,3},{2,0},{3,1},{4,6},{5,7},{6,4},{7,5},{8,10},{9,11},{10,... | collective-permute-start | bytes 393224 | tf_op jit(solution)/shard_map/ppermute | solution.py:200
  74.8 8.5 %collective-permute-start.14 = (bf16[64,1280]{1,0:T(8,128)(2,1)S(1)}, bf16[64,1280]{1,0:T(8,128)(2,1)S(1)}, u32[]{:S(2)}, u32[]{:S(2)}) collective-permute-start(bf16[64,1280]{1,0:T(8,128)(2,1)S(1)} %get-tuple-element.41), channel_id=1, source_target_pairs={{0,3},{1,2},{2,1},{3,0},{4,7},{5,6},{6,5},{7,4},{8,11},{9,10},{10,... | collective-permute-start | bytes 491528 | tf_op jit(solution)/shard_map/ppermute | solution.py:200
  78.0 8.8 %collective-permute-start.15 = (bf16[64,1280]{1,0:T(8,128)(2,1)S(1)}, bf16[64,1280]{1,0:T(8,128)(2,1)S(1)}, u32[]{:S(2)}, u32[]{:S(2)}) collective-permute-start(bf16[64,1280]{1,0:T(8,128)(2,1)S(1)} %get-tuple-element.42), channel_id=1, source_target_pairs={{0,2},{1,3},{2,0},{3,1},{4,6},{5,7},{6,4},{7,5},{8,10},{9,11},{10,... | collective-permute-start | bytes 491528 | tf_op jit(solution)/shard_map/ppermute | solution.py:200
  80.8 6.0 %collective-permute-start.16 = (bf16[64,1280]{1,0:T(8,128)(2,1)S(1)}, bf16[64,1280]{1,0:T(8,128)(2,1)S(1)}, u32[]{:S(2)}, u32[]{:S(2)}) collective-permute-start(bf16[64,1280]{1,0:T(8,128)(2,1)S(1)} %get-tuple-element.43), channel_id=1, source_target_pairs={{0,1},{1,0},{2,3},{3,2},{4,5},{5,4},{6,7},{7,6},{8,9},{9,8},{10,11... | collective-permute-start | bytes 491528 | tf_op jit(solution)/shard_map/ppermute | solution.py:200
  88.2 30.4 %collective-permute-start.18 = (bf16[64,4096]{1,0:T(8,128)(2,1)S(1)}, bf16[64,4096]{1,0:T(8,128)(2,1)S(1)}, u32[]{:S(2)}, u32[]{:S(2)}) collective-permute-start(bf16[64,4096]{1,0:T(8,128)(2,1)S(1)} %get-tuple-element.46), channel_id=1, source_target_pairs={{0,4},{4,0},{8,12},{12,8},{16,20},{20,16},{24,28},{28,24},{32,36},... | collective-permute-start | bytes 1572872 | tf_op jit(solution)/shard_map/ppermute | solution.py:225
  90.1 30.7 %collective-permute-start.17 = (bf16[64,4096]{1,0:T(8,128)(2,1)S(1)}, bf16[64,4096]{1,0:T(8,128)(2,1)S(1)}, u32[]{:S(2)}, u32[]{:S(2)}) collective-permute-start(bf16[64,4096]{1,0:T(8,128)(2,1)S(1)} %get-tuple-element.45), channel_id=1, source_target_pairs={{4,8},{8,4},{12,16},{16,12},{20,24},{24,20},{28,32},{32,28},{36,40... | collective-permute-start | bytes 1572872 | tf_op jit(solution)/shard_map/ppermute | solution.py:228
  99.4 8.6 %collective-permute-start.19 = (f32[64,256]{1,0:T(8,128)S(1)}, f32[64,256]{1,0:T(8,128)S(1)}, u32[]{:S(2)}, u32[]{:S(2)}) collective-permute-start(f32[64,256]{1,0:T(8,128)S(1)} %convert_add_fusion), channel_id=1, source_target_pairs={{0,16},{16,0},{32,48},{48,32},{64,80},{80,64},{96,112},{112,96},{1... | collective-permute-start | bytes 196616 | tf_op jit(solution)/shard_map/ppermute | solution.py:211
  108.0 8.7 %collective-permute-start.20 = (f32[64,256]{1,0:T(8,128)S(1)}, f32[64,256]{1,0:T(8,128)S(1)}, u32[]{:S(2)}, u32[]{:S(2)}) collective-permute-start(f32[64,256]{1,0:T(8,128)S(1)} %add.31), channel_id=1, source_target_pairs={{0,32},{16,48},{32,0},{48,16},{64,96},{80,112},{96,64},{112,80},{1... | collective-permute-start | bytes 196616 | tf_op jit(solution)/shard_map/ppermute | solution.py:211
  109.9 9.7 %collective-permute-start.21 = (bf16[64,1024]{1,0:T(8,128)(2,1)S(1)}, bf16[64,1024]{1,0:T(8,128)(2,1)S(1)}, u32[]{:S(2)}, u32[]{:S(2)}) collective-permute-start(bf16[64,1024]{1,0:T(8,128)(2,1)S(1)} %get-tuple-element.50), channel_id=1, source_target_pairs={{0,3},{1,2},{2,1},{3,0},{4,7},{5,6},{6,5},{7,4},{8,11},{9,10},{10,... | collective-permute-start | bytes 393224 | tf_op jit(solution)/shard_map/ppermute | solution.py:200
  113.6 7.2 %collective-permute-start.22 = (bf16[64,1024]{1,0:T(8,128)(2,1)S(1)}, bf16[64,1024]{1,0:T(8,128)(2,1)S(1)}, u32[]{:S(2)}, u32[]{:S(2)}) collective-permute-start(bf16[64,1024]{1,0:T(8,128)(2,1)S(1)} %get-tuple-element.51), channel_id=1, source_target_pairs={{0,2},{1,3},{2,0},{3,1},{4,6},{5,7},{6,4},{7,5},{8,10},{9,11},{10,... | collective-permute-start | bytes 393224 | tf_op jit(solution)/shard_map/ppermute | solution.py:200
  116.6 4.1 %collective-permute-start.23 = (bf16[64,1024]{1,0:T(8,128)(2,1)S(1)}, bf16[64,1024]{1,0:T(8,128)(2,1)S(1)}, u32[]{:S(2)}, u32[]{:S(2)}) collective-permute-start(bf16[64,1024]{1,0:T(8,128)(2,1)S(1)} %get-tuple-element.52), channel_id=1, source_target_pairs={{0,1},{1,0},{2,3},{3,2},{4,5},{5,4},{6,7},{7,6},{8,9},{9,8},{10,11... | collective-permute-start | bytes 393224 | tf_op jit(solution)/shard_map/ppermute | solution.py:200
  121.7 31.2 %collective-permute-start.24 = (bf16[64,4096]{1,0:T(8,128)(2,1)S(1)}, bf16[64,4096]{1,0:T(8,128)(2,1)S(1)}, u32[]{:S(2)}, u32[]{:S(2)}) collective-permute-start(bf16[64,4096]{1,0:T(8,128)(2,1)S(1)} %shard_map.101), channel_id=1, source_target_pairs={{0,4},{4,0},{8,12},{12,8},{16,20},{20,16},{24,28},{28,24},{32,36},... | collective-permute-start | bytes 1572872 | tf_op jit(solution)/shard_map/ppermute | solution.py:225
  123.7 30.3 %collective-permute-start.25 = (bf16[64,4096]{1,0:T(8,128)(2,1)S(1)}, bf16[64,4096]{1,0:T(8,128)(2,1)S(1)}, u32[]{:S(2)}, u32[]{:S(2)}) collective-permute-start(bf16[64,4096]{1,0:T(8,128)(2,1)S(1)} %shard_map.100), channel_id=1, source_target_pairs={{4,8},{8,4},{12,16},{16,12},{20,24},{24,20},{28,32},{32,28},{36,40... | collective-permute-start | bytes 1572872 | tf_op jit(solution)/shard_map/ppermute | solution.py:228
  128.6 16.2 %collective-permute-start.26 = (f32[64,256]{1,0:T(8,128)S(1)}, f32[64,256]{1,0:T(8,128)S(1)}, u32[]{:S(2)}, u32[]{:S(2)}) collective-permute-start(f32[64,256]{1,0:T(8,128)S(1)} %add.32), channel_id=1, source_target_pairs={{0,128},{16,144},{32,160},{48,176},{64,192},{80,208},{96,224},{112... | collective-permute-start | bytes 196616 | tf_op jit(solution)/shard_map/ppermute | solution.py:211
  130.7 22.2 %collective-permute-start.27 = (f32[64,256]{1,0:T(8,128)S(1)}, f32[64,256]{1,0:T(8,128)S(1)}, u32[]{:S(2)}, u32[]{:S(2)}) collective-permute-start(f32[64,256]{1,0:T(8,128)S(1)} %add.32), channel_id=1, source_target_pairs={{0,64},{16,80},{32,96},{48,112},{64,0},{80,16},{96,32},{112,48},{1... | collective-permute-start | bytes 196616 | tf_op jit(solution)/shard_map/ppermute | solution.py:211
  136.4 16.5 %collective-permute-start.28 = (f32[64,256]{1,0:T(8,128)S(1)}, f32[64,256]{1,0:T(8,128)S(1)}, u32[]{:S(2)}, u32[]{:S(2)}) collective-permute-start(f32[64,256]{1,0:T(8,128)S(1)} %add.32), channel_id=1, source_target_pairs={{0,192},{16,208},{32,224},{48,240},{64,128},{80,144},{96,160},{112... | collective-permute-start | bytes 196616 | tf_op jit(solution)/shard_map/ppermute | solution.py:211
  (3 other events, 2.1 us)

commit v11 on v9

--- a/solution.py
+++ b/solution.py
@@ -76,7 +76,7 @@
     gather_terms((values, rows, cols, count[0]), odd, total, 1 + 2 * place[0])
 
 
-def pack_kernel(place, cotangent, weight, *packed):
+def pack_kernel(values, rows, cols, count, place, own, cotangent, weight, *packed):
     width = packed[0].shape[1] - weight.shape[1]
     for step, out in enumerate(packed):
         out[:, :width] = cotangent[:, wide_lanes(place[1] ^ PARTNERS[step], width)]
@@ -242,8 +242,8 @@
     odd1 = odd_swap(own)
     given = call(
         pack_kernel,
-        (place, cotangent.T, weight.T),
-        [SMEM, VMEM, VMEM],
+        tables + (own, cotangent.T, weight.T),
+        table_specs + [VMEM] * 3,
         arrays(n_cols, (feat_cols, width + full)),
     )
     even1, _ = lax.optimization_barrier((even1, given[0]))

time: 159 us -> 155 us (0.975)
  waiting for transfers between devices: 21.4 us -> 18.5 us
    ppermute x12, waiting for transfers between devices: 10.5 us -> 7.63 us  [swapped(): lax.ppermute(value, COLS, pairs(step))]
where the time goes in v11:
time: 155 us; the launch traced here: 153 us
  starting transfers between devices  103 us (66%)
  waiting for transfers between devices  18.5 us (12%)
  blocking collectives  11.9 us (8%)
  Pallas kernels  11.6 us (7%)
  local copies, waits for them, and re-layouts  5.99 us (4%)
  between operations  1.66 us (1%)
    ppermute x4, starting transfers between devices, odd_swap(): return lax.ppermute(value, ROWS, odd_pairs)  37 us
    ppermute x12, starting transfers between devices, swapped(): lax.ppermute(value, COLS, pairs(step))  35.9 us
    ppermute x5, starting transfers between devices, paired(): lax.ppermute(value, axis, [(source, source ^ step) for source in range(co...  20 us
    all_to_all x1, blocking collectives, summed(): lax.all_to_all(copies, axis, 0, 0, tiled=True).astype(jnp.float32).sum(0)  11.9 us
    pallas_call x9, Pallas kernels, call(): pl.pallas_call(kernel, out_shape=outs, in_specs=specs, out_specs=[VMEM] *...  11.6 us
    ppermute x4, starting transfers between devices, even_swap(): return lax.ppermute(value, ROWS, even_pairs)  9.71 us
    ppermute x5, waiting for transfers between devices, paired(): lax.ppermute(value, axis, [(source, source ^ step) for source in range(co...  9.34 us
    ppermute x12, waiting for transfers between devices, swapped(): lax.ppermute(value, COLS, pairs(step))  7.63 us
  transfers between devices with their start and end apart: 25, of which 8 were waited for; matrix products, arithmetic and copies ran while one was open for 0% of the time, Pallas kernels for 4%

profile of v11, /device:TPU:1, one launch (start us, length us, event | category | flops | bytes accessed | tf_op | source)
XLA Modules:
  0.0 153.1 jit_solution(17802769178723571829)
XLA Ops:
  0.6 4.0 %collective-permute-start.1 = (bf16[64,4096]{1,0:T(8,128)(2,1)}, bf16[64,4096]{1,0:T(8,128)(2,1)S(1)}, u32[]{:S(2)}, u32[]{:S(2)}) collective-permute-start(bf16[64,4096]{1,0:T(8,128)(2,1)} %bitcast.9), channel_id=1, source_target_pairs={{0,4},{4,0},{8,12},{12,8},{16,20},{20,16},{24,28},{28,24},{32,36},... | collective-permute-start | bytes 1572872 | tf_op jit(solution)/shard_map/ppermute | solution.py:224
  4.6 15.3 %collective-permute-start = (bf16[64,4096]{1,0:T(8,128)(2,1)}, bf16[64,4096]{1,0:T(8,128)(2,1)S(1)}, u32[]{:S(2)}, u32[]{:S(2)}) collective-permute-start(bf16[64,4096]{1,0:T(8,128)(2,1)} %bitcast.10), channel_id=1, source_target_pairs={{4,8},{8,4},{12,16},{16,12},{20,24},{24,20},{28,32},{32,28},{36,40... | collective-permute-start | bytes 1572872 | tf_op jit(solution)/shard_map/ppermute | solution.py:227
  20.6 1.8 %copy-done = bf16[88,128,128]{2,1,0:T(8,128)(2,1)S(1)} copy-done((bf16[88,128,128]{2,1,0:T(8,128)(2,1)S(1)}, bf16[88,128,128]{2,1,0:T(8,128)(2,1)}, u32[]{:S(2)}) %copy-start) | copy-done | bytes 2883608
  27.2 5.1 %collective-permute-start.3 = (bf16[64,4096]{1,0:T(8,128)(2,1)S(1)}, bf16[64,4096]{1,0:T(8,128)(2,1)S(1)}, u32[]{:S(2)}, u32[]{:S(2)}) collective-permute-start(bf16[64,4096]{1,0:T(8,128)(2,1)S(1)} %collective-permute-done.1.even), channel_id=1, source_target_pairs={{4,8},{8,4},{12,16},{16,12},{20,24},{24,20},{28,32},{32,28},{36,40... | collective-permute-start | bytes 1572872 | tf_op jit(solution)/shard_map/ppermute | solution.py:227
  33.8 1.9 %collective-permute-start.2 = (bf16[64,4096]{1,0:T(8,128)(2,1)S(1)}, bf16[64,4096]{1,0:T(8,128)(2,1)S(1)}, u32[]{:S(2)}, u32[]{:S(2)}) collective-permute-start(bf16[64,4096]{1,0:T(8,128)(2,1)S(1)} %collective-permute-done.odd), channel_id=1, source_target_pairs={{0,4},{4,0},{8,12},{12,8},{16,20},{20,16},{24,28},{28,24},{32,36},... | collective-permute-start | bytes 1572872 | tf_op jit(solution)/shard_map/ppermute | solution.py:224
  35.7 4.0 %collective-permute-start.7 = (bf16[64,1280]{1,0:T(8,128)(2,1)S(1)}, bf16[64,1280]{1,0:T(8,128)(2,1)S(1)}, u32[]{:S(2)}, u32[]{:S(2)}) collective-permute-start(bf16[64,1280]{1,0:T(8,128)(2,1)S(1)} %get-tuple-element.41), channel_id=1, source_target_pairs={{0,3},{1,2},{2,1},{3,0},{4,7},{5,6},{6,5},{7,4},{8,11},{9,10},{10,... | collective-permute-start | bytes 491528 | tf_op jit(solution)/shard_map/ppermute | solution.py:199
  39.8 3.0 %collective-permute-start.8 = (bf16[64,1280]{1,0:T(8,128)(2,1)S(1)}, bf16[64,1280]{1,0:T(8,128)(2,1)S(1)}, u32[]{:S(2)}, u32[]{:S(2)}) collective-permute-start(bf16[64,1280]{1,0:T(8,128)(2,1)S(1)} %get-tuple-element.42), channel_id=1, source_target_pairs={{0,2},{1,3},{2,0},{3,1},{4,6},{5,7},{6,4},{7,5},{8,10},{9,11},{10,... | collective-permute-start | bytes 491528 | tf_op jit(solution)/shard_map/ppermute | solution.py:199
  42.7 1.9 %collective-permute-start.9 = (bf16[64,1280]{1,0:T(8,128)(2,1)S(1)}, bf16[64,1280]{1,0:T(8,128)(2,1)S(1)}, u32[]{:S(2)}, u32[]{:S(2)}) collective-permute-start(bf16[64,1280]{1,0:T(8,128)(2,1)S(1)} %get-tuple-element.43), channel_id=1, source_target_pairs={{0,1},{1,0},{2,3},{3,2},{4,5},{5,4},{6,7},{7,6},{8,9},{9,8},{10,11... | collective-permute-start | bytes 491528 | tf_op jit(solution)/shard_map/ppermute | solution.py:199
  48.8 4.9 %collective-permute-start.4 = (bf16[64,1024]{1,0:T(8,128)(2,1)S(1)}, bf16[64,1024]{1,0:T(8,128)(2,1)S(1)}, u32[]{:S(2)}, u32[]{:S(2)}) collective-permute-start(bf16[64,1024]{1,0:T(8,128)(2,1)S(1)} %get-tuple-element.38), channel_id=1, source_target_pairs={{0,3},{1,2},{2,1},{3,0},{4,7},{5,6},{6,5},{7,4},{8,11},{9,10},{10,... | collective-permute-start | bytes 393224 | tf_op jit(solution)/shard_map/ppermute | solution.py:199
  53.8 3.0 %collective-permute-start.5 = (bf16[64,1024]{1,0:T(8,128)(2,1)S(1)}, bf16[64,1024]{1,0:T(8,128)(2,1)S(1)}, u32[]{:S(2)}, u32[]{:S(2)}) collective-permute-start(bf16[64,1024]{1,0:T(8,128)(2,1)S(1)} %get-tuple-element.39), channel_id=1, source_target_pairs={{0,2},{1,3},{2,0},{3,1},{4,6},{5,7},{6,4},{7,5},{8,10},{9,11},{10,... | collective-permute-start | bytes 393224 | tf_op jit(solution)/shard_map/ppermute | solution.py:199
  56.8 1.9 %collective-permute-start.6 = (bf16[64,1024]{1,0:T(8,128)(2,1)S(1)}, bf16[64,1024]{1,0:T(8,128)(2,1)S(1)}, u32[]{:S(2)}, u32[]{:S(2)}) collective-permute-start(bf16[64,1024]{1,0:T(8,128)(2,1)S(1)} %get-tuple-element.40), channel_id=1, source_target_pairs={{0,1},{1,0},{2,3},{3,2},{4,5},{5,4},{6,7},{7,6},{8,9},{9,8},{10,11... | collective-permute-start | bytes 393224 | tf_op jit(solution)/shard_map/ppermute | solution.py:199
  58.7 2.3 %collective-permute-done.5.refs_2_ = bf16[64,1024]{1,0:T(8,128)(2,1)S(1)} collective-permute-done((bf16[64,1024]{1,0:T(8,128)(2,1)S(1)}, bf16[64,1024]{1,0:T(8,128)(2,1)S(1)}, u32[]{:S(2)}, u32[]{:S(2)}) %collective-permute-start.5) | collective-permute-done | bytes 131104 | tf_op jit(solution)/shard_map/ppermute | solution.py:199
  62.6 2.8 %collective-permute-start.10 = (bf16[64,1280]{1,0:T(8,128)(2,1)S(1)}, bf16[64,1280]{1,0:T(8,128)(2,1)S(1)}, u32[]{:S(2)}, u32[]{:S(2)}) collective-permute-start(bf16[64,1280]{1,0:T(8,128)(2,1)S(1)} %get-tuple-element.45), channel_id=1, source_target_pairs={{0,3},{1,2},{2,1},{3,0},{4,7},{5,6},{6,5},{7,4},{8,11},{9,10},{10,... | collective-permute-start | bytes 491528 | tf_op jit(solution)/shard_map/ppermute | solution.py:199
  65.5 2.9 %collective-permute-start.11 = (bf16[64,1280]{1,0:T(8,128)(2,1)S(1)}, bf16[64,1280]{1,0:T(8,128)(2,1)S(1)}, u32[]{:S(2)}, u32[]{:S(2)}) collective-permute-start(bf16[64,1280]{1,0:T(8,128)(2,1)S(1)} %get-tuple-element.46), channel_id=1, source_target_pairs={{0,2},{1,3},{2,0},{3,1},{4,6},{5,7},{6,4},{7,5},{8,10},{9,11},{10,... | collective-permute-start | bytes 491528 | tf_op jit(solution)/shard_map/ppermute | solution.py:199
  68.4 2.1 %collective-permute-start.12 = (bf16[64,1280]{1,0:T(8,128)(2,1)S(1)}, bf16[64,1280]{1,0:T(8,128)(2,1)S(1)}, u32[]{:S(2)}, u32[]{:S(2)}) collective-permute-start(bf16[64,1280]{1,0:T(8,128)(2,1)S(1)} %get-tuple-element.47), channel_id=1, source_target_pairs={{0,1},{1,0},{2,3},{3,2},{4,5},{5,4},{6,7},{7,6},{8,9},{9,8},{10,11... | collective-permute-start | bytes 491528 | tf_op jit(solution)/shard_map/ppermute | solution.py:199
  71.1 3.5 %collective-permute-done.11.refs_2_ = bf16[64,1280]{1,0:T(8,128)(2,1)S(1)} collective-permute-done((bf16[64,1280]{1,0:T(8,128)(2,1)S(1)}, bf16[64,1280]{1,0:T(8,128)(2,1)S(1)}, u32[]{:S(2)}, u32[]{:S(2)}) %collective-permute-start.11) | collective-permute-done | bytes 163872 | tf_op jit(solution)/shard_map/ppermute | solution.py:199
  76.0 1.9 %collective-permute-start.14 = (bf16[64,4096]{1,0:T(8,128)(2,1)S(1)}, bf16[64,4096]{1,0:T(8,128)(2,1)S(1)}, u32[]{:S(2)}, u32[]{:S(2)}) collective-permute-start(bf16[64,4096]{1,0:T(8,128)(2,1)S(1)} %get-tuple-element.50), channel_id=1, source_target_pairs={{0,4},{4,0},{8,12},{12,8},{16,20},{20,16},{24,28},{28,24},{32,36},... | collective-permute-start | bytes 1572872 | tf_op jit(solution)/shard_map/ppermute | solution.py:224
  77.9 6.2 %collective-permute-start.13 = (bf16[64,4096]{1,0:T(8,128)(2,1)S(1)}, bf16[64,4096]{1,0:T(8,128)(2,1)S(1)}, u32[]{:S(2)}, u32[]{:S(2)}) collective-permute-start(bf16[64,4096]{1,0:T(8,128)(2,1)S(1)} %get-tuple-element.49), channel_id=1, source_target_pairs={{4,8},{8,4},{12,16},{16,12},{20,24},{24,20},{28,32},{32,28},{36,40... | collective-permute-start | bytes 1572872 | tf_op jit(solution)/shard_map/ppermute | solution.py:227
  84.2 1.9 %collective-permute-start.15 = (f32[64,256]{1,0:T(8,128)S(1)}, f32[64,256]{1,0:T(8,128)S(1)}, u32[]{:S(2)}, u32[]{:S(2)}) collective-permute-start(f32[64,256]{1,0:T(8,128)S(1)} %convert_add_fusion), channel_id=1, source_target_pairs={{0,16},{16,0},{32,48},{48,32},{64,80},{80,64},{96,112},{112,96},{1... | collective-permute-start | bytes 196616 | tf_op jit(solution)/shard_map/ppermute | solution.py:210
  86.1 3.4 %collective-permute-done.15 = f32[64,256]{1,0:T(8,128)S(1)} collective-permute-done((f32[64,256]{1,0:T(8,128)S(1)}, f32[64,256]{1,0:T(8,128)S(1)}, u32[]{:S(2)}, u32[]{:S(2)}) %collective-permute-start.15) | collective-permute-done | bytes 65568 | tf_op jit(solution)/shard_map/ppermute | solution.py:210
  89.5 1.9 %collective-permute-start.16 = (f32[64,256]{1,0:T(8,128)S(1)}, f32[64,256]{1,0:T(8,128)S(1)}, u32[]{:S(2)}, u32[]{:S(2)}) collective-permute-start(f32[64,256]{1,0:T(8,128)S(1)} %add.31), channel_id=1, source_target_pairs={{0,32},{16,48},{32,0},{48,16},{64,96},{80,112},{96,64},{112,80},{1... | collective-permute-start | bytes 196616 | tf_op jit(solution)/shard_map/ppermute | solution.py:210
  91.4 4.3 %collective-permute-start.17 = (bf16[64,1024]{1,0:T(8,128)(2,1)S(1)}, bf16[64,1024]{1,0:T(8,128)(2,1)S(1)}, u32[]{:S(2)}, u32[]{:S(2)}) collective-permute-start(bf16[64,1024]{1,0:T(8,128)(2,1)S(1)} %get-tuple-element.54), channel_id=1, source_target_pairs={{0,3},{1,2},{2,1},{3,0},{4,7},{5,6},{6,5},{7,4},{8,11},{9,10},{10,... | collective-permute-start | bytes 393224 | tf_op jit(solution)/shard_map/ppermute | solution.py:199
  95.7 3.0 %collective-permute-start.18 = (bf16[64,1024]{1,0:T(8,128)(2,1)S(1)}, bf16[64,1024]{1,0:T(8,128)(2,1)S(1)}, u32[]{:S(2)}, u32[]{:S(2)}) collective-permute-start(bf16[64,1024]{1,0:T(8,128)(2,1)S(1)} %get-tuple-element.55), channel_id=1, source_target_pairs={{0,2},{1,3},{2,0},{3,1},{4,6},{5,7},{6,4},{7,5},{8,10},{9,11},{10,... | collective-permute-start | bytes 393224 | tf_op jit(solution)/shard_map/ppermute | solution.py:199
  98.7 2.0 %collective-permute-start.19 = (bf16[64,1024]{1,0:T(8,128)(2,1)S(1)}, bf16[64,1024]{1,0:T(8,128)(2,1)S(1)}, u32[]{:S(2)}, u32[]{:S(2)}) collective-permute-start(bf16[64,1024]{1,0:T(8,128)(2,1)S(1)} %get-tuple-element.56), channel_id=1, source_target_pairs={{0,1},{1,0},{2,3},{3,2},{4,5},{5,4},{6,7},{7,6},{8,9},{9,8},{10,11... | collective-permute-start | bytes 393224 | tf_op jit(solution)/shard_map/ppermute | solution.py:199
  103.9 1.9 %collective-permute-start.20 = (bf16[64,4096]{1,0:T(8,128)(2,1)S(1)}, bf16[64,4096]{1,0:T(8,128)(2,1)S(1)}, u32[]{:S(2)}, u32[]{:S(2)}) collective-permute-start(bf16[64,4096]{1,0:T(8,128)(2,1)S(1)} %shard_map.101), channel_id=1, source_target_pairs={{0,4},{4,0},{8,12},{12,8},{16,20},{20,16},{24,28},{28,24},{32,36},... | collective-permute-start | bytes 1572872 | tf_op jit(solution)/shard_map/ppermute | solution.py:224
  105.8 10.4 %collective-permute-start.21 = (bf16[64,4096]{1,0:T(8,128)(2,1)S(1)}, bf16[64,4096]{1,0:T(8,128)(2,1)S(1)}, u32[]{:S(2)}, u32[]{:S(2)}) collective-permute-start(bf16[64,4096]{1,0:T(8,128)(2,1)S(1)} %shard_map.100), channel_id=1, source_target_pairs={{4,8},{8,4},{12,16},{16,12},{20,24},{24,20},{28,32},{32,28},{36,40... | collective-permute-start | bytes 1572872 | tf_op jit(solution)/shard_map/ppermute | solution.py:227
  116.2 2.4 %collective-permute-start.24 = (f32[64,256]{1,0:T(8,128)S(1)}, f32[64,256]{1,0:T(8,128)S(1)}, u32[]{:S(2)}, u32[]{:S(2)}) collective-permute-start(f32[64,256]{1,0:T(8,128)S(1)} %add.32), channel_id=1, source_target_pairs={{0,192},{16,208},{32,224},{48,240},{64,128},{80,144},{96,160},{112... | collective-permute-start | bytes 196616 | tf_op jit(solution)/shard_map/ppermute | solution.py:210
  118.7 1.9 %collective-permute-start.23 = (f32[64,256]{1,0:T(8,128)S(1)}, f32[64,256]{1,0:T(8,128)S(1)}, u32[]{:S(2)}, u32[]{:S(2)}) collective-permute-start(f32[64,256]{1,0:T(8,128)S(1)} %add.32), channel_id=1, source_target_pairs={{0,64},{16,80},{32,96},{48,112},{64,0},{80,16},{96,32},{112,48},{1... | collective-permute-start | bytes 196616 | tf_op jit(solution)/shard_map/ppermute | solution.py:210
  120.6 11.8 %collective-permute-start.22 = (f32[64,256]{1,0:T(8,128)S(1)}, f32[64,256]{1,0:T(8,128)S(1)}, u32[]{:S(2)}, u32[]{:S(2)}) collective-permute-start(f32[64,256]{1,0:T(8,128)S(1)} %add.32), channel_id=1, source_target_pairs={{0,128},{16,144},{32,160},{48,176},{64,192},{80,208},{96,224},{112... | collective-permute-start | bytes 196616 | tf_op jit(solution)/shard_map/ppermute | solution.py:210
  132.4 6.0 %collective-permute-done.24 = f32[64,256]{1,0:T(8,128)S(1)} collective-permute-done((f32[64,256]{1,0:T(8,128)S(1)}, f32[64,256]{1,0:T(8,128)S(1)}, u32[]{:S(2)}, u32[]{:S(2)}) %collective-permute-start.24) | collective-permute-done | bytes 65568 | tf_op jit(solution)/shard_map/ppermute | solution.py:210
  138.4 2.0 %shard_map.102 = (bf16[64,4096]{1,0:T(8,128)(2,1)}, bf16[64,4096]{1,0:T(8,128)(2,1)}) custom-call(bf16[88,128,128]{2,1,0:T(8,128)(2,1)S(1)} %copy-done.1, s32[88]{0:T(128)S(1)} %copy-done.5, s32[88]{0:T(128)S(1)} %copy-done.6, s32[1]{0:T(128)S(6)} %copy.10.count, s32[2]{0:T(128)S(1)} %pad_add_fusion.place, bf16[4,64,1024]{2,1,0:T(8,128)(2,1)S(1)} %get-tuple-element.48.grad, ...), custom_call_target="tpu_custom_call" | custom-call | flops 37748736 | bytes 6030028 | tf_op jit(solution)/shard_map/pallas_call | solution.py:183
  140.5 11.9 %all_to_all.5 = bf16[8,64,256]{2,1,0:T(8,128)(2,1)S(1)} all-to-all(bf16[8,64,256]{2,1,0:T(8,128)(2,1)S(1)} %broadcast_in_dim.3), channel_id=1, replica_groups=mesh['yh'=2,'z'=16,'x'=4,'yl'=2,'core'=2] {'yh','x'}, dimensions={0} | all-to-all | bytes 524288 | tf_op jit(solution)/shard_map/all_to_all | solution.py:205
  (50 shorter events, 17.9 us)
Async XLA Ops:
  0.6 26.6 %collective-permute-start.1 = (bf16[64,4096]{1,0:T(8,128)(2,1)}, bf16[64,4096]{1,0:T(8,128)(2,1)S(1)}, u32[]{:S(2)}, u32[]{:S(2)}) collective-permute-start(bf16[64,4096]{1,0:T(8,128)(2,1)} %bitcast.9), channel_id=1, source_target_pairs={{0,4},{4,0},{8,12},{12,8},{16,20},{20,16},{24,28},{28,24},{32,36},... | collective-permute-start | bytes 1572872 | tf_op jit(solution)/shard_map/ppermute | solution.py:224
  4.6 29.2 %collective-permute-start = (bf16[64,4096]{1,0:T(8,128)(2,1)}, bf16[64,4096]{1,0:T(8,128)(2,1)S(1)}, u32[]{:S(2)}, u32[]{:S(2)}) collective-permute-start(bf16[64,4096]{1,0:T(8,128)(2,1)} %bitcast.10), channel_id=1, source_target_pairs={{4,8},{8,4},{12,16},{16,12},{20,24},{24,20},{28,32},{32,28},{36,40... | collective-permute-start | bytes 1572872 | tf_op jit(solution)/shard_map/ppermute | solution.py:227
  20.6 1.8 %copy-start = (bf16[88,128,128]{2,1,0:T(8,128)(2,1)S(1)}, bf16[88,128,128]{2,1,0:T(8,128)(2,1)}, u32[]{:S(2)}) copy-start(bf16[88,128,128]{2,1,0:T(8,128)(2,1)} %values.15) | copy-start | bytes 8650756
  22.4 1.0 copy-start.2
  23.5 1.0 copy-start.3
  24.5 0.8 copy-start.4
  25.3 0.7 copy-start.5
  25.9 0.7 copy-start.6
  27.2 19.8 %collective-permute-start.3 = (bf16[64,4096]{1,0:T(8,128)(2,1)S(1)}, bf16[64,4096]{1,0:T(8,128)(2,1)S(1)}, u32[]{:S(2)}, u32[]{:S(2)}) collective-permute-start(bf16[64,4096]{1,0:T(8,128)(2,1)S(1)} %collective-permute-done.1.even), channel_id=1, source_target_pairs={{4,8},{8,4},{12,16},{16,12},{20,24},{24,20},{28,32},{32,28},{36,40... | collective-permute-start | bytes 1572872 | tf_op jit(solution)/shard_map/ppermute | solution.py:227
  33.8 13.5 %collective-permute-start.2 = (bf16[64,4096]{1,0:T(8,128)(2,1)S(1)}, bf16[64,4096]{1,0:T(8,128)(2,1)S(1)}, u32[]{:S(2)}, u32[]{:S(2)}) collective-permute-start(bf16[64,4096]{1,0:T(8,128)(2,1)S(1)} %collective-permute-done.odd), channel_id=1, source_target_pairs={{0,4},{4,0},{8,12},{12,8},{16,20},{20,16},{24,28},{28,24},{32,36},... | collective-permute-start | bytes 1572872 | tf_op jit(solution)/shard_map/ppermute | solution.py:224
  35.7 21.0 %collective-permute-start.7 = (bf16[64,1280]{1,0:T(8,128)(2,1)S(1)}, bf16[64,1280]{1,0:T(8,128)(2,1)S(1)}, u32[]{:S(2)}, u32[]{:S(2)}) collective-permute-start(bf16[64,1280]{1,0:T(8,128)(2,1)S(1)} %get-tuple-element.41), channel_id=1, source_target_pairs={{0,3},{1,2},{2,1},{3,0},{4,7},{5,6},{6,5},{7,4},{8,11},{9,10},{10,... | collective-permute-start | bytes 491528 | tf_op jit(solution)/shard_map/ppermute | solution.py:199
  39.8 19.0 %collective-permute-start.8 = (bf16[64,1280]{1,0:T(8,128)(2,1)S(1)}, bf16[64,1280]{1,0:T(8,128)(2,1)S(1)}, u32[]{:S(2)}, u32[]{:S(2)}) collective-permute-start(bf16[64,1280]{1,0:T(8,128)(2,1)S(1)} %get-tuple-element.42), channel_id=1, source_target_pairs={{0,2},{1,3},{2,0},{3,1},{4,6},{5,7},{6,4},{7,5},{8,10},{9,11},{10,... | collective-permute-start | bytes 491528 | tf_op jit(solution)/shard_map/ppermute | solution.py:199
  42.7 16.0 %collective-permute-start.9 = (bf16[64,1280]{1,0:T(8,128)(2,1)S(1)}, bf16[64,1280]{1,0:T(8,128)(2,1)S(1)}, u32[]{:S(2)}, u32[]{:S(2)}) collective-permute-start(bf16[64,1280]{1,0:T(8,128)(2,1)S(1)} %get-tuple-element.43), channel_id=1, source_target_pairs={{0,1},{1,0},{2,3},{3,2},{4,5},{5,4},{6,7},{7,6},{8,9},{9,8},{10,11... | collective-permute-start | bytes 491528 | tf_op jit(solution)/shard_map/ppermute | solution.py:199
  45.8 28.9 %copy-start.1 = (bf16[88,128,128]{2,1,0:T(8,128)(2,1)S(1)}, bf16[88,128,128]{2,1,0:T(8,128)(2,1)}, u32[]{:S(2)}) copy-start(bf16[88,128,128]{2,1,0:T(8,128)(2,1)} %values.15) | copy-start | bytes 8650756
  48.8 9.9 %collective-permute-start.4 = (bf16[64,1024]{1,0:T(8,128)(2,1)S(1)}, bf16[64,1024]{1,0:T(8,128)(2,1)S(1)}, u32[]{:S(2)}, u32[]{:S(2)}) collective-permute-start(bf16[64,1024]{1,0:T(8,128)(2,1)S(1)} %get-tuple-element.38), channel_id=1, source_target_pairs={{0,3},{1,2},{2,1},{3,0},{4,7},{5,6},{6,5},{7,4},{8,11},{9,10},{10,... | collective-permute-start | bytes 393224 | tf_op jit(solution)/shard_map/ppermute | solution.py:199
  53.8 7.2 %collective-permute-start.5 = (bf16[64,1024]{1,0:T(8,128)(2,1)S(1)}, bf16[64,1024]{1,0:T(8,128)(2,1)S(1)}, u32[]{:S(2)}, u32[]{:S(2)}) collective-permute-start(bf16[64,1024]{1,0:T(8,128)(2,1)S(1)} %get-tuple-element.39), channel_id=1, source_target_pairs={{0,2},{1,3},{2,0},{3,1},{4,6},{5,7},{6,4},{7,5},{8,10},{9,11},{10,... | collective-permute-start | bytes 393224 | tf_op jit(solution)/shard_map/ppermute | solution.py:199
  56.8 4.2 %collective-permute-start.6 = (bf16[64,1024]{1,0:T(8,128)(2,1)S(1)}, bf16[64,1024]{1,0:T(8,128)(2,1)S(1)}, u32[]{:S(2)}, u32[]{:S(2)}) collective-permute-start(bf16[64,1024]{1,0:T(8,128)(2,1)S(1)} %get-tuple-element.40), channel_id=1, source_target_pairs={{0,1},{1,0},{2,3},{3,2},{4,5},{5,4},{6,7},{7,6},{8,9},{9,8},{10,11... | collective-permute-start | bytes 393224 | tf_op jit(solution)/shard_map/ppermute | solution.py:199
  62.6 8.5 %collective-permute-start.10 = (bf16[64,1280]{1,0:T(8,128)(2,1)S(1)}, bf16[64,1280]{1,0:T(8,128)(2,1)S(1)}, u32[]{:S(2)}, u32[]{:S(2)}) collective-permute-start(bf16[64,1280]{1,0:T(8,128)(2,1)S(1)} %get-tuple-element.45), channel_id=1, source_target_pairs={{0,3},{1,2},{2,1},{3,0},{4,7},{5,6},{6,5},{7,4},{8,11},{9,10},{10,... | collective-permute-start | bytes 491528 | tf_op jit(solution)/shard_map/ppermute | solution.py:199
  65.5 9.1 %collective-permute-start.11 = (bf16[64,1280]{1,0:T(8,128)(2,1)S(1)}, bf16[64,1280]{1,0:T(8,128)(2,1)S(1)}, u32[]{:S(2)}, u32[]{:S(2)}) collective-permute-start(bf16[64,1280]{1,0:T(8,128)(2,1)S(1)} %get-tuple-element.46), channel_id=1, source_target_pairs={{0,2},{1,3},{2,0},{3,1},{4,6},{5,7},{6,4},{7,5},{8,10},{9,11},{10,... | collective-permute-start | bytes 491528 | tf_op jit(solution)/shard_map/ppermute | solution.py:199
  68.4 6.2 %collective-permute-start.12 = (bf16[64,1280]{1,0:T(8,128)(2,1)S(1)}, bf16[64,1280]{1,0:T(8,128)(2,1)S(1)}, u32[]{:S(2)}, u32[]{:S(2)}) collective-permute-start(bf16[64,1280]{1,0:T(8,128)(2,1)S(1)} %get-tuple-element.47), channel_id=1, source_target_pairs={{0,1},{1,0},{2,3},{3,2},{4,5},{5,4},{6,7},{7,6},{8,9},{9,8},{10,11... | collective-permute-start | bytes 491528 | tf_op jit(solution)/shard_map/ppermute | solution.py:199
  76.0 24.8 %collective-permute-start.14 = (bf16[64,4096]{1,0:T(8,128)(2,1)S(1)}, bf16[64,4096]{1,0:T(8,128)(2,1)S(1)}, u32[]{:S(2)}, u32[]{:S(2)}) collective-permute-start(bf16[64,4096]{1,0:T(8,128)(2,1)S(1)} %get-tuple-element.50), channel_id=1, source_target_pairs={{0,4},{4,0},{8,12},{12,8},{16,20},{20,16},{24,28},{28,24},{32,36},... | collective-permute-start | bytes 1572872 | tf_op jit(solution)/shard_map/ppermute | solution.py:224
  77.9 25.1 %collective-permute-start.13 = (bf16[64,4096]{1,0:T(8,128)(2,1)S(1)}, bf16[64,4096]{1,0:T(8,128)(2,1)S(1)}, u32[]{:S(2)}, u32[]{:S(2)}) collective-permute-start(bf16[64,4096]{1,0:T(8,128)(2,1)S(1)} %get-tuple-element.49), channel_id=1, source_target_pairs={{4,8},{8,4},{12,16},{16,12},{20,24},{24,20},{28,32},{32,28},{36,40... | collective-permute-start | bytes 1572872 | tf_op jit(solution)/shard_map/ppermute | solution.py:227
  84.2 5.3 %collective-permute-start.15 = (f32[64,256]{1,0:T(8,128)S(1)}, f32[64,256]{1,0:T(8,128)S(1)}, u32[]{:S(2)}, u32[]{:S(2)}) collective-permute-start(f32[64,256]{1,0:T(8,128)S(1)} %convert_add_fusion), channel_id=1, source_target_pairs={{0,16},{16,0},{32,48},{48,32},{64,80},{80,64},{96,112},{112,96},{1... | collective-permute-start | bytes 196616 | tf_op jit(solution)/shard_map/ppermute | solution.py:210
  89.5 9.2 %collective-permute-start.16 = (f32[64,256]{1,0:T(8,128)S(1)}, f32[64,256]{1,0:T(8,128)S(1)}, u32[]{:S(2)}, u32[]{:S(2)}) collective-permute-start(f32[64,256]{1,0:T(8,128)S(1)} %add.31), channel_id=1, source_target_pairs={{0,32},{16,48},{32,0},{48,16},{64,96},{80,112},{96,64},{112,80},{1... | collective-permute-start | bytes 196616 | tf_op jit(solution)/shard_map/ppermute | solution.py:210
  91.4 10.3 %collective-permute-start.17 = (bf16[64,1024]{1,0:T(8,128)(2,1)S(1)}, bf16[64,1024]{1,0:T(8,128)(2,1)S(1)}, u32[]{:S(2)}, u32[]{:S(2)}) collective-permute-start(bf16[64,1024]{1,0:T(8,128)(2,1)S(1)} %get-tuple-element.54), channel_id=1, source_target_pairs={{0,3},{1,2},{2,1},{3,0},{4,7},{5,6},{6,5},{7,4},{8,11},{9,10},{10,... | collective-permute-start | bytes 393224 | tf_op jit(solution)/shard_map/ppermute | solution.py:199
  95.7 7.2 %collective-permute-start.18 = (bf16[64,1024]{1,0:T(8,128)(2,1)S(1)}, bf16[64,1024]{1,0:T(8,128)(2,1)S(1)}, u32[]{:S(2)}, u32[]{:S(2)}) collective-permute-start(bf16[64,1024]{1,0:T(8,128)(2,1)S(1)} %get-tuple-element.55), channel_id=1, source_target_pairs={{0,2},{1,3},{2,0},{3,1},{4,6},{5,7},{6,4},{7,5},{8,10},{9,11},{10,... | collective-permute-start | bytes 393224 | tf_op jit(solution)/shard_map/ppermute | solution.py:199
  98.7 4.2 %collective-permute-start.19 = (bf16[64,1024]{1,0:T(8,128)(2,1)S(1)}, bf16[64,1024]{1,0:T(8,128)(2,1)S(1)}, u32[]{:S(2)}, u32[]{:S(2)}) collective-permute-start(bf16[64,1024]{1,0:T(8,128)(2,1)S(1)} %get-tuple-element.56), channel_id=1, source_target_pairs={{0,1},{1,0},{2,3},{3,2},{4,5},{5,4},{6,7},{7,6},{8,9},{9,8},{10,11... | collective-permute-start | bytes 393224 | tf_op jit(solution)/shard_map/ppermute | solution.py:199
  103.9 34.5 %collective-permute-start.20 = (bf16[64,4096]{1,0:T(8,128)(2,1)S(1)}, bf16[64,4096]{1,0:T(8,128)(2,1)S(1)}, u32[]{:S(2)}, u32[]{:S(2)}) collective-permute-start(bf16[64,4096]{1,0:T(8,128)(2,1)S(1)} %shard_map.101), channel_id=1, source_target_pairs={{0,4},{4,0},{8,12},{12,8},{16,20},{20,16},{24,28},{28,24},{32,36},... | collective-permute-start | bytes 1572872 | tf_op jit(solution)/shard_map/ppermute | solution.py:224
  105.8 32.6 %collective-permute-start.21 = (bf16[64,4096]{1,0:T(8,128)(2,1)S(1)}, bf16[64,4096]{1,0:T(8,128)(2,1)S(1)}, u32[]{:S(2)}, u32[]{:S(2)}) collective-permute-start(bf16[64,4096]{1,0:T(8,128)(2,1)S(1)} %shard_map.100), channel_id=1, source_target_pairs={{4,8},{8,4},{12,16},{16,12},{20,24},{24,20},{28,32},{32,28},{36,40... | collective-permute-start | bytes 1572872 | tf_op jit(solution)/shard_map/ppermute | solution.py:227
  116.2 22.2 %collective-permute-start.24 = (f32[64,256]{1,0:T(8,128)S(1)}, f32[64,256]{1,0:T(8,128)S(1)}, u32[]{:S(2)}, u32[]{:S(2)}) collective-permute-start(f32[64,256]{1,0:T(8,128)S(1)} %add.32), channel_id=1, source_target_pairs={{0,192},{16,208},{32,224},{48,240},{64,128},{80,144},{96,160},{112... | collective-permute-start | bytes 196616 | tf_op jit(solution)/shard_map/ppermute | solution.py:210
  118.7 19.7 %collective-permute-start.23 = (f32[64,256]{1,0:T(8,128)S(1)}, f32[64,256]{1,0:T(8,128)S(1)}, u32[]{:S(2)}, u32[]{:S(2)}) collective-permute-start(f32[64,256]{1,0:T(8,128)S(1)} %add.32), channel_id=1, source_target_pairs={{0,64},{16,80},{32,96},{48,112},{64,0},{80,16},{96,32},{112,48},{1... | collective-permute-start | bytes 196616 | tf_op jit(solution)/shard_map/ppermute | solution.py:210
  120.6 17.8 %collective-permute-start.22 = (f32[64,256]{1,0:T(8,128)S(1)}, f32[64,256]{1,0:T(8,128)S(1)}, u32[]{:S(2)}, u32[]{:S(2)}) collective-permute-start(f32[64,256]{1,0:T(8,128)S(1)} %add.32), channel_id=1, source_target_pairs={{0,128},{16,144},{32,160},{48,176},{64,192},{80,208},{96,224},{112... | collective-permute-start | bytes 196616 | tf_op jit(solution)/shard_map/ppermute | solution.py:210

commit v12 on v11

--- a/solution.py
+++ b/solution.py
@@ -292,10 +292,10 @@
         scratch=[total, total],
         flops=36 * tile_flops,
     )
+    weight_grad = weight_grad + paired(weight_grad, "z", 1)
+    even_far, odd_far, weight_grad = lax.optimization_barrier((even_far, odd_far, weight_grad))
     even_in = even_swap(even_far)
     odd_in = odd_swap(odd_far)
-    weight_grad, _ = lax.optimization_barrier((weight_grad, even_far))
-    weight_grad = weight_grad + paired(weight_grad, "z", 1)
     weight_grad = weight_grad + paired(weight_grad, "z", 2)
 
     def near_terms(offset, sign, received):

time: 155 us -> 156 us (level)
  waiting for transfers between devices: 18.5 us -> 22.9 us
  starting transfers between devices: 103 us -> 99.8 us
    ppermute x12, waiting for transfers between devices: 7.63 us -> 12.7 us  [swapped(): lax.ppermute(value, COLS, pairs(step))]
    ppermute x4, starting transfers between devices: 37 us -> 33.9 us  [odd_swap(): return lax.ppermute(value, ROWS, odd_pairs)]
    ppermute x5, waiting for transfers between devices: 9.34 us -> 7.62 us  [paired(): lax.ppermute(value, axis, [(source, source ^ step) for source in range(co...]
  transfers between devices with their start and end apart: 25 -> 25, of which waited for: 8 -> 10; matrix products, arithmetic and copies ran while one was open for 0% -> 0% of each run, Pallas kernels for 4% -> 5%
where the time goes in v12:
time: 156 us; the launch traced here: 155 us
  starting transfers between devices  99.8 us (64%)
  waiting for transfers between devices  22.9 us (15%)
  blocking collectives  12.3 us (8%)
  Pallas kernels  11.6 us (7%)
  local copies, waits for them, and re-layouts  5.99 us (4%)
  between operations  1.65 us (1%)
    ppermute x12, starting transfers between devices, swapped(): lax.ppermute(value, COLS, pairs(step))  36.1 us
    ppermute x4, starting transfers between devices, odd_swap(): return lax.ppermute(value, ROWS, odd_pairs)  33.9 us
    ppermute x5, starting transfers between devices, paired(): lax.ppermute(value, axis, [(source, source ^ step) for source in range(co...  20 us
    ppermute x12, waiting for transfers between devices, swapped(): lax.ppermute(value, COLS, pairs(step))  12.7 us
    all_to_all x1, blocking collectives, summed(): lax.all_to_all(copies, axis, 0, 0, tiled=True).astype(jnp.float32).sum(0)  12.3 us
    pallas_call x9, Pallas kernels, call(): pl.pallas_call(kernel, out_shape=outs, in_specs=specs, out_specs=[VMEM] *...  11.6 us
    ppermute x4, starting transfers between devices, even_swap(): return lax.ppermute(value, ROWS, even_pairs)  9.72 us
    ppermute x5, waiting for transfers between devices, paired(): lax.ppermute(value, axis, [(source, source ^ step) for source in range(co...  7.62 us
  transfers between devices with their start and end apart: 25, of which 10 were waited for; matrix products, arithmetic and copies ran while one was open for 0% of the time, Pallas kernels for 5%

profile of v12, /device:TPU:1, one launch (start us, length us, event | category | flops | bytes accessed | tf_op | source)
XLA Modules:
  0.0 155.1 jit_solution(2063504753915158694)
XLA Ops:
  0.6 4.0 %collective-permute-start.1 = (bf16[64,4096]{1,0:T(8,128)(2,1)}, bf16[64,4096]{1,0:T(8,128)(2,1)S(1)}, u32[]{:S(2)}, u32[]{:S(2)}) collective-permute-start(bf16[64,4096]{1,0:T(8,128)(2,1)} %bitcast.9), channel_id=1, source_target_pairs={{0,4},{4,0},{8,12},{12,8},{16,20},{20,16},{24,28},{28,24},{32,36},... | collective-permute-start | bytes 1572872 | tf_op jit(solution)/shard_map/ppermute | solution.py:224
  4.6 15.3 %collective-permute-start = (bf16[64,4096]{1,0:T(8,128)(2,1)}, bf16[64,4096]{1,0:T(8,128)(2,1)S(1)}, u32[]{:S(2)}, u32[]{:S(2)}) collective-permute-start(bf16[64,4096]{1,0:T(8,128)(2,1)} %bitcast.10), channel_id=1, source_target_pairs={{4,8},{8,4},{12,16},{16,12},{20,24},{24,20},{28,32},{32,28},{36,40... | collective-permute-start | bytes 1572872 | tf_op jit(solution)/shard_map/ppermute | solution.py:227
  27.2 5.1 %collective-permute-start.3 = (bf16[64,4096]{1,0:T(8,128)(2,1)S(1)}, bf16[64,4096]{1,0:T(8,128)(2,1)S(1)}, u32[]{:S(2)}, u32[]{:S(2)}) collective-permute-start(bf16[64,4096]{1,0:T(8,128)(2,1)S(1)} %collective-permute-done.1.even), channel_id=1, source_target_pairs={{4,8},{8,4},{12,16},{16,12},{20,24},{24,20},{28,32},{32,28},{36,40... | collective-permute-start | bytes 1572872 | tf_op jit(solution)/shard_map/ppermute | solution.py:227
  33.8 1.9 %collective-permute-start.2 = (bf16[64,4096]{1,0:T(8,128)(2,1)S(1)}, bf16[64,4096]{1,0:T(8,128)(2,1)S(1)}, u32[]{:S(2)}, u32[]{:S(2)}) collective-permute-start(bf16[64,4096]{1,0:T(8,128)(2,1)S(1)} %collective-permute-done.odd), channel_id=1, source_target_pairs={{0,4},{4,0},{8,12},{12,8},{16,20},{20,16},{24,28},{28,24},{32,36},... | collective-permute-start | bytes 1572872 | tf_op jit(solution)/shard_map/ppermute | solution.py:224
  35.7 4.0 %collective-permute-start.7 = (bf16[64,1280]{1,0:T(8,128)(2,1)S(1)}, bf16[64,1280]{1,0:T(8,128)(2,1)S(1)}, u32[]{:S(2)}, u32[]{:S(2)}) collective-permute-start(bf16[64,1280]{1,0:T(8,128)(2,1)S(1)} %get-tuple-element.43), channel_id=1, source_target_pairs={{0,3},{1,2},{2,1},{3,0},{4,7},{5,6},{6,5},{7,4},{8,11},{9,10},{10,... | collective-permute-start | bytes 491528 | tf_op jit(solution)/shard_map/ppermute | solution.py:199
  39.8 3.0 %collective-permute-start.8 = (bf16[64,1280]{1,0:T(8,128)(2,1)S(1)}, bf16[64,1280]{1,0:T(8,128)(2,1)S(1)}, u32[]{:S(2)}, u32[]{:S(2)}) collective-permute-start(bf16[64,1280]{1,0:T(8,128)(2,1)S(1)} %get-tuple-element.44), channel_id=1, source_target_pairs={{0,2},{1,3},{2,0},{3,1},{4,6},{5,7},{6,4},{7,5},{8,10},{9,11},{10,... | collective-permute-start | bytes 491528 | tf_op jit(solution)/shard_map/ppermute | solution.py:199
  42.7 1.9 %collective-permute-start.9 = (bf16[64,1280]{1,0:T(8,128)(2,1)S(1)}, bf16[64,1280]{1,0:T(8,128)(2,1)S(1)}, u32[]{:S(2)}, u32[]{:S(2)}) collective-permute-start(bf16[64,1280]{1,0:T(8,128)(2,1)S(1)} %get-tuple-element.45), channel_id=1, source_target_pairs={{0,1},{1,0},{2,3},{3,2},{4,5},{5,4},{6,7},{7,6},{8,9},{9,8},{10,11... | collective-permute-start | bytes 491528 | tf_op jit(solution)/shard_map/ppermute | solution.py:199
  48.8 4.9 %collective-permute-start.4 = (bf16[64,1024]{1,0:T(8,128)(2,1)S(1)}, bf16[64,1024]{1,0:T(8,128)(2,1)S(1)}, u32[]{:S(2)}, u32[]{:S(2)}) collective-permute-start(bf16[64,1024]{1,0:T(8,128)(2,1)S(1)} %get-tuple-element.40), channel_id=1, source_target_pairs={{0,3},{1,2},{2,1},{3,0},{4,7},{5,6},{6,5},{7,4},{8,11},{9,10},{10,... | collective-permute-start | bytes 393224 | tf_op jit(solution)/shard_map/ppermute | solution.py:199
  53.8 3.0 %collective-permute-start.5 = (bf16[64,1024]{1,0:T(8,128)(2,1)S(1)}, bf16[64,1024]{1,0:T(8,128)(2,1)S(1)}, u32[]{:S(2)}, u32[]{:S(2)}) collective-permute-start(bf16[64,1024]{1,0:T(8,128)(2,1)S(1)} %get-tuple-element.41), channel_id=1, source_target_pairs={{0,2},{1,3},{2,0},{3,1},{4,6},{5,7},{6,4},{7,5},{8,10},{9,11},{10,... | collective-permute-start | bytes 393224 | tf_op jit(solution)/shard_map/ppermute | solution.py:199
  56.8 1.9 %collective-permute-start.6 = (bf16[64,1024]{1,0:T(8,128)(2,1)S(1)}, bf16[64,1024]{1,0:T(8,128)(2,1)S(1)}, u32[]{:S(2)}, u32[]{:S(2)}) collective-permute-start(bf16[64,1024]{1,0:T(8,128)(2,1)S(1)} %get-tuple-element.42), channel_id=1, source_target_pairs={{0,1},{1,0},{2,3},{3,2},{4,5},{5,4},{6,7},{7,6},{8,9},{9,8},{10,11... | collective-permute-start | bytes 393224 | tf_op jit(solution)/shard_map/ppermute | solution.py:199
  58.7 2.3 %collective-permute-done.5.refs_2_ = bf16[64,1024]{1,0:T(8,128)(2,1)S(1)} collective-permute-done((bf16[64,1024]{1,0:T(8,128)(2,1)S(1)}, bf16[64,1024]{1,0:T(8,128)(2,1)S(1)}, u32[]{:S(2)}, u32[]{:S(2)}) %collective-permute-start.5) | collective-permute-done | bytes 131104 | tf_op jit(solution)/shard_map/ppermute | solution.py:199
  62.6 2.8 %collective-permute-start.10 = (bf16[64,1280]{1,0:T(8,128)(2,1)S(1)}, bf16[64,1280]{1,0:T(8,128)(2,1)S(1)}, u32[]{:S(2)}, u32[]{:S(2)}) collective-permute-start(bf16[64,1280]{1,0:T(8,128)(2,1)S(1)} %get-tuple-element.47), channel_id=1, source_target_pairs={{0,3},{1,2},{2,1},{3,0},{4,7},{5,6},{6,5},{7,4},{8,11},{9,10},{10,... | collective-permute-start | bytes 491528 | tf_op jit(solution)/shard_map/ppermute | solution.py:199
  65.5 2.9 %collective-permute-start.11 = (bf16[64,1280]{1,0:T(8,128)(2,1)S(1)}, bf16[64,1280]{1,0:T(8,128)(2,1)S(1)}, u32[]{:S(2)}, u32[]{:S(2)}) collective-permute-start(bf16[64,1280]{1,0:T(8,128)(2,1)S(1)} %get-tuple-element.48), channel_id=1, source_target_pairs={{0,2},{1,3},{2,0},{3,1},{4,6},{5,7},{6,4},{7,5},{8,10},{9,11},{10,... | collective-permute-start | bytes 491528 | tf_op jit(solution)/shard_map/ppermute | solution.py:199
  68.4 2.1 %collective-permute-start.12 = (bf16[64,1280]{1,0:T(8,128)(2,1)S(1)}, bf16[64,1280]{1,0:T(8,128)(2,1)S(1)}, u32[]{:S(2)}, u32[]{:S(2)}) collective-permute-start(bf16[64,1280]{1,0:T(8,128)(2,1)S(1)} %get-tuple-element.49), channel_id=1, source_target_pairs={{0,1},{1,0},{2,3},{3,2},{4,5},{5,4},{6,7},{7,6},{8,9},{9,8},{10,11... | collective-permute-start | bytes 491528 | tf_op jit(solution)/shard_map/ppermute | solution.py:199
  71.1 3.5 %collective-permute-done.11.refs_2_ = bf16[64,1280]{1,0:T(8,128)(2,1)S(1)} collective-permute-done((bf16[64,1280]{1,0:T(8,128)(2,1)S(1)}, bf16[64,1280]{1,0:T(8,128)(2,1)S(1)}, u32[]{:S(2)}, u32[]{:S(2)}) %collective-permute-start.11) | collective-permute-done | bytes 163872 | tf_op jit(solution)/shard_map/ppermute | solution.py:199
  74.6 1.9 %collective-permute-start.13 = (f32[64,256]{1,0:T(8,128)S(1)}, f32[64,256]{1,0:T(8,128)S(1)}, u32[]{:S(2)}, u32[]{:S(2)}) collective-permute-start(f32[64,256]{1,0:T(8,128)S(1)} %convert_add_fusion), channel_id=1, source_target_pairs={{0,16},{16,0},{32,48},{48,32},{64,80},{80,64},{96,112},{112,96},{1... | collective-permute-start | bytes 196616 | tf_op jit(solution)/shard_map/ppermute | solution.py:210
  79.7 1.9 %collective-permute-start.15 = (bf16[64,4096]{1,0:T(8,128)(2,1)S(1)}, bf16[64,4096]{1,0:T(8,128)(2,1)S(1)}, u32[]{:S(2)}, u32[]{:S(2)}) collective-permute-start(bf16[64,4096]{1,0:T(8,128)(2,1)S(1)} %get-tuple-element.54), channel_id=1, source_target_pairs={{0,4},{4,0},{8,12},{12,8},{16,20},{20,16},{24,28},{28,24},{32,36},... | collective-permute-start | bytes 1572872 | tf_op jit(solution)/shard_map/ppermute | solution.py:224
  81.6 6.2 %collective-permute-start.14 = (bf16[64,4096]{1,0:T(8,128)(2,1)S(1)}, bf16[64,4096]{1,0:T(8,128)(2,1)S(1)}, u32[]{:S(2)}, u32[]{:S(2)}) collective-permute-start(bf16[64,4096]{1,0:T(8,128)(2,1)S(1)} %get-tuple-element.53), channel_id=1, source_target_pairs={{4,8},{8,4},{12,16},{16,12},{20,24},{24,20},{28,32},{32,28},{36,40... | collective-permute-start | bytes 1572872 | tf_op jit(solution)/shard_map/ppermute | solution.py:227
  87.9 1.9 %collective-permute-start.16 = (f32[64,256]{1,0:T(8,128)S(1)}, f32[64,256]{1,0:T(8,128)S(1)}, u32[]{:S(2)}, u32[]{:S(2)}) collective-permute-start(f32[64,256]{1,0:T(8,128)S(1)} %add.31), channel_id=1, source_target_pairs={{0,32},{16,48},{32,0},{48,16},{64,96},{80,112},{96,64},{112,80},{1... | collective-permute-start | bytes 196616 | tf_op jit(solution)/shard_map/ppermute | solution.py:210
  89.8 4.6 %collective-permute-start.17 = (bf16[64,1024]{1,0:T(8,128)(2,1)S(1)}, bf16[64,1024]{1,0:T(8,128)(2,1)S(1)}, u32[]{:S(2)}, u32[]{:S(2)}) collective-permute-start(bf16[64,1024]{1,0:T(8,128)(2,1)S(1)} %get-tuple-element.58), channel_id=1, source_target_pairs={{0,3},{1,2},{2,1},{3,0},{4,7},{5,6},{6,5},{7,4},{8,11},{9,10},{10,... | collective-permute-start | bytes 393224 | tf_op jit(solution)/shard_map/ppermute | solution.py:199
  94.4 3.0 %collective-permute-start.18 = (bf16[64,1024]{1,0:T(8,128)(2,1)S(1)}, bf16[64,1024]{1,0:T(8,128)(2,1)S(1)}, u32[]{:S(2)}, u32[]{:S(2)}) collective-permute-start(bf16[64,1024]{1,0:T(8,128)(2,1)S(1)} %get-tuple-element.59), channel_id=1, source_target_pairs={{0,2},{1,3},{2,0},{3,1},{4,6},{5,7},{6,4},{7,5},{8,10},{9,11},{10,... | collective-permute-start | bytes 393224 | tf_op jit(solution)/shard_map/ppermute | solution.py:199
  97.4 1.9 %collective-permute-start.19 = (bf16[64,1024]{1,0:T(8,128)(2,1)S(1)}, bf16[64,1024]{1,0:T(8,128)(2,1)S(1)}, u32[]{:S(2)}, u32[]{:S(2)}) collective-permute-start(bf16[64,1024]{1,0:T(8,128)(2,1)S(1)} %get-tuple-element.60), channel_id=1, source_target_pairs={{0,1},{1,0},{2,3},{3,2},{4,5},{5,4},{6,7},{7,6},{8,9},{9,8},{10,11... | collective-permute-start | bytes 393224 | tf_op jit(solution)/shard_map/ppermute | solution.py:199
  100.3 3.5 %collective-permute-done.17.refs_1_ = bf16[64,1024]{1,0:T(8,128)(2,1)S(1)} collective-permute-done((bf16[64,1024]{1,0:T(8,128)(2,1)S(1)}, bf16[64,1024]{1,0:T(8,128)(2,1)S(1)}, u32[]{:S(2)}, u32[]{:S(2)}) %collective-permute-start.17) | collective-permute-done | bytes 131104 | tf_op jit(solution)/shard_map/ppermute | solution.py:199
  103.8 2.8 %collective-permute-done.18.refs_2_ = bf16[64,1024]{1,0:T(8,128)(2,1)S(1)} collective-permute-done((bf16[64,1024]{1,0:T(8,128)(2,1)S(1)}, bf16[64,1024]{1,0:T(8,128)(2,1)S(1)}, u32[]{:S(2)}, u32[]{:S(2)}) %collective-permute-start.18) | collective-permute-done | bytes 131104 | tf_op jit(solution)/shard_map/ppermute | solution.py:199
  107.6 1.9 %collective-permute-start.20 = (bf16[64,4096]{1,0:T(8,128)(2,1)S(1)}, bf16[64,4096]{1,0:T(8,128)(2,1)S(1)}, u32[]{:S(2)}, u32[]{:S(2)}) collective-permute-start(bf16[64,4096]{1,0:T(8,128)(2,1)S(1)} %shard_map.101), channel_id=1, source_target_pairs={{0,4},{4,0},{8,12},{12,8},{16,20},{20,16},{24,28},{28,24},{32,36},... | collective-permute-start | bytes 1572872 | tf_op jit(solution)/shard_map/ppermute | solution.py:224
  109.5 7.3 %collective-permute-start.21 = (bf16[64,4096]{1,0:T(8,128)(2,1)S(1)}, bf16[64,4096]{1,0:T(8,128)(2,1)S(1)}, u32[]{:S(2)}, u32[]{:S(2)}) collective-permute-start(bf16[64,4096]{1,0:T(8,128)(2,1)S(1)} %shard_map.100), channel_id=1, source_target_pairs={{4,8},{8,4},{12,16},{16,12},{20,24},{24,20},{28,32},{32,28},{36,40... | collective-permute-start | bytes 1572872 | tf_op jit(solution)/shard_map/ppermute | solution.py:227
  116.8 1.9 %collective-permute-start.24 = (f32[64,256]{1,0:T(8,128)S(1)}, f32[64,256]{1,0:T(8,128)S(1)}, u32[]{:S(2)}, u32[]{:S(2)}) collective-permute-start(f32[64,256]{1,0:T(8,128)S(1)} %add.32), channel_id=1, source_target_pairs={{0,192},{16,208},{32,224},{48,240},{64,128},{80,144},{96,160},{112... | collective-permute-start | bytes 196616 | tf_op jit(solution)/shard_map/ppermute | solution.py:210
  118.7 1.9 %collective-permute-start.23 = (f32[64,256]{1,0:T(8,128)S(1)}, f32[64,256]{1,0:T(8,128)S(1)}, u32[]{:S(2)}, u32[]{:S(2)}) collective-permute-start(f32[64,256]{1,0:T(8,128)S(1)} %add.32), channel_id=1, source_target_pairs={{0,64},{16,80},{32,96},{48,112},{64,0},{80,16},{96,32},{112,48},{1... | collective-permute-start | bytes 196616 | tf_op jit(solution)/shard_map/ppermute | solution.py:210
  120.7 12.3 %collective-permute-start.22 = (f32[64,256]{1,0:T(8,128)S(1)}, f32[64,256]{1,0:T(8,128)S(1)}, u32[]{:S(2)}, u32[]{:S(2)}) collective-permute-start(f32[64,256]{1,0:T(8,128)S(1)} %add.32), channel_id=1, source_target_pairs={{0,128},{16,144},{32,160},{48,176},{64,192},{80,208},{96,224},{112... | collective-permute-start | bytes 196616 | tf_op jit(solution)/shard_map/ppermute | solution.py:210
  133.0 5.9 %collective-permute-done.24 = f32[64,256]{1,0:T(8,128)S(1)} collective-permute-done((f32[64,256]{1,0:T(8,128)S(1)}, f32[64,256]{1,0:T(8,128)S(1)}, u32[]{:S(2)}, u32[]{:S(2)}) %collective-permute-start.24) | collective-permute-done | bytes 65568 | tf_op jit(solution)/shard_map/ppermute | solution.py:210
  140.1 2.0 %shard_map.102 = (bf16[64,4096]{1,0:T(8,128)(2,1)}, bf16[64,4096]{1,0:T(8,128)(2,1)}) custom-call(bf16[88,128,128]{2,1,0:T(8,128)(2,1)S(1)} %copy-done.1, s32[88]{0:T(128)S(1)} %copy-done.5, s32[88]{0:T(128)S(1)} %copy-done.6, s32[1]{0:T(128)S(6)} %copy.10.count, s32[2]{0:T(128)S(1)} %pad_add_fusion.place, bf16[4,64,1024]{2,1,0:T(8,128)(2,1)S(1)} %get-tuple-element.50.grad, ...), custom_call_target="tpu_custom_call" | custom-call | flops 37748736 | bytes 6030028 | tf_op jit(solution)/shard_map/pallas_call | solution.py:183
  142.1 12.3 %all_to_all.5 = bf16[8,64,256]{2,1,0:T(8,128)(2,1)S(1)} all-to-all(bf16[8,64,256]{2,1,0:T(8,128)(2,1)S(1)} %broadcast_in_dim.3), channel_id=1, replica_groups=mesh['yh'=2,'z'=16,'x'=4,'yl'=2,'core'=2] {'yh','x'}, dimensions={0} | all-to-all | bytes 524288 | tf_op jit(solution)/shard_map/all_to_all | solution.py:205
  (50 shorter events, 21.3 us)
Async XLA Ops:
  0.6 26.6 %collective-permute-start.1 = (bf16[64,4096]{1,0:T(8,128)(2,1)}, bf16[64,4096]{1,0:T(8,128)(2,1)S(1)}, u32[]{:S(2)}, u32[]{:S(2)}) collective-permute-start(bf16[64,4096]{1,0:T(8,128)(2,1)} %bitcast.9), channel_id=1, source_target_pairs={{0,4},{4,0},{8,12},{12,8},{16,20},{20,16},{24,28},{28,24},{32,36},... | collective-permute-start | bytes 1572872 | tf_op jit(solution)/shard_map/ppermute | solution.py:224
  4.6 29.2 %collective-permute-start = (bf16[64,4096]{1,0:T(8,128)(2,1)}, bf16[64,4096]{1,0:T(8,128)(2,1)S(1)}, u32[]{:S(2)}, u32[]{:S(2)}) collective-permute-start(bf16[64,4096]{1,0:T(8,128)(2,1)} %bitcast.10), channel_id=1, source_target_pairs={{4,8},{8,4},{12,16},{16,12},{20,24},{24,20},{28,32},{32,28},{36,40... | collective-permute-start | bytes 1572872 | tf_op jit(solution)/shard_map/ppermute | solution.py:227
  20.6 1.8 %copy-start = (bf16[88,128,128]{2,1,0:T(8,128)(2,1)S(1)}, bf16[88,128,128]{2,1,0:T(8,128)(2,1)}, u32[]{:S(2)}) copy-start(bf16[88,128,128]{2,1,0:T(8,128)(2,1)} %values.15) | copy-start | bytes 8650756
  22.4 1.0 copy-start.2
  23.5 1.0 copy-start.3
  24.5 0.8 copy-start.4
  25.3 0.7 copy-start.5
  25.9 0.7 copy-start.6
  27.2 19.8 %collective-permute-start.3 = (bf16[64,4096]{1,0:T(8,128)(2,1)S(1)}, bf16[64,4096]{1,0:T(8,128)(2,1)S(1)}, u32[]{:S(2)}, u32[]{:S(2)}) collective-permute-start(bf16[64,4096]{1,0:T(8,128)(2,1)S(1)} %collective-permute-done.1.even), channel_id=1, source_target_pairs={{4,8},{8,4},{12,16},{16,12},{20,24},{24,20},{28,32},{32,28},{36,40... | collective-permute-start | bytes 1572872 | tf_op jit(solution)/shard_map/ppermute | solution.py:227
  33.8 13.5 %collective-permute-start.2 = (bf16[64,4096]{1,0:T(8,128)(2,1)S(1)}, bf16[64,4096]{1,0:T(8,128)(2,1)S(1)}, u32[]{:S(2)}, u32[]{:S(2)}) collective-permute-start(bf16[64,4096]{1,0:T(8,128)(2,1)S(1)} %collective-permute-done.odd), channel_id=1, source_target_pairs={{0,4},{4,0},{8,12},{12,8},{16,20},{20,16},{24,28},{28,24},{32,36},... | collective-permute-start | bytes 1572872 | tf_op jit(solution)/shard_map/ppermute | solution.py:224
  35.7 21.0 %collective-permute-start.7 = (bf16[64,1280]{1,0:T(8,128)(2,1)S(1)}, bf16[64,1280]{1,0:T(8,128)(2,1)S(1)}, u32[]{:S(2)}, u32[]{:S(2)}) collective-permute-start(bf16[64,1280]{1,0:T(8,128)(2,1)S(1)} %get-tuple-element.43), channel_id=1, source_target_pairs={{0,3},{1,2},{2,1},{3,0},{4,7},{5,6},{6,5},{7,4},{8,11},{9,10},{10,... | collective-permute-start | bytes 491528 | tf_op jit(solution)/shard_map/ppermute | solution.py:199
  39.8 19.0 %collective-permute-start.8 = (bf16[64,1280]{1,0:T(8,128)(2,1)S(1)}, bf16[64,1280]{1,0:T(8,128)(2,1)S(1)}, u32[]{:S(2)}, u32[]{:S(2)}) collective-permute-start(bf16[64,1280]{1,0:T(8,128)(2,1)S(1)} %get-tuple-element.44), channel_id=1, source_target_pairs={{0,2},{1,3},{2,0},{3,1},{4,6},{5,7},{6,4},{7,5},{8,10},{9,11},{10,... | collective-permute-start | bytes 491528 | tf_op jit(solution)/shard_map/ppermute | solution.py:199
  42.7 16.0 %collective-permute-start.9 = (bf16[64,1280]{1,0:T(8,128)(2,1)S(1)}, bf16[64,1280]{1,0:T(8,128)(2,1)S(1)}, u32[]{:S(2)}, u32[]{:S(2)}) collective-permute-start(bf16[64,1280]{1,0:T(8,128)(2,1)S(1)} %get-tuple-element.45), channel_id=1, source_target_pairs={{0,1},{1,0},{2,3},{3,2},{4,5},{5,4},{6,7},{7,6},{8,9},{9,8},{10,11... | collective-permute-start | bytes 491528 | tf_op jit(solution)/shard_map/ppermute | solution.py:199
  45.8 30.8 %copy-start.1 = (bf16[88,128,128]{2,1,0:T(8,128)(2,1)S(1)}, bf16[88,128,128]{2,1,0:T(8,128)(2,1)}, u32[]{:S(2)}) copy-start(bf16[88,128,128]{2,1,0:T(8,128)(2,1)} %values.15) | copy-start | bytes 8650756
  48.8 9.9 %collective-permute-start.4 = (bf16[64,1024]{1,0:T(8,128)(2,1)S(1)}, bf16[64,1024]{1,0:T(8,128)(2,1)S(1)}, u32[]{:S(2)}, u32[]{:S(2)}) collective-permute-start(bf16[64,1024]{1,0:T(8,128)(2,1)S(1)} %get-tuple-element.40), channel_id=1, source_target_pairs={{0,3},{1,2},{2,1},{3,0},{4,7},{5,6},{6,5},{7,4},{8,11},{9,10},{10,... | collective-permute-start | bytes 393224 | tf_op jit(solution)/shard_map/ppermute | solution.py:199
  53.8 7.2 %collective-permute-start.5 = (bf16[64,1024]{1,0:T(8,128)(2,1)S(1)}, bf16[64,1024]{1,0:T(8,128)(2,1)S(1)}, u32[]{:S(2)}, u32[]{:S(2)}) collective-permute-start(bf16[64,1024]{1,0:T(8,128)(2,1)S(1)} %get-tuple-element.41), channel_id=1, source_target_pairs={{0,2},{1,3},{2,0},{3,1},{4,6},{5,7},{6,4},{7,5},{8,10},{9,11},{10,... | collective-permute-start | bytes 393224 | tf_op jit(solution)/shard_map/ppermute | solution.py:199
  56.8 4.2 %collective-permute-start.6 = (bf16[64,1024]{1,0:T(8,128)(2,1)S(1)}, bf16[64,1024]{1,0:T(8,128)(2,1)S(1)}, u32[]{:S(2)}, u32[]{:S(2)}) collective-permute-start(bf16[64,1024]{1,0:T(8,128)(2,1)S(1)} %get-tuple-element.42), channel_id=1, source_target_pairs={{0,1},{1,0},{2,3},{3,2},{4,5},{5,4},{6,7},{7,6},{8,9},{9,8},{10,11... | collective-permute-start | bytes 393224 | tf_op jit(solution)/shard_map/ppermute | solution.py:199
  62.6 8.5 %collective-permute-start.10 = (bf16[64,1280]{1,0:T(8,128)(2,1)S(1)}, bf16[64,1280]{1,0:T(8,128)(2,1)S(1)}, u32[]{:S(2)}, u32[]{:S(2)}) collective-permute-start(bf16[64,1280]{1,0:T(8,128)(2,1)S(1)} %get-tuple-element.47), channel_id=1, source_target_pairs={{0,3},{1,2},{2,1},{3,0},{4,7},{5,6},{6,5},{7,4},{8,11},{9,10},{10,... | collective-permute-start | bytes 491528 | tf_op jit(solution)/shard_map/ppermute | solution.py:199
  65.5 9.1 %collective-permute-start.11 = (bf16[64,1280]{1,0:T(8,128)(2,1)S(1)}, bf16[64,1280]{1,0:T(8,128)(2,1)S(1)}, u32[]{:S(2)}, u32[]{:S(2)}) collective-permute-start(bf16[64,1280]{1,0:T(8,128)(2,1)S(1)} %get-tuple-element.48), channel_id=1, source_target_pairs={{0,2},{1,3},{2,0},{3,1},{4,6},{5,7},{6,4},{7,5},{8,10},{9,11},{10,... | collective-permute-start | bytes 491528 | tf_op jit(solution)/shard_map/ppermute | solution.py:199
  68.4 6.2 %collective-permute-start.12 = (bf16[64,1280]{1,0:T(8,128)(2,1)S(1)}, bf16[64,1280]{1,0:T(8,128)(2,1)S(1)}, u32[]{:S(2)}, u32[]{:S(2)}) collective-permute-start(bf16[64,1280]{1,0:T(8,128)(2,1)S(1)} %get-tuple-element.49), channel_id=1, source_target_pairs={{0,1},{1,0},{2,3},{3,2},{4,5},{5,4},{6,7},{7,6},{8,9},{9,8},{10,11... | collective-permute-start | bytes 491528 | tf_op jit(solution)/shard_map/ppermute | solution.py:199
  74.6 5.0 %collective-permute-start.13 = (f32[64,256]{1,0:T(8,128)S(1)}, f32[64,256]{1,0:T(8,128)S(1)}, u32[]{:S(2)}, u32[]{:S(2)}) collective-permute-start(f32[64,256]{1,0:T(8,128)S(1)} %convert_add_fusion), channel_id=1, source_target_pairs={{0,16},{16,0},{32,48},{48,32},{64,80},{80,64},{96,112},{112,96},{1... | collective-permute-start | bytes 196616 | tf_op jit(solution)/shard_map/ppermute | solution.py:210
  79.7 19.7 %collective-permute-start.15 = (bf16[64,4096]{1,0:T(8,128)(2,1)S(1)}, bf16[64,4096]{1,0:T(8,128)(2,1)S(1)}, u32[]{:S(2)}, u32[]{:S(2)}) collective-permute-start(bf16[64,4096]{1,0:T(8,128)(2,1)S(1)} %get-tuple-element.54), channel_id=1, source_target_pairs={{0,4},{4,0},{8,12},{12,8},{16,20},{20,16},{24,28},{28,24},{32,36},... | collective-permute-start | bytes 1572872 | tf_op jit(solution)/shard_map/ppermute | solution.py:224
  81.6 25.0 %collective-permute-start.14 = (bf16[64,4096]{1,0:T(8,128)(2,1)S(1)}, bf16[64,4096]{1,0:T(8,128)(2,1)S(1)}, u32[]{:S(2)}, u32[]{:S(2)}) collective-permute-start(bf16[64,4096]{1,0:T(8,128)(2,1)S(1)} %get-tuple-element.53), channel_id=1, source_target_pairs={{4,8},{8,4},{12,16},{16,12},{20,24},{24,20},{28,32},{32,28},{36,40... | collective-permute-start | bytes 1572872 | tf_op jit(solution)/shard_map/ppermute | solution.py:227
  87.9 9.5 %collective-permute-start.16 = (f32[64,256]{1,0:T(8,128)S(1)}, f32[64,256]{1,0:T(8,128)S(1)}, u32[]{:S(2)}, u32[]{:S(2)}) collective-permute-start(f32[64,256]{1,0:T(8,128)S(1)} %add.31), channel_id=1, source_target_pairs={{0,32},{16,48},{32,0},{48,16},{64,96},{80,112},{96,64},{112,80},{1... | collective-permute-start | bytes 196616 | tf_op jit(solution)/shard_map/ppermute | solution.py:210
  89.8 14.0 %collective-permute-start.17 = (bf16[64,1024]{1,0:T(8,128)(2,1)S(1)}, bf16[64,1024]{1,0:T(8,128)(2,1)S(1)}, u32[]{:S(2)}, u32[]{:S(2)}) collective-permute-start(bf16[64,1024]{1,0:T(8,128)(2,1)S(1)} %get-tuple-element.58), channel_id=1, source_target_pairs={{0,3},{1,2},{2,1},{3,0},{4,7},{5,6},{6,5},{7,4},{8,11},{9,10},{10,... | collective-permute-start | bytes 393224 | tf_op jit(solution)/shard_map/ppermute | solution.py:199
  94.4 12.2 %collective-permute-start.18 = (bf16[64,1024]{1,0:T(8,128)(2,1)S(1)}, bf16[64,1024]{1,0:T(8,128)(2,1)S(1)}, u32[]{:S(2)}, u32[]{:S(2)}) collective-permute-start(bf16[64,1024]{1,0:T(8,128)(2,1)S(1)} %get-tuple-element.59), channel_id=1, source_target_pairs={{0,2},{1,3},{2,0},{3,1},{4,6},{5,7},{6,4},{7,5},{8,10},{9,11},{10,... | collective-permute-start | bytes 393224 | tf_op jit(solution)/shard_map/ppermute | solution.py:199
  97.4 9.3 %collective-permute-start.19 = (bf16[64,1024]{1,0:T(8,128)(2,1)S(1)}, bf16[64,1024]{1,0:T(8,128)(2,1)S(1)}, u32[]{:S(2)}, u32[]{:S(2)}) collective-permute-start(bf16[64,1024]{1,0:T(8,128)(2,1)S(1)} %get-tuple-element.60), channel_id=1, source_target_pairs={{0,1},{1,0},{2,3},{3,2},{4,5},{5,4},{6,7},{7,6},{8,9},{9,8},{10,11... | collective-permute-start | bytes 393224 | tf_op jit(solution)/shard_map/ppermute | solution.py:199
  107.6 31.4 %collective-permute-start.20 = (bf16[64,4096]{1,0:T(8,128)(2,1)S(1)}, bf16[64,4096]{1,0:T(8,128)(2,1)S(1)}, u32[]{:S(2)}, u32[]{:S(2)}) collective-permute-start(bf16[64,4096]{1,0:T(8,128)(2,1)S(1)} %shard_map.101), channel_id=1, source_target_pairs={{0,4},{4,0},{8,12},{12,8},{16,20},{20,16},{24,28},{28,24},{32,36},... | collective-permute-start | bytes 1572872 | tf_op jit(solution)/shard_map/ppermute | solution.py:224
  109.5 30.6 %collective-permute-start.21 = (bf16[64,4096]{1,0:T(8,128)(2,1)S(1)}, bf16[64,4096]{1,0:T(8,128)(2,1)S(1)}, u32[]{:S(2)}, u32[]{:S(2)}) collective-permute-start(bf16[64,4096]{1,0:T(8,128)(2,1)S(1)} %shard_map.100), channel_id=1, source_target_pairs={{4,8},{8,4},{12,16},{16,12},{20,24},{24,20},{28,32},{32,28},{36,40... | collective-permute-start | bytes 1572872 | tf_op jit(solution)/shard_map/ppermute | solution.py:227
  116.8 22.1 %collective-permute-start.24 = (f32[64,256]{1,0:T(8,128)S(1)}, f32[64,256]{1,0:T(8,128)S(1)}, u32[]{:S(2)}, u32[]{:S(2)}) collective-permute-start(f32[64,256]{1,0:T(8,128)S(1)} %add.32), channel_id=1, source_target_pairs={{0,192},{16,208},{32,224},{48,240},{64,128},{80,144},{96,160},{112... | collective-permute-start | bytes 196616 | tf_op jit(solution)/shard_map/ppermute | solution.py:210
  118.7 20.2 %collective-permute-start.23 = (f32[64,256]{1,0:T(8,128)S(1)}, f32[64,256]{1,0:T(8,128)S(1)}, u32[]{:S(2)}, u32[]{:S(2)}) collective-permute-start(f32[64,256]{1,0:T(8,128)S(1)} %add.32), channel_id=1, source_target_pairs={{0,64},{16,80},{32,96},{48,112},{64,0},{80,16},{96,32},{112,48},{1... | collective-permute-start | bytes 196616 | tf_op jit(solution)/shard_map/ppermute | solution.py:210
  120.7 18.3 %collective-permute-start.22 = (f32[64,256]{1,0:T(8,128)S(1)}, f32[64,256]{1,0:T(8,128)S(1)}, u32[]{:S(2)}, u32[]{:S(2)}) collective-permute-start(f32[64,256]{1,0:T(8,128)S(1)} %add.32), channel_id=1, source_target_pairs={{0,128},{16,144},{32,160},{48,176},{64,192},{80,208},{96,224},{112... | collective-permute-start | bytes 196616 | tf_op jit(solution)/shard_map/ppermute | solution.py:210

commit v13 on v12

--- a/solution.py
+++ b/solution.py
@@ -312,8 +312,9 @@
     odd_near = near_terms(1, 2, even_in)
     odd_last = odd_swap(odd_near)
     output = swapped(output)
-    odd_in, *_ = lax.optimization_barrier((odd_in, odd_near, *output))
+    odd_in, _ = lax.optimization_barrier((odd_in, odd_near))
     even_near = near_terms(3, -2, odd_in)
+    even_near, *_ = lax.optimization_barrier((even_near, *output))
     even_last = even_swap(even_near)
     weight_grad, _ = lax.optimization_barrier((weight_grad, even_near))
     moved = [paired(weight_grad, "z", step) for step in (4, 12, 8)]

time: 156 us -> 156 us (level)
  transfers between devices with their start and end apart: 25 -> 25, of which waited for: 10 -> 11; matrix products, arithmetic and copies ran while one was open for 0% -> 0% of each run, Pallas kernels for 5% -> 5%
where the time goes in v13:
time: 156 us; the launch traced here: 154 us
  starting transfers between devices  99.8 us (64%)
  waiting for transfers between devices  22 us (14%)
  blocking collectives  11.8 us (8%)
  Pallas kernels  11.6 us (7%)
  local copies, waits for them, and re-layouts  5.99 us (4%)
  between operations  1.65 us (1%)
    ppermute x12, starting transfers between devices, swapped(): lax.ppermute(value, COLS, pairs(step))  36.1 us
    ppermute x4, starting transfers between devices, odd_swap(): return lax.ppermute(value, ROWS, odd_pairs)  33.9 us
    ppermute x5, starting transfers between devices, paired(): lax.ppermute(value, axis, [(source, source ^ step) for source in range(co...  20 us
    all_to_all x1, blocking collectives, summed(): lax.all_to_all(copies, axis, 0, 0, tiled=True).astype(jnp.float32).sum(0)  11.8 us
    pallas_call x9, Pallas kernels, call(): pl.pallas_call(kernel, out_shape=outs, in_specs=specs, out_specs=[VMEM] *...  11.6 us
    ppermute x12, waiting for transfers between devices, swapped(): lax.ppermute(value, COLS, pairs(step))  11.3 us
    ppermute x4, starting transfers between devices, even_swap(): return lax.ppermute(value, ROWS, even_pairs)  9.7 us
    ppermute x5, waiting for transfers between devices, paired(): lax.ppermute(value, axis, [(source, source ^ step) for source in range(co...  7.62 us
  transfers between devices with their start and end apart: 25, of which 11 were waited for; matrix products, arithmetic and copies ran while one was open for 0% of the time, Pallas kernels for 5%

profile of v13, /device:TPU:1, one launch (start us, length us, event | category | flops | bytes accessed | tf_op | source)
XLA Modules:
  0.0 153.7 jit_solution(16704462813343978496)
XLA Ops:
  0.6 4.0 %collective-permute-start.1 = (bf16[64,4096]{1,0:T(8,128)(2,1)}, bf16[64,4096]{1,0:T(8,128)(2,1)S(1)}, u32[]{:S(2)}, u32[]{:S(2)}) collective-permute-start(bf16[64,4096]{1,0:T(8,128)(2,1)} %bitcast.9), channel_id=1, source_target_pairs={{0,4},{4,0},{8,12},{12,8},{16,20},{20,16},{24,28},{28,24},{32,36},... | collective-permute-start | bytes 1572872 | tf_op jit(solution)/shard_map/ppermute | solution.py:224
  4.6 15.3 %collective-permute-start = (bf16[64,4096]{1,0:T(8,128)(2,1)}, bf16[64,4096]{1,0:T(8,128)(2,1)S(1)}, u32[]{:S(2)}, u32[]{:S(2)}) collective-permute-start(bf16[64,4096]{1,0:T(8,128)(2,1)} %bitcast.10), channel_id=1, source_target_pairs={{4,8},{8,4},{12,16},{16,12},{20,24},{24,20},{28,32},{32,28},{36,40... | collective-permute-start | bytes 1572872 | tf_op jit(solution)/shard_map/ppermute | solution.py:227
  27.2 5.1 %collective-permute-start.3 = (bf16[64,4096]{1,0:T(8,128)(2,1)S(1)}, bf16[64,4096]{1,0:T(8,128)(2,1)S(1)}, u32[]{:S(2)}, u32[]{:S(2)}) collective-permute-start(bf16[64,4096]{1,0:T(8,128)(2,1)S(1)} %collective-permute-done.1.even), channel_id=1, source_target_pairs={{4,8},{8,4},{12,16},{16,12},{20,24},{24,20},{28,32},{32,28},{36,40... | collective-permute-start | bytes 1572872 | tf_op jit(solution)/shard_map/ppermute | solution.py:227
  33.8 1.9 %collective-permute-start.2 = (bf16[64,4096]{1,0:T(8,128)(2,1)S(1)}, bf16[64,4096]{1,0:T(8,128)(2,1)S(1)}, u32[]{:S(2)}, u32[]{:S(2)}) collective-permute-start(bf16[64,4096]{1,0:T(8,128)(2,1)S(1)} %collective-permute-done.odd), channel_id=1, source_target_pairs={{0,4},{4,0},{8,12},{12,8},{16,20},{20,16},{24,28},{28,24},{32,36},... | collective-permute-start | bytes 1572872 | tf_op jit(solution)/shard_map/ppermute | solution.py:224
  35.7 4.0 %collective-permute-start.7 = (bf16[64,1280]{1,0:T(8,128)(2,1)S(1)}, bf16[64,1280]{1,0:T(8,128)(2,1)S(1)}, u32[]{:S(2)}, u32[]{:S(2)}) collective-permute-start(bf16[64,1280]{1,0:T(8,128)(2,1)S(1)} %get-tuple-element.44), channel_id=1, source_target_pairs={{0,3},{1,2},{2,1},{3,0},{4,7},{5,6},{6,5},{7,4},{8,11},{9,10},{10,... | collective-permute-start | bytes 491528 | tf_op jit(solution)/shard_map/ppermute | solution.py:199
  39.8 3.0 %collective-permute-start.8 = (bf16[64,1280]{1,0:T(8,128)(2,1)S(1)}, bf16[64,1280]{1,0:T(8,128)(2,1)S(1)}, u32[]{:S(2)}, u32[]{:S(2)}) collective-permute-start(bf16[64,1280]{1,0:T(8,128)(2,1)S(1)} %get-tuple-element.45), channel_id=1, source_target_pairs={{0,2},{1,3},{2,0},{3,1},{4,6},{5,7},{6,4},{7,5},{8,10},{9,11},{10,... | collective-permute-start | bytes 491528 | tf_op jit(solution)/shard_map/ppermute | solution.py:199
  42.7 1.9 %collective-permute-start.9 = (bf16[64,1280]{1,0:T(8,128)(2,1)S(1)}, bf16[64,1280]{1,0:T(8,128)(2,1)S(1)}, u32[]{:S(2)}, u32[]{:S(2)}) collective-permute-start(bf16[64,1280]{1,0:T(8,128)(2,1)S(1)} %get-tuple-element.46), channel_id=1, source_target_pairs={{0,1},{1,0},{2,3},{3,2},{4,5},{5,4},{6,7},{7,6},{8,9},{9,8},{10,11... | collective-permute-start | bytes 491528 | tf_op jit(solution)/shard_map/ppermute | solution.py:199
  48.8 4.9 %collective-permute-start.4 = (bf16[64,1024]{1,0:T(8,128)(2,1)S(1)}, bf16[64,1024]{1,0:T(8,128)(2,1)S(1)}, u32[]{:S(2)}, u32[]{:S(2)}) collective-permute-start(bf16[64,1024]{1,0:T(8,128)(2,1)S(1)} %get-tuple-element.41), channel_id=1, source_target_pairs={{0,3},{1,2},{2,1},{3,0},{4,7},{5,6},{6,5},{7,4},{8,11},{9,10},{10,... | collective-permute-start | bytes 393224 | tf_op jit(solution)/shard_map/ppermute | solution.py:199
  53.8 3.0 %collective-permute-start.5 = (bf16[64,1024]{1,0:T(8,128)(2,1)S(1)}, bf16[64,1024]{1,0:T(8,128)(2,1)S(1)}, u32[]{:S(2)}, u32[]{:S(2)}) collective-permute-start(bf16[64,1024]{1,0:T(8,128)(2,1)S(1)} %get-tuple-element.42), channel_id=1, source_target_pairs={{0,2},{1,3},{2,0},{3,1},{4,6},{5,7},{6,4},{7,5},{8,10},{9,11},{10,... | collective-permute-start | bytes 393224 | tf_op jit(solution)/shard_map/ppermute | solution.py:199
  56.8 1.9 %collective-permute-start.6 = (bf16[64,1024]{1,0:T(8,128)(2,1)S(1)}, bf16[64,1024]{1,0:T(8,128)(2,1)S(1)}, u32[]{:S(2)}, u32[]{:S(2)}) collective-permute-start(bf16[64,1024]{1,0:T(8,128)(2,1)S(1)} %get-tuple-element.43), channel_id=1, source_target_pairs={{0,1},{1,0},{2,3},{3,2},{4,5},{5,4},{6,7},{7,6},{8,9},{9,8},{10,11... | collective-permute-start | bytes 393224 | tf_op jit(solution)/shard_map/ppermute | solution.py:199
  58.8 2.3 %collective-permute-done.5.refs_2_ = bf16[64,1024]{1,0:T(8,128)(2,1)S(1)} collective-permute-done((bf16[64,1024]{1,0:T(8,128)(2,1)S(1)}, bf16[64,1024]{1,0:T(8,128)(2,1)S(1)}, u32[]{:S(2)}, u32[]{:S(2)}) %collective-permute-start.5) | collective-permute-done | bytes 131104 | tf_op jit(solution)/shard_map/ppermute | solution.py:199
  62.6 2.8 %collective-permute-start.10 = (bf16[64,1280]{1,0:T(8,128)(2,1)S(1)}, bf16[64,1280]{1,0:T(8,128)(2,1)S(1)}, u32[]{:S(2)}, u32[]{:S(2)}) collective-permute-start(bf16[64,1280]{1,0:T(8,128)(2,1)S(1)} %get-tuple-element.48), channel_id=1, source_target_pairs={{0,3},{1,2},{2,1},{3,0},{4,7},{5,6},{6,5},{7,4},{8,11},{9,10},{10,... | collective-permute-start | bytes 491528 | tf_op jit(solution)/shard_map/ppermute | solution.py:199
  65.5 2.9 %collective-permute-start.11 = (bf16[64,1280]{1,0:T(8,128)(2,1)S(1)}, bf16[64,1280]{1,0:T(8,128)(2,1)S(1)}, u32[]{:S(2)}, u32[]{:S(2)}) collective-permute-start(bf16[64,1280]{1,0:T(8,128)(2,1)S(1)} %get-tuple-element.49), channel_id=1, source_target_pairs={{0,2},{1,3},{2,0},{3,1},{4,6},{5,7},{6,4},{7,5},{8,10},{9,11},{10,... | collective-permute-start | bytes 491528 | tf_op jit(solution)/shard_map/ppermute | solution.py:199
  68.4 2.1 %collective-permute-start.12 = (bf16[64,1280]{1,0:T(8,128)(2,1)S(1)}, bf16[64,1280]{1,0:T(8,128)(2,1)S(1)}, u32[]{:S(2)}, u32[]{:S(2)}) collective-permute-start(bf16[64,1280]{1,0:T(8,128)(2,1)S(1)} %get-tuple-element.50), channel_id=1, source_target_pairs={{0,1},{1,0},{2,3},{3,2},{4,5},{5,4},{6,7},{7,6},{8,9},{9,8},{10,11... | collective-permute-start | bytes 491528 | tf_op jit(solution)/shard_map/ppermute | solution.py:199
  71.1 3.5 %collective-permute-done.11.refs_2_ = bf16[64,1280]{1,0:T(8,128)(2,1)S(1)} collective-permute-done((bf16[64,1280]{1,0:T(8,128)(2,1)S(1)}, bf16[64,1280]{1,0:T(8,128)(2,1)S(1)}, u32[]{:S(2)}, u32[]{:S(2)}) %collective-permute-start.11) | collective-permute-done | bytes 163872 | tf_op jit(solution)/shard_map/ppermute | solution.py:199
  74.7 1.9 %collective-permute-start.13 = (f32[64,256]{1,0:T(8,128)S(1)}, f32[64,256]{1,0:T(8,128)S(1)}, u32[]{:S(2)}, u32[]{:S(2)}) collective-permute-start(f32[64,256]{1,0:T(8,128)S(1)} %convert_add_fusion), channel_id=1, source_target_pairs={{0,16},{16,0},{32,48},{48,32},{64,80},{80,64},{96,112},{112,96},{1... | collective-permute-start | bytes 196616 | tf_op jit(solution)/shard_map/ppermute | solution.py:210
  79.7 1.9 %collective-permute-start.15 = (bf16[64,4096]{1,0:T(8,128)(2,1)S(1)}, bf16[64,4096]{1,0:T(8,128)(2,1)S(1)}, u32[]{:S(2)}, u32[]{:S(2)}) collective-permute-start(bf16[64,4096]{1,0:T(8,128)(2,1)S(1)} %get-tuple-element.55), channel_id=1, source_target_pairs={{0,4},{4,0},{8,12},{12,8},{16,20},{20,16},{24,28},{28,24},{32,36},... | collective-permute-start | bytes 1572872 | tf_op jit(solution)/shard_map/ppermute | solution.py:224
  81.6 6.2 %collective-permute-start.14 = (bf16[64,4096]{1,0:T(8,128)(2,1)S(1)}, bf16[64,4096]{1,0:T(8,128)(2,1)S(1)}, u32[]{:S(2)}, u32[]{:S(2)}) collective-permute-start(bf16[64,4096]{1,0:T(8,128)(2,1)S(1)} %get-tuple-element.54), channel_id=1, source_target_pairs={{4,8},{8,4},{12,16},{16,12},{20,24},{24,20},{28,32},{32,28},{36,40... | collective-permute-start | bytes 1572872 | tf_op jit(solution)/shard_map/ppermute | solution.py:227
  87.8 1.9 %collective-permute-start.16 = (f32[64,256]{1,0:T(8,128)S(1)}, f32[64,256]{1,0:T(8,128)S(1)}, u32[]{:S(2)}, u32[]{:S(2)}) collective-permute-start(f32[64,256]{1,0:T(8,128)S(1)} %add.31), channel_id=1, source_target_pairs={{0,32},{16,48},{32,0},{48,16},{64,96},{80,112},{96,64},{112,80},{1... | collective-permute-start | bytes 196616 | tf_op jit(solution)/shard_map/ppermute | solution.py:210
  89.8 4.6 %collective-permute-start.17 = (bf16[64,1024]{1,0:T(8,128)(2,1)S(1)}, bf16[64,1024]{1,0:T(8,128)(2,1)S(1)}, u32[]{:S(2)}, u32[]{:S(2)}) collective-permute-start(bf16[64,1024]{1,0:T(8,128)(2,1)S(1)} %get-tuple-element.60), channel_id=1, source_target_pairs={{0,3},{1,2},{2,1},{3,0},{4,7},{5,6},{6,5},{7,4},{8,11},{9,10},{10,... | collective-permute-start | bytes 393224 | tf_op jit(solution)/shard_map/ppermute | solution.py:199
  94.4 3.0 %collective-permute-start.18 = (bf16[64,1024]{1,0:T(8,128)(2,1)S(1)}, bf16[64,1024]{1,0:T(8,128)(2,1)S(1)}, u32[]{:S(2)}, u32[]{:S(2)}) collective-permute-start(bf16[64,1024]{1,0:T(8,128)(2,1)S(1)} %get-tuple-element.61), channel_id=1, source_target_pairs={{0,2},{1,3},{2,0},{3,1},{4,6},{5,7},{6,4},{7,5},{8,10},{9,11},{10,... | collective-permute-start | bytes 393224 | tf_op jit(solution)/shard_map/ppermute | solution.py:199
  97.4 1.9 %collective-permute-start.19 = (bf16[64,1024]{1,0:T(8,128)(2,1)S(1)}, bf16[64,1024]{1,0:T(8,128)(2,1)S(1)}, u32[]{:S(2)}, u32[]{:S(2)}) collective-permute-start(bf16[64,1024]{1,0:T(8,128)(2,1)S(1)} %get-tuple-element.62), channel_id=1, source_target_pairs={{0,1},{1,0},{2,3},{3,2},{4,5},{5,4},{6,7},{7,6},{8,9},{9,8},{10,11... | collective-permute-start | bytes 393224 | tf_op jit(solution)/shard_map/ppermute | solution.py:199
  101.7 2.1 %collective-permute-done.17.refs_1_ = bf16[64,1024]{1,0:T(8,128)(2,1)S(1)} collective-permute-done((bf16[64,1024]{1,0:T(8,128)(2,1)S(1)}, bf16[64,1024]{1,0:T(8,128)(2,1)S(1)}, u32[]{:S(2)}, u32[]{:S(2)}) %collective-permute-start.17) | collective-permute-done | bytes 131104 | tf_op jit(solution)/shard_map/ppermute | solution.py:199
  103.8 2.8 %collective-permute-done.18.refs_2_ = bf16[64,1024]{1,0:T(8,128)(2,1)S(1)} collective-permute-done((bf16[64,1024]{1,0:T(8,128)(2,1)S(1)}, bf16[64,1024]{1,0:T(8,128)(2,1)S(1)}, u32[]{:S(2)}, u32[]{:S(2)}) %collective-permute-start.18) | collective-permute-done | bytes 131104 | tf_op jit(solution)/shard_map/ppermute | solution.py:199
  106.6 1.9 %collective-permute-start.20 = (bf16[64,4096]{1,0:T(8,128)(2,1)S(1)}, bf16[64,4096]{1,0:T(8,128)(2,1)S(1)}, u32[]{:S(2)}, u32[]{:S(2)}) collective-permute-start(bf16[64,4096]{1,0:T(8,128)(2,1)S(1)} %shard_map.101), channel_id=1, source_target_pairs={{0,4},{4,0},{8,12},{12,8},{16,20},{20,16},{24,28},{28,24},{32,36},... | collective-permute-start | bytes 1572872 | tf_op jit(solution)/shard_map/ppermute | solution.py:224
  108.5 7.3 %collective-permute-start.21 = (bf16[64,4096]{1,0:T(8,128)(2,1)S(1)}, bf16[64,4096]{1,0:T(8,128)(2,1)S(1)}, u32[]{:S(2)}, u32[]{:S(2)}) collective-permute-start(bf16[64,4096]{1,0:T(8,128)(2,1)S(1)} %shard_map.100), channel_id=1, source_target_pairs={{4,8},{8,4},{12,16},{16,12},{20,24},{24,20},{28,32},{32,28},{36,40... | collective-permute-start | bytes 1572872 | tf_op jit(solution)/shard_map/ppermute | solution.py:227
  115.8 1.9 %collective-permute-start.24 = (f32[64,256]{1,0:T(8,128)S(1)}, f32[64,256]{1,0:T(8,128)S(1)}, u32[]{:S(2)}, u32[]{:S(2)}) collective-permute-start(f32[64,256]{1,0:T(8,128)S(1)} %add.32), channel_id=1, source_target_pairs={{0,192},{16,208},{32,224},{48,240},{64,128},{80,144},{96,160},{112... | collective-permute-start | bytes 196616 | tf_op jit(solution)/shard_map/ppermute | solution.py:210
  117.8 1.9 %collective-permute-start.23 = (f32[64,256]{1,0:T(8,128)S(1)}, f32[64,256]{1,0:T(8,128)S(1)}, u32[]{:S(2)}, u32[]{:S(2)}) collective-permute-start(f32[64,256]{1,0:T(8,128)S(1)} %add.32), channel_id=1, source_target_pairs={{0,64},{16,80},{32,96},{48,112},{64,0},{80,16},{96,32},{112,48},{1... | collective-permute-start | bytes 196616 | tf_op jit(solution)/shard_map/ppermute | solution.py:210
  119.7 12.3 %collective-permute-start.22 = (f32[64,256]{1,0:T(8,128)S(1)}, f32[64,256]{1,0:T(8,128)S(1)}, u32[]{:S(2)}, u32[]{:S(2)}) collective-permute-start(f32[64,256]{1,0:T(8,128)S(1)} %add.32), channel_id=1, source_target_pairs={{0,128},{16,144},{32,160},{48,176},{64,192},{80,208},{96,224},{112... | collective-permute-start | bytes 196616 | tf_op jit(solution)/shard_map/ppermute | solution.py:210
  132.1 5.9 %collective-permute-done.24 = f32[64,256]{1,0:T(8,128)S(1)} collective-permute-done((f32[64,256]{1,0:T(8,128)S(1)}, f32[64,256]{1,0:T(8,128)S(1)}, u32[]{:S(2)}, u32[]{:S(2)}) %collective-permute-start.24) | collective-permute-done | bytes 65568 | tf_op jit(solution)/shard_map/ppermute | solution.py:210
  139.1 2.0 %shard_map.102 = (bf16[64,4096]{1,0:T(8,128)(2,1)}, bf16[64,4096]{1,0:T(8,128)(2,1)}) custom-call(bf16[88,128,128]{2,1,0:T(8,128)(2,1)S(1)} %copy-done.1, s32[88]{0:T(128)S(1)} %copy-done.5, s32[88]{0:T(128)S(1)} %copy-done.6, s32[1]{0:T(128)S(6)} %copy.10.count, s32[2]{0:T(128)S(1)} %pad_add_fusion.place, bf16[4,64,1024]{2,1,0:T(8,128)(2,1)S(1)} %get-tuple-element.51.grad, ...), custom_call_target="tpu_custom_call" | custom-call | flops 37748736 | bytes 6030028 | tf_op jit(solution)/shard_map/pallas_call | solution.py:183
  141.1 11.8 %all_to_all.5 = bf16[8,64,256]{2,1,0:T(8,128)(2,1)S(1)} all-to-all(bf16[8,64,256]{2,1,0:T(8,128)(2,1)S(1)} %broadcast_in_dim.3), channel_id=1, replica_groups=mesh['yh'=2,'z'=16,'x'=4,'yl'=2,'core'=2] {'yh','x'}, dimensions={0} | all-to-all | bytes 524288 | tf_op jit(solution)/shard_map/all_to_all | solution.py:205
  (50 shorter events, 21.7 us)
Async XLA Ops:
  0.6 26.6 %collective-permute-start.1 = (bf16[64,4096]{1,0:T(8,128)(2,1)}, bf16[64,4096]{1,0:T(8,128)(2,1)S(1)}, u32[]{:S(2)}, u32[]{:S(2)}) collective-permute-start(bf16[64,4096]{1,0:T(8,128)(2,1)} %bitcast.9), channel_id=1, source_target_pairs={{0,4},{4,0},{8,12},{12,8},{16,20},{20,16},{24,28},{28,24},{32,36},... | collective-permute-start | bytes 1572872 | tf_op jit(solution)/shard_map/ppermute | solution.py:224
  4.6 29.2 %collective-permute-start = (bf16[64,4096]{1,0:T(8,128)(2,1)}, bf16[64,4096]{1,0:T(8,128)(2,1)S(1)}, u32[]{:S(2)}, u32[]{:S(2)}) collective-permute-start(bf16[64,4096]{1,0:T(8,128)(2,1)} %bitcast.10), channel_id=1, source_target_pairs={{4,8},{8,4},{12,16},{16,12},{20,24},{24,20},{28,32},{32,28},{36,40... | collective-permute-start | bytes 1572872 | tf_op jit(solution)/shard_map/ppermute | solution.py:227
  20.6 1.8 %copy-start = (bf16[88,128,128]{2,1,0:T(8,128)(2,1)S(1)}, bf16[88,128,128]{2,1,0:T(8,128)(2,1)}, u32[]{:S(2)}) copy-start(bf16[88,128,128]{2,1,0:T(8,128)(2,1)} %values.15) | copy-start | bytes 8650756
  22.4 1.0 copy-start.2
  23.5 1.0 copy-start.3
  24.5 0.8 copy-start.4
  25.3 0.7 copy-start.5
  25.9 0.7 copy-start.6
  27.2 19.8 %collective-permute-start.3 = (bf16[64,4096]{1,0:T(8,128)(2,1)S(1)}, bf16[64,4096]{1,0:T(8,128)(2,1)S(1)}, u32[]{:S(2)}, u32[]{:S(2)}) collective-permute-start(bf16[64,4096]{1,0:T(8,128)(2,1)S(1)} %collective-permute-done.1.even), channel_id=1, source_target_pairs={{4,8},{8,4},{12,16},{16,12},{20,24},{24,20},{28,32},{32,28},{36,40... | collective-permute-start | bytes 1572872 | tf_op jit(solution)/shard_map/ppermute | solution.py:227
  33.8 13.5 %collective-permute-start.2 = (bf16[64,4096]{1,0:T(8,128)(2,1)S(1)}, bf16[64,4096]{1,0:T(8,128)(2,1)S(1)}, u32[]{:S(2)}, u32[]{:S(2)}) collective-permute-start(bf16[64,4096]{1,0:T(8,128)(2,1)S(1)} %collective-permute-done.odd), channel_id=1, source_target_pairs={{0,4},{4,0},{8,12},{12,8},{16,20},{20,16},{24,28},{28,24},{32,36},... | collective-permute-start | bytes 1572872 | tf_op jit(solution)/shard_map/ppermute | solution.py:224
  35.7 21.0 %collective-permute-start.7 = (bf16[64,1280]{1,0:T(8,128)(2,1)S(1)}, bf16[64,1280]{1,0:T(8,128)(2,1)S(1)}, u32[]{:S(2)}, u32[]{:S(2)}) collective-permute-start(bf16[64,1280]{1,0:T(8,128)(2,1)S(1)} %get-tuple-element.44), channel_id=1, source_target_pairs={{0,3},{1,2},{2,1},{3,0},{4,7},{5,6},{6,5},{7,4},{8,11},{9,10},{10,... | collective-permute-start | bytes 491528 | tf_op jit(solution)/shard_map/ppermute | solution.py:199
  39.8 19.0 %collective-permute-start.8 = (bf16[64,1280]{1,0:T(8,128)(2,1)S(1)}, bf16[64,1280]{1,0:T(8,128)(2,1)S(1)}, u32[]{:S(2)}, u32[]{:S(2)}) collective-permute-start(bf16[64,1280]{1,0:T(8,128)(2,1)S(1)} %get-tuple-element.45), channel_id=1, source_target_pairs={{0,2},{1,3},{2,0},{3,1},{4,6},{5,7},{6,4},{7,5},{8,10},{9,11},{10,... | collective-permute-start | bytes 491528 | tf_op jit(solution)/shard_map/ppermute | solution.py:199
  42.7 16.0 %collective-permute-start.9 = (bf16[64,1280]{1,0:T(8,128)(2,1)S(1)}, bf16[64,1280]{1,0:T(8,128)(2,1)S(1)}, u32[]{:S(2)}, u32[]{:S(2)}) collective-permute-start(bf16[64,1280]{1,0:T(8,128)(2,1)S(1)} %get-tuple-element.46), channel_id=1, source_target_pairs={{0,1},{1,0},{2,3},{3,2},{4,5},{5,4},{6,7},{7,6},{8,9},{9,8},{10,11... | collective-permute-start | bytes 491528 | tf_op jit(solution)/shard_map/ppermute | solution.py:199
  45.8 30.8 %copy-start.1 = (bf16[88,128,128]{2,1,0:T(8,128)(2,1)S(1)}, bf16[88,128,128]{2,1,0:T(8,128)(2,1)}, u32[]{:S(2)}) copy-start(bf16[88,128,128]{2,1,0:T(8,128)(2,1)} %values.15) | copy-start | bytes 8650756
  48.8 9.9 %collective-permute-start.4 = (bf16[64,1024]{1,0:T(8,128)(2,1)S(1)}, bf16[64,1024]{1,0:T(8,128)(2,1)S(1)}, u32[]{:S(2)}, u32[]{:S(2)}) collective-permute-start(bf16[64,1024]{1,0:T(8,128)(2,1)S(1)} %get-tuple-element.41), channel_id=1, source_target_pairs={{0,3},{1,2},{2,1},{3,0},{4,7},{5,6},{6,5},{7,4},{8,11},{9,10},{10,... | collective-permute-start | bytes 393224 | tf_op jit(solution)/shard_map/ppermute | solution.py:199
  53.8 7.2 %collective-permute-start.5 = (bf16[64,1024]{1,0:T(8,128)(2,1)S(1)}, bf16[64,1024]{1,0:T(8,128)(2,1)S(1)}, u32[]{:S(2)}, u32[]{:S(2)}) collective-permute-start(bf16[64,1024]{1,0:T(8,128)(2,1)S(1)} %get-tuple-element.42), channel_id=1, source_target_pairs={{0,2},{1,3},{2,0},{3,1},{4,6},{5,7},{6,4},{7,5},{8,10},{9,11},{10,... | collective-permute-start | bytes 393224 | tf_op jit(solution)/shard_map/ppermute | solution.py:199
  56.8 4.2 %collective-permute-start.6 = (bf16[64,1024]{1,0:T(8,128)(2,1)S(1)}, bf16[64,1024]{1,0:T(8,128)(2,1)S(1)}, u32[]{:S(2)}, u32[]{:S(2)}) collective-permute-start(bf16[64,1024]{1,0:T(8,128)(2,1)S(1)} %get-tuple-element.43), channel_id=1, source_target_pairs={{0,1},{1,0},{2,3},{3,2},{4,5},{5,4},{6,7},{7,6},{8,9},{9,8},{10,11... | collective-permute-start | bytes 393224 | tf_op jit(solution)/shard_map/ppermute | solution.py:199
  62.6 8.5 %collective-permute-start.10 = (bf16[64,1280]{1,0:T(8,128)(2,1)S(1)}, bf16[64,1280]{1,0:T(8,128)(2,1)S(1)}, u32[]{:S(2)}, u32[]{:S(2)}) collective-permute-start(bf16[64,1280]{1,0:T(8,128)(2,1)S(1)} %get-tuple-element.48), channel_id=1, source_target_pairs={{0,3},{1,2},{2,1},{3,0},{4,7},{5,6},{6,5},{7,4},{8,11},{9,10},{10,... | collective-permute-start | bytes 491528 | tf_op jit(solution)/shard_map/ppermute | solution.py:199
  65.5 9.1 %collective-permute-start.11 = (bf16[64,1280]{1,0:T(8,128)(2,1)S(1)}, bf16[64,1280]{1,0:T(8,128)(2,1)S(1)}, u32[]{:S(2)}, u32[]{:S(2)}) collective-permute-start(bf16[64,1280]{1,0:T(8,128)(2,1)S(1)} %get-tuple-element.49), channel_id=1, source_target_pairs={{0,2},{1,3},{2,0},{3,1},{4,6},{5,7},{6,4},{7,5},{8,10},{9,11},{10,... | collective-permute-start | bytes 491528 | tf_op jit(solution)/shard_map/ppermute | solution.py:199
  68.4 6.2 %collective-permute-start.12 = (bf16[64,1280]{1,0:T(8,128)(2,1)S(1)}, bf16[64,1280]{1,0:T(8,128)(2,1)S(1)}, u32[]{:S(2)}, u32[]{:S(2)}) collective-permute-start(bf16[64,1280]{1,0:T(8,128)(2,1)S(1)} %get-tuple-element.50), channel_id=1, source_target_pairs={{0,1},{1,0},{2,3},{3,2},{4,5},{5,4},{6,7},{7,6},{8,9},{9,8},{10,11... | collective-permute-start | bytes 491528 | tf_op jit(solution)/shard_map/ppermute | solution.py:199
  74.7 5.0 %collective-permute-start.13 = (f32[64,256]{1,0:T(8,128)S(1)}, f32[64,256]{1,0:T(8,128)S(1)}, u32[]{:S(2)}, u32[]{:S(2)}) collective-permute-start(f32[64,256]{1,0:T(8,128)S(1)} %convert_add_fusion), channel_id=1, source_target_pairs={{0,16},{16,0},{32,48},{48,32},{64,80},{80,64},{96,112},{112,96},{1... | collective-permute-start | bytes 196616 | tf_op jit(solution)/shard_map/ppermute | solution.py:210
  79.7 19.7 %collective-permute-start.15 = (bf16[64,4096]{1,0:T(8,128)(2,1)S(1)}, bf16[64,4096]{1,0:T(8,128)(2,1)S(1)}, u32[]{:S(2)}, u32[]{:S(2)}) collective-permute-start(bf16[64,4096]{1,0:T(8,128)(2,1)S(1)} %get-tuple-element.55), channel_id=1, source_target_pairs={{0,4},{4,0},{8,12},{12,8},{16,20},{20,16},{24,28},{28,24},{32,36},... | collective-permute-start | bytes 1572872 | tf_op jit(solution)/shard_map/ppermute | solution.py:224
  81.6 19.1 %collective-permute-start.14 = (bf16[64,4096]{1,0:T(8,128)(2,1)S(1)}, bf16[64,4096]{1,0:T(8,128)(2,1)S(1)}, u32[]{:S(2)}, u32[]{:S(2)}) collective-permute-start(bf16[64,4096]{1,0:T(8,128)(2,1)S(1)} %get-tuple-element.54), channel_id=1, source_target_pairs={{4,8},{8,4},{12,16},{16,12},{20,24},{24,20},{28,32},{32,28},{36,40... | collective-permute-start | bytes 1572872 | tf_op jit(solution)/shard_map/ppermute | solution.py:227
  87.8 9.5 %collective-permute-start.16 = (f32[64,256]{1,0:T(8,128)S(1)}, f32[64,256]{1,0:T(8,128)S(1)}, u32[]{:S(2)}, u32[]{:S(2)}) collective-permute-start(f32[64,256]{1,0:T(8,128)S(1)} %add.31), channel_id=1, source_target_pairs={{0,32},{16,48},{32,0},{48,16},{64,96},{80,112},{96,64},{112,80},{1... | collective-permute-start | bytes 196616 | tf_op jit(solution)/shard_map/ppermute | solution.py:210
  89.8 14.0 %collective-permute-start.17 = (bf16[64,1024]{1,0:T(8,128)(2,1)S(1)}, bf16[64,1024]{1,0:T(8,128)(2,1)S(1)}, u32[]{:S(2)}, u32[]{:S(2)}) collective-permute-start(bf16[64,1024]{1,0:T(8,128)(2,1)S(1)} %get-tuple-element.60), channel_id=1, source_target_pairs={{0,3},{1,2},{2,1},{3,0},{4,7},{5,6},{6,5},{7,4},{8,11},{9,10},{10,... | collective-permute-start | bytes 393224 | tf_op jit(solution)/shard_map/ppermute | solution.py:199
  94.4 12.2 %collective-permute-start.18 = (bf16[64,1024]{1,0:T(8,128)(2,1)S(1)}, bf16[64,1024]{1,0:T(8,128)(2,1)S(1)}, u32[]{:S(2)}, u32[]{:S(2)}) collective-permute-start(bf16[64,1024]{1,0:T(8,128)(2,1)S(1)} %get-tuple-element.61), channel_id=1, source_target_pairs={{0,2},{1,3},{2,0},{3,1},{4,6},{5,7},{6,4},{7,5},{8,10},{9,11},{10,... | collective-permute-start | bytes 393224 | tf_op jit(solution)/shard_map/ppermute | solution.py:199
  97.4 9.3 %collective-permute-start.19 = (bf16[64,1024]{1,0:T(8,128)(2,1)S(1)}, bf16[64,1024]{1,0:T(8,128)(2,1)S(1)}, u32[]{:S(2)}, u32[]{:S(2)}) collective-permute-start(bf16[64,1024]{1,0:T(8,128)(2,1)S(1)} %get-tuple-element.62), channel_id=1, source_target_pairs={{0,1},{1,0},{2,3},{3,2},{4,5},{5,4},{6,7},{7,6},{8,9},{9,8},{10,11... | collective-permute-start | bytes 393224 | tf_op jit(solution)/shard_map/ppermute | solution.py:199
  106.6 31.4 %collective-permute-start.20 = (bf16[64,4096]{1,0:T(8,128)(2,1)S(1)}, bf16[64,4096]{1,0:T(8,128)(2,1)S(1)}, u32[]{:S(2)}, u32[]{:S(2)}) collective-permute-start(bf16[64,4096]{1,0:T(8,128)(2,1)S(1)} %shard_map.101), channel_id=1, source_target_pairs={{0,4},{4,0},{8,12},{12,8},{16,20},{20,16},{24,28},{28,24},{32,36},... | collective-permute-start | bytes 1572872 | tf_op jit(solution)/shard_map/ppermute | solution.py:224
  108.5 30.6 %collective-permute-start.21 = (bf16[64,4096]{1,0:T(8,128)(2,1)S(1)}, bf16[64,4096]{1,0:T(8,128)(2,1)S(1)}, u32[]{:S(2)}, u32[]{:S(2)}) collective-permute-start(bf16[64,4096]{1,0:T(8,128)(2,1)S(1)} %shard_map.100), channel_id=1, source_target_pairs={{4,8},{8,4},{12,16},{16,12},{20,24},{24,20},{28,32},{32,28},{36,40... | collective-permute-start | bytes 1572872 | tf_op jit(solution)/shard_map/ppermute | solution.py:227
  115.8 22.1 %collective-permute-start.24 = (f32[64,256]{1,0:T(8,128)S(1)}, f32[64,256]{1,0:T(8,128)S(1)}, u32[]{:S(2)}, u32[]{:S(2)}) collective-permute-start(f32[64,256]{1,0:T(8,128)S(1)} %add.32), channel_id=1, source_target_pairs={{0,192},{16,208},{32,224},{48,240},{64,128},{80,144},{96,160},{112... | collective-permute-start | bytes 196616 | tf_op jit(solution)/shard_map/ppermute | solution.py:210
  117.8 20.2 %collective-permute-start.23 = (f32[64,256]{1,0:T(8,128)S(1)}, f32[64,256]{1,0:T(8,128)S(1)}, u32[]{:S(2)}, u32[]{:S(2)}) collective-permute-start(f32[64,256]{1,0:T(8,128)S(1)} %add.32), channel_id=1, source_target_pairs={{0,64},{16,80},{32,96},{48,112},{64,0},{80,16},{96,32},{112,48},{1... | collective-permute-start | bytes 196616 | tf_op jit(solution)/shard_map/ppermute | solution.py:210
  119.7 18.3 %collective-permute-start.22 = (f32[64,256]{1,0:T(8,128)S(1)}, f32[64,256]{1,0:T(8,128)S(1)}, u32[]{:S(2)}, u32[]{:S(2)}) collective-permute-start(f32[64,256]{1,0:T(8,128)S(1)} %add.32), channel_id=1, source_target_pairs={{0,128},{16,144},{32,160},{48,176},{64,192},{80,208},{96,224},{112... | collective-permute-start | bytes 196616 | tf_op jit(solution)/shard_map/ppermute | solution.py:210

commit v14 on v11

--- a/solution.py
+++ b/solution.py
@@ -312,8 +312,9 @@
     odd_near = near_terms(1, 2, even_in)
     odd_last = odd_swap(odd_near)
     output = swapped(output)
-    odd_in, *_ = lax.optimization_barrier((odd_in, odd_near, *output))
+    odd_in, _ = lax.optimization_barrier((odd_in, odd_near))
     even_near = near_terms(3, -2, odd_in)
+    even_near, *_ = lax.optimization_barrier((even_near, *output))
     even_last = even_swap(even_near)
     weight_grad, _ = lax.optimization_barrier((weight_grad, even_near))
     moved = [paired(weight_grad, "z", step) for step in (4, 12, 8)]

time: 155 us -> 154 us (level)
  no operation moved by 1% of the time
where the time goes in v14:
time: 154 us; the launch traced here: 152 us
  starting transfers between devices  103 us (67%)
  waiting for transfers between devices  17.5 us (11%)
  blocking collectives  11.9 us (8%)
  Pallas kernels  11.6 us (8%)
  local copies, waits for them, and re-layouts  5.99 us (4%)
  between operations  1.67 us (1%)
    ppermute x4, starting transfers between devices, odd_swap(): return lax.ppermute(value, ROWS, odd_pairs)  37 us
    ppermute x12, starting transfers between devices, swapped(): lax.ppermute(value, COLS, pairs(step))  35.9 us
    ppermute x5, starting transfers between devices, paired(): lax.ppermute(value, axis, [(source, source ^ step) for source in range(co...  20 us
    all_to_all x1, blocking collectives, summed(): lax.all_to_all(copies, axis, 0, 0, tiled=True).astype(jnp.float32).sum(0)  11.9 us
    pallas_call x9, Pallas kernels, call(): pl.pallas_call(kernel, out_shape=outs, in_specs=specs, out_specs=[VMEM] *...  11.6 us
    ppermute x4, starting transfers between devices, even_swap(): return lax.ppermute(value, ROWS, even_pairs)  9.71 us
    ppermute x5, waiting for transfers between devices, paired(): lax.ppermute(value, axis, [(source, source ^ step) for source in range(co...  9.34 us
    ppermute x12, waiting for transfers between devices, swapped(): lax.ppermute(value, COLS, pairs(step))  6.64 us
  transfers between devices with their start and end apart: 25, of which 8 were waited for; matrix products, arithmetic and copies ran while one was open for 0% of the time, Pallas kernels for 4%

profile of v14, /device:TPU:1, one launch (start us, length us, event | category | flops | bytes accessed | tf_op | source)
XLA Modules:
  0.0 152.1 jit_solution(11816762668357652957)
XLA Ops:
  0.6 4.0 %collective-permute-start.1 = (bf16[64,4096]{1,0:T(8,128)(2,1)}, bf16[64,4096]{1,0:T(8,128)(2,1)S(1)}, u32[]{:S(2)}, u32[]{:S(2)}) collective-permute-start(bf16[64,4096]{1,0:T(8,128)(2,1)} %bitcast.9), channel_id=1, source_target_pairs={{0,4},{4,0},{8,12},{12,8},{16,20},{20,16},{24,28},{28,24},{32,36},... | collective-permute-start | bytes 1572872 | tf_op jit(solution)/shard_map/ppermute | solution.py:224
  4.6 15.3 %collective-permute-start = (bf16[64,4096]{1,0:T(8,128)(2,1)}, bf16[64,4096]{1,0:T(8,128)(2,1)S(1)}, u32[]{:S(2)}, u32[]{:S(2)}) collective-permute-start(bf16[64,4096]{1,0:T(8,128)(2,1)} %bitcast.10), channel_id=1, source_target_pairs={{4,8},{8,4},{12,16},{16,12},{20,24},{24,20},{28,32},{32,28},{36,40... | collective-permute-start | bytes 1572872 | tf_op jit(solution)/shard_map/ppermute | solution.py:227
  20.6 1.8 %copy-done = bf16[88,128,128]{2,1,0:T(8,128)(2,1)S(1)} copy-done((bf16[88,128,128]{2,1,0:T(8,128)(2,1)S(1)}, bf16[88,128,128]{2,1,0:T(8,128)(2,1)}, u32[]{:S(2)}) %copy-start) | copy-done | bytes 2883608
  27.2 5.1 %collective-permute-start.3 = (bf16[64,4096]{1,0:T(8,128)(2,1)S(1)}, bf16[64,4096]{1,0:T(8,128)(2,1)S(1)}, u32[]{:S(2)}, u32[]{:S(2)}) collective-permute-start(bf16[64,4096]{1,0:T(8,128)(2,1)S(1)} %collective-permute-done.1.even), channel_id=1, source_target_pairs={{4,8},{8,4},{12,16},{16,12},{20,24},{24,20},{28,32},{32,28},{36,40... | collective-permute-start | bytes 1572872 | tf_op jit(solution)/shard_map/ppermute | solution.py:227
  33.8 1.9 %collective-permute-start.2 = (bf16[64,4096]{1,0:T(8,128)(2,1)S(1)}, bf16[64,4096]{1,0:T(8,128)(2,1)S(1)}, u32[]{:S(2)}, u32[]{:S(2)}) collective-permute-start(bf16[64,4096]{1,0:T(8,128)(2,1)S(1)} %collective-permute-done.odd), channel_id=1, source_target_pairs={{0,4},{4,0},{8,12},{12,8},{16,20},{20,16},{24,28},{28,24},{32,36},... | collective-permute-start | bytes 1572872 | tf_op jit(solution)/shard_map/ppermute | solution.py:224
  35.7 4.0 %collective-permute-start.7 = (bf16[64,1280]{1,0:T(8,128)(2,1)S(1)}, bf16[64,1280]{1,0:T(8,128)(2,1)S(1)}, u32[]{:S(2)}, u32[]{:S(2)}) collective-permute-start(bf16[64,1280]{1,0:T(8,128)(2,1)S(1)} %get-tuple-element.42), channel_id=1, source_target_pairs={{0,3},{1,2},{2,1},{3,0},{4,7},{5,6},{6,5},{7,4},{8,11},{9,10},{10,... | collective-permute-start | bytes 491528 | tf_op jit(solution)/shard_map/ppermute | solution.py:199
  39.8 3.0 %collective-permute-start.8 = (bf16[64,1280]{1,0:T(8,128)(2,1)S(1)}, bf16[64,1280]{1,0:T(8,128)(2,1)S(1)}, u32[]{:S(2)}, u32[]{:S(2)}) collective-permute-start(bf16[64,1280]{1,0:T(8,128)(2,1)S(1)} %get-tuple-element.43), channel_id=1, source_target_pairs={{0,2},{1,3},{2,0},{3,1},{4,6},{5,7},{6,4},{7,5},{8,10},{9,11},{10,... | collective-permute-start | bytes 491528 | tf_op jit(solution)/shard_map/ppermute | solution.py:199
  42.7 1.9 %collective-permute-start.9 = (bf16[64,1280]{1,0:T(8,128)(2,1)S(1)}, bf16[64,1280]{1,0:T(8,128)(2,1)S(1)}, u32[]{:S(2)}, u32[]{:S(2)}) collective-permute-start(bf16[64,1280]{1,0:T(8,128)(2,1)S(1)} %get-tuple-element.44), channel_id=1, source_target_pairs={{0,1},{1,0},{2,3},{3,2},{4,5},{5,4},{6,7},{7,6},{8,9},{9,8},{10,11... | collective-permute-start | bytes 491528 | tf_op jit(solution)/shard_map/ppermute | solution.py:199
  48.8 4.9 %collective-permute-start.4 = (bf16[64,1024]{1,0:T(8,128)(2,1)S(1)}, bf16[64,1024]{1,0:T(8,128)(2,1)S(1)}, u32[]{:S(2)}, u32[]{:S(2)}) collective-permute-start(bf16[64,1024]{1,0:T(8,128)(2,1)S(1)} %get-tuple-element.39), channel_id=1, source_target_pairs={{0,3},{1,2},{2,1},{3,0},{4,7},{5,6},{6,5},{7,4},{8,11},{9,10},{10,... | collective-permute-start | bytes 393224 | tf_op jit(solution)/shard_map/ppermute | solution.py:199
  53.8 3.0 %collective-permute-start.5 = (bf16[64,1024]{1,0:T(8,128)(2,1)S(1)}, bf16[64,1024]{1,0:T(8,128)(2,1)S(1)}, u32[]{:S(2)}, u32[]{:S(2)}) collective-permute-start(bf16[64,1024]{1,0:T(8,128)(2,1)S(1)} %get-tuple-element.40), channel_id=1, source_target_pairs={{0,2},{1,3},{2,0},{3,1},{4,6},{5,7},{6,4},{7,5},{8,10},{9,11},{10,... | collective-permute-start | bytes 393224 | tf_op jit(solution)/shard_map/ppermute | solution.py:199
  56.8 1.9 %collective-permute-start.6 = (bf16[64,1024]{1,0:T(8,128)(2,1)S(1)}, bf16[64,1024]{1,0:T(8,128)(2,1)S(1)}, u32[]{:S(2)}, u32[]{:S(2)}) collective-permute-start(bf16[64,1024]{1,0:T(8,128)(2,1)S(1)} %get-tuple-element.41), channel_id=1, source_target_pairs={{0,1},{1,0},{2,3},{3,2},{4,5},{5,4},{6,7},{7,6},{8,9},{9,8},{10,11... | collective-permute-start | bytes 393224 | tf_op jit(solution)/shard_map/ppermute | solution.py:199
  58.7 2.3 %collective-permute-done.5.refs_2_ = bf16[64,1024]{1,0:T(8,128)(2,1)S(1)} collective-permute-done((bf16[64,1024]{1,0:T(8,128)(2,1)S(1)}, bf16[64,1024]{1,0:T(8,128)(2,1)S(1)}, u32[]{:S(2)}, u32[]{:S(2)}) %collective-permute-start.5) | collective-permute-done | bytes 131104 | tf_op jit(solution)/shard_map/ppermute | solution.py:199
  62.6 2.8 %collective-permute-start.10 = (bf16[64,1280]{1,0:T(8,128)(2,1)S(1)}, bf16[64,1280]{1,0:T(8,128)(2,1)S(1)}, u32[]{:S(2)}, u32[]{:S(2)}) collective-permute-start(bf16[64,1280]{1,0:T(8,128)(2,1)S(1)} %get-tuple-element.46), channel_id=1, source_target_pairs={{0,3},{1,2},{2,1},{3,0},{4,7},{5,6},{6,5},{7,4},{8,11},{9,10},{10,... | collective-permute-start | bytes 491528 | tf_op jit(solution)/shard_map/ppermute | solution.py:199
  65.5 2.9 %collective-permute-start.11 = (bf16[64,1280]{1,0:T(8,128)(2,1)S(1)}, bf16[64,1280]{1,0:T(8,128)(2,1)S(1)}, u32[]{:S(2)}, u32[]{:S(2)}) collective-permute-start(bf16[64,1280]{1,0:T(8,128)(2,1)S(1)} %get-tuple-element.47), channel_id=1, source_target_pairs={{0,2},{1,3},{2,0},{3,1},{4,6},{5,7},{6,4},{7,5},{8,10},{9,11},{10,... | collective-permute-start | bytes 491528 | tf_op jit(solution)/shard_map/ppermute | solution.py:199
  68.4 2.1 %collective-permute-start.12 = (bf16[64,1280]{1,0:T(8,128)(2,1)S(1)}, bf16[64,1280]{1,0:T(8,128)(2,1)S(1)}, u32[]{:S(2)}, u32[]{:S(2)}) collective-permute-start(bf16[64,1280]{1,0:T(8,128)(2,1)S(1)} %get-tuple-element.48), channel_id=1, source_target_pairs={{0,1},{1,0},{2,3},{3,2},{4,5},{5,4},{6,7},{7,6},{8,9},{9,8},{10,11... | collective-permute-start | bytes 491528 | tf_op jit(solution)/shard_map/ppermute | solution.py:199
  71.1 3.5 %collective-permute-done.11.refs_2_ = bf16[64,1280]{1,0:T(8,128)(2,1)S(1)} collective-permute-done((bf16[64,1280]{1,0:T(8,128)(2,1)S(1)}, bf16[64,1280]{1,0:T(8,128)(2,1)S(1)}, u32[]{:S(2)}, u32[]{:S(2)}) %collective-permute-start.11) | collective-permute-done | bytes 163872 | tf_op jit(solution)/shard_map/ppermute | solution.py:199
  76.0 1.9 %collective-permute-start.14 = (bf16[64,4096]{1,0:T(8,128)(2,1)S(1)}, bf16[64,4096]{1,0:T(8,128)(2,1)S(1)}, u32[]{:S(2)}, u32[]{:S(2)}) collective-permute-start(bf16[64,4096]{1,0:T(8,128)(2,1)S(1)} %get-tuple-element.51), channel_id=1, source_target_pairs={{0,4},{4,0},{8,12},{12,8},{16,20},{20,16},{24,28},{28,24},{32,36},... | collective-permute-start | bytes 1572872 | tf_op jit(solution)/shard_map/ppermute | solution.py:224
  77.9 6.2 %collective-permute-start.13 = (bf16[64,4096]{1,0:T(8,128)(2,1)S(1)}, bf16[64,4096]{1,0:T(8,128)(2,1)S(1)}, u32[]{:S(2)}, u32[]{:S(2)}) collective-permute-start(bf16[64,4096]{1,0:T(8,128)(2,1)S(1)} %get-tuple-element.50), channel_id=1, source_target_pairs={{4,8},{8,4},{12,16},{16,12},{20,24},{24,20},{28,32},{32,28},{36,40... | collective-permute-start | bytes 1572872 | tf_op jit(solution)/shard_map/ppermute | solution.py:227
  84.2 1.9 %collective-permute-start.15 = (f32[64,256]{1,0:T(8,128)S(1)}, f32[64,256]{1,0:T(8,128)S(1)}, u32[]{:S(2)}, u32[]{:S(2)}) collective-permute-start(f32[64,256]{1,0:T(8,128)S(1)} %convert_add_fusion), channel_id=1, source_target_pairs={{0,16},{16,0},{32,48},{48,32},{64,80},{80,64},{96,112},{112,96},{1... | collective-permute-start | bytes 196616 | tf_op jit(solution)/shard_map/ppermute | solution.py:210
  86.1 3.4 %collective-permute-done.15 = f32[64,256]{1,0:T(8,128)S(1)} collective-permute-done((f32[64,256]{1,0:T(8,128)S(1)}, f32[64,256]{1,0:T(8,128)S(1)}, u32[]{:S(2)}, u32[]{:S(2)}) %collective-permute-start.15) | collective-permute-done | bytes 65568 | tf_op jit(solution)/shard_map/ppermute | solution.py:210
  89.5 1.9 %collective-permute-start.16 = (f32[64,256]{1,0:T(8,128)S(1)}, f32[64,256]{1,0:T(8,128)S(1)}, u32[]{:S(2)}, u32[]{:S(2)}) collective-permute-start(f32[64,256]{1,0:T(8,128)S(1)} %add.31), channel_id=1, source_target_pairs={{0,32},{16,48},{32,0},{48,16},{64,96},{80,112},{96,64},{112,80},{1... | collective-permute-start | bytes 196616 | tf_op jit(solution)/shard_map/ppermute | solution.py:210
  91.4 4.3 %collective-permute-start.17 = (bf16[64,1024]{1,0:T(8,128)(2,1)S(1)}, bf16[64,1024]{1,0:T(8,128)(2,1)S(1)}, u32[]{:S(2)}, u32[]{:S(2)}) collective-permute-start(bf16[64,1024]{1,0:T(8,128)(2,1)S(1)} %get-tuple-element.56), channel_id=1, source_target_pairs={{0,3},{1,2},{2,1},{3,0},{4,7},{5,6},{6,5},{7,4},{8,11},{9,10},{10,... | collective-permute-start | bytes 393224 | tf_op jit(solution)/shard_map/ppermute | solution.py:199
  95.7 3.0 %collective-permute-start.18 = (bf16[64,1024]{1,0:T(8,128)(2,1)S(1)}, bf16[64,1024]{1,0:T(8,128)(2,1)S(1)}, u32[]{:S(2)}, u32[]{:S(2)}) collective-permute-start(bf16[64,1024]{1,0:T(8,128)(2,1)S(1)} %get-tuple-element.57), channel_id=1, source_target_pairs={{0,2},{1,3},{2,0},{3,1},{4,6},{5,7},{6,4},{7,5},{8,10},{9,11},{10,... | collective-permute-start | bytes 393224 | tf_op jit(solution)/shard_map/ppermute | solution.py:199
  98.7 2.0 %collective-permute-start.19 = (bf16[64,1024]{1,0:T(8,128)(2,1)S(1)}, bf16[64,1024]{1,0:T(8,128)(2,1)S(1)}, u32[]{:S(2)}, u32[]{:S(2)}) collective-permute-start(bf16[64,1024]{1,0:T(8,128)(2,1)S(1)} %get-tuple-element.58), channel_id=1, source_target_pairs={{0,1},{1,0},{2,3},{3,2},{4,5},{5,4},{6,7},{7,6},{8,9},{9,8},{10,11... | collective-permute-start | bytes 393224 | tf_op jit(solution)/shard_map/ppermute | solution.py:199
  103.0 1.9 %collective-permute-start.20 = (bf16[64,4096]{1,0:T(8,128)(2,1)S(1)}, bf16[64,4096]{1,0:T(8,128)(2,1)S(1)}, u32[]{:S(2)}, u32[]{:S(2)}) collective-permute-start(bf16[64,4096]{1,0:T(8,128)(2,1)S(1)} %shard_map.101), channel_id=1, source_target_pairs={{0,4},{4,0},{8,12},{12,8},{16,20},{20,16},{24,28},{28,24},{32,36},... | collective-permute-start | bytes 1572872 | tf_op jit(solution)/shard_map/ppermute | solution.py:224
  104.9 10.4 %collective-permute-start.21 = (bf16[64,4096]{1,0:T(8,128)(2,1)S(1)}, bf16[64,4096]{1,0:T(8,128)(2,1)S(1)}, u32[]{:S(2)}, u32[]{:S(2)}) collective-permute-start(bf16[64,4096]{1,0:T(8,128)(2,1)S(1)} %shard_map.100), channel_id=1, source_target_pairs={{4,8},{8,4},{12,16},{16,12},{20,24},{24,20},{28,32},{32,28},{36,40... | collective-permute-start | bytes 1572872 | tf_op jit(solution)/shard_map/ppermute | solution.py:227
  115.3 2.4 %collective-permute-start.24 = (f32[64,256]{1,0:T(8,128)S(1)}, f32[64,256]{1,0:T(8,128)S(1)}, u32[]{:S(2)}, u32[]{:S(2)}) collective-permute-start(f32[64,256]{1,0:T(8,128)S(1)} %add.32), channel_id=1, source_target_pairs={{0,192},{16,208},{32,224},{48,240},{64,128},{80,144},{96,160},{112... | collective-permute-start | bytes 196616 | tf_op jit(solution)/shard_map/ppermute | solution.py:210
  117.7 1.9 %collective-permute-start.23 = (f32[64,256]{1,0:T(8,128)S(1)}, f32[64,256]{1,0:T(8,128)S(1)}, u32[]{:S(2)}, u32[]{:S(2)}) collective-permute-start(f32[64,256]{1,0:T(8,128)S(1)} %add.32), channel_id=1, source_target_pairs={{0,64},{16,80},{32,96},{48,112},{64,0},{80,16},{96,32},{112,48},{1... | collective-permute-start | bytes 196616 | tf_op jit(solution)/shard_map/ppermute | solution.py:210
  119.6 11.8 %collective-permute-start.22 = (f32[64,256]{1,0:T(8,128)S(1)}, f32[64,256]{1,0:T(8,128)S(1)}, u32[]{:S(2)}, u32[]{:S(2)}) collective-permute-start(f32[64,256]{1,0:T(8,128)S(1)} %add.32), channel_id=1, source_target_pairs={{0,128},{16,144},{32,160},{48,176},{64,192},{80,208},{96,224},{112... | collective-permute-start | bytes 196616 | tf_op jit(solution)/shard_map/ppermute | solution.py:210
  131.5 6.0 %collective-permute-done.24 = f32[64,256]{1,0:T(8,128)S(1)} collective-permute-done((f32[64,256]{1,0:T(8,128)S(1)}, f32[64,256]{1,0:T(8,128)S(1)}, u32[]{:S(2)}, u32[]{:S(2)}) %collective-permute-start.24) | collective-permute-done | bytes 65568 | tf_op jit(solution)/shard_map/ppermute | solution.py:210
  137.5 2.0 %shard_map.102 = (bf16[64,4096]{1,0:T(8,128)(2,1)}, bf16[64,4096]{1,0:T(8,128)(2,1)}) custom-call(bf16[88,128,128]{2,1,0:T(8,128)(2,1)S(1)} %copy-done.1, s32[88]{0:T(128)S(1)} %copy-done.5, s32[88]{0:T(128)S(1)} %copy-done.6, s32[1]{0:T(128)S(6)} %copy.10.count, s32[2]{0:T(128)S(1)} %pad_add_fusion.place, bf16[4,64,1024]{2,1,0:T(8,128)(2,1)S(1)} %get-tuple-element.49.grad, ...), custom_call_target="tpu_custom_call" | custom-call | flops 37748736 | bytes 6030028 | tf_op jit(solution)/shard_map/pallas_call | solution.py:183
  139.5 11.9 %all_to_all.5 = bf16[8,64,256]{2,1,0:T(8,128)(2,1)S(1)} all-to-all(bf16[8,64,256]{2,1,0:T(8,128)(2,1)S(1)} %broadcast_in_dim.3), channel_id=1, replica_groups=mesh['yh'=2,'z'=16,'x'=4,'yl'=2,'core'=2] {'yh','x'}, dimensions={0} | all-to-all | bytes 524288 | tf_op jit(solution)/shard_map/all_to_all | solution.py:205
  (50 shorter events, 17.0 us)
Async XLA Ops:
  0.6 26.6 %collective-permute-start.1 = (bf16[64,4096]{1,0:T(8,128)(2,1)}, bf16[64,4096]{1,0:T(8,128)(2,1)S(1)}, u32[]{:S(2)}, u32[]{:S(2)}) collective-permute-start(bf16[64,4096]{1,0:T(8,128)(2,1)} %bitcast.9), channel_id=1, source_target_pairs={{0,4},{4,0},{8,12},{12,8},{16,20},{20,16},{24,28},{28,24},{32,36},... | collective-permute-start | bytes 1572872 | tf_op jit(solution)/shard_map/ppermute | solution.py:224
  4.6 29.2 %collective-permute-start = (bf16[64,4096]{1,0:T(8,128)(2,1)}, bf16[64,4096]{1,0:T(8,128)(2,1)S(1)}, u32[]{:S(2)}, u32[]{:S(2)}) collective-permute-start(bf16[64,4096]{1,0:T(8,128)(2,1)} %bitcast.10), channel_id=1, source_target_pairs={{4,8},{8,4},{12,16},{16,12},{20,24},{24,20},{28,32},{32,28},{36,40... | collective-permute-start | bytes 1572872 | tf_op jit(solution)/shard_map/ppermute | solution.py:227
  20.6 1.8 %copy-start = (bf16[88,128,128]{2,1,0:T(8,128)(2,1)S(1)}, bf16[88,128,128]{2,1,0:T(8,128)(2,1)}, u32[]{:S(2)}) copy-start(bf16[88,128,128]{2,1,0:T(8,128)(2,1)} %values.15) | copy-start | bytes 8650756
  22.4 1.0 copy-start.2
  23.5 1.0 copy-start.3
  24.5 0.8 copy-start.4
  25.3 0.7 copy-start.5
  25.9 0.7 copy-start.6
  27.2 19.8 %collective-permute-start.3 = (bf16[64,4096]{1,0:T(8,128)(2,1)S(1)}, bf16[64,4096]{1,0:T(8,128)(2,1)S(1)}, u32[]{:S(2)}, u32[]{:S(2)}) collective-permute-start(bf16[64,4096]{1,0:T(8,128)(2,1)S(1)} %collective-permute-done.1.even), channel_id=1, source_target_pairs={{4,8},{8,4},{12,16},{16,12},{20,24},{24,20},{28,32},{32,28},{36,40... | collective-permute-start | bytes 1572872 | tf_op jit(solution)/shard_map/ppermute | solution.py:227
  33.8 13.5 %collective-permute-start.2 = (bf16[64,4096]{1,0:T(8,128)(2,1)S(1)}, bf16[64,4096]{1,0:T(8,128)(2,1)S(1)}, u32[]{:S(2)}, u32[]{:S(2)}) collective-permute-start(bf16[64,4096]{1,0:T(8,128)(2,1)S(1)} %collective-permute-done.odd), channel_id=1, source_target_pairs={{0,4},{4,0},{8,12},{12,8},{16,20},{20,16},{24,28},{28,24},{32,36},... | collective-permute-start | bytes 1572872 | tf_op jit(solution)/shard_map/ppermute | solution.py:224
  35.7 21.0 %collective-permute-start.7 = (bf16[64,1280]{1,0:T(8,128)(2,1)S(1)}, bf16[64,1280]{1,0:T(8,128)(2,1)S(1)}, u32[]{:S(2)}, u32[]{:S(2)}) collective-permute-start(bf16[64,1280]{1,0:T(8,128)(2,1)S(1)} %get-tuple-element.42), channel_id=1, source_target_pairs={{0,3},{1,2},{2,1},{3,0},{4,7},{5,6},{6,5},{7,4},{8,11},{9,10},{10,... | collective-permute-start | bytes 491528 | tf_op jit(solution)/shard_map/ppermute | solution.py:199
  39.8 19.0 %collective-permute-start.8 = (bf16[64,1280]{1,0:T(8,128)(2,1)S(1)}, bf16[64,1280]{1,0:T(8,128)(2,1)S(1)}, u32[]{:S(2)}, u32[]{:S(2)}) collective-permute-start(bf16[64,1280]{1,0:T(8,128)(2,1)S(1)} %get-tuple-element.43), channel_id=1, source_target_pairs={{0,2},{1,3},{2,0},{3,1},{4,6},{5,7},{6,4},{7,5},{8,10},{9,11},{10,... | collective-permute-start | bytes 491528 | tf_op jit(solution)/shard_map/ppermute | solution.py:199
  42.7 16.0 %collective-permute-start.9 = (bf16[64,1280]{1,0:T(8,128)(2,1)S(1)}, bf16[64,1280]{1,0:T(8,128)(2,1)S(1)}, u32[]{:S(2)}, u32[]{:S(2)}) collective-permute-start(bf16[64,1280]{1,0:T(8,128)(2,1)S(1)} %get-tuple-element.44), channel_id=1, source_target_pairs={{0,1},{1,0},{2,3},{3,2},{4,5},{5,4},{6,7},{7,6},{8,9},{9,8},{10,11... | collective-permute-start | bytes 491528 | tf_op jit(solution)/shard_map/ppermute | solution.py:199
  45.8 28.9 %copy-start.1 = (bf16[88,128,128]{2,1,0:T(8,128)(2,1)S(1)}, bf16[88,128,128]{2,1,0:T(8,128)(2,1)}, u32[]{:S(2)}) copy-start(bf16[88,128,128]{2,1,0:T(8,128)(2,1)} %values.15) | copy-start | bytes 8650756
  48.8 9.9 %collective-permute-start.4 = (bf16[64,1024]{1,0:T(8,128)(2,1)S(1)}, bf16[64,1024]{1,0:T(8,128)(2,1)S(1)}, u32[]{:S(2)}, u32[]{:S(2)}) collective-permute-start(bf16[64,1024]{1,0:T(8,128)(2,1)S(1)} %get-tuple-element.39), channel_id=1, source_target_pairs={{0,3},{1,2},{2,1},{3,0},{4,7},{5,6},{6,5},{7,4},{8,11},{9,10},{10,... | collective-permute-start | bytes 393224 | tf_op jit(solution)/shard_map/ppermute | solution.py:199
  53.8 7.2 %collective-permute-start.5 = (bf16[64,1024]{1,0:T(8,128)(2,1)S(1)}, bf16[64,1024]{1,0:T(8,128)(2,1)S(1)}, u32[]{:S(2)}, u32[]{:S(2)}) collective-permute-start(bf16[64,1024]{1,0:T(8,128)(2,1)S(1)} %get-tuple-element.40), channel_id=1, source_target_pairs={{0,2},{1,3},{2,0},{3,1},{4,6},{5,7},{6,4},{7,5},{8,10},{9,11},{10,... | collective-permute-start | bytes 393224 | tf_op jit(solution)/shard_map/ppermute | solution.py:199
  56.8 4.2 %collective-permute-start.6 = (bf16[64,1024]{1,0:T(8,128)(2,1)S(1)}, bf16[64,1024]{1,0:T(8,128)(2,1)S(1)}, u32[]{:S(2)}, u32[]{:S(2)}) collective-permute-start(bf16[64,1024]{1,0:T(8,128)(2,1)S(1)} %get-tuple-element.41), channel_id=1, source_target_pairs={{0,1},{1,0},{2,3},{3,2},{4,5},{5,4},{6,7},{7,6},{8,9},{9,8},{10,11... | collective-permute-start | bytes 393224 | tf_op jit(solution)/shard_map/ppermute | solution.py:199
  62.6 8.5 %collective-permute-start.10 = (bf16[64,1280]{1,0:T(8,128)(2,1)S(1)}, bf16[64,1280]{1,0:T(8,128)(2,1)S(1)}, u32[]{:S(2)}, u32[]{:S(2)}) collective-permute-start(bf16[64,1280]{1,0:T(8,128)(2,1)S(1)} %get-tuple-element.46), channel_id=1, source_target_pairs={{0,3},{1,2},{2,1},{3,0},{4,7},{5,6},{6,5},{7,4},{8,11},{9,10},{10,... | collective-permute-start | bytes 491528 | tf_op jit(solution)/shard_map/ppermute | solution.py:199
  65.5 9.1 %collective-permute-start.11 = (bf16[64,1280]{1,0:T(8,128)(2,1)S(1)}, bf16[64,1280]{1,0:T(8,128)(2,1)S(1)}, u32[]{:S(2)}, u32[]{:S(2)}) collective-permute-start(bf16[64,1280]{1,0:T(8,128)(2,1)S(1)} %get-tuple-element.47), channel_id=1, source_target_pairs={{0,2},{1,3},{2,0},{3,1},{4,6},{5,7},{6,4},{7,5},{8,10},{9,11},{10,... | collective-permute-start | bytes 491528 | tf_op jit(solution)/shard_map/ppermute | solution.py:199
  68.4 6.2 %collective-permute-start.12 = (bf16[64,1280]{1,0:T(8,128)(2,1)S(1)}, bf16[64,1280]{1,0:T(8,128)(2,1)S(1)}, u32[]{:S(2)}, u32[]{:S(2)}) collective-permute-start(bf16[64,1280]{1,0:T(8,128)(2,1)S(1)} %get-tuple-element.48), channel_id=1, source_target_pairs={{0,1},{1,0},{2,3},{3,2},{4,5},{5,4},{6,7},{7,6},{8,9},{9,8},{10,11... | collective-permute-start | bytes 491528 | tf_op jit(solution)/shard_map/ppermute | solution.py:199
  76.0 24.8 %collective-permute-start.14 = (bf16[64,4096]{1,0:T(8,128)(2,1)S(1)}, bf16[64,4096]{1,0:T(8,128)(2,1)S(1)}, u32[]{:S(2)}, u32[]{:S(2)}) collective-permute-start(bf16[64,4096]{1,0:T(8,128)(2,1)S(1)} %get-tuple-element.51), channel_id=1, source_target_pairs={{0,4},{4,0},{8,12},{12,8},{16,20},{20,16},{24,28},{28,24},{32,36},... | collective-permute-start | bytes 1572872 | tf_op jit(solution)/shard_map/ppermute | solution.py:224
  77.9 23.8 %collective-permute-start.13 = (bf16[64,4096]{1,0:T(8,128)(2,1)S(1)}, bf16[64,4096]{1,0:T(8,128)(2,1)S(1)}, u32[]{:S(2)}, u32[]{:S(2)}) collective-permute-start(bf16[64,4096]{1,0:T(8,128)(2,1)S(1)} %get-tuple-element.50), channel_id=1, source_target_pairs={{4,8},{8,4},{12,16},{16,12},{20,24},{24,20},{28,32},{32,28},{36,40... | collective-permute-start | bytes 1572872 | tf_op jit(solution)/shard_map/ppermute | solution.py:227
  84.2 5.3 %collective-permute-start.15 = (f32[64,256]{1,0:T(8,128)S(1)}, f32[64,256]{1,0:T(8,128)S(1)}, u32[]{:S(2)}, u32[]{:S(2)}) collective-permute-start(f32[64,256]{1,0:T(8,128)S(1)} %convert_add_fusion), channel_id=1, source_target_pairs={{0,16},{16,0},{32,48},{48,32},{64,80},{80,64},{96,112},{112,96},{1... | collective-permute-start | bytes 196616 | tf_op jit(solution)/shard_map/ppermute | solution.py:210
  89.5 9.2 %collective-permute-start.16 = (f32[64,256]{1,0:T(8,128)S(1)}, f32[64,256]{1,0:T(8,128)S(1)}, u32[]{:S(2)}, u32[]{:S(2)}) collective-permute-start(f32[64,256]{1,0:T(8,128)S(1)} %add.31), channel_id=1, source_target_pairs={{0,32},{16,48},{32,0},{48,16},{64,96},{80,112},{96,64},{112,80},{1... | collective-permute-start | bytes 196616 | tf_op jit(solution)/shard_map/ppermute | solution.py:210
  91.4 11.2 %collective-permute-start.17 = (bf16[64,1024]{1,0:T(8,128)(2,1)S(1)}, bf16[64,1024]{1,0:T(8,128)(2,1)S(1)}, u32[]{:S(2)}, u32[]{:S(2)}) collective-permute-start(bf16[64,1024]{1,0:T(8,128)(2,1)S(1)} %get-tuple-element.56), channel_id=1, source_target_pairs={{0,3},{1,2},{2,1},{3,0},{4,7},{5,6},{6,5},{7,4},{8,11},{9,10},{10,... | collective-permute-start | bytes 393224 | tf_op jit(solution)/shard_map/ppermute | solution.py:199
  95.7 7.2 %collective-permute-start.18 = (bf16[64,1024]{1,0:T(8,128)(2,1)S(1)}, bf16[64,1024]{1,0:T(8,128)(2,1)S(1)}, u32[]{:S(2)}, u32[]{:S(2)}) collective-permute-start(bf16[64,1024]{1,0:T(8,128)(2,1)S(1)} %get-tuple-element.57), channel_id=1, source_target_pairs={{0,2},{1,3},{2,0},{3,1},{4,6},{5,7},{6,4},{7,5},{8,10},{9,11},{10,... | collective-permute-start | bytes 393224 | tf_op jit(solution)/shard_map/ppermute | solution.py:199
  98.7 4.2 %collective-permute-start.19 = (bf16[64,1024]{1,0:T(8,128)(2,1)S(1)}, bf16[64,1024]{1,0:T(8,128)(2,1)S(1)}, u32[]{:S(2)}, u32[]{:S(2)}) collective-permute-start(bf16[64,1024]{1,0:T(8,128)(2,1)S(1)} %get-tuple-element.58), channel_id=1, source_target_pairs={{0,1},{1,0},{2,3},{3,2},{4,5},{5,4},{6,7},{7,6},{8,9},{9,8},{10,11... | collective-permute-start | bytes 393224 | tf_op jit(solution)/shard_map/ppermute | solution.py:199
  103.0 34.5 %collective-permute-start.20 = (bf16[64,4096]{1,0:T(8,128)(2,1)S(1)}, bf16[64,4096]{1,0:T(8,128)(2,1)S(1)}, u32[]{:S(2)}, u32[]{:S(2)}) collective-permute-start(bf16[64,4096]{1,0:T(8,128)(2,1)S(1)} %shard_map.101), channel_id=1, source_target_pairs={{0,4},{4,0},{8,12},{12,8},{16,20},{20,16},{24,28},{28,24},{32,36},... | collective-permute-start | bytes 1572872 | tf_op jit(solution)/shard_map/ppermute | solution.py:224
  104.9 32.6 %collective-permute-start.21 = (bf16[64,4096]{1,0:T(8,128)(2,1)S(1)}, bf16[64,4096]{1,0:T(8,128)(2,1)S(1)}, u32[]{:S(2)}, u32[]{:S(2)}) collective-permute-start(bf16[64,4096]{1,0:T(8,128)(2,1)S(1)} %shard_map.100), channel_id=1, source_target_pairs={{4,8},{8,4},{12,16},{16,12},{20,24},{24,20},{28,32},{32,28},{36,40... | collective-permute-start | bytes 1572872 | tf_op jit(solution)/shard_map/ppermute | solution.py:227
  115.3 22.2 %collective-permute-start.24 = (f32[64,256]{1,0:T(8,128)S(1)}, f32[64,256]{1,0:T(8,128)S(1)}, u32[]{:S(2)}, u32[]{:S(2)}) collective-permute-start(f32[64,256]{1,0:T(8,128)S(1)} %add.32), channel_id=1, source_target_pairs={{0,192},{16,208},{32,224},{48,240},{64,128},{80,144},{96,160},{112... | collective-permute-start | bytes 196616 | tf_op jit(solution)/shard_map/ppermute | solution.py:210
  117.7 19.7 %collective-permute-start.23 = (f32[64,256]{1,0:T(8,128)S(1)}, f32[64,256]{1,0:T(8,128)S(1)}, u32[]{:S(2)}, u32[]{:S(2)}) collective-permute-start(f32[64,256]{1,0:T(8,128)S(1)} %add.32), channel_id=1, source_target_pairs={{0,64},{16,80},{32,96},{48,112},{64,0},{80,16},{96,32},{112,48},{1... | collective-permute-start | bytes 196616 | tf_op jit(solution)/shard_map/ppermute | solution.py:210
  119.6 17.8 %collective-permute-start.22 = (f32[64,256]{1,0:T(8,128)S(1)}, f32[64,256]{1,0:T(8,128)S(1)}, u32[]{:S(2)}, u32[]{:S(2)}) collective-permute-start(f32[64,256]{1,0:T(8,128)S(1)} %add.32), channel_id=1, source_target_pairs={{0,128},{16,144},{32,160},{48,176},{64,192},{80,208},{96,224},{112... | collective-permute-start | bytes 196616 | tf_op jit(solution)/shard_map/ppermute | solution.py:210
